TPU v7x, 32 devices: a whole 2x2x4 slice. The times are simulated.
32 devices in a mesh: groups: 2 (over y), rows: 4 (over z), tm: 2 (over x), cols: 2 (over core).
Axes of the slice: x: 2, y: 2, z: 4, core: 2. Of those that a mesh axis runs over, the one named last changes fastest.
Arguments:
- latents: bfloat16 [20, 4, 80, 384], P(('groups', 'tm'), 'rows', 'cols'), parts along dimension 0, may hold values from -16 to 16
- gain_one: float32 [384], replicated, may hold values from 0.1 to 1.9
- conv_one: bfloat16 [27, 384, 384], P(None, 'rows'), may hold values from -0.0625 to 0.0625
- bias_one: float32 [384], replicated, may hold values from -3 to 3
- gain_two: float32 [384], replicated, may hold values from 0.1 to 1.9
- conv_two: bfloat16 [27, 384, 384], P(None, 'rows'), may hold values from -0.0625 to 0.0625
- bias_two: float32 [384], replicated, may hold values from -3 to 3
Outputs:
- block_out: bfloat16 [20, 4, 80, 384], P(('groups', 'tm'), 'rows', 'cols'), parts along dimension 0
There are 2 independent parts, one for each index of `groups`. A program takes and returns all parts, laid end to end along the dimension named above; an argument that names none is the same for every part. Nothing has to cross between parts.
All inputs are finite; a program needn't handle non-finite values.
Results may differ from a plain program's by a relative error of at most 0.006.
Values may be sent and summed in bfloat16 or wider, within the bound.
No kernel may reach another device: no remote copies, remote signals or barrier semaphores. Data moves between devices by JAX's collectives and lax.ppermute only.
A program may use at most 64 MiB of HBM per device.

v0:
```python
import functools

import jax
import jax.numpy as jnp
from jax import lax
from jax.experimental import pallas as pl
from jax.experimental.pallas import tpu as pltpu
from jax.sharding import PartitionSpec as P


AXES = ("rows", "tm", "cols")
EDGE = 2
PAST = 2
TAPS = 3
VMEM = pltpu.VMEM


def activate(values, gain_values):
    values = values.astype(jnp.float32)
    mean_square = jnp.mean(values * values, axis=-1, keepdims=True)
    return jax.nn.silu(values * lax.rsqrt(mean_square + 1e-06) * gain_values)


def call(body, out_shape, scratch, flops, moved, *operands, far=()):
    operands = [pltpu.with_memory_space_constraint(v, pltpu.HBM) if i in far else v for i, v in enumerate(operands)]
    spaces = [pltpu.HBM if i in far else VMEM for i in range(len(operands))]
    return pl.pallas_call(
        body,
        out_shape=out_shape,
        in_specs=[pl.BlockSpec(memory_space=space) for space in spaces],
        out_specs=jax.tree.map(lambda _: pl.BlockSpec(memory_space=VMEM), out_shape),
        scratch_shapes=scratch,
        cost_estimate=pl.CostEstimate(flops=flops, bytes_accessed=moved, transcendentals=0),
        compiler_params=pltpu.CompilerParams(vmem_limit_bytes=48 << 20),
    )(*operands)


def ring_of(center, right, left):
    gap = jnp.zeros((8 - right.shape[0] - left.shape[0], center.shape[1]), center.dtype)
    return jnp.concatenate([center, right, gap, left], axis=0)


def padded_rows(count):
    return -(-count // 8) * 8


def own_part(vector, row, width):
    parts = vector.shape[1] // width
    return sum(jnp.where(row == s, vector[:, s * width : (s + 1) * width], 0.0) for s in range(parts))


def own_body(own_ref, *refs):
    count = (len(refs) - 3) // 2
    far, out_ref, near, (held, sems) = refs[:count], refs[count], refs[count + 1 : 2 * count + 1], refs[2 * count + 1 :]
    copies = [pltpu.make_async_copy(a, b, sems.at[i]) for i, (a, b) in enumerate(zip((own_ref, *far), (held, *near)))]
    for copy in copies:
        copy.start()
    copies[0].wait()
    copies[1].wait()
    frames, breadth, channels = held.shape
    values = activate(held[...], near[0][...].reshape(1, channels))
    out_ref[...] = values.reshape(frames * breadth, channels).astype(jnp.bfloat16)
    for copy in copies[2:]:
        copy.wait()


def ends_body(center_ref, other_ref, gain_ref, out_ref):
    frames, breadth, channels = other_ref.shape
    gain_values = gain_ref[...].reshape(1, channels)
    half = lax.axis_index("cols")
    right = jnp.where(half == 0, activate(other_ref[:, 0:EDGE], gain_values), 0.0)
    left = jnp.where(half == 1, activate(other_ref[:, breadth - EDGE : breadth], gain_values), 0.0)
    ends = [edge[f] for f in range(frames) for edge in (right, left)]
    count = frames * breadth
    rest = out_ref.shape[0] - count - 2 * EDGE * frames
    ends.append(jnp.zeros((rest, channels), jnp.float32))
    out_ref[0:count] = center_ref[...]
    out_ref[count:] = jnp.concatenate(ends, axis=0).astype(jnp.bfloat16)


def clear_ends(padded):
    edge = jnp.zeros((padded.shape[0],) + padded.shape[2:], padded.dtype)
    padded[:, 0] = edge
    padded[:, padded.shape[1] - 1] = edge


def fill_first(padded, at, rows_values, breadth, picks, ends):
    values = rows_values.astype(jnp.float32)
    for i, (frame, end) in enumerate(zip(picks, ends)):
        center = values[frame * breadth : (frame + 1) * breadth]
        right, left = values[end : end + EDGE], values[end + EDGE : end + 2 * EDGE]
        padded[i + at[0], at[1]] = ring_of(center, right, left).astype(jnp.bfloat16)


def conv_sum(padded, weight_ref, bias_row):
    frames, height, ring, channels = padded.shape[0] - PAST, padded.shape[1] - 2, padded.shape[2], padded.shape[3]
    width = weight_ref.shape[1] // TAPS
    count = frames * height * ring
    windows = [
        padded[t : t + frames, r : r + height].reshape(count, channels) for t in range(TAPS) for r in range(TAPS)
    ]
    kernels = [weight_ref[i] for i in range(TAPS * TAPS)]
    product = lax.dot_general(
        jnp.concatenate(windows, axis=1),
        jnp.concatenate(kernels, axis=1),
        (((1,), (1,)), ((), ())),
        preferred_element_type=jnp.float32,
    )
    product = product.reshape(frames * height, ring, TAPS * width)
    before = pltpu.roll(product[:, :, 0:width], 1, 1)
    after = pltpu.roll(product[:, :, 2 * width : 3 * width], ring - 1, 1)
    summed = before + product[:, :, width : 2 * width] + after + bias_row
    return summed.reshape(frames, height, ring, width)


def block_number():
    return lax.axis_index("tm") // 2 * 2 + lax.axis_index("cols")


def pack_first(summed, out_ref, breadth):
    frames, height, ring, width = summed.shape
    rest = out_ref.shape[0] - frames * (breadth + 2)
    packed = []
    for h in range(height):
        centers = [summed[f, h, 0:breadth] for f in range(frames)]
        ends = [summed[f, h, w : w + 1] for f in range(frames) for w in (breadth, ring - 1)]
        if rest:
            ends.append(jnp.zeros((rest, width), jnp.float32))
        packed.append(jnp.concatenate(centers + ends, axis=0))
    out_ref[...] = jnp.concatenate(packed, axis=1).astype(jnp.bfloat16)


def first_late_body(breadth, *refs):
    *pieces, weight_ref, bias_ref, out_ref, padded = refs
    row = lax.axis_index("rows")
    clear_ends(padded)
    frames = padded.shape[0]
    ends = [frames * breadth + 2 * EDGE * f for f in range(frames)]
    for k, piece in enumerate(pieces):
        fill_first(padded, (0, (row ^ k) + 1), piece[...], breadth, range(frames), ends)
    bias_row = own_part(bias_ref[...].reshape(1, -1), row, weight_ref.shape[1] // TAPS)
    pack_first(conv_sum(padded, weight_ref, bias_row), out_ref, breadth)


def first_early_body(breadth, frames, *refs):
    *pieces, past_ref, weight_ref, bias_ref, out_ref, padded = refs
    row = lax.axis_index("rows")
    clear_ends(padded)
    total = frames * breadth
    skipped = (frames - PAST) * breadth
    for k, piece in enumerate(pieces):
        past = past_ref[k]
        past = jnp.where(block_number() > 0, past, jnp.zeros_like(past))
        ends = [total + 2 * EDGE * (frames - PAST + j) - skipped for j in range(PAST)]
        fill_first(padded, (0, (row ^ k) + 1), past, breadth, range(PAST), ends)
        ends = [total + 2 * EDGE * j for j in range(PAST)]
        fill_first(padded, (PAST, (row ^ k) + 1), piece[...], breadth, range(PAST), ends)
    bias_row = own_part(bias_ref[...].reshape(1, -1), row, weight_ref.shape[1] // TAPS)
    pack_first(conv_sum(padded, weight_ref, bias_row), out_ref, breadth)


def regroup(pieces, gain_ref, held, breadth, frames, store):
    row = lax.axis_index("rows")
    half = lax.axis_index("tm") % 2
    height, channels = len(pieces), pieces[0].shape[1]
    width = channels // height
    for k, piece in enumerate(pieces):
        held[row ^ k] = piece[...].astype(jnp.float32)
    gain_values = gain_ref[...].reshape(1, channels)
    for h in range(height):
        joined = [held[s, :, h * width : (h + 1) * width] for s in range(height)]
        values = activate(jnp.concatenate(joined, axis=1), gain_values)
        for f in range(frames):
            end = frames * breadth + 2 * f
            right = jnp.where(half == 0, values[end : end + 1], 0.0)
            left = jnp.where(half == 1, values[end + 1 : end + 2], 0.0)
            ring = ring_of(values[f * breadth : (f + 1) * breadth], right, left)
            store(h, f, ring.astype(jnp.bfloat16))


def regroup_body(breadth, *refs):
    *pieces, gain_ref, out_ref, last_ref, held = refs
    middle, late = out_ref.shape[1], last_ref.shape[1]

    def store(h, f, ring):
        if f < middle:
            out_ref[h, f] = ring
        else:
            last_ref[h, f - middle] = ring

    regroup(pieces, gain_ref, held, breadth, middle + late, store)


def second_body(breadth, *refs):
    height = (len(refs) - 9) // 2
    pieces, refs = refs[:height], refs[height:]
    middle_ref, last_ref, past_ref, gain_ref, weight_ref, bias_ref = refs[:6]
    outs, (padded, held, branch) = refs[6 : 6 + height], refs[6 + height :]
    row = lax.axis_index("rows")
    clear_ends(padded)

    def store(h, f, ring):
        padded[PAST + f, h + 1] = ring

    regroup(pieces, gain_ref, held, breadth, PAST, store)
    middle, late = middle_ref.shape[1], last_ref.shape[1]
    for h in range(height):
        past = past_ref[h]
        padded[0:PAST, h + 1] = jnp.where(block_number() > 0, past, jnp.zeros_like(past))
        padded[2 * PAST : 2 * PAST + middle, h + 1] = middle_ref[h]
        padded[2 * PAST + middle : 2 * PAST + middle + late, h + 1] = last_ref[h]
    bias_row = own_part(bias_ref[...].reshape(1, -1), row, weight_ref.shape[1] // TAPS)
    summed = conv_sum(padded, weight_ref, bias_row)
    frames, width = summed.shape[0], summed.shape[3]
    for h in range(height):
        branch[h, 0 : frames * breadth] = summed[:, h, 0:breadth].reshape(frames * breadth, width)
    for k, out_ref in enumerate(outs):
        chosen = branch[row ^ k]
        rows = out_ref.shape[0]
        parts = [chosen[i * rows : (i + 1) * rows] for i in range(height)]
        out_ref[...] = jnp.concatenate(parts, axis=1).astype(jnp.bfloat16)


def last_body(latents_ref, *refs):
    *pieces, out_ref, held = refs
    row = lax.axis_index("rows")
    height = len(pieces)
    frames, breadth, channels = latents_ref.shape
    width = channels // height
    for k, piece in enumerate(pieces):
        values = piece[...].astype(jnp.float32)
        parts = [values[:, i * width : (i + 1) * width] for i in range(height)]
        held[row ^ k] = jnp.concatenate(parts, axis=0)
    branch = jnp.concatenate([held[s] for s in range(height)], axis=1)
    branch = branch[0 : frames * breadth].reshape(frames, breadth, channels)
    out_ref[...] = (latents_ref[...].astype(jnp.float32) + branch).astype(jnp.bfloat16)


def shards(shape, latents, gain_one, conv_one, bias_one, gain_two, conv_two, bias_two):
    rows, tm, cols = (shape[name] for name in AXES)
    frames, height, breadth, channels = latents.shape
    width = channels // rows
    ring = breadth + 8
    late, middle = frames - PAST, frames - 2 * PAST
    bf16, f32 = jnp.bfloat16, jnp.float32
    own = latents.reshape(frames, breadth, channels)
    every = [(z, x, c) for z in range(rows) for x in range(tm) for c in range(cols)]
    place = {device: i for i, device in enumerate(every)}

    def moved(values, target):
        return lax.ppermute(values, AXES, [(place[device], place[target(*device)]) for device in every])

    def turned(values, k):
        return moved(values, lambda z, x, c: (z ^ k, x // 2 * 2 + c, x % 2))

    def following(values):
        return moved(values, lambda z, x, c: (z, x, 1) if c == 0 else (z, (x + 2) % tm, 0))

    def spread(values):
        return [values] + [lax.ppermute(values, "rows", [(z, z ^ k) for z in range(rows)]) for k in range(1, rows)]

    other = lax.ppermute(own, "cols", [(0, 1), (1, 0)])
    weights = [w.reshape(TAPS * TAPS, TAPS * width, channels) for w in (conv_one, conv_two)]
    sds = jax.ShapeDtypeStruct
    size = frames * ring * channels
    work = 2 * ring * channels * rows * 27 * width

    def padded(count):
        return VMEM((count, rows + 2, ring, channels), bf16)

    total = padded_rows(frames * (breadth + 2 * EDGE))
    small = (gain_one, bias_one, gain_two, bias_two, weights[0])
    center, gain_one, bias_one, gain_two, bias_two, near = call(
        own_body, [sds((frames * breadth, channels), bf16)] + [sds(v.shape, v.dtype) for v in small],
        [VMEM((frames, breadth, channels), bf16), pltpu.SemaphoreType.DMA((1 + len(small),))],
        10 * size, 6 * size, own, *small, far=range(1 + len(small)),
    )
    act = call(ends_body, sds((total, channels), bf16), [], size, 4 * size, center, other, gain_one)
    pieces = [turned(act, k) for k in range(rows)]
    past = following(jnp.stack([piece[late * breadth :] for piece in pieces]))
    late_rows, early_rows = padded_rows(late * (breadth + 2)), padded_rows(PAST * (breadth + 2))
    part = call(
        functools.partial(first_late_body, breadth), sds((late_rows, channels), bf16), [padded(frames)],
        late * work, 20 * size, *pieces, near, bias_one,
    )
    late_parts = spread(part)
    part = call(
        functools.partial(first_early_body, breadth, frames), sds((early_rows, channels), bf16),
        [padded(2 * PAST)], PAST * work, 20 * size, *pieces, past, near, bias_one,
    )
    early_parts = spread(part)
    second, last = call(
        functools.partial(regroup_body, breadth),
        [sds((rows, middle, ring, channels), bf16), sds((rows, PAST, ring, channels), bf16)],
        [VMEM((rows, late_rows, channels), f32)], 10 * size * rows, 4 * size * rows, *late_parts, gain_two,
    )
    past = following(last)
    back_rows = padded_rows(-(-frames * breadth // rows))
    branch = call(
        functools.partial(second_body, breadth), [sds((back_rows, channels), bf16)] * rows,
        [padded(frames + PAST), VMEM((rows, early_rows, channels), f32), VMEM((rows, back_rows * rows, width), f32)],
        frames * work, 20 * size, *early_parts, second, last, past, gain_two, weights[1], bias_two,
    )
    branch = [turned(piece, k) for k, piece in enumerate(branch)]
    result = call(
        last_body, sds((frames, breadth, channels), bf16), [VMEM((rows, back_rows * rows, width), f32)],
        2 * size, 6 * size, own, *branch,
    )
    return result.reshape(frames, height, breadth, channels)


def solution(mesh):
    shape = dict(mesh.shape)
    return jax.shard_map(
        functools.partial(shards, shape),
        mesh=mesh,
        in_specs=(
            P(("groups", "tm"), "rows", "cols", None),
            P(),
            P(None, "rows", None),
            P(),
            P(),
            P(None, "rows", None),
            P(),
        ),
        out_specs=P(("groups", "tm"), "rows", "cols", None),
        check_vma=False,
    )
```

profile of v0, /device:TPU:1, one launch (start us, length us, event | category | flops | bytes accessed | tf_op | source)
XLA Modules:
  0.0 68.3 jit_solution(16934617980086615616)
XLA Ops:
  0.0 0.0 collective-permute-start
  0.0 1.8 %shard_map.73 = (bf16[200,384]{1,0:T(8,128)(2,1)S(1)}, f32[384]{0:T(512)S(1)}, f32[384]{0:T(512)S(1)}, f32[384]{0:T(512)S(1)}, f32[384]{0:T(512)S(1)}, /*index=5*/bf16[9,288,384]{2,1,0:T(8,128)(2,1)S(1)}) custom-call(bf16[5,40,384]{2,1,0:T(8,128)(2,1)} %bitcast.15, f32[384]{0:T(512)} %refs_0_.1, f32[384]{0:T(512)} %refs_1_.1, f32[384]{0:T(512)} %refs_2_.1, ...), custom_call_target="tpu_custom_call" | custom-call | flops 921600 | bytes 552960 | tf_op jit(solution)/shard_map/pallas_call | solution.py:27
  1.8 0.0 collective-permute-done.other_ref
  1.8 0.1 shard_map.74
  1.9 5.7 %collective-permute-start.4 = (bf16[224,384]{1,0:T(8,128)(2,1)S(1)}, bf16[224,384]{1,0:T(8,128)(2,1)S(1)}, u32[]{:S(2)}, u32[]{:S(2)}) collective-permute-start(bf16[224,384]{1,0:T(8,128)(2,1)S(1)} %shard_map.74), channel_id=1, source_target_pairs={{0,12},{1,14},{2,13},{3,15},{4,8},{5,10},{6,9},{7,11},{8,4},{9,6},... | collective-permute-start | bytes 516104 | tf_op jit(solution)/shard_map/ppermute | solution.py:251
  7.6 2.5 %collective-permute-start.1 = (bf16[224,384]{1,0:T(8,128)(2,1)S(1)}, bf16[224,384]{1,0:T(8,128)(2,1)S(1)}, u32[]{:S(2)}, u32[]{:S(2)}) collective-permute-start(bf16[224,384]{1,0:T(8,128)(2,1)S(1)} %shard_map.74), channel_id=1, source_target_pairs={{0,0},{1,2},{2,1},{3,3},{4,4},{5,6},{6,5},{7,7},{8,8},{9,10},{10,9... | collective-permute-start | bytes 516104 | tf_op jit(solution)/shard_map/ppermute | solution.py:251
  10.2 0.2 collective-permute-start.2
  10.3 1.0 %collective-permute-start.3 = (bf16[224,384]{1,0:T(8,128)(2,1)S(1)}, bf16[224,384]{1,0:T(8,128)(2,1)S(1)}, u32[]{:S(2)}, u32[]{:S(2)}) collective-permute-start(bf16[224,384]{1,0:T(8,128)(2,1)S(1)} %shard_map.74), channel_id=1, source_target_pairs={{0,8},{1,10},{2,9},{3,11},{4,12},{5,14},{6,13},{7,15},{8,0},{9,2},... | collective-permute-start | bytes 516104 | tf_op jit(solution)/shard_map/ppermute | solution.py:251
  11.3 1.2 %collective-permute-done.4.refs_3_ = bf16[224,384]{1,0:T(8,128)(2,1)S(1)} collective-permute-done((bf16[224,384]{1,0:T(8,128)(2,1)S(1)}, bf16[224,384]{1,0:T(8,128)(2,1)S(1)}, u32[]{:S(2)}, u32[]{:S(2)}) %collective-permute-start.4) | collective-permute-done | bytes 172064 | tf_op jit(solution)/shard_map/ppermute | solution.py:251
  12.6 10.0 %collective-permute-done.3.refs_2_ = bf16[224,384]{1,0:T(8,128)(2,1)S(1)} collective-permute-done((bf16[224,384]{1,0:T(8,128)(2,1)S(1)}, bf16[224,384]{1,0:T(8,128)(2,1)S(1)}, u32[]{:S(2)}, u32[]{:S(2)}) %collective-permute-start.3) | collective-permute-done | bytes 172064 | tf_op jit(solution)/shard_map/ppermute | solution.py:251
  22.6 0.0 collective-permute-done.2.refs_1_
  22.6 0.0 collective-permute-done.1.refs_0_
  22.6 0.1 pad_maximum_fusion
  22.7 0.1 collective-permute-start.5
  22.8 2.6 %shard_map.76.refs_0_ = bf16[128,384]{1,0:T(8,128)(2,1)S(1)} custom-call(bf16[224,384]{1,0:T(8,128)(2,1)S(1)} %collective-permute-done.1.refs_0_, bf16[224,384]{1,0:T(8,128)(2,1)S(1)} %collective-permute-done.2.refs_1_, bf16[224,384]{1,0:T(8,128)(2,1)S(1)} %collective-permute-done.3.refs_2_, bf16[224,384]{1,0:T(8,128)(2,1)S(1)} %collective-permute-done.4.refs_3_, ...), custom_call_target="tpu_custom_call" | custom-call | flops 1146617856 | bytes 1843200 | tf_op jit(solution)/shard_map/pallas_call | solution.py:27
  25.4 0.0 copy-start.1
  25.4 0.1 collective-permute-start.9
  25.5 2.5 %collective-permute-start.10 = (bf16[128,384]{1,0:T(8,128)(2,1)S(1)}, bf16[128,384]{1,0:T(8,128)(2,1)S(1)}, u32[]{:S(2)}, u32[]{:S(2)}) collective-permute-start(bf16[128,384]{1,0:T(8,128)(2,1)S(1)} %shard_map.76.refs_0_), channel_id=1, source_target_pairs={{0,8},{4,12},{8,0},{12,4},{1,9},{5,13},{9,1},{13,5},{2,10},{6,14},... | collective-permute-start | bytes 294920 | tf_op jit(solution)/shard_map/ppermute | solution.py:260
  28.0 1.1 %collective-permute-start.11 = (bf16[128,384]{1,0:T(8,128)(2,1)S(1)}, bf16[128,384]{1,0:T(8,128)(2,1)S(1)}, u32[]{:S(2)}, u32[]{:S(2)}) collective-permute-start(bf16[128,384]{1,0:T(8,128)(2,1)S(1)} %shard_map.76.refs_0_), channel_id=1, source_target_pairs={{0,12},{4,8},{8,4},{12,0},{1,13},{5,9},{9,5},{13,1},{2,14},{6,10},... | collective-permute-start | bytes 294920 | tf_op jit(solution)/shard_map/ppermute | solution.py:260
  29.0 1.5 %collective-permute-done.9.refs_1_ = bf16[128,384]{1,0:T(8,128)(2,1)S(1)} collective-permute-done((bf16[128,384]{1,0:T(8,128)(2,1)S(1)}, bf16[128,384]{1,0:T(8,128)(2,1)S(1)}, u32[]{:S(2)}, u32[]{:S(2)}) %collective-permute-start.9) | collective-permute-done | bytes 98336 | tf_op jit(solution)/shard_map/ppermute | solution.py:260
  30.5 0.0 collective-permute-done.10.refs_2_
  30.5 4.0 %collective-permute-done.11.refs_3_ = bf16[128,384]{1,0:T(8,128)(2,1)S(1)} collective-permute-done((bf16[128,384]{1,0:T(8,128)(2,1)S(1)}, bf16[128,384]{1,0:T(8,128)(2,1)S(1)}, u32[]{:S(2)}, u32[]{:S(2)}) %collective-permute-start.11) | collective-permute-done | bytes 98336 | tf_op jit(solution)/shard_map/ppermute | solution.py:260
  34.5 0.7 %shard_map.77 = (bf16[4,1,48,384]{3,2,1,0:T(8,128)(2,1)S(1)}, bf16[4,2,48,384]{3,2,1,0:T(8,128)(2,1)S(1)}) custom-call(bf16[128,384]{1,0:T(8,128)(2,1)S(1)} %shard_map.76.refs_0_, bf16[128,384]{1,0:T(8,128)(2,1)S(1)} %collective-permute-done.9.refs_1_, bf16[128,384]{1,0:T(8,128)(2,1)S(1)} %collective-permute-done.10.refs_2_, ...), custom_call_target="tpu_custom_call" | custom-call | flops 3686400 | bytes 1474560 | tf_op jit(solution)/shard_map/pallas_call | solution.py:27
  35.2 2.5 %collective-permute-start.12 = (bf16[4,2,48,384]{3,2,1,0:T(8,128)(2,1)S(1)}, bf16[4,2,48,384]{3,2,1,0:T(8,128)(2,1)S(1)}, u32[]{:S(2)}, u32[]{:S(2)}) collective-permute-start(bf16[4,2,48,384]{3,2,1,0:T(8,128)(2,1)S(1)} %get-tuple-element.23.refs_5_), channel_id=1, source_target_pairs={{0,1},{1,0},{2,3},{3,2},{4,5},{5,4},{6,7},{7,6},{8,9},{9,8},{10,11... | collective-permute-start | bytes 884744 | tf_op jit(solution)/shard_map/ppermute | solution.py:251
  37.7 0.0 collective-permute-done.5.refs_4_
  37.7 1.9 %shard_map.75.refs_0_ = bf16[88,384]{1,0:T(8,128)(2,1)S(1)} custom-call(bf16[224,384]{1,0:T(8,128)(2,1)S(1)} %collective-permute-done.1.refs_0_, bf16[224,384]{1,0:T(8,128)(2,1)S(1)} %collective-permute-done.2.refs_1_, bf16[224,384]{1,0:T(8,128)(2,1)S(1)} %collective-permute-done.3.refs_2_, bf16[224,384]{1,0:T(8,128)(2,1)S(1)} %collective-permute-done.4.refs_3_, ...), custom_call_target="tpu_custom_call" | custom-call | flops 764411904 | bytes 1843200 | tf_op jit(solution)/shard_map/pallas_call | solution.py:27
  39.6 1.5 %collective-permute-start.6 = (bf16[88,384]{1,0:T(8,128)(2,1)S(1)}, bf16[88,384]{1,0:T(8,128)(2,1)S(1)}, u32[]{:S(2)}, u32[]{:S(2)}) collective-permute-start(bf16[88,384]{1,0:T(8,128)(2,1)S(1)} %shard_map.75.refs_0_), channel_id=1, source_target_pairs={{0,4},{4,0},{8,12},{12,8},{1,5},{5,1},{9,13},{13,9},{2,6},{6,2},{1... | collective-permute-start | bytes 202760 | tf_op jit(solution)/shard_map/ppermute | solution.py:260
  41.1 1.1 %collective-permute-start.7 = (bf16[88,384]{1,0:T(8,128)(2,1)S(1)}, bf16[88,384]{1,0:T(8,128)(2,1)S(1)}, u32[]{:S(2)}, u32[]{:S(2)}) collective-permute-start(bf16[88,384]{1,0:T(8,128)(2,1)S(1)} %shard_map.75.refs_0_), channel_id=1, source_target_pairs={{0,8},{4,12},{8,0},{12,4},{1,9},{5,13},{9,1},{13,5},{2,10},{6,14},... | collective-permute-start | bytes 202760 | tf_op jit(solution)/shard_map/ppermute | solution.py:260
  42.2 1.1 %collective-permute-start.8 = (bf16[88,384]{1,0:T(8,128)(2,1)S(1)}, bf16[88,384]{1,0:T(8,128)(2,1)S(1)}, u32[]{:S(2)}, u32[]{:S(2)}) collective-permute-start(bf16[88,384]{1,0:T(8,128)(2,1)S(1)} %shard_map.75.refs_0_), channel_id=1, source_target_pairs={{0,12},{4,8},{8,4},{12,0},{1,13},{5,9},{9,5},{13,1},{2,14},{6,10},... | collective-permute-start | bytes 202760 | tf_op jit(solution)/shard_map/ppermute | solution.py:260
  43.3 0.1 collective-permute-done.6.refs_1_
  43.4 1.8 %collective-permute-done.7.refs_2_ = bf16[88,384]{1,0:T(8,128)(2,1)S(1)} collective-permute-done((bf16[88,384]{1,0:T(8,128)(2,1)S(1)}, bf16[88,384]{1,0:T(8,128)(2,1)S(1)}, u32[]{:S(2)}, u32[]{:S(2)}) %collective-permute-start.7) | collective-permute-done | bytes 67616 | tf_op jit(solution)/shard_map/ppermute | solution.py:260
  45.2 3.3 %collective-permute-done.8.refs_3_ = bf16[88,384]{1,0:T(8,128)(2,1)S(1)} collective-permute-done((bf16[88,384]{1,0:T(8,128)(2,1)S(1)}, bf16[88,384]{1,0:T(8,128)(2,1)S(1)}, u32[]{:S(2)}, u32[]{:S(2)}) %collective-permute-start.8) | collective-permute-done | bytes 67616 | tf_op jit(solution)/shard_map/ppermute | solution.py:260
  48.4 0.0 collective-permute-done.12.refs_6_
  48.4 0.0 copy-done.1
  48.4 0.0 copy-start
  48.4 4.5 %shard_map.78 = (bf16[56,384]{1,0:T(8,128)(2,1)S(1)}, bf16[56,384]{1,0:T(8,128)(2,1)S(1)}, bf16[56,384]{1,0:T(8,128)(2,1)S(1)}, bf16[56,384]{1,0:T(8,128)(2,1)S(1)}) custom-call(bf16[88,384]{1,0:T(8,128)(2,1)S(1)} %shard_map.75.refs_0_, bf16[88,384]{1,0:T(8,128)(2,1)S(1)} %collective-permute-done.6.refs_1_, ...), custom_call_target="tpu_custom_call" | custom-call | flops 1911029760 | bytes 1843200 | tf_op jit(solution)/shard_map/pallas_call | solution.py:27
  52.9 4.8 %collective-permute-start.13 = (bf16[56,384]{1,0:T(8,128)(2,1)S(1)}, bf16[56,384]{1,0:T(8,128)(2,1)S(1)}, u32[]{:S(2)}, u32[]{:S(2)}) collective-permute-start(bf16[56,384]{1,0:T(8,128)(2,1)S(1)} %get-tuple-element.25), channel_id=1, source_target_pairs={{0,0},{1,2},{2,1},{3,3},{4,4},{5,6},{6,5},{7,7},{8,8},{9,10},{10,9... | collective-permute-start | bytes 129032 | tf_op jit(solution)/shard_map/ppermute | solution.py:251
  57.7 1.0 %collective-permute-start.14 = (bf16[56,384]{1,0:T(8,128)(2,1)S(1)}, bf16[56,384]{1,0:T(8,128)(2,1)S(1)}, u32[]{:S(2)}, u32[]{:S(2)}) collective-permute-start(bf16[56,384]{1,0:T(8,128)(2,1)S(1)} %get-tuple-element.26), channel_id=1, source_target_pairs={{0,4},{1,6},{2,5},{3,7},{4,0},{5,2},{6,1},{7,3},{8,12},{9,14},{10,... | collective-permute-start | bytes 129032 | tf_op jit(solution)/shard_map/ppermute | solution.py:251
  58.7 2.4 %collective-permute-start.15 = (bf16[56,384]{1,0:T(8,128)(2,1)S(1)}, bf16[56,384]{1,0:T(8,128)(2,1)S(1)}, u32[]{:S(2)}, u32[]{:S(2)}) collective-permute-start(bf16[56,384]{1,0:T(8,128)(2,1)S(1)} %get-tuple-element.27), channel_id=1, source_target_pairs={{0,8},{1,10},{2,9},{3,11},{4,12},{5,14},{6,13},{7,15},{8,0},{9,2},... | collective-permute-start | bytes 129032 | tf_op jit(solution)/shard_map/ppermute | solution.py:251
  61.2 1.2 %collective-permute-start.16 = (bf16[56,384]{1,0:T(8,128)(2,1)S(1)}, bf16[56,384]{1,0:T(8,128)(2,1)S(1)}, u32[]{:S(2)}, u32[]{:S(2)}) collective-permute-start(bf16[56,384]{1,0:T(8,128)(2,1)S(1)} %get-tuple-element.28), channel_id=1, source_target_pairs={{0,12},{1,14},{2,13},{3,15},{4,8},{5,10},{6,9},{7,11},{8,4},{9,6},... | collective-permute-start | bytes 129032 | tf_op jit(solution)/shard_map/ppermute | solution.py:251
  62.4 0.0 collective-permute-done.13.refs_0_
  62.4 0.2 collective-permute-done.14.refs_1_
  62.6 1.4 %collective-permute-done.15.refs_2_ = bf16[56,384]{1,0:T(8,128)(2,1)S(1)} collective-permute-done((bf16[56,384]{1,0:T(8,128)(2,1)S(1)}, bf16[56,384]{1,0:T(8,128)(2,1)S(1)}, u32[]{:S(2)}, u32[]{:S(2)}) %collective-permute-start.15) | collective-permute-done | bytes 43040 | tf_op jit(solution)/shard_map/ppermute | solution.py:251
  64.0 3.3 %collective-permute-done.16.refs_3_ = bf16[56,384]{1,0:T(8,128)(2,1)S(1)} collective-permute-done((bf16[56,384]{1,0:T(8,128)(2,1)S(1)}, bf16[56,384]{1,0:T(8,128)(2,1)S(1)}, u32[]{:S(2)}, u32[]{:S(2)}) %collective-permute-start.16) | collective-permute-done | bytes 43040 | tf_op jit(solution)/shard_map/ppermute | solution.py:251
  67.3 0.0 copy-done
  67.3 1.0 %shard_map.79 = bf16[5,40,384]{2,1,0:T(8,128)(2,1)} custom-call(bf16[5,40,384]{2,1,0:T(8,128)(2,1)S(1)} %bitcast.16, bf16[56,384]{1,0:T(8,128)(2,1)S(1)} %collective-permute-done.13.refs_0_, bf16[56,384]{1,0:T(8,128)(2,1)S(1)} %collective-permute-done.14.refs_1_, bf16[56,384]{1,0:T(8,128)(2,1)S(1)} %collective-permute-done.15.refs_2_, ...), custom_call_target="tpu_custom_call" | custom-call | flops 184320 | bytes 552960 | tf_op jit(solution)/shard_map/pallas_call | solution.py:27
  (4 shorter events, 0.0 us)
Async XLA Ops:
  0.0 1.8 %collective-permute-start = (bf16[5,40,384]{2,1,0:T(8,128)(2,1)}, bf16[5,40,384]{2,1,0:T(8,128)(2,1)S(1)}, u32[]{:S(2)}, u32[]{:S(2)}) collective-permute-start(bf16[5,40,384]{2,1,0:T(8,128)(2,1)} %bitcast.14), channel_id=1, source_target_pairs={{0,1},{1,0},{2,3},{3,2},{4,5},{5,4},{6,7},{7,6},{8,9},{9,8},{10,11... | collective-permute-start | bytes 460808 | tf_op jit(solution)/shard_map/ppermute | solution.py:262
  1.9 10.7 %collective-permute-start.4 = (bf16[224,384]{1,0:T(8,128)(2,1)S(1)}, bf16[224,384]{1,0:T(8,128)(2,1)S(1)}, u32[]{:S(2)}, u32[]{:S(2)}) collective-permute-start(bf16[224,384]{1,0:T(8,128)(2,1)S(1)} %shard_map.74), channel_id=1, source_target_pairs={{0,12},{1,14},{2,13},{3,15},{4,8},{5,10},{6,9},{7,11},{8,4},{9,6},... | collective-permute-start | bytes 516104 | tf_op jit(solution)/shard_map/ppermute | solution.py:251
  7.6 15.0 %collective-permute-start.1 = (bf16[224,384]{1,0:T(8,128)(2,1)S(1)}, bf16[224,384]{1,0:T(8,128)(2,1)S(1)}, u32[]{:S(2)}, u32[]{:S(2)}) collective-permute-start(bf16[224,384]{1,0:T(8,128)(2,1)S(1)} %shard_map.74), channel_id=1, source_target_pairs={{0,0},{1,2},{2,1},{3,3},{4,4},{5,6},{6,5},{7,7},{8,8},{9,10},{10,9... | collective-permute-start | bytes 516104 | tf_op jit(solution)/shard_map/ppermute | solution.py:251
  10.2 12.4 %collective-permute-start.2 = (bf16[224,384]{1,0:T(8,128)(2,1)S(1)}, bf16[224,384]{1,0:T(8,128)(2,1)S(1)}, u32[]{:S(2)}, u32[]{:S(2)}) collective-permute-start(bf16[224,384]{1,0:T(8,128)(2,1)S(1)} %shard_map.74), channel_id=1, source_target_pairs={{0,4},{1,6},{2,5},{3,7},{4,0},{5,2},{6,1},{7,3},{8,12},{9,14},{10,... | collective-permute-start | bytes 516104 | tf_op jit(solution)/shard_map/ppermute | solution.py:251
  10.3 12.3 %collective-permute-start.3 = (bf16[224,384]{1,0:T(8,128)(2,1)S(1)}, bf16[224,384]{1,0:T(8,128)(2,1)S(1)}, u32[]{:S(2)}, u32[]{:S(2)}) collective-permute-start(bf16[224,384]{1,0:T(8,128)(2,1)S(1)} %shard_map.74), channel_id=1, source_target_pairs={{0,8},{1,10},{2,9},{3,11},{4,12},{5,14},{6,13},{7,15},{8,0},{9,2},... | collective-permute-start | bytes 516104 | tf_op jit(solution)/shard_map/ppermute | solution.py:251
  22.7 15.0 %collective-permute-start.5 = (bf16[4,104,384]{2,1,0:T(8,128)(2,1)S(1)}, bf16[4,104,384]{2,1,0:T(8,128)(2,1)S(1)}, u32[]{:S(2)}, u32[]{:S(2)}) collective-permute-start(bf16[4,104,384]{2,1,0:T(8,128)(2,1)S(1)} %pad_maximum_fusion), channel_id=1, source_target_pairs={{0,1},{1,0},{2,3},{3,2},{4,5},{5,4},{6,7},{7,6},{8,9},{9,8},{10,11... | collective-permute-start | bytes 958472 | tf_op jit(solution)/shard_map/ppermute | solution.py:251
  25.4 23.0 %copy-start.1 = (bf16[27,96,384]{2,1,0:T(8,128)(2,1)S(1)}, bf16[27,96,384]{2,1,0:T(8,128)(2,1)}, u32[]{:S(2)}) copy-start(bf16[27,96,384]{2,1,0:T(8,128)(2,1)} %param.12) | copy-start | bytes 5971972
  25.4 5.1 %collective-permute-start.9 = (bf16[128,384]{1,0:T(8,128)(2,1)S(1)}, bf16[128,384]{1,0:T(8,128)(2,1)S(1)}, u32[]{:S(2)}, u32[]{:S(2)}) collective-permute-start(bf16[128,384]{1,0:T(8,128)(2,1)S(1)} %shard_map.76.refs_0_), channel_id=1, source_target_pairs={{0,4},{4,0},{8,12},{12,8},{1,5},{5,1},{9,13},{13,9},{2,6},{6,2},{1... | collective-permute-start | bytes 294920 | tf_op jit(solution)/shard_map/ppermute | solution.py:260
  25.5 5.0 %collective-permute-start.10 = (bf16[128,384]{1,0:T(8,128)(2,1)S(1)}, bf16[128,384]{1,0:T(8,128)(2,1)S(1)}, u32[]{:S(2)}, u32[]{:S(2)}) collective-permute-start(bf16[128,384]{1,0:T(8,128)(2,1)S(1)} %shard_map.76.refs_0_), channel_id=1, source_target_pairs={{0,8},{4,12},{8,0},{12,4},{1,9},{5,13},{9,1},{13,5},{2,10},{6,14},... | collective-permute-start | bytes 294920 | tf_op jit(solution)/shard_map/ppermute | solution.py:260
  28.0 6.5 %collective-permute-start.11 = (bf16[128,384]{1,0:T(8,128)(2,1)S(1)}, bf16[128,384]{1,0:T(8,128)(2,1)S(1)}, u32[]{:S(2)}, u32[]{:S(2)}) collective-permute-start(bf16[128,384]{1,0:T(8,128)(2,1)S(1)} %shard_map.76.refs_0_), channel_id=1, source_target_pairs={{0,12},{4,8},{8,4},{12,0},{1,13},{5,9},{9,5},{13,1},{2,14},{6,10},... | collective-permute-start | bytes 294920 | tf_op jit(solution)/shard_map/ppermute | solution.py:260
  35.2 13.2 %collective-permute-start.12 = (bf16[4,2,48,384]{3,2,1,0:T(8,128)(2,1)S(1)}, bf16[4,2,48,384]{3,2,1,0:T(8,128)(2,1)S(1)}, u32[]{:S(2)}, u32[]{:S(2)}) collective-permute-start(bf16[4,2,48,384]{3,2,1,0:T(8,128)(2,1)S(1)} %get-tuple-element.23.refs_5_), channel_id=1, source_target_pairs={{0,1},{1,0},{2,3},{3,2},{4,5},{5,4},{6,7},{7,6},{8,9},{9,8},{10,11... | collective-permute-start | bytes 884744 | tf_op jit(solution)/shard_map/ppermute | solution.py:251
  39.6 3.7 %collective-permute-start.6 = (bf16[88,384]{1,0:T(8,128)(2,1)S(1)}, bf16[88,384]{1,0:T(8,128)(2,1)S(1)}, u32[]{:S(2)}, u32[]{:S(2)}) collective-permute-start(bf16[88,384]{1,0:T(8,128)(2,1)S(1)} %shard_map.75.refs_0_), channel_id=1, source_target_pairs={{0,4},{4,0},{8,12},{12,8},{1,5},{5,1},{9,13},{13,9},{2,6},{6,2},{1... | collective-permute-start | bytes 202760 | tf_op jit(solution)/shard_map/ppermute | solution.py:260
  41.1 4.0 %collective-permute-start.7 = (bf16[88,384]{1,0:T(8,128)(2,1)S(1)}, bf16[88,384]{1,0:T(8,128)(2,1)S(1)}, u32[]{:S(2)}, u32[]{:S(2)}) collective-permute-start(bf16[88,384]{1,0:T(8,128)(2,1)S(1)} %shard_map.75.refs_0_), channel_id=1, source_target_pairs={{0,8},{4,12},{8,0},{12,4},{1,9},{5,13},{9,1},{13,5},{2,10},{6,14},... | collective-permute-start | bytes 202760 | tf_op jit(solution)/shard_map/ppermute | solution.py:260
  42.2 6.3 %collective-permute-start.8 = (bf16[88,384]{1,0:T(8,128)(2,1)S(1)}, bf16[88,384]{1,0:T(8,128)(2,1)S(1)}, u32[]{:S(2)}, u32[]{:S(2)}) collective-permute-start(bf16[88,384]{1,0:T(8,128)(2,1)S(1)} %shard_map.75.refs_0_), channel_id=1, source_target_pairs={{0,12},{4,8},{8,4},{12,0},{1,13},{5,9},{9,5},{13,1},{2,14},{6,10},... | collective-permute-start | bytes 202760 | tf_op jit(solution)/shard_map/ppermute | solution.py:260
  48.4 18.9 %copy-start = (bf16[5,1,40,384]{3,2,1,0:T(8,128)(2,1)S(1)}, bf16[5,1,40,384]{3,2,1,0:T(8,128)(2,1)}, u32[]{:S(2)}) copy-start(bf16[5,1,40,384]{3,2,1,0:T(8,128)(2,1)} %param.7) | copy-start | bytes 460804
  52.9 9.5 %collective-permute-start.13 = (bf16[56,384]{1,0:T(8,128)(2,1)S(1)}, bf16[56,384]{1,0:T(8,128)(2,1)S(1)}, u32[]{:S(2)}, u32[]{:S(2)}) collective-permute-start(bf16[56,384]{1,0:T(8,128)(2,1)S(1)} %get-tuple-element.25), channel_id=1, source_target_pairs={{0,0},{1,2},{2,1},{3,3},{4,4},{5,6},{6,5},{7,7},{8,8},{9,10},{10,9... | collective-permute-start | bytes 129032 | tf_op jit(solution)/shard_map/ppermute | solution.py:251
  57.7 4.9 %collective-permute-start.14 = (bf16[56,384]{1,0:T(8,128)(2,1)S(1)}, bf16[56,384]{1,0:T(8,128)(2,1)S(1)}, u32[]{:S(2)}, u32[]{:S(2)}) collective-permute-start(bf16[56,384]{1,0:T(8,128)(2,1)S(1)} %get-tuple-element.26), channel_id=1, source_target_pairs={{0,4},{1,6},{2,5},{3,7},{4,0},{5,2},{6,1},{7,3},{8,12},{9,14},{10,... | collective-permute-start | bytes 129032 | tf_op jit(solution)/shard_map/ppermute | solution.py:251
  58.7 5.3 %collective-permute-start.15 = (bf16[56,384]{1,0:T(8,128)(2,1)S(1)}, bf16[56,384]{1,0:T(8,128)(2,1)S(1)}, u32[]{:S(2)}, u32[]{:S(2)}) collective-permute-start(bf16[56,384]{1,0:T(8,128)(2,1)S(1)} %get-tuple-element.27), channel_id=1, source_target_pairs={{0,8},{1,10},{2,9},{3,11},{4,12},{5,14},{6,13},{7,15},{8,0},{9,2},... | collective-permute-start | bytes 129032 | tf_op jit(solution)/shard_map/ppermute | solution.py:251
  61.2 6.1 %collective-permute-start.16 = (bf16[56,384]{1,0:T(8,128)(2,1)S(1)}, bf16[56,384]{1,0:T(8,128)(2,1)S(1)}, u32[]{:S(2)}, u32[]{:S(2)}) collective-permute-start(bf16[56,384]{1,0:T(8,128)(2,1)S(1)} %get-tuple-element.28), channel_id=1, source_target_pairs={{0,12},{1,14},{2,13},{3,15},{4,8},{5,10},{6,9},{7,11},{8,4},{9,6},... | collective-permute-start | bytes 129032 | tf_op jit(solution)/shard_map/ppermute | solution.py:251
where the time goes:
time: 68.4 us; the launch traced here: 68.3 us
  starting transfers between devices  28.7 us (42%)
  waiting for transfers between devices  26.8 us (39%)
  Pallas kernels  12.5 us (18%)
    ppermute x10, starting transfers between devices, moved(): lax.ppermute(values, AXES, [(place[device], place[target(*device)]) for d...  21.4 us
    ppermute x10, waiting for transfers between devices, moved(): lax.ppermute(values, AXES, [(place[device], place[target(*device)]) for d...  16.2 us
    pallas_call x7, Pallas kernels, call(): pl.pallas_call(body, out_shape=out_shape, in_specs=[pl.BlockSpec(memory_s...  12.5 us
    ppermute x6, waiting for transfers between devices, spread(): lax.ppermute(values, 'rows', [(z, z ^ k) for z in range(rows)])  10.6 us
    ppermute x6, starting transfers between devices, spread(): lax.ppermute(values, 'rows', [(z, z ^ k) for z in range(rows)])  7.27 us
  transfers between devices with their start and end apart: 17, of which 10 were waited for; matrix products, arithmetic and copies ran while one was open for 0% of the time, Pallas kernels for 10%

commit v1 on v0

v1 whole, which is shorter than its diff:
```python
import functools

import jax
import jax.numpy as jnp
from jax import lax
from jax.experimental import pallas as pl
from jax.experimental.pallas import tpu as pltpu
from jax.sharding import PartitionSpec as P


AXES = ("rows", "tm", "cols")
EDGE = 2
PAST = 2
TAPS = 3
VMEM = pltpu.VMEM


def activate(values, gain_values):
    values = values.astype(jnp.float32)
    mean_square = jnp.mean(values * values, axis=-1, keepdims=True)
    return jax.nn.silu(values * lax.rsqrt(mean_square + 1e-06) * gain_values)


def call(body, out_shape, scratch, flops, moved, *operands, far=()):
    operands = [pltpu.with_memory_space_constraint(v, pltpu.HBM) if i in far else v for i, v in enumerate(operands)]
    spaces = [pltpu.HBM if i in far else VMEM for i in range(len(operands))]
    return pl.pallas_call(
        body,
        out_shape=out_shape,
        in_specs=[pl.BlockSpec(memory_space=space) for space in spaces],
        out_specs=jax.tree.map(lambda _: pl.BlockSpec(memory_space=VMEM), out_shape),
        scratch_shapes=scratch,
        cost_estimate=pl.CostEstimate(flops=flops, bytes_accessed=moved, transcendentals=0),
        compiler_params=pltpu.CompilerParams(vmem_limit_bytes=48 << 20),
    )(*operands)


def ring_of(center, end, half):
    gap = jnp.zeros((8 - end.shape[0], center.shape[1]), center.dtype)
    after = jnp.concatenate([end, gap], axis=0)
    before = jnp.concatenate([gap, end], axis=0)
    return jnp.concatenate([center, jnp.where(half == 0, after, before)], axis=0)


def padded_rows(count):
    return -(-count // 8) * 8


def own_part(vector, row, width):
    parts = vector.shape[1] // width
    return sum(jnp.where(row == s, vector[:, s * width : (s + 1) * width], 0.0) for s in range(parts))


def own_body(own_ref, far_gain_ref, out_ref, gain_ref, held, sems):
    copies = [
        pltpu.make_async_copy(own_ref, held, sems.at[0]),
        pltpu.make_async_copy(far_gain_ref, gain_ref, sems.at[1]),
    ]
    for copy in copies:
        copy.start()
    for copy in copies:
        copy.wait()
    frames, breadth, channels = held.shape
    values = activate(held[...], gain_ref[...].reshape(1, channels))
    out_ref[...] = values.reshape(frames * breadth, channels).astype(jnp.bfloat16)


def ends_body(other_ref, gain_ref, *refs):
    count = (len(refs) - 2) // 2
    far, out_ref, near, sems = refs[:count], refs[count], refs[count + 1 : 2 * count + 1], refs[2 * count + 1]
    copies = [pltpu.make_async_copy(a, b, sems.at[i]) for i, (a, b) in enumerate(zip(far, near))]
    for copy in copies:
        copy.start()
    frames, breadth, channels = other_ref.shape
    half = lax.axis_index("cols")
    chosen = jnp.where(half == 0, other_ref[:, 0:8].astype(jnp.float32), other_ref[:, breadth - 8 :].astype(jnp.float32))
    values = activate(chosen, gain_ref[...].reshape(1, channels))
    ends = [jnp.where(half == 0, values[f, 0:EDGE], values[f, 8 - EDGE : 8]) for f in range(frames)]
    rest = out_ref.shape[0] - EDGE * frames
    if rest:
        ends.append(jnp.zeros((rest, channels), jnp.float32))
    out_ref[...] = jnp.concatenate(ends, axis=0).astype(jnp.bfloat16)
    for copy in copies:
        copy.wait()


def fill_first(padded, at, centers, ends, picks, breadth):
    half = lax.axis_index("tm") % 2
    for i, (frame, end) in enumerate(picks):
        center = centers[frame * breadth : (frame + 1) * breadth]
        padded[i + at[0], at[1]] = ring_of(center, ends[end * EDGE : (end + 1) * EDGE], half).astype(jnp.bfloat16)


def conv_sum(padded, weight_ref, bias_row):
    frames, height, ring, channels = padded.shape[0] - PAST, padded.shape[1], padded.shape[2], padded.shape[3]
    wide = weight_ref.shape[1] // TAPS
    width = wide // TAPS
    windows = [padded[t : t + frames].reshape(frames * height * ring, channels) for t in range(TAPS)]
    product = lax.dot_general(
        jnp.concatenate(windows, axis=1),
        jnp.concatenate([weight_ref[t] for t in range(TAPS)], axis=1),
        (((1,), (1,)), ((), ())),
        preferred_element_type=jnp.float32,
    )
    product = product.reshape(frames, height, ring, TAPS * wide)
    rows = []
    for h in range(height):
        near = [
            product[:, h + r - 1, :, r * wide : (r + 1) * wide] for r in range(TAPS) if 0 <= h + r - 1 < height
        ]
        row = sum(near[1:], near[0])
        before = pltpu.roll(row[:, :, 0:width], 1, 1)
        after = pltpu.roll(row[:, :, 2 * width : 3 * width], ring - 1, 1)
        rows.append(before + row[:, :, width : 2 * width] + after + bias_row)
    return rows


def block_number():
    return lax.axis_index("tm") // 2 * 2 + lax.axis_index("cols")


def pack_first(rows, out_ref, breadth):
    half = lax.axis_index("tm") % 2
    frames, ring, width = rows[0].shape
    rest = out_ref.shape[0] - frames * (breadth + 1)
    packed = []
    for row in rows:
        centers = [row[f, 0:breadth] for f in range(frames)]
        ends = [jnp.where(half == 0, row[f, breadth : breadth + 1], row[f, ring - 1 : ring]) for f in range(frames)]
        if rest:
            ends.append(jnp.zeros((rest, width), jnp.float32))
        packed.append(jnp.concatenate(centers + ends, axis=0))
    out_ref[...] = jnp.concatenate(packed, axis=1).astype(jnp.bfloat16)


def bias_part(bias_ref, row, weight_ref):
    return own_part(bias_ref[...].reshape(1, -1), row, weight_ref.shape[1] // TAPS // TAPS)


def first_late_body(breadth, height, *refs):
    centers, ends = refs[:height], refs[height : 2 * height]
    weight_ref, bias_ref, out_ref, padded = refs[2 * height :]
    row = lax.axis_index("rows")
    picks = [(f, f) for f in range(padded.shape[0])]
    for k in range(height):
        center, end = centers[k][...].astype(jnp.float32), ends[k][...].astype(jnp.float32)
        fill_first(padded, (0, row ^ k), center, end, picks, breadth)
    pack_first(conv_sum(padded, weight_ref, bias_part(bias_ref, row, weight_ref)), out_ref, breadth)


def first_early_body(breadth, height, frames, *refs):
    centers, ends = refs[:height], refs[height : 2 * height]
    past_ref, weight_ref, bias_ref, out_ref, padded = refs[2 * height :]
    row = lax.axis_index("rows")
    for k in range(height):
        past = past_ref[k].astype(jnp.float32)
        past = jnp.where(block_number() > 0, past, jnp.zeros_like(past))
        picks = [(j, frames - PAST + j) for j in range(PAST)]
        fill_first(padded, (0, row ^ k), past[0 : PAST * breadth], past[PAST * breadth :], picks, breadth)
        center, end = centers[k][0 : PAST * breadth].astype(jnp.float32), ends[k][...].astype(jnp.float32)
        fill_first(padded, (PAST, row ^ k), center, end, [(j, j) for j in range(PAST)], breadth)
    pack_first(conv_sum(padded, weight_ref, bias_part(bias_ref, row, weight_ref)), out_ref, breadth)


def regroup(pieces, gain_ref, held, breadth, frames, store):
    row = lax.axis_index("rows")
    half = lax.axis_index("tm") % 2
    height, channels = len(pieces), pieces[0].shape[1]
    width = channels // height
    for k, piece in enumerate(pieces):
        held[row ^ k] = piece[...].astype(jnp.float32)
    gain_values = gain_ref[...].reshape(1, channels)
    for h in range(height):
        joined = [held[s, :, h * width : (h + 1) * width] for s in range(height)]
        values = activate(jnp.concatenate(joined, axis=1), gain_values)
        for f in range(frames):
            end = frames * breadth + f
            ring = ring_of(values[f * breadth : (f + 1) * breadth], values[end : end + 1], half)
            store(h, f, ring.astype(jnp.bfloat16))


def regroup_body(breadth, *refs):
    *pieces, gain_ref, out_ref, last_ref, held = refs
    middle, late = out_ref.shape[1], last_ref.shape[1]

    def store(h, f, ring):
        if f < middle:
            out_ref[h, f] = ring
        else:
            last_ref[h, f - middle] = ring

    regroup(pieces, gain_ref, held, breadth, middle + late, store)


def second_body(breadth, *refs):
    height = (len(refs) - 9) // 2
    pieces, refs = refs[:height], refs[height:]
    middle_ref, last_ref, past_ref, gain_ref, weight_ref, bias_ref = refs[:6]
    outs, (padded, held, branch) = refs[6 : 6 + height], refs[6 + height :]
    row = lax.axis_index("rows")

    def store(h, f, ring):
        padded[PAST + f, h] = ring

    regroup(pieces, gain_ref, held, breadth, PAST, store)
    middle, late = middle_ref.shape[1], last_ref.shape[1]
    for h in range(height):
        past = past_ref[h]
        padded[0:PAST, h] = jnp.where(block_number() > 0, past, jnp.zeros_like(past))
        padded[2 * PAST : 2 * PAST + middle, h] = middle_ref[h]
        padded[2 * PAST + middle : 2 * PAST + middle + late, h] = last_ref[h]
    summed = conv_sum(padded, weight_ref, bias_part(bias_ref, row, weight_ref))
    frames, _, width = summed[0].shape
    for h in range(height):
        branch[h, 0 : frames * breadth] = summed[h][:, 0:breadth].reshape(frames * breadth, width)
    for k, out_ref in enumerate(outs):
        chosen = branch[row ^ k]
        rows = out_ref.shape[0]
        parts = [chosen[i * rows : (i + 1) * rows] for i in range(height)]
        out_ref[...] = jnp.concatenate(parts, axis=1).astype(jnp.bfloat16)


def last_body(latents_ref, *refs):
    *pieces, out_ref, held = refs
    row = lax.axis_index("rows")
    height = len(pieces)
    frames, breadth, channels = latents_ref.shape
    width = channels // height
    for k, piece in enumerate(pieces):
        values = piece[...].astype(jnp.float32)
        parts = [values[:, i * width : (i + 1) * width] for i in range(height)]
        held[row ^ k] = jnp.concatenate(parts, axis=0)
    branch = jnp.concatenate([held[s] for s in range(height)], axis=1)
    branch = branch[0 : frames * breadth].reshape(frames, breadth, channels)
    out_ref[...] = (latents_ref[...].astype(jnp.float32) + branch).astype(jnp.bfloat16)


def shards(shape, latents, gain_one, conv_one, bias_one, gain_two, conv_two, bias_two):
    rows, tm, cols = (shape[name] for name in AXES)
    frames, height, breadth, channels = latents.shape
    width = channels // rows
    ring = breadth + 8
    late, middle = frames - PAST, frames - 2 * PAST
    bf16, f32 = jnp.bfloat16, jnp.float32
    own = latents.reshape(frames, breadth, channels)
    every = [(z, x, c) for z in range(rows) for x in range(tm) for c in range(cols)]
    place = {device: i for i, device in enumerate(every)}

    def moved(values, target):
        return lax.ppermute(values, AXES, [(place[device], place[target(*device)]) for device in every])

    def turned(values, k):
        return moved(values, lambda z, x, c: (z ^ k, x // 2 * 2 + c, x % 2))

    def following(values):
        return moved(values, lambda z, x, c: (z, x, 1) if c == 0 else (z, (x + 2) % tm, 0))

    def spread(values):
        parts = [values]
        for k in range(1, rows):
            parts.append(lax.ppermute(values, "rows", [(z, z ^ k) for z in range(rows)]))
        return parts

    def turn(values):
        parts = []
        for k in range(rows):
            parts.append(turned(values[k], k))
        return parts

    other = lax.ppermute(own, "cols", [(0, 1), (1, 0)])
    weights = [w.reshape(TAPS, TAPS * TAPS * width, channels) for w in (conv_one, conv_two)]
    sds = jax.ShapeDtypeStruct
    size = frames * ring * channels
    work = 2 * ring * channels * rows * 27 * width

    def padded(count):
        return VMEM((count, rows, ring, channels), bf16)

    center, gain_one = call(
        own_body, [sds((frames * breadth, channels), bf16), sds(gain_one.shape, f32)],
        [VMEM((frames, breadth, channels), bf16), pltpu.SemaphoreType.DMA((2,))],
        10 * size, 6 * size, own, gain_one, far=(0, 1),
    )
    centers = turn([center] * rows)
    small = (bias_one, gain_two, bias_two, weights[0])
    end, bias_one, gain_two, bias_two, near = call(
        ends_body, [sds((padded_rows(EDGE * frames), channels), bf16)] + [sds(v.shape, v.dtype) for v in small],
        [pltpu.SemaphoreType.DMA((len(small),))], size, 4 * size, other, gain_one, *small, far=range(2, 2 + len(small)),
    )
    ends = turn([end] * rows)
    past = following(
        jnp.stack([jnp.concatenate([a[late * breadth :], b], axis=0) for a, b in zip(centers, ends)])
    )
    late_rows, early_rows = padded_rows(late * (breadth + 1)), padded_rows(PAST * (breadth + 1))
    part = call(
        functools.partial(first_late_body, breadth, rows), sds((late_rows, channels), bf16),
        [padded(frames)], late * work, 20 * size, *centers, *ends, near, bias_one,
    )
    late_parts = spread(part)
    part = call(
        functools.partial(first_early_body, breadth, rows, frames), sds((early_rows, channels), bf16),
        [padded(2 * PAST)], PAST * work, 20 * size, *centers, *ends, past, near, bias_one,
    )
    early_parts = spread(part)
    second, last = call(
        functools.partial(regroup_body, breadth),
        [sds((rows, middle, ring, channels), bf16), sds((rows, PAST, ring, channels), bf16)],
        [VMEM((rows, late_rows, channels), f32)], 10 * size * rows, 4 * size * rows, *late_parts, gain_two,
    )
    past = following(last)
    back_rows = padded_rows(-(-frames * breadth // rows))
    branch = call(
        functools.partial(second_body, breadth), [sds((back_rows, channels), bf16)] * rows,
        [padded(frames + PAST), VMEM((rows, early_rows, channels), f32), VMEM((rows, back_rows * rows, width), f32)],
        frames * work, 20 * size, *early_parts, second, last, past, gain_two, weights[1], bias_two,
    )
    branch = turn(branch)
    result = call(
        last_body, sds((frames, breadth, channels), bf16), [VMEM((rows, back_rows * rows, width), f32)],
        2 * size, 6 * size, own, *branch,
    )
    return result.reshape(frames, height, breadth, channels)


def solution(mesh):
    shape = dict(mesh.shape)
    return jax.shard_map(
        functools.partial(shards, shape),
        mesh=mesh,
        in_specs=(
            P(("groups", "tm"), "rows", "cols", None),
            P(),
            P(None, "rows", None),
            P(),
            P(),
            P(None, "rows", None),
            P(),
        ),
        out_specs=P(("groups", "tm"), "rows", "cols", None),
        check_vma=False,
    )
```

time: 68.4 us -> 71.8 us (1.050)
  starting transfers between devices: 28.7 us -> 39.1 us
  waiting for transfers between devices: 26.8 us -> 19.9 us
    ppermute x10 -> x14, starting transfers between devices: 21.4 us -> 31.4 us  [moved(): lax.ppermute(values, AXES, [(place[device], place[target(*device)]) for d...]
    ppermute x10 -> x14, waiting for transfers between devices: 16.2 us -> 8.17 us  [moved(): lax.ppermute(values, AXES, [(place[device], place[target(*device)]) for d...]
    ppermute x6, waiting for transfers between devices: 10.6 us -> 11.7 us  [spread(): lax.ppermute(values, 'rows', [(z, z ^ k) for z in range(rows)])]
  transfers between devices with their start and end apart: 17 -> 21, of which waited for: 10 -> 11; matrix products, arithmetic and copies ran while one was open for 0% -> 0% of each run, Pallas kernels for 10% -> 10%
where the time goes in v1:
time: 71.8 us; the launch traced here: 71.7 us
  starting transfers between devices  39.1 us (54%)
  waiting for transfers between devices  19.9 us (28%)
  Pallas kernels  12.3 us (17%)
    ppermute x14, starting transfers between devices, moved(): lax.ppermute(values, AXES, [(place[device], place[target(*device)]) for d...  31.4 us
    pallas_call x7, Pallas kernels, call(): pl.pallas_call(body, out_shape=out_shape, in_specs=[pl.BlockSpec(memory_s...  12.3 us
    ppermute x6, waiting for transfers between devices, spread(): lax.ppermute(values, 'rows', [(z, z ^ k) for z in range(rows)])  11.7 us
    ppermute x14, waiting for transfers between devices, moved(): lax.ppermute(values, AXES, [(place[device], place[target(*device)]) for d...  8.17 us
    ppermute x6, starting transfers between devices, spread(): lax.ppermute(values, 'rows', [(z, z ^ k) for z in range(rows)])  7.74 us
  transfers between devices with their start and end apart: 21, of which 11 were waited for; matrix products, arithmetic and copies ran while one was open for 0% of the time, Pallas kernels for 10%

profile of v1, /device:TPU:1, one launch (start us, length us, event | category | flops | bytes accessed | tf_op | source)
XLA Modules:
  0.0 71.7 jit_solution(16279046479873213362)
XLA Ops:
  0.0 0.0 collective-permute-start.4
  0.0 1.1 %shard_map.73 = (bf16[200,384]{1,0:T(8,128)(2,1)S(1)}, f32[384]{0:T(512)S(1)}) custom-call(bf16[5,40,384]{2,1,0:T(8,128)(2,1)} %bitcast.15, f32[384]{0:T(512)} %far_gain_ref.1), custom_call_target="tpu_custom_call" | custom-call | flops 921600 | bytes 552960 | tf_op jit(solution)/shard_map/pallas_call | solution.py:27
  1.1 5.7 %collective-permute-start.3 = (bf16[200,384]{1,0:T(8,128)(2,1)S(1)}, bf16[200,384]{1,0:T(8,128)(2,1)S(1)}, u32[]{:S(2)}, u32[]{:S(2)}) collective-permute-start(bf16[200,384]{1,0:T(8,128)(2,1)S(1)} %get-tuple-element.18), channel_id=1, source_target_pairs={{0,12},{1,14},{2,13},{3,15},{4,8},{5,10},{6,9},{7,11},{8,4},{9,6},... | collective-permute-start | bytes 460808 | tf_op jit(solution)/shard_map/ppermute | solution.py:250
  6.8 0.0 collective-permute-start.2
  6.8 1.4 %collective-permute-start.1 = (bf16[200,384]{1,0:T(8,128)(2,1)S(1)}, bf16[200,384]{1,0:T(8,128)(2,1)S(1)}, u32[]{:S(2)}, u32[]{:S(2)}) collective-permute-start(bf16[200,384]{1,0:T(8,128)(2,1)S(1)} %get-tuple-element.18), channel_id=1, source_target_pairs={{0,4},{1,6},{2,5},{3,7},{4,0},{5,2},{6,1},{7,3},{8,12},{9,14},{10,... | collective-permute-start | bytes 460808 | tf_op jit(solution)/shard_map/ppermute | solution.py:250
  8.2 2.3 %collective-permute-start = (bf16[200,384]{1,0:T(8,128)(2,1)S(1)}, bf16[200,384]{1,0:T(8,128)(2,1)S(1)}, u32[]{:S(2)}, u32[]{:S(2)}) collective-permute-start(bf16[200,384]{1,0:T(8,128)(2,1)S(1)} %get-tuple-element.18), channel_id=1, source_target_pairs={{0,0},{1,2},{2,1},{3,3},{4,4},{5,6},{6,5},{7,7},{8,8},{9,10},{10,9... | collective-permute-start | bytes 460808 | tf_op jit(solution)/shard_map/ppermute | solution.py:250
  10.5 0.0 collective-permute-done.4.other_ref
  10.5 1.6 %shard_map.74 = (bf16[16,384]{1,0:T(8,128)(2,1)S(1)}, f32[384]{0:T(512)S(1)}, f32[384]{0:T(512)S(1)}, f32[384]{0:T(512)S(1)}, bf16[3,864,384]{2,1,0:T(8,128)(2,1)S(1)}) custom-call(bf16[5,40,384]{2,1,0:T(8,128)(2,1)S(1)} %collective-permute-done.4.other_ref, f32[384]{0:T(512)S(1)} %get-tuple-element.19.gain_ref, f32[384]{0:T(512)} %refs_0_.1, f32[384]{0:T(512)} %refs_1_.1, ...), custom_call_target="tpu_custom_call" | custom-call | flops 92160 | bytes 368640 | tf_op jit(solution)/shard_map/pallas_call | solution.py:27
  12.2 4.4 %collective-permute-start.8 = (bf16[16,384]{1,0:T(8,128)(2,1)S(1)}, bf16[16,384]{1,0:T(8,128)(2,1)S(1)}, u32[]{:S(2)}, u32[]{:S(2)}) collective-permute-start(bf16[16,384]{1,0:T(8,128)(2,1)S(1)} %get-tuple-element.20), channel_id=1, source_target_pairs={{0,12},{1,14},{2,13},{3,15},{4,8},{5,10},{6,9},{7,11},{8,4},{9,6},... | collective-permute-start | bytes 36872 | tf_op jit(solution)/shard_map/ppermute | solution.py:250
  16.6 0.0 collective-permute-done.3.refs_3_
  16.6 2.5 %collective-permute-start.5 = (bf16[16,384]{1,0:T(8,128)(2,1)S(1)}, bf16[16,384]{1,0:T(8,128)(2,1)S(1)}, u32[]{:S(2)}, u32[]{:S(2)}) collective-permute-start(bf16[16,384]{1,0:T(8,128)(2,1)S(1)} %get-tuple-element.20), channel_id=1, source_target_pairs={{0,0},{1,2},{2,1},{3,3},{4,4},{5,6},{6,5},{7,7},{8,8},{9,10},{10,9... | collective-permute-start | bytes 36872 | tf_op jit(solution)/shard_map/ppermute | solution.py:250
  19.2 1.4 %collective-permute-done.2.refs_2_ = bf16[200,384]{1,0:T(8,128)(2,1)S(1)} collective-permute-done((bf16[200,384]{1,0:T(8,128)(2,1)S(1)}, bf16[200,384]{1,0:T(8,128)(2,1)S(1)}, u32[]{:S(2)}, u32[]{:S(2)}) %collective-permute-start.2) | collective-permute-done | bytes 153632 | tf_op jit(solution)/shard_map/ppermute | solution.py:250
  20.6 0.6 collective-permute-start.6
  21.2 0.0 collective-permute-done.1.refs_1_
  21.2 3.1 %collective-permute-start.7 = (bf16[16,384]{1,0:T(8,128)(2,1)S(1)}, bf16[16,384]{1,0:T(8,128)(2,1)S(1)}, u32[]{:S(2)}, u32[]{:S(2)}) collective-permute-start(bf16[16,384]{1,0:T(8,128)(2,1)S(1)} %get-tuple-element.20), channel_id=1, source_target_pairs={{0,8},{1,10},{2,9},{3,11},{4,12},{5,14},{6,13},{7,15},{8,0},{9,2},... | collective-permute-start | bytes 36872 | tf_op jit(solution)/shard_map/ppermute | solution.py:250
  24.3 0.0 collective-permute-done.refs_0_
  24.4 1.8 %collective-permute-done.7.refs_6_ = bf16[16,384]{1,0:T(8,128)(2,1)S(1)} collective-permute-done((bf16[16,384]{1,0:T(8,128)(2,1)S(1)}, bf16[16,384]{1,0:T(8,128)(2,1)S(1)}, u32[]{:S(2)}, u32[]{:S(2)}) %collective-permute-start.7) | collective-permute-done | bytes 12320 | tf_op jit(solution)/shard_map/ppermute | solution.py:250
  26.2 0.0 collective-permute-done.6.refs_5_
  26.2 0.0 collective-permute-done.5.refs_4_
  26.2 0.1 pad_maximum_fusion
  26.3 0.1 collective-permute-start.9
  26.4 2.3 %shard_map.76.refs_0_ = bf16[128,384]{1,0:T(8,128)(2,1)S(1)} custom-call(bf16[200,384]{1,0:T(8,128)(2,1)S(1)} %collective-permute-done.refs_0_, bf16[200,384]{1,0:T(8,128)(2,1)S(1)} %collective-permute-done.1.refs_1_, bf16[200,384]{1,0:T(8,128)(2,1)S(1)} %collective-permute-done.2.refs_2_, bf16[200,384]{1,0:T(8,128)(2,1)S(1)} %collective-permute-done.3.refs_3_, ...), custom_call_target="tpu_custom_call" | custom-call | flops 1146617856 | bytes 1843200 | tf_op jit(solution)/shard_map/pallas_call | solution.py:27
  28.6 1.9 %collective-permute-start.13 = (bf16[128,384]{1,0:T(8,128)(2,1)S(1)}, bf16[128,384]{1,0:T(8,128)(2,1)S(1)}, u32[]{:S(2)}, u32[]{:S(2)}) collective-permute-start(bf16[128,384]{1,0:T(8,128)(2,1)S(1)} %shard_map.76.refs_0_), channel_id=1, source_target_pairs={{0,4},{4,0},{8,12},{12,8},{1,5},{5,1},{9,13},{13,9},{2,6},{6,2},{1... | collective-permute-start | bytes 294920 | tf_op jit(solution)/shard_map/ppermute | solution.py:261
  30.6 1.1 %collective-permute-start.14 = (bf16[128,384]{1,0:T(8,128)(2,1)S(1)}, bf16[128,384]{1,0:T(8,128)(2,1)S(1)}, u32[]{:S(2)}, u32[]{:S(2)}) collective-permute-start(bf16[128,384]{1,0:T(8,128)(2,1)S(1)} %shard_map.76.refs_0_), channel_id=1, source_target_pairs={{0,8},{4,12},{8,0},{12,4},{1,9},{5,13},{9,1},{13,5},{2,10},{6,14},... | collective-permute-start | bytes 294920 | tf_op jit(solution)/shard_map/ppermute | solution.py:261
  31.7 1.1 %collective-permute-start.15 = (bf16[128,384]{1,0:T(8,128)(2,1)S(1)}, bf16[128,384]{1,0:T(8,128)(2,1)S(1)}, u32[]{:S(2)}, u32[]{:S(2)}) collective-permute-start(bf16[128,384]{1,0:T(8,128)(2,1)S(1)} %shard_map.76.refs_0_), channel_id=1, source_target_pairs={{0,12},{4,8},{8,4},{12,0},{1,13},{5,9},{9,5},{13,1},{2,14},{6,10},... | collective-permute-start | bytes 294920 | tf_op jit(solution)/shard_map/ppermute | solution.py:261
  32.8 0.5 collective-permute-done.13.refs_1_
  33.3 1.7 %collective-permute-done.14.refs_2_ = bf16[128,384]{1,0:T(8,128)(2,1)S(1)} collective-permute-done((bf16[128,384]{1,0:T(8,128)(2,1)S(1)}, bf16[128,384]{1,0:T(8,128)(2,1)S(1)}, u32[]{:S(2)}, u32[]{:S(2)}) %collective-permute-start.14) | collective-permute-done | bytes 98336 | tf_op jit(solution)/shard_map/ppermute | solution.py:261
  35.0 4.4 %collective-permute-done.15.refs_3_ = bf16[128,384]{1,0:T(8,128)(2,1)S(1)} collective-permute-done((bf16[128,384]{1,0:T(8,128)(2,1)S(1)}, bf16[128,384]{1,0:T(8,128)(2,1)S(1)}, u32[]{:S(2)}, u32[]{:S(2)}) %collective-permute-start.15) | collective-permute-done | bytes 98336 | tf_op jit(solution)/shard_map/ppermute | solution.py:261
  39.4 0.7 %shard_map.77 = (bf16[4,1,48,384]{3,2,1,0:T(8,128)(2,1)S(1)}, bf16[4,2,48,384]{3,2,1,0:T(8,128)(2,1)S(1)}) custom-call(bf16[128,384]{1,0:T(8,128)(2,1)S(1)} %shard_map.76.refs_0_, bf16[128,384]{1,0:T(8,128)(2,1)S(1)} %collective-permute-done.13.refs_1_, bf16[128,384]{1,0:T(8,128)(2,1)S(1)} %collective-permute-done.14.refs_2_, ...), custom_call_target="tpu_custom_call" | custom-call | flops 3686400 | bytes 1474560 | tf_op jit(solution)/shard_map/pallas_call | solution.py:27
  40.2 2.6 %collective-permute-start.16 = (bf16[4,2,48,384]{3,2,1,0:T(8,128)(2,1)S(1)}, bf16[4,2,48,384]{3,2,1,0:T(8,128)(2,1)S(1)}, u32[]{:S(2)}, u32[]{:S(2)}) collective-permute-start(bf16[4,2,48,384]{3,2,1,0:T(8,128)(2,1)S(1)} %get-tuple-element.25.refs_5_), channel_id=1, source_target_pairs={{0,1},{1,0},{2,3},{3,2},{4,5},{5,4},{6,7},{7,6},{8,9},{9,8},{10,11... | collective-permute-start | bytes 884744 | tf_op jit(solution)/shard_map/ppermute | solution.py:250
  42.8 0.0 collective-permute-done.9.refs_8_
  42.8 1.6 %shard_map.75.refs_0_ = bf16[88,384]{1,0:T(8,128)(2,1)S(1)} custom-call(bf16[200,384]{1,0:T(8,128)(2,1)S(1)} %collective-permute-done.refs_0_, bf16[200,384]{1,0:T(8,128)(2,1)S(1)} %collective-permute-done.1.refs_1_, bf16[200,384]{1,0:T(8,128)(2,1)S(1)} %collective-permute-done.2.refs_2_, bf16[200,384]{1,0:T(8,128)(2,1)S(1)} %collective-permute-done.3.refs_3_, ...), custom_call_target="tpu_custom_call" | custom-call | flops 764411904 | bytes 1843200 | tf_op jit(solution)/shard_map/pallas_call | solution.py:27
  44.4 1.4 %collective-permute-start.10 = (bf16[88,384]{1,0:T(8,128)(2,1)S(1)}, bf16[88,384]{1,0:T(8,128)(2,1)S(1)}, u32[]{:S(2)}, u32[]{:S(2)}) collective-permute-start(bf16[88,384]{1,0:T(8,128)(2,1)S(1)} %shard_map.75.refs_0_), channel_id=1, source_target_pairs={{0,4},{4,0},{8,12},{12,8},{1,5},{5,1},{9,13},{13,9},{2,6},{6,2},{1... | collective-permute-start | bytes 202760 | tf_op jit(solution)/shard_map/ppermute | solution.py:261
  45.8 1.0 %collective-permute-start.11 = (bf16[88,384]{1,0:T(8,128)(2,1)S(1)}, bf16[88,384]{1,0:T(8,128)(2,1)S(1)}, u32[]{:S(2)}, u32[]{:S(2)}) collective-permute-start(bf16[88,384]{1,0:T(8,128)(2,1)S(1)} %shard_map.75.refs_0_), channel_id=1, source_target_pairs={{0,8},{4,12},{8,0},{12,4},{1,9},{5,13},{9,1},{13,5},{2,10},{6,14},... | collective-permute-start | bytes 202760 | tf_op jit(solution)/shard_map/ppermute | solution.py:261
  46.8 1.2 %collective-permute-start.12 = (bf16[88,384]{1,0:T(8,128)(2,1)S(1)}, bf16[88,384]{1,0:T(8,128)(2,1)S(1)}, u32[]{:S(2)}, u32[]{:S(2)}) collective-permute-start(bf16[88,384]{1,0:T(8,128)(2,1)S(1)} %shard_map.75.refs_0_), channel_id=1, source_target_pairs={{0,12},{4,8},{8,4},{12,0},{1,13},{5,9},{9,5},{13,1},{2,14},{6,10},... | collective-permute-start | bytes 202760 | tf_op jit(solution)/shard_map/ppermute | solution.py:261
  48.0 0.1 collective-permute-done.10.refs_1_
  48.2 1.7 %collective-permute-done.11.refs_2_ = bf16[88,384]{1,0:T(8,128)(2,1)S(1)} collective-permute-done((bf16[88,384]{1,0:T(8,128)(2,1)S(1)}, bf16[88,384]{1,0:T(8,128)(2,1)S(1)}, u32[]{:S(2)}, u32[]{:S(2)}) %collective-permute-start.11) | collective-permute-done | bytes 67616 | tf_op jit(solution)/shard_map/ppermute | solution.py:261
  49.9 3.2 %collective-permute-done.12.refs_3_ = bf16[88,384]{1,0:T(8,128)(2,1)S(1)} collective-permute-done((bf16[88,384]{1,0:T(8,128)(2,1)S(1)}, bf16[88,384]{1,0:T(8,128)(2,1)S(1)}, u32[]{:S(2)}, u32[]{:S(2)}) %collective-permute-start.12) | collective-permute-done | bytes 67616 | tf_op jit(solution)/shard_map/ppermute | solution.py:261
  53.1 4.0 %shard_map.78 = (bf16[56,384]{1,0:T(8,128)(2,1)S(1)}, bf16[56,384]{1,0:T(8,128)(2,1)S(1)}, bf16[56,384]{1,0:T(8,128)(2,1)S(1)}, bf16[56,384]{1,0:T(8,128)(2,1)S(1)}) custom-call(bf16[88,384]{1,0:T(8,128)(2,1)S(1)} %shard_map.75.refs_0_, bf16[88,384]{1,0:T(8,128)(2,1)S(1)} %collective-permute-done.10.refs_1_, ...), custom_call_target="tpu_custom_call" | custom-call | flops 1911029760 | bytes 1843200 | tf_op jit(solution)/shard_map/pallas_call | solution.py:27
  57.1 4.0 %collective-permute-start.17 = (bf16[56,384]{1,0:T(8,128)(2,1)S(1)}, bf16[56,384]{1,0:T(8,128)(2,1)S(1)}, u32[]{:S(2)}, u32[]{:S(2)}) collective-permute-start(bf16[56,384]{1,0:T(8,128)(2,1)S(1)} %get-tuple-element.27), channel_id=1, source_target_pairs={{0,0},{1,2},{2,1},{3,3},{4,4},{5,6},{6,5},{7,7},{8,8},{9,10},{10,9... | collective-permute-start | bytes 129032 | tf_op jit(solution)/shard_map/ppermute | solution.py:250
  61.1 1.4 %collective-permute-start.18 = (bf16[56,384]{1,0:T(8,128)(2,1)S(1)}, bf16[56,384]{1,0:T(8,128)(2,1)S(1)}, u32[]{:S(2)}, u32[]{:S(2)}) collective-permute-start(bf16[56,384]{1,0:T(8,128)(2,1)S(1)} %get-tuple-element.28), channel_id=1, source_target_pairs={{0,4},{1,6},{2,5},{3,7},{4,0},{5,2},{6,1},{7,3},{8,12},{9,14},{10,... | collective-permute-start | bytes 129032 | tf_op jit(solution)/shard_map/ppermute | solution.py:250
  62.5 2.1 %collective-permute-start.19 = (bf16[56,384]{1,0:T(8,128)(2,1)S(1)}, bf16[56,384]{1,0:T(8,128)(2,1)S(1)}, u32[]{:S(2)}, u32[]{:S(2)}) collective-permute-start(bf16[56,384]{1,0:T(8,128)(2,1)S(1)} %get-tuple-element.29), channel_id=1, source_target_pairs={{0,8},{1,10},{2,9},{3,11},{4,12},{5,14},{6,13},{7,15},{8,0},{9,2},... | collective-permute-start | bytes 129032 | tf_op jit(solution)/shard_map/ppermute | solution.py:250
  64.5 1.2 %collective-permute-start.20 = (bf16[56,384]{1,0:T(8,128)(2,1)S(1)}, bf16[56,384]{1,0:T(8,128)(2,1)S(1)}, u32[]{:S(2)}, u32[]{:S(2)}) collective-permute-start(bf16[56,384]{1,0:T(8,128)(2,1)S(1)} %get-tuple-element.30), channel_id=1, source_target_pairs={{0,12},{1,14},{2,13},{3,15},{4,8},{5,10},{6,9},{7,11},{8,4},{9,6},... | collective-permute-start | bytes 129032 | tf_op jit(solution)/shard_map/ppermute | solution.py:250
  65.7 0.0 collective-permute-done.17.refs_0_
  65.7 0.2 collective-permute-done.18.refs_1_
  66.0 2.2 %collective-permute-done.19.refs_2_ = bf16[56,384]{1,0:T(8,128)(2,1)S(1)} collective-permute-done((bf16[56,384]{1,0:T(8,128)(2,1)S(1)}, bf16[56,384]{1,0:T(8,128)(2,1)S(1)}, u32[]{:S(2)}, u32[]{:S(2)}) %collective-permute-start.19) | collective-permute-done | bytes 43040 | tf_op jit(solution)/shard_map/ppermute | solution.py:250
  68.2 2.5 %collective-permute-done.20.refs_3_ = bf16[56,384]{1,0:T(8,128)(2,1)S(1)} collective-permute-done((bf16[56,384]{1,0:T(8,128)(2,1)S(1)}, bf16[56,384]{1,0:T(8,128)(2,1)S(1)}, u32[]{:S(2)}, u32[]{:S(2)}) %collective-permute-start.20) | collective-permute-done | bytes 43040 | tf_op jit(solution)/shard_map/ppermute | solution.py:250
  70.7 1.0 %shard_map.79 = bf16[5,40,384]{2,1,0:T(8,128)(2,1)} custom-call(bf16[5,40,384]{2,1,0:T(8,128)(2,1)S(1)} %bitcast.16, bf16[56,384]{1,0:T(8,128)(2,1)S(1)} %collective-permute-done.17.refs_0_, bf16[56,384]{1,0:T(8,128)(2,1)S(1)} %collective-permute-done.18.refs_1_, bf16[56,384]{1,0:T(8,128)(2,1)S(1)} %collective-permute-done.19.refs_2_, ...), custom_call_target="tpu_custom_call" | custom-call | flops 184320 | bytes 552960 | tf_op jit(solution)/shard_map/pallas_call | solution.py:27
  (14 shorter events, 0.1 us)
Async XLA Ops:
  0.0 10.5 %collective-permute-start.4 = (bf16[5,40,384]{2,1,0:T(8,128)(2,1)}, bf16[5,40,384]{2,1,0:T(8,128)(2,1)S(1)}, u32[]{:S(2)}, u32[]{:S(2)}) collective-permute-start(bf16[5,40,384]{2,1,0:T(8,128)(2,1)} %bitcast.14), channel_id=1, source_target_pairs={{0,1},{1,0},{2,3},{3,2},{4,5},{5,4},{6,7},{7,6},{8,9},{9,8},{10,11... | collective-permute-start | bytes 460808 | tf_op jit(solution)/shard_map/ppermute | solution.py:270
  1.1 15.5 %collective-permute-start.3 = (bf16[200,384]{1,0:T(8,128)(2,1)S(1)}, bf16[200,384]{1,0:T(8,128)(2,1)S(1)}, u32[]{:S(2)}, u32[]{:S(2)}) collective-permute-start(bf16[200,384]{1,0:T(8,128)(2,1)S(1)} %get-tuple-element.18), channel_id=1, source_target_pairs={{0,12},{1,14},{2,13},{3,15},{4,8},{5,10},{6,9},{7,11},{8,4},{9,6},... | collective-permute-start | bytes 460808 | tf_op jit(solution)/shard_map/ppermute | solution.py:250
  6.8 13.8 %collective-permute-start.2 = (bf16[200,384]{1,0:T(8,128)(2,1)S(1)}, bf16[200,384]{1,0:T(8,128)(2,1)S(1)}, u32[]{:S(2)}, u32[]{:S(2)}) collective-permute-start(bf16[200,384]{1,0:T(8,128)(2,1)S(1)} %get-tuple-element.18), channel_id=1, source_target_pairs={{0,8},{1,10},{2,9},{3,11},{4,12},{5,14},{6,13},{7,15},{8,0},{9,2},... | collective-permute-start | bytes 460808 | tf_op jit(solution)/shard_map/ppermute | solution.py:250
  6.8 14.4 %collective-permute-start.1 = (bf16[200,384]{1,0:T(8,128)(2,1)S(1)}, bf16[200,384]{1,0:T(8,128)(2,1)S(1)}, u32[]{:S(2)}, u32[]{:S(2)}) collective-permute-start(bf16[200,384]{1,0:T(8,128)(2,1)S(1)} %get-tuple-element.18), channel_id=1, source_target_pairs={{0,4},{1,6},{2,5},{3,7},{4,0},{5,2},{6,1},{7,3},{8,12},{9,14},{10,... | collective-permute-start | bytes 460808 | tf_op jit(solution)/shard_map/ppermute | solution.py:250
  8.2 16.1 %collective-permute-start = (bf16[200,384]{1,0:T(8,128)(2,1)S(1)}, bf16[200,384]{1,0:T(8,128)(2,1)S(1)}, u32[]{:S(2)}, u32[]{:S(2)}) collective-permute-start(bf16[200,384]{1,0:T(8,128)(2,1)S(1)} %get-tuple-element.18), channel_id=1, source_target_pairs={{0,0},{1,2},{2,1},{3,3},{4,4},{5,6},{6,5},{7,7},{8,8},{9,10},{10,9... | collective-permute-start | bytes 460808 | tf_op jit(solution)/shard_map/ppermute | solution.py:250
  12.2 12.2 %collective-permute-start.8 = (bf16[16,384]{1,0:T(8,128)(2,1)S(1)}, bf16[16,384]{1,0:T(8,128)(2,1)S(1)}, u32[]{:S(2)}, u32[]{:S(2)}) collective-permute-start(bf16[16,384]{1,0:T(8,128)(2,1)S(1)} %get-tuple-element.20), channel_id=1, source_target_pairs={{0,12},{1,14},{2,13},{3,15},{4,8},{5,10},{6,9},{7,11},{8,4},{9,6},... | collective-permute-start | bytes 36872 | tf_op jit(solution)/shard_map/ppermute | solution.py:250
  16.6 9.6 %collective-permute-start.5 = (bf16[16,384]{1,0:T(8,128)(2,1)S(1)}, bf16[16,384]{1,0:T(8,128)(2,1)S(1)}, u32[]{:S(2)}, u32[]{:S(2)}) collective-permute-start(bf16[16,384]{1,0:T(8,128)(2,1)S(1)} %get-tuple-element.20), channel_id=1, source_target_pairs={{0,0},{1,2},{2,1},{3,3},{4,4},{5,6},{6,5},{7,7},{8,8},{9,10},{10,9... | collective-permute-start | bytes 36872 | tf_op jit(solution)/shard_map/ppermute | solution.py:250
  20.6 5.6 %collective-permute-start.6 = (bf16[16,384]{1,0:T(8,128)(2,1)S(1)}, bf16[16,384]{1,0:T(8,128)(2,1)S(1)}, u32[]{:S(2)}, u32[]{:S(2)}) collective-permute-start(bf16[16,384]{1,0:T(8,128)(2,1)S(1)} %get-tuple-element.20), channel_id=1, source_target_pairs={{0,4},{1,6},{2,5},{3,7},{4,0},{5,2},{6,1},{7,3},{8,12},{9,14},{10,... | collective-permute-start | bytes 36872 | tf_op jit(solution)/shard_map/ppermute | solution.py:250
  21.2 5.0 %collective-permute-start.7 = (bf16[16,384]{1,0:T(8,128)(2,1)S(1)}, bf16[16,384]{1,0:T(8,128)(2,1)S(1)}, u32[]{:S(2)}, u32[]{:S(2)}) collective-permute-start(bf16[16,384]{1,0:T(8,128)(2,1)S(1)} %get-tuple-element.20), channel_id=1, source_target_pairs={{0,8},{1,10},{2,9},{3,11},{4,12},{5,14},{6,13},{7,15},{8,0},{9,2},... | collective-permute-start | bytes 36872 | tf_op jit(solution)/shard_map/ppermute | solution.py:250
  26.3 16.5 %collective-permute-start.9 = (bf16[4,96,384]{2,1,0:T(8,128)(2,1)S(1)}, bf16[4,96,384]{2,1,0:T(8,128)(2,1)S(1)}, u32[]{:S(2)}, u32[]{:S(2)}) collective-permute-start(bf16[4,96,384]{2,1,0:T(8,128)(2,1)S(1)} %pad_maximum_fusion), channel_id=1, source_target_pairs={{0,1},{1,0},{2,3},{3,2},{4,5},{5,4},{6,7},{7,6},{8,9},{9,8},{10,11... | collective-permute-start | bytes 884744 | tf_op jit(solution)/shard_map/ppermute | solution.py:250
  28.6 24.5 %copy-start.1 = (bf16[27,96,384]{2,1,0:T(8,128)(2,1)S(1)}, bf16[27,96,384]{2,1,0:T(8,128)(2,1)}, u32[]{:S(2)}) copy-start(bf16[27,96,384]{2,1,0:T(8,128)(2,1)} %param.12) | copy-start | bytes 5971972
  28.6 4.6 %collective-permute-start.13 = (bf16[128,384]{1,0:T(8,128)(2,1)S(1)}, bf16[128,384]{1,0:T(8,128)(2,1)S(1)}, u32[]{:S(2)}, u32[]{:S(2)}) collective-permute-start(bf16[128,384]{1,0:T(8,128)(2,1)S(1)} %shard_map.76.refs_0_), channel_id=1, source_target_pairs={{0,4},{4,0},{8,12},{12,8},{1,5},{5,1},{9,13},{13,9},{2,6},{6,2},{1... | collective-permute-start | bytes 294920 | tf_op jit(solution)/shard_map/ppermute | solution.py:261
  30.6 4.4 %collective-permute-start.14 = (bf16[128,384]{1,0:T(8,128)(2,1)S(1)}, bf16[128,384]{1,0:T(8,128)(2,1)S(1)}, u32[]{:S(2)}, u32[]{:S(2)}) collective-permute-start(bf16[128,384]{1,0:T(8,128)(2,1)S(1)} %shard_map.76.refs_0_), channel_id=1, source_target_pairs={{0,8},{4,12},{8,0},{12,4},{1,9},{5,13},{9,1},{13,5},{2,10},{6,14},... | collective-permute-start | bytes 294920 | tf_op jit(solution)/shard_map/ppermute | solution.py:261
  31.7 7.8 %collective-permute-start.15 = (bf16[128,384]{1,0:T(8,128)(2,1)S(1)}, bf16[128,384]{1,0:T(8,128)(2,1)S(1)}, u32[]{:S(2)}, u32[]{:S(2)}) collective-permute-start(bf16[128,384]{1,0:T(8,128)(2,1)S(1)} %shard_map.76.refs_0_), channel_id=1, source_target_pairs={{0,12},{4,8},{8,4},{12,0},{1,13},{5,9},{9,5},{13,1},{2,14},{6,10},... | collective-permute-start | bytes 294920 | tf_op jit(solution)/shard_map/ppermute | solution.py:261
  40.2 12.9 %collective-permute-start.16 = (bf16[4,2,48,384]{3,2,1,0:T(8,128)(2,1)S(1)}, bf16[4,2,48,384]{3,2,1,0:T(8,128)(2,1)S(1)}, u32[]{:S(2)}, u32[]{:S(2)}) collective-permute-start(bf16[4,2,48,384]{3,2,1,0:T(8,128)(2,1)S(1)} %get-tuple-element.25.refs_5_), channel_id=1, source_target_pairs={{0,1},{1,0},{2,3},{3,2},{4,5},{5,4},{6,7},{7,6},{8,9},{9,8},{10,11... | collective-permute-start | bytes 884744 | tf_op jit(solution)/shard_map/ppermute | solution.py:250
  44.4 3.7 %collective-permute-start.10 = (bf16[88,384]{1,0:T(8,128)(2,1)S(1)}, bf16[88,384]{1,0:T(8,128)(2,1)S(1)}, u32[]{:S(2)}, u32[]{:S(2)}) collective-permute-start(bf16[88,384]{1,0:T(8,128)(2,1)S(1)} %shard_map.75.refs_0_), channel_id=1, source_target_pairs={{0,4},{4,0},{8,12},{12,8},{1,5},{5,1},{9,13},{13,9},{2,6},{6,2},{1... | collective-permute-start | bytes 202760 | tf_op jit(solution)/shard_map/ppermute | solution.py:261
  45.8 4.1 %collective-permute-start.11 = (bf16[88,384]{1,0:T(8,128)(2,1)S(1)}, bf16[88,384]{1,0:T(8,128)(2,1)S(1)}, u32[]{:S(2)}, u32[]{:S(2)}) collective-permute-start(bf16[88,384]{1,0:T(8,128)(2,1)S(1)} %shard_map.75.refs_0_), channel_id=1, source_target_pairs={{0,8},{4,12},{8,0},{12,4},{1,9},{5,13},{9,1},{13,5},{2,10},{6,14},... | collective-permute-start | bytes 202760 | tf_op jit(solution)/shard_map/ppermute | solution.py:261
  46.8 6.3 %collective-permute-start.12 = (bf16[88,384]{1,0:T(8,128)(2,1)S(1)}, bf16[88,384]{1,0:T(8,128)(2,1)S(1)}, u32[]{:S(2)}, u32[]{:S(2)}) collective-permute-start(bf16[88,384]{1,0:T(8,128)(2,1)S(1)} %shard_map.75.refs_0_), channel_id=1, source_target_pairs={{0,12},{4,8},{8,4},{12,0},{1,13},{5,9},{9,5},{13,1},{2,14},{6,10},... | collective-permute-start | bytes 202760 | tf_op jit(solution)/shard_map/ppermute | solution.py:261
  53.1 17.6 %copy-start = (bf16[5,1,40,384]{3,2,1,0:T(8,128)(2,1)S(1)}, bf16[5,1,40,384]{3,2,1,0:T(8,128)(2,1)}, u32[]{:S(2)}) copy-start(bf16[5,1,40,384]{3,2,1,0:T(8,128)(2,1)} %param.7) | copy-start | bytes 460804
  57.1 8.6 %collective-permute-start.17 = (bf16[56,384]{1,0:T(8,128)(2,1)S(1)}, bf16[56,384]{1,0:T(8,128)(2,1)S(1)}, u32[]{:S(2)}, u32[]{:S(2)}) collective-permute-start(bf16[56,384]{1,0:T(8,128)(2,1)S(1)} %get-tuple-element.27), channel_id=1, source_target_pairs={{0,0},{1,2},{2,1},{3,3},{4,4},{5,6},{6,5},{7,7},{8,8},{9,10},{10,9... | collective-permute-start | bytes 129032 | tf_op jit(solution)/shard_map/ppermute | solution.py:250
  61.1 4.9 %collective-permute-start.18 = (bf16[56,384]{1,0:T(8,128)(2,1)S(1)}, bf16[56,384]{1,0:T(8,128)(2,1)S(1)}, u32[]{:S(2)}, u32[]{:S(2)}) collective-permute-start(bf16[56,384]{1,0:T(8,128)(2,1)S(1)} %get-tuple-element.28), channel_id=1, source_target_pairs={{0,4},{1,6},{2,5},{3,7},{4,0},{5,2},{6,1},{7,3},{8,12},{9,14},{10,... | collective-permute-start | bytes 129032 | tf_op jit(solution)/shard_map/ppermute | solution.py:250
  62.5 5.7 %collective-permute-start.19 = (bf16[56,384]{1,0:T(8,128)(2,1)S(1)}, bf16[56,384]{1,0:T(8,128)(2,1)S(1)}, u32[]{:S(2)}, u32[]{:S(2)}) collective-permute-start(bf16[56,384]{1,0:T(8,128)(2,1)S(1)} %get-tuple-element.29), channel_id=1, source_target_pairs={{0,8},{1,10},{2,9},{3,11},{4,12},{5,14},{6,13},{7,15},{8,0},{9,2},... | collective-permute-start | bytes 129032 | tf_op jit(solution)/shard_map/ppermute | solution.py:250
  64.5 6.1 %collective-permute-start.20 = (bf16[56,384]{1,0:T(8,128)(2,1)S(1)}, bf16[56,384]{1,0:T(8,128)(2,1)S(1)}, u32[]{:S(2)}, u32[]{:S(2)}) collective-permute-start(bf16[56,384]{1,0:T(8,128)(2,1)S(1)} %get-tuple-element.30), channel_id=1, source_target_pairs={{0,12},{1,14},{2,13},{3,15},{4,8},{5,10},{6,9},{7,11},{8,4},{9,6},... | collective-permute-start | bytes 129032 | tf_op jit(solution)/shard_map/ppermute | solution.py:250

commit v2 on v1

--- a/solution.py
+++ b/solution.py
@@ -65,21 +65,26 @@
     out_ref[...] = values.reshape(frames * breadth, channels).astype(jnp.bfloat16)
 
 
-def ends_body(other_ref, gain_ref, *refs):
-    count = (len(refs) - 2) // 2
-    far, out_ref, near, sems = refs[:count], refs[count], refs[count + 1 : 2 * count + 1], refs[2 * count + 1]
-    copies = [pltpu.make_async_copy(a, b, sems.at[i]) for i, (a, b) in enumerate(zip(far, near))]
-    for copy in copies:
-        copy.start()
+def ends_body(center_ref, other_ref, gain_ref, out_ref):
     frames, breadth, channels = other_ref.shape
     half = lax.axis_index("cols")
     chosen = jnp.where(half == 0, other_ref[:, 0:8].astype(jnp.float32), other_ref[:, breadth - 8 :].astype(jnp.float32))
     values = activate(chosen, gain_ref[...].reshape(1, channels))
     ends = [jnp.where(half == 0, values[f, 0:EDGE], values[f, 8 - EDGE : 8]) for f in range(frames)]
-    rest = out_ref.shape[0] - EDGE * frames
+    count = frames * breadth
+    rest = out_ref.shape[0] - count - EDGE * frames
     if rest:
         ends.append(jnp.zeros((rest, channels), jnp.float32))
-    out_ref[...] = jnp.concatenate(ends, axis=0).astype(jnp.bfloat16)
+    out_ref[0:count] = center_ref[...]
+    out_ref[count:] = jnp.concatenate(ends, axis=0).astype(jnp.bfloat16)
+
+
+def stage_body(*refs):
+    count = len(refs) // 2
+    far, near, sems = refs[:count], refs[count : 2 * count], refs[2 * count]
+    copies = [pltpu.make_async_copy(a, b, sems.at[i]) for i, (a, b) in enumerate(zip(far, near))]
+    for copy in copies:
+        copy.start()
     for copy in copies:
         copy.wait()
 
@@ -138,26 +143,26 @@
 
 
 def first_late_body(breadth, height, *refs):
-    centers, ends = refs[:height], refs[height : 2 * height]
-    weight_ref, bias_ref, out_ref, padded = refs[2 * height :]
-    row = lax.axis_index("rows")
-    picks = [(f, f) for f in range(padded.shape[0])]
+    *pieces, weight_ref, bias_ref, out_ref, padded = refs
+    row = lax.axis_index("rows")
+    frames = padded.shape[0]
+    picks = [(f, f) for f in range(frames)]
     for k in range(height):
-        center, end = centers[k][...].astype(jnp.float32), ends[k][...].astype(jnp.float32)
-        fill_first(padded, (0, row ^ k), center, end, picks, breadth)
+        values = pieces[k][...].astype(jnp.float32)
+        fill_first(padded, (0, row ^ k), values, values[frames * breadth :], picks, breadth)
     pack_first(conv_sum(padded, weight_ref, bias_part(bias_ref, row, weight_ref)), out_ref, breadth)
 
 
 def first_early_body(breadth, height, frames, *refs):
-    centers, ends = refs[:height], refs[height : 2 * height]
-    past_ref, weight_ref, bias_ref, out_ref, padded = refs[2 * height :]
+    *pieces, past_ref, weight_ref, bias_ref, out_ref, padded = refs
     row = lax.axis_index("rows")
     for k in range(height):
         past = past_ref[k].astype(jnp.float32)
         past = jnp.where(block_number() > 0, past, jnp.zeros_like(past))
         picks = [(j, frames - PAST + j) for j in range(PAST)]
         fill_first(padded, (0, row ^ k), past[0 : PAST * breadth], past[PAST * breadth :], picks, breadth)
-        center, end = centers[k][0 : PAST * breadth].astype(jnp.float32), ends[k][...].astype(jnp.float32)
+        center = pieces[k][0 : PAST * breadth].astype(jnp.float32)
+        end = pieces[k][frames * breadth :].astype(jnp.float32)
         fill_first(padded, (PAST, row ^ k), center, end, [(j, j) for j in range(PAST)], breadth)
     pack_first(conv_sum(padded, weight_ref, bias_part(bias_ref, row, weight_ref)), out_ref, breadth)
 
@@ -281,25 +286,24 @@
         [VMEM((frames, breadth, channels), bf16), pltpu.SemaphoreType.DMA((2,))],
         10 * size, 6 * size, own, gain_one, far=(0, 1),
     )
-    centers = turn([center] * rows)
+    total = frames * breadth + padded_rows(EDGE * frames)
+    band = call(ends_body, sds((total, channels), bf16), [], size, 4 * size, center, other, gain_one)
+    pieces = turn([band] * rows)
     small = (bias_one, gain_two, bias_two, weights[0])
-    end, bias_one, gain_two, bias_two, near = call(
-        ends_body, [sds((padded_rows(EDGE * frames), channels), bf16)] + [sds(v.shape, v.dtype) for v in small],
-        [pltpu.SemaphoreType.DMA((len(small),))], size, 4 * size, other, gain_one, *small, far=range(2, 2 + len(small)),
-    )
-    ends = turn([end] * rows)
-    past = following(
-        jnp.stack([jnp.concatenate([a[late * breadth :], b], axis=0) for a, b in zip(centers, ends)])
-    )
+    bias_one, gain_two, bias_two, near = call(
+        stage_body, [sds(v.shape, v.dtype) for v in small], [pltpu.SemaphoreType.DMA((len(small),))],
+        size, 4 * size, *small, far=range(len(small)),
+    )
+    past = following(jnp.stack([piece[late * breadth :] for piece in pieces]))
     late_rows, early_rows = padded_rows(late * (breadth + 1)), padded_rows(PAST * (breadth + 1))
     part = call(
         functools.partial(first_late_body, breadth, rows), sds((late_rows, channels), bf16),
-        [padded(frames)], late * work, 20 * size, *centers, *ends, near, bias_one,
+        [padded(frames)], late * work, 20 * size, *pieces, near, bias_one,
     )
     late_parts = spread(part)
     part = call(
         functools.partial(first_early_body, breadth, rows, frames), sds((early_rows, channels), bf16),
-        [padded(2 * PAST)], PAST * work, 20 * size, *centers, *ends, past, near, bias_one,
+        [padded(2 * PAST)], PAST * work, 20 * size, *pieces, past, near, bias_one,
     )
     early_parts = spread(part)
     second, last = call(

time: 71.8 us -> 65.6 us (0.914)
  starting transfers between devices: 39.1 us -> 25.8 us
  waiting for transfers between devices: 19.9 us -> 26.9 us
    ppermute x14 -> x10, starting transfers between devices: 31.4 us -> 18.6 us  [moved(): lax.ppermute(values, AXES, [(place[device], place[target(*device)]) for d...]
    ppermute x14 -> x10, waiting for transfers between devices: 8.17 us -> 14 us  [moved(): lax.ppermute(values, AXES, [(place[device], place[target(*device)]) for d...]
    pallas_call x7 -> x8, Pallas kernels: 12.3 us -> 12.4 us  [call(): pl.pallas_call(body, out_shape=out_shape, in_specs=[pl.BlockSpec(memory_s...]
  transfers between devices with their start and end apart: 21 -> 17, of which waited for: 11 -> 8; matrix products, arithmetic and copies ran while one was open for 0% -> 0% of each run, Pallas kernels for 10% -> 11%
where the time goes in v2:
time: 65.6 us; the launch traced here: 65.4 us
  waiting for transfers between devices  26.9 us (41%)
  starting transfers between devices  25.8 us (39%)
  Pallas kernels  12.4 us (19%)
    ppermute x10, starting transfers between devices, moved(): lax.ppermute(values, AXES, [(place[device], place[target(*device)]) for d...  18.6 us
    ppermute x10, waiting for transfers between devices, moved(): lax.ppermute(values, AXES, [(place[device], place[target(*device)]) for d...  14 us
    ppermute x6, waiting for transfers between devices, spread(): lax.ppermute(values, 'rows', [(z, z ^ k) for z in range(rows)])  12.4 us
    pallas_call x8, Pallas kernels, call(): pl.pallas_call(body, out_shape=out_shape, in_specs=[pl.BlockSpec(memory_s...  12.4 us
    ppermute x6, starting transfers between devices, spread(): lax.ppermute(values, 'rows', [(z, z ^ k) for z in range(rows)])  7.22 us
  transfers between devices with their start and end apart: 17, of which 8 were waited for; matrix products, arithmetic and copies ran while one was open for 0% of the time, Pallas kernels for 11%

profile of v2, /device:TPU:1, one launch (start us, length us, event | category | flops | bytes accessed | tf_op | source)
XLA Modules:
  0.0 65.4 jit_solution(748553921280729327)
XLA Ops:
  0.0 0.0 collective-permute-start
  0.0 1.1 %shard_map.73 = (bf16[200,384]{1,0:T(8,128)(2,1)S(1)}, f32[384]{0:T(512)S(1)}) custom-call(bf16[5,40,384]{2,1,0:T(8,128)(2,1)} %bitcast.15, f32[384]{0:T(512)} %far_gain_ref.1), custom_call_target="tpu_custom_call" | custom-call | flops 921600 | bytes 552960 | tf_op jit(solution)/shard_map/pallas_call | solution.py:27
  1.1 0.5 collective-permute-done.other_ref
  1.6 0.1 shard_map.74
  1.7 5.7 %collective-permute-start.4 = (bf16[216,384]{1,0:T(8,128)(2,1)S(1)}, bf16[216,384]{1,0:T(8,128)(2,1)S(1)}, u32[]{:S(2)}, u32[]{:S(2)}) collective-permute-start(bf16[216,384]{1,0:T(8,128)(2,1)S(1)} %shard_map.74), channel_id=1, source_target_pairs={{0,12},{1,14},{2,13},{3,15},{4,8},{5,10},{6,9},{7,11},{8,4},{9,6},... | collective-permute-start | bytes 497672 | tf_op jit(solution)/shard_map/ppermute | solution.py:255
  7.4 1.6 %shard_map.75 = (f32[384]{0:T(512)S(1)}, f32[384]{0:T(512)S(1)}, f32[384]{0:T(512)S(1)}, bf16[3,864,384]{2,1,0:T(8,128)(2,1)S(1)}) custom-call(f32[384]{0:T(512)} %refs_0_.1, f32[384]{0:T(512)} %refs_1_.1, f32[384]{0:T(512)} %refs_2_.1, bf16[3,864,384]{2,1,0:T(8,128)(2,1)} %bitcast.18), custom_call_target="tpu_custom_call" | custom-call | flops 92160 | bytes 368640 | tf_op jit(solution)/shard_map/pallas_call | solution.py:27
  9.0 0.1 collective-permute-start.3
  9.1 1.4 %collective-permute-start.2 = (bf16[216,384]{1,0:T(8,128)(2,1)S(1)}, bf16[216,384]{1,0:T(8,128)(2,1)S(1)}, u32[]{:S(2)}, u32[]{:S(2)}) collective-permute-start(bf16[216,384]{1,0:T(8,128)(2,1)S(1)} %shard_map.74), channel_id=1, source_target_pairs={{0,4},{1,6},{2,5},{3,7},{4,0},{5,2},{6,1},{7,3},{8,12},{9,14},{10,... | collective-permute-start | bytes 497672 | tf_op jit(solution)/shard_map/ppermute | solution.py:255
  10.5 2.3 %collective-permute-start.1 = (bf16[216,384]{1,0:T(8,128)(2,1)S(1)}, bf16[216,384]{1,0:T(8,128)(2,1)S(1)}, u32[]{:S(2)}, u32[]{:S(2)}) collective-permute-start(bf16[216,384]{1,0:T(8,128)(2,1)S(1)} %shard_map.74), channel_id=1, source_target_pairs={{0,0},{1,2},{2,1},{3,3},{4,4},{5,6},{6,5},{7,7},{8,8},{9,10},{10,9... | collective-permute-start | bytes 497672 | tf_op jit(solution)/shard_map/ppermute | solution.py:255
  12.8 0.0 collective-permute-done.4.refs_3_
  12.8 8.7 %collective-permute-done.3.refs_2_ = bf16[216,384]{1,0:T(8,128)(2,1)S(1)} collective-permute-done((bf16[216,384]{1,0:T(8,128)(2,1)S(1)}, bf16[216,384]{1,0:T(8,128)(2,1)S(1)}, u32[]{:S(2)}, u32[]{:S(2)}) %collective-permute-start.3) | collective-permute-done | bytes 165920 | tf_op jit(solution)/shard_map/ppermute | solution.py:255
  21.5 0.0 collective-permute-done.2.refs_1_
  21.5 0.0 collective-permute-done.1.refs_0_
  21.5 0.1 pad_maximum_fusion
  21.6 0.3 collective-permute-start.5
  21.9 2.2 %shard_map.77.refs_0_ = bf16[128,384]{1,0:T(8,128)(2,1)S(1)} custom-call(bf16[216,384]{1,0:T(8,128)(2,1)S(1)} %collective-permute-done.1.refs_0_, bf16[216,384]{1,0:T(8,128)(2,1)S(1)} %collective-permute-done.2.refs_1_, bf16[216,384]{1,0:T(8,128)(2,1)S(1)} %collective-permute-done.3.refs_2_, bf16[216,384]{1,0:T(8,128)(2,1)S(1)} %collective-permute-done.4.refs_3_, ...), custom_call_target="tpu_custom_call" | custom-call | flops 1146617856 | bytes 1843200 | tf_op jit(solution)/shard_map/pallas_call | solution.py:27
  24.1 0.0 copy-start.1
  24.1 2.3 %collective-permute-start.11 = (bf16[128,384]{1,0:T(8,128)(2,1)S(1)}, bf16[128,384]{1,0:T(8,128)(2,1)S(1)}, u32[]{:S(2)}, u32[]{:S(2)}) collective-permute-start(bf16[128,384]{1,0:T(8,128)(2,1)S(1)} %shard_map.77.refs_0_), channel_id=1, source_target_pairs={{0,12},{4,8},{8,4},{12,0},{1,13},{5,9},{9,5},{13,1},{2,14},{6,10},... | collective-permute-start | bytes 294920 | tf_op jit(solution)/shard_map/ppermute | solution.py:266
  26.4 0.0 collective-permute-start.10
  26.4 1.4 %collective-permute-start.9 = (bf16[128,384]{1,0:T(8,128)(2,1)S(1)}, bf16[128,384]{1,0:T(8,128)(2,1)S(1)}, u32[]{:S(2)}, u32[]{:S(2)}) collective-permute-start(bf16[128,384]{1,0:T(8,128)(2,1)S(1)} %shard_map.77.refs_0_), channel_id=1, source_target_pairs={{0,4},{4,0},{8,12},{12,8},{1,5},{5,1},{9,13},{13,9},{2,6},{6,2},{1... | collective-permute-start | bytes 294920 | tf_op jit(solution)/shard_map/ppermute | solution.py:266
  27.8 2.3 %collective-permute-done.11.refs_3_ = bf16[128,384]{1,0:T(8,128)(2,1)S(1)} collective-permute-done((bf16[128,384]{1,0:T(8,128)(2,1)S(1)}, bf16[128,384]{1,0:T(8,128)(2,1)S(1)}, u32[]{:S(2)}, u32[]{:S(2)}) %collective-permute-start.11) | collective-permute-done | bytes 98336 | tf_op jit(solution)/shard_map/ppermute | solution.py:266
  30.1 4.9 %collective-permute-done.10.refs_2_ = bf16[128,384]{1,0:T(8,128)(2,1)S(1)} collective-permute-done((bf16[128,384]{1,0:T(8,128)(2,1)S(1)}, bf16[128,384]{1,0:T(8,128)(2,1)S(1)}, u32[]{:S(2)}, u32[]{:S(2)}) %collective-permute-start.10) | collective-permute-done | bytes 98336 | tf_op jit(solution)/shard_map/ppermute | solution.py:266
  34.9 0.0 collective-permute-done.9.refs_1_
  34.9 0.7 %shard_map.78 = (bf16[4,1,48,384]{3,2,1,0:T(8,128)(2,1)S(1)}, bf16[4,2,48,384]{3,2,1,0:T(8,128)(2,1)S(1)}) custom-call(bf16[128,384]{1,0:T(8,128)(2,1)S(1)} %shard_map.77.refs_0_, bf16[128,384]{1,0:T(8,128)(2,1)S(1)} %collective-permute-done.9.refs_1_, bf16[128,384]{1,0:T(8,128)(2,1)S(1)} %collective-permute-done.10.refs_2_, ...), custom_call_target="tpu_custom_call" | custom-call | flops 3686400 | bytes 1474560 | tf_op jit(solution)/shard_map/pallas_call | solution.py:27
  35.7 0.6 collective-permute-start.12
  36.2 0.0 collective-permute-done.5.refs_4_
  36.2 1.6 %shard_map.76.refs_0_ = bf16[88,384]{1,0:T(8,128)(2,1)S(1)} custom-call(bf16[216,384]{1,0:T(8,128)(2,1)S(1)} %collective-permute-done.1.refs_0_, bf16[216,384]{1,0:T(8,128)(2,1)S(1)} %collective-permute-done.2.refs_1_, bf16[216,384]{1,0:T(8,128)(2,1)S(1)} %collective-permute-done.3.refs_2_, bf16[216,384]{1,0:T(8,128)(2,1)S(1)} %collective-permute-done.4.refs_3_, ...), custom_call_target="tpu_custom_call" | custom-call | flops 764411904 | bytes 1843200 | tf_op jit(solution)/shard_map/pallas_call | solution.py:27
  37.9 2.2 %collective-permute-start.8 = (bf16[88,384]{1,0:T(8,128)(2,1)S(1)}, bf16[88,384]{1,0:T(8,128)(2,1)S(1)}, u32[]{:S(2)}, u32[]{:S(2)}) collective-permute-start(bf16[88,384]{1,0:T(8,128)(2,1)S(1)} %shard_map.76.refs_0_), channel_id=1, source_target_pairs={{0,12},{4,8},{8,4},{12,0},{1,13},{5,9},{9,5},{13,1},{2,14},{6,10},... | collective-permute-start | bytes 202760 | tf_op jit(solution)/shard_map/ppermute | solution.py:266
  40.1 0.0 collective-permute-start.7
  40.1 1.4 %collective-permute-start.6 = (bf16[88,384]{1,0:T(8,128)(2,1)S(1)}, bf16[88,384]{1,0:T(8,128)(2,1)S(1)}, u32[]{:S(2)}, u32[]{:S(2)}) collective-permute-start(bf16[88,384]{1,0:T(8,128)(2,1)S(1)} %shard_map.76.refs_0_), channel_id=1, source_target_pairs={{0,4},{4,0},{8,12},{12,8},{1,5},{5,1},{9,13},{13,9},{2,6},{6,2},{1... | collective-permute-start | bytes 202760 | tf_op jit(solution)/shard_map/ppermute | solution.py:266
  41.5 1.9 %collective-permute-done.8.refs_3_ = bf16[88,384]{1,0:T(8,128)(2,1)S(1)} collective-permute-done((bf16[88,384]{1,0:T(8,128)(2,1)S(1)}, bf16[88,384]{1,0:T(8,128)(2,1)S(1)}, u32[]{:S(2)}, u32[]{:S(2)}) %collective-permute-start.8) | collective-permute-done | bytes 67616 | tf_op jit(solution)/shard_map/ppermute | solution.py:266
  43.4 3.3 %collective-permute-done.7.refs_2_ = bf16[88,384]{1,0:T(8,128)(2,1)S(1)} collective-permute-done((bf16[88,384]{1,0:T(8,128)(2,1)S(1)}, bf16[88,384]{1,0:T(8,128)(2,1)S(1)}, u32[]{:S(2)}, u32[]{:S(2)}) %collective-permute-start.7) | collective-permute-done | bytes 67616 | tf_op jit(solution)/shard_map/ppermute | solution.py:266
  46.7 0.0 collective-permute-done.6.refs_1_
  46.7 0.0 collective-permute-done.12.refs_6_
  46.7 0.0 copy-done.1
  46.7 0.0 copy-start
  46.7 4.0 %shard_map.79 = (bf16[56,384]{1,0:T(8,128)(2,1)S(1)}, bf16[56,384]{1,0:T(8,128)(2,1)S(1)}, bf16[56,384]{1,0:T(8,128)(2,1)S(1)}, bf16[56,384]{1,0:T(8,128)(2,1)S(1)}) custom-call(bf16[88,384]{1,0:T(8,128)(2,1)S(1)} %shard_map.76.refs_0_, bf16[88,384]{1,0:T(8,128)(2,1)S(1)} %collective-permute-done.6.refs_1_, ...), custom_call_target="tpu_custom_call" | custom-call | flops 1911029760 | bytes 1843200 | tf_op jit(solution)/shard_map/pallas_call | solution.py:27
  50.7 3.8 %collective-permute-start.13 = (bf16[56,384]{1,0:T(8,128)(2,1)S(1)}, bf16[56,384]{1,0:T(8,128)(2,1)S(1)}, u32[]{:S(2)}, u32[]{:S(2)}) collective-permute-start(bf16[56,384]{1,0:T(8,128)(2,1)S(1)} %get-tuple-element.25), channel_id=1, source_target_pairs={{0,0},{1,2},{2,1},{3,3},{4,4},{5,6},{6,5},{7,7},{8,8},{9,10},{10,9... | collective-permute-start | bytes 129032 | tf_op jit(solution)/shard_map/ppermute | solution.py:255
  54.6 0.2 collective-permute-start.14
  54.8 3.5 %collective-permute-start.15 = (bf16[56,384]{1,0:T(8,128)(2,1)S(1)}, bf16[56,384]{1,0:T(8,128)(2,1)S(1)}, u32[]{:S(2)}, u32[]{:S(2)}) collective-permute-start(bf16[56,384]{1,0:T(8,128)(2,1)S(1)} %get-tuple-element.27), channel_id=1, source_target_pairs={{0,8},{1,10},{2,9},{3,11},{4,12},{5,14},{6,13},{7,15},{8,0},{9,2},... | collective-permute-start | bytes 129032 | tf_op jit(solution)/shard_map/ppermute | solution.py:255
  58.3 0.8 %collective-permute-start.16 = (bf16[56,384]{1,0:T(8,128)(2,1)S(1)}, bf16[56,384]{1,0:T(8,128)(2,1)S(1)}, u32[]{:S(2)}, u32[]{:S(2)}) collective-permute-start(bf16[56,384]{1,0:T(8,128)(2,1)S(1)} %get-tuple-element.28), channel_id=1, source_target_pairs={{0,12},{1,14},{2,13},{3,15},{4,8},{5,10},{6,9},{7,11},{8,4},{9,6},... | collective-permute-start | bytes 129032 | tf_op jit(solution)/shard_map/ppermute | solution.py:255
  59.1 0.0 collective-permute-done.13.refs_0_
  59.1 0.0 collective-permute-done.14.refs_1_
  59.1 1.7 %collective-permute-done.15.refs_2_ = bf16[56,384]{1,0:T(8,128)(2,1)S(1)} collective-permute-done((bf16[56,384]{1,0:T(8,128)(2,1)S(1)}, bf16[56,384]{1,0:T(8,128)(2,1)S(1)}, u32[]{:S(2)}, u32[]{:S(2)}) %collective-permute-start.15) | collective-permute-done | bytes 43040 | tf_op jit(solution)/shard_map/ppermute | solution.py:255
  60.8 3.6 %collective-permute-done.16.refs_3_ = bf16[56,384]{1,0:T(8,128)(2,1)S(1)} collective-permute-done((bf16[56,384]{1,0:T(8,128)(2,1)S(1)}, bf16[56,384]{1,0:T(8,128)(2,1)S(1)}, u32[]{:S(2)}, u32[]{:S(2)}) %collective-permute-start.16) | collective-permute-done | bytes 43040 | tf_op jit(solution)/shard_map/ppermute | solution.py:255
  64.4 0.0 copy-done
  64.4 1.0 %shard_map.80 = bf16[5,40,384]{2,1,0:T(8,128)(2,1)} custom-call(bf16[5,40,384]{2,1,0:T(8,128)(2,1)S(1)} %bitcast.16, bf16[56,384]{1,0:T(8,128)(2,1)S(1)} %collective-permute-done.13.refs_0_, bf16[56,384]{1,0:T(8,128)(2,1)S(1)} %collective-permute-done.14.refs_1_, bf16[56,384]{1,0:T(8,128)(2,1)S(1)} %collective-permute-done.15.refs_2_, ...), custom_call_target="tpu_custom_call" | custom-call | flops 184320 | bytes 552960 | tf_op jit(solution)/shard_map/pallas_call | solution.py:27
  (4 shorter events, 0.0 us)
Async XLA Ops:
  0.0 1.6 %collective-permute-start = (bf16[5,40,384]{2,1,0:T(8,128)(2,1)}, bf16[5,40,384]{2,1,0:T(8,128)(2,1)S(1)}, u32[]{:S(2)}, u32[]{:S(2)}) collective-permute-start(bf16[5,40,384]{2,1,0:T(8,128)(2,1)} %bitcast.14), channel_id=1, source_target_pairs={{0,1},{1,0},{2,3},{3,2},{4,5},{5,4},{6,7},{7,6},{8,9},{9,8},{10,11... | collective-permute-start | bytes 460808 | tf_op jit(solution)/shard_map/ppermute | solution.py:275
  1.7 11.1 %collective-permute-start.4 = (bf16[216,384]{1,0:T(8,128)(2,1)S(1)}, bf16[216,384]{1,0:T(8,128)(2,1)S(1)}, u32[]{:S(2)}, u32[]{:S(2)}) collective-permute-start(bf16[216,384]{1,0:T(8,128)(2,1)S(1)} %shard_map.74), channel_id=1, source_target_pairs={{0,12},{1,14},{2,13},{3,15},{4,8},{5,10},{6,9},{7,11},{8,4},{9,6},... | collective-permute-start | bytes 497672 | tf_op jit(solution)/shard_map/ppermute | solution.py:255
  9.0 12.4 %collective-permute-start.3 = (bf16[216,384]{1,0:T(8,128)(2,1)S(1)}, bf16[216,384]{1,0:T(8,128)(2,1)S(1)}, u32[]{:S(2)}, u32[]{:S(2)}) collective-permute-start(bf16[216,384]{1,0:T(8,128)(2,1)S(1)} %shard_map.74), channel_id=1, source_target_pairs={{0,8},{1,10},{2,9},{3,11},{4,12},{5,14},{6,13},{7,15},{8,0},{9,2},... | collective-permute-start | bytes 497672 | tf_op jit(solution)/shard_map/ppermute | solution.py:255
  9.1 12.4 %collective-permute-start.2 = (bf16[216,384]{1,0:T(8,128)(2,1)S(1)}, bf16[216,384]{1,0:T(8,128)(2,1)S(1)}, u32[]{:S(2)}, u32[]{:S(2)}) collective-permute-start(bf16[216,384]{1,0:T(8,128)(2,1)S(1)} %shard_map.74), channel_id=1, source_target_pairs={{0,4},{1,6},{2,5},{3,7},{4,0},{5,2},{6,1},{7,3},{8,12},{9,14},{10,... | collective-permute-start | bytes 497672 | tf_op jit(solution)/shard_map/ppermute | solution.py:255
  10.5 11.0 %collective-permute-start.1 = (bf16[216,384]{1,0:T(8,128)(2,1)S(1)}, bf16[216,384]{1,0:T(8,128)(2,1)S(1)}, u32[]{:S(2)}, u32[]{:S(2)}) collective-permute-start(bf16[216,384]{1,0:T(8,128)(2,1)S(1)} %shard_map.74), channel_id=1, source_target_pairs={{0,0},{1,2},{2,1},{3,3},{4,4},{5,6},{6,5},{7,7},{8,8},{9,10},{10,9... | collective-permute-start | bytes 497672 | tf_op jit(solution)/shard_map/ppermute | solution.py:255
  21.6 14.6 %collective-permute-start.5 = (bf16[4,96,384]{2,1,0:T(8,128)(2,1)S(1)}, bf16[4,96,384]{2,1,0:T(8,128)(2,1)S(1)}, u32[]{:S(2)}, u32[]{:S(2)}) collective-permute-start(bf16[4,96,384]{2,1,0:T(8,128)(2,1)S(1)} %pad_maximum_fusion), channel_id=1, source_target_pairs={{0,1},{1,0},{2,3},{3,2},{4,5},{5,4},{6,7},{7,6},{8,9},{9,8},{10,11... | collective-permute-start | bytes 884744 | tf_op jit(solution)/shard_map/ppermute | solution.py:255
  24.1 22.6 %copy-start.1 = (bf16[27,96,384]{2,1,0:T(8,128)(2,1)S(1)}, bf16[27,96,384]{2,1,0:T(8,128)(2,1)}, u32[]{:S(2)}) copy-start(bf16[27,96,384]{2,1,0:T(8,128)(2,1)} %param.12) | copy-start | bytes 5971972
  24.1 5.9 %collective-permute-start.11 = (bf16[128,384]{1,0:T(8,128)(2,1)S(1)}, bf16[128,384]{1,0:T(8,128)(2,1)S(1)}, u32[]{:S(2)}, u32[]{:S(2)}) collective-permute-start(bf16[128,384]{1,0:T(8,128)(2,1)S(1)} %shard_map.77.refs_0_), channel_id=1, source_target_pairs={{0,12},{4,8},{8,4},{12,0},{1,13},{5,9},{9,5},{13,1},{2,14},{6,10},... | collective-permute-start | bytes 294920 | tf_op jit(solution)/shard_map/ppermute | solution.py:266
  26.4 8.5 %collective-permute-start.10 = (bf16[128,384]{1,0:T(8,128)(2,1)S(1)}, bf16[128,384]{1,0:T(8,128)(2,1)S(1)}, u32[]{:S(2)}, u32[]{:S(2)}) collective-permute-start(bf16[128,384]{1,0:T(8,128)(2,1)S(1)} %shard_map.77.refs_0_), channel_id=1, source_target_pairs={{0,8},{4,12},{8,0},{12,4},{1,9},{5,13},{9,1},{13,5},{2,10},{6,14},... | collective-permute-start | bytes 294920 | tf_op jit(solution)/shard_map/ppermute | solution.py:266
  26.4 8.5 %collective-permute-start.9 = (bf16[128,384]{1,0:T(8,128)(2,1)S(1)}, bf16[128,384]{1,0:T(8,128)(2,1)S(1)}, u32[]{:S(2)}, u32[]{:S(2)}) collective-permute-start(bf16[128,384]{1,0:T(8,128)(2,1)S(1)} %shard_map.77.refs_0_), channel_id=1, source_target_pairs={{0,4},{4,0},{8,12},{12,8},{1,5},{5,1},{9,13},{13,9},{2,6},{6,2},{1... | collective-permute-start | bytes 294920 | tf_op jit(solution)/shard_map/ppermute | solution.py:266
  35.7 11.0 %collective-permute-start.12 = (bf16[4,2,48,384]{3,2,1,0:T(8,128)(2,1)S(1)}, bf16[4,2,48,384]{3,2,1,0:T(8,128)(2,1)S(1)}, u32[]{:S(2)}, u32[]{:S(2)}) collective-permute-start(bf16[4,2,48,384]{3,2,1,0:T(8,128)(2,1)S(1)} %get-tuple-element.23.refs_5_), channel_id=1, source_target_pairs={{0,1},{1,0},{2,3},{3,2},{4,5},{5,4},{6,7},{7,6},{8,9},{9,8},{10,11... | collective-permute-start | bytes 884744 | tf_op jit(solution)/shard_map/ppermute | solution.py:255
  37.9 5.5 %collective-permute-start.8 = (bf16[88,384]{1,0:T(8,128)(2,1)S(1)}, bf16[88,384]{1,0:T(8,128)(2,1)S(1)}, u32[]{:S(2)}, u32[]{:S(2)}) collective-permute-start(bf16[88,384]{1,0:T(8,128)(2,1)S(1)} %shard_map.76.refs_0_), channel_id=1, source_target_pairs={{0,12},{4,8},{8,4},{12,0},{1,13},{5,9},{9,5},{13,1},{2,14},{6,10},... | collective-permute-start | bytes 202760 | tf_op jit(solution)/shard_map/ppermute | solution.py:266
  40.1 6.6 %collective-permute-start.7 = (bf16[88,384]{1,0:T(8,128)(2,1)S(1)}, bf16[88,384]{1,0:T(8,128)(2,1)S(1)}, u32[]{:S(2)}, u32[]{:S(2)}) collective-permute-start(bf16[88,384]{1,0:T(8,128)(2,1)S(1)} %shard_map.76.refs_0_), channel_id=1, source_target_pairs={{0,8},{4,12},{8,0},{12,4},{1,9},{5,13},{9,1},{13,5},{2,10},{6,14},... | collective-permute-start | bytes 202760 | tf_op jit(solution)/shard_map/ppermute | solution.py:266
  40.1 6.6 %collective-permute-start.6 = (bf16[88,384]{1,0:T(8,128)(2,1)S(1)}, bf16[88,384]{1,0:T(8,128)(2,1)S(1)}, u32[]{:S(2)}, u32[]{:S(2)}) collective-permute-start(bf16[88,384]{1,0:T(8,128)(2,1)S(1)} %shard_map.76.refs_0_), channel_id=1, source_target_pairs={{0,4},{4,0},{8,12},{12,8},{1,5},{5,1},{9,13},{13,9},{2,6},{6,2},{1... | collective-permute-start | bytes 202760 | tf_op jit(solution)/shard_map/ppermute | solution.py:266
  46.7 17.7 %copy-start = (bf16[5,1,40,384]{3,2,1,0:T(8,128)(2,1)S(1)}, bf16[5,1,40,384]{3,2,1,0:T(8,128)(2,1)}, u32[]{:S(2)}) copy-start(bf16[5,1,40,384]{3,2,1,0:T(8,128)(2,1)} %param.7) | copy-start | bytes 460804
  50.7 8.3 %collective-permute-start.13 = (bf16[56,384]{1,0:T(8,128)(2,1)S(1)}, bf16[56,384]{1,0:T(8,128)(2,1)S(1)}, u32[]{:S(2)}, u32[]{:S(2)}) collective-permute-start(bf16[56,384]{1,0:T(8,128)(2,1)S(1)} %get-tuple-element.25), channel_id=1, source_target_pairs={{0,0},{1,2},{2,1},{3,3},{4,4},{5,6},{6,5},{7,7},{8,8},{9,10},{10,9... | collective-permute-start | bytes 129032 | tf_op jit(solution)/shard_map/ppermute | solution.py:255
  54.6 4.5 %collective-permute-start.14 = (bf16[56,384]{1,0:T(8,128)(2,1)S(1)}, bf16[56,384]{1,0:T(8,128)(2,1)S(1)}, u32[]{:S(2)}, u32[]{:S(2)}) collective-permute-start(bf16[56,384]{1,0:T(8,128)(2,1)S(1)} %get-tuple-element.26), channel_id=1, source_target_pairs={{0,4},{1,6},{2,5},{3,7},{4,0},{5,2},{6,1},{7,3},{8,12},{9,14},{10,... | collective-permute-start | bytes 129032 | tf_op jit(solution)/shard_map/ppermute | solution.py:255
  54.8 6.0 %collective-permute-start.15 = (bf16[56,384]{1,0:T(8,128)(2,1)S(1)}, bf16[56,384]{1,0:T(8,128)(2,1)S(1)}, u32[]{:S(2)}, u32[]{:S(2)}) collective-permute-start(bf16[56,384]{1,0:T(8,128)(2,1)S(1)} %get-tuple-element.27), channel_id=1, source_target_pairs={{0,8},{1,10},{2,9},{3,11},{4,12},{5,14},{6,13},{7,15},{8,0},{9,2},... | collective-permute-start | bytes 129032 | tf_op jit(solution)/shard_map/ppermute | solution.py:255
  58.3 6.1 %collective-permute-start.16 = (bf16[56,384]{1,0:T(8,128)(2,1)S(1)}, bf16[56,384]{1,0:T(8,128)(2,1)S(1)}, u32[]{:S(2)}, u32[]{:S(2)}) collective-permute-start(bf16[56,384]{1,0:T(8,128)(2,1)S(1)} %get-tuple-element.28), channel_id=1, source_target_pairs={{0,12},{1,14},{2,13},{3,15},{4,8},{5,10},{6,9},{7,11},{8,4},{9,6},... | collective-permute-start | bytes 129032 | tf_op jit(solution)/shard_map/ppermute | solution.py:255

commit v3 on v2

--- a/solution.py
+++ b/solution.py
@@ -96,28 +96,65 @@
         padded[i + at[0], at[1]] = ring_of(center, ends[end * EDGE : (end + 1) * EDGE], half).astype(jnp.bfloat16)
 
 
+def multiply(windows, weight_ref, taps):
+    return lax.dot_general(
+        jnp.concatenate(windows, axis=1),
+        jnp.concatenate([weight_ref[t] for t in taps], axis=1),
+        (((1,), (1,)), ((), ())),
+        preferred_element_type=jnp.float32,
+    )
+
+
+def row_sums(product):
+    height, wide = product.shape[1], product.shape[3] // TAPS
+    rows = []
+    for h in range(height):
+        near = [product[:, h + r - 1, :, r * wide : (r + 1) * wide] for r in range(TAPS) if 0 <= h + r - 1 < height]
+        rows.append(sum(near[1:], near[0]))
+    return rows
+
+
+def column_sum(row, bias_row):
+    ring, width = row.shape[1], row.shape[2] // TAPS
+    before = pltpu.roll(row[:, :, 0:width], 1, 1)
+    after = pltpu.roll(row[:, :, 2 * width : 3 * width], ring - 1, 1)
+    return before + row[:, :, width : 2 * width] + after + bias_row
+
+
 def conv_sum(padded, weight_ref, bias_row):
     frames, height, ring, channels = padded.shape[0] - PAST, padded.shape[1], padded.shape[2], padded.shape[3]
-    wide = weight_ref.shape[1] // TAPS
-    width = wide // TAPS
     windows = [padded[t : t + frames].reshape(frames * height * ring, channels) for t in range(TAPS)]
-    product = lax.dot_general(
-        jnp.concatenate(windows, axis=1),
-        jnp.concatenate([weight_ref[t] for t in range(TAPS)], axis=1),
-        (((1,), (1,)), ((), ())),
-        preferred_element_type=jnp.float32,
-    )
-    product = product.reshape(frames, height, ring, TAPS * wide)
-    rows = []
-    for h in range(height):
-        near = [
-            product[:, h + r - 1, :, r * wide : (r + 1) * wide] for r in range(TAPS) if 0 <= h + r - 1 < height
-        ]
-        row = sum(near[1:], near[0])
-        before = pltpu.roll(row[:, :, 0:width], 1, 1)
-        after = pltpu.roll(row[:, :, 2 * width : 3 * width], ring - 1, 1)
-        rows.append(before + row[:, :, width : 2 * width] + after + bias_row)
-    return rows
+    product = multiply(windows, weight_ref, range(TAPS)).reshape(frames, height, ring, -1)
+    return [column_sum(row, bias_row) for row in row_sums(product)]
+
+
+def pair_sums(padded, base, weight_ref, total):
+    frames, ring, channels = padded.shape[0] - PAST, padded.shape[2], padded.shape[3]
+    windows = [padded[t : t + frames, pl.ds(base, 2)].reshape(frames * 2 * ring, channels) for t in range(TAPS)]
+    product = multiply(windows, weight_ref, range(TAPS)).reshape(frames, 2, ring, -1)
+    wide = product.shape[3] // TAPS
+    taps = [[product[:, i, :, r * wide : (r + 1) * wide] for r in range(TAPS)] for i in range(2)]
+    total[base] += taps[0][2]
+    total[base + 1] += taps[0][1] + taps[1][2]
+    total[base + 2] += taps[0][0] + taps[1][1]
+    total[base + 3] += taps[1][0]
+
+
+def frame_terms(frames, early):
+    groups = {}
+    for f in range(frames):
+        taps = tuple(t for t in range(TAPS) if (PAST <= f + t < 2 * PAST) == early)
+        groups.setdefault(taps, []).append(f)
+    return [(taps, outs) for taps, outs in groups.items() if taps]
+
+
+def frame_sums(frame_of, frames, early, weight_ref, height, ring, add):
+    for taps, outs in frame_terms(frames, early):
+        windows = [jnp.concatenate([frame_of(f + t) for f in outs], axis=0) for t in taps]
+        product = multiply(windows, weight_ref, taps).reshape(len(outs), height, ring, -1)
+        for h, row in enumerate(row_sums(product)):
+            for i, f in enumerate(outs):
+                add(f, h, row[i])
 
 
 def block_number():
@@ -142,15 +179,31 @@
     return own_part(bias_ref[...].reshape(1, -1), row, weight_ref.shape[1] // TAPS // TAPS)
 
 
-def first_late_body(breadth, height, *refs):
-    *pieces, weight_ref, bias_ref, out_ref, padded = refs
-    row = lax.axis_index("rows")
+def fill_pair(padded, pieces, base, row, breadth):
     frames = padded.shape[0]
-    picks = [(f, f) for f in range(frames)]
-    for k in range(height):
-        values = pieces[k][...].astype(jnp.float32)
-        fill_first(padded, (0, row ^ k), values, values[frames * breadth :], picks, breadth)
-    pack_first(conv_sum(padded, weight_ref, bias_part(bias_ref, row, weight_ref)), out_ref, breadth)
+    for i, piece in enumerate(pieces):
+        values = piece[...].astype(jnp.float32)
+        picks = [(f, f) for f in range(frames)]
+        fill_first(padded, (0, row ^ (base + i)), values, values[frames * breadth :], picks, breadth)
+
+
+def first_near_body(breadth, *refs):
+    *pieces, weight_ref, total, padded = refs
+    row = lax.axis_index("rows")
+    fill_pair(padded, pieces, 0, row, breadth)
+    total[...] = jnp.zeros_like(total)
+    pair_sums(padded, row // 2 * 2, weight_ref, total)
+
+
+def first_late_body(breadth, *refs):
+    *pieces, near_ref, weight_ref, bias_ref, out_ref, padded, total = refs
+    row = lax.axis_index("rows")
+    fill_pair(padded, pieces, 2, row, breadth)
+    total[...] = near_ref[...]
+    for pair in range(1, len(pieces) // 2 + 1):
+        pair_sums(padded, (row // 2 ^ pair) * 2, weight_ref, total)
+    bias_row = bias_part(bias_ref, row, weight_ref)
+    pack_first([column_sum(total[h + 1], bias_row) for h in range(len(pieces) + 2)], out_ref, breadth)
 
 
 def first_early_body(breadth, height, frames, *refs):
@@ -197,27 +250,58 @@
     regroup(pieces, gain_ref, held, breadth, middle + late, store)
 
 
+def second_part_body(frames, middle_ref, last_ref, past_ref, weight_ref, total):
+    height, middle, ring, channels = middle_ref.shape
+    done = set()
+
+    def frame_of(p):
+        if p < PAST:
+            values = past_ref[:, p]
+            values = jnp.where(block_number() > 0, values, jnp.zeros_like(values))
+        elif p < 2 * PAST + middle:
+            values = middle_ref[:, p - 2 * PAST]
+        else:
+            values = last_ref[:, p - 2 * PAST - middle]
+        return values.reshape(height * ring, channels)
+
+    def add(f, h, values):
+        done.add(f)
+        total[h, f] = values
+
+    frame_sums(frame_of, frames, False, weight_ref, height, ring, add)
+    for f in range(frames):
+        if f not in done:
+            total[:, f] = jnp.zeros((height,) + total.shape[2:], jnp.float32)
+
+
 def second_body(breadth, *refs):
-    height = (len(refs) - 9) // 2
+    height = (len(refs) - 7) // 2
     pieces, refs = refs[:height], refs[height:]
-    middle_ref, last_ref, past_ref, gain_ref, weight_ref, bias_ref = refs[:6]
-    outs, (padded, held, branch) = refs[6 : 6 + height], refs[6 + height :]
+    part_ref, gain_ref, weight_ref, bias_ref = refs[:4]
+    outs, (early, held, branch) = refs[4 : 4 + height], refs[4 + height :]
     row = lax.axis_index("rows")
 
     def store(h, f, ring):
-        padded[PAST + f, h] = ring
+        early[f, h] = ring
 
     regroup(pieces, gain_ref, held, breadth, PAST, store)
-    middle, late = middle_ref.shape[1], last_ref.shape[1]
+    _, frames, ring, _ = part_ref.shape
+    channels = early.shape[3]
+    sums = {}
+
+    def add(f, h, values):
+        sums[f, h] = part_ref[h, f] + values
+
+    def frame_of(p):
+        return early[p - PAST].reshape(height * ring, channels)
+
+    frame_sums(frame_of, frames, True, weight_ref, height, ring, add)
+    bias_row = bias_part(bias_ref, row, weight_ref)
     for h in range(height):
-        past = past_ref[h]
-        padded[0:PAST, h] = jnp.where(block_number() > 0, past, jnp.zeros_like(past))
-        padded[2 * PAST : 2 * PAST + middle, h] = middle_ref[h]
-        padded[2 * PAST + middle : 2 * PAST + middle + late, h] = last_ref[h]
-    summed = conv_sum(padded, weight_ref, bias_part(bias_ref, row, weight_ref))
-    frames, _, width = summed[0].shape
-    for h in range(height):
-        branch[h, 0 : frames * breadth] = summed[h][:, 0:breadth].reshape(frames * breadth, width)
+        for f in range(frames):
+            values = sums[f, h] if (f, h) in sums else part_ref[h, f]
+            values = column_sum(values[None], bias_row)[0]
+            branch[h, f * breadth : (f + 1) * breadth] = values[0:breadth]
     for k, out_ref in enumerate(outs):
         chosen = branch[row ^ k]
         rows = out_ref.shape[0]
@@ -296,9 +380,14 @@
     )
     past = following(jnp.stack([piece[late * breadth :] for piece in pieces]))
     late_rows, early_rows = padded_rows(late * (breadth + 1)), padded_rows(PAST * (breadth + 1))
+    near_sums = call(
+        functools.partial(first_near_body, breadth), sds((rows + 2, late, ring, TAPS * width), f32),
+        [padded(frames)], late * work // 2, 10 * size, *pieces[:2], near,
+    )
     part = call(
-        functools.partial(first_late_body, breadth, rows), sds((late_rows, channels), bf16),
-        [padded(frames)], late * work, 20 * size, *pieces, near, bias_one,
+        functools.partial(first_late_body, breadth), sds((late_rows, channels), bf16),
+        [padded(frames), VMEM((rows + 2, late, ring, TAPS * width), f32)],
+        late * work // 2, 10 * size, *pieces[2:], near_sums, near, bias_one,
     )
     late_parts = spread(part)
     part = call(
@@ -313,10 +402,14 @@
     )
     past = following(last)
     back_rows = padded_rows(-(-frames * breadth // rows))
+    part = call(
+        functools.partial(second_part_body, frames), sds((rows, frames, ring, TAPS * width), f32), [],
+        frames * work // 2, 20 * size, second, last, past, weights[1],
+    )
     branch = call(
         functools.partial(second_body, breadth), [sds((back_rows, channels), bf16)] * rows,
-        [padded(frames + PAST), VMEM((rows, early_rows, channels), f32), VMEM((rows, back_rows * rows, width), f32)],
-        frames * work, 20 * size, *early_parts, second, last, past, gain_two, weights[1], bias_two,
+        [padded(PAST), VMEM((rows, early_rows, channels), f32), VMEM((rows, back_rows * rows, width), f32)],
+        frames * work // 2, 20 * size, *early_parts, part, gain_two, weights[1], bias_two,
     )
     branch = turn(branch)
     result = call(

time: 65.6 us -> 62.9 us (0.959)
  waiting for transfers between devices: 26.9 us -> 23.5 us
  Pallas kernels: 12.4 us -> 13.5 us
    ppermute x6, waiting for transfers between devices: 12.4 us -> 9.55 us  [spread(): lax.ppermute(values, 'rows', [(z, z ^ k) for z in range(rows)])]
    pallas_call x8 -> x10, Pallas kernels: 12.4 us -> 13.5 us  [call(): pl.pallas_call(body, out_shape=out_shape, in_specs=[pl.BlockSpec(memory_s...]
  transfers between devices with their start and end apart: 17 -> 17, of which waited for: 8 -> 8; matrix products, arithmetic and copies ran while one was open for 0% -> 0% of each run, Pallas kernels for 11% -> 14%
where the time goes in v3:
time: 62.9 us; the launch traced here: 62.7 us
  starting transfers between devices  25.5 us (41%)
  waiting for transfers between devices  23.5 us (37%)
  Pallas kernels  13.5 us (21%)
    ppermute x10, starting transfers between devices, moved(): lax.ppermute(values, AXES, [(place[device], place[target(*device)]) for d...  18.2 us
    ppermute x10, waiting for transfers between devices, moved(): lax.ppermute(values, AXES, [(place[device], place[target(*device)]) for d...  13.5 us
    pallas_call x10, Pallas kernels, call(): pl.pallas_call(body, out_shape=out_shape, in_specs=[pl.BlockSpec(memory_s...  13.5 us
    ppermute x6, waiting for transfers between devices, spread(): lax.ppermute(values, 'rows', [(z, z ^ k) for z in range(rows)])  9.55 us
    ppermute x6, starting transfers between devices, spread(): lax.ppermute(values, 'rows', [(z, z ^ k) for z in range(rows)])  7.23 us
  transfers between devices with their start and end apart: 17, of which 8 were waited for; matrix products, arithmetic and copies ran while one was open for 0% of the time, Pallas kernels for 14%

profile of v3, /device:TPU:1, one launch (start us, length us, event | category | flops | bytes accessed | tf_op | source)
XLA Modules:
  0.0 62.7 jit_solution(10717081286961321983)
XLA Ops:
  0.0 0.0 collective-permute-start
  0.0 1.1 %shard_map.73 = (bf16[200,384]{1,0:T(8,128)(2,1)S(1)}, f32[384]{0:T(512)S(1)}) custom-call(bf16[5,40,384]{2,1,0:T(8,128)(2,1)} %bitcast.17, f32[384]{0:T(512)} %far_gain_ref.1), custom_call_target="tpu_custom_call" | custom-call | flops 921600 | bytes 552960 | tf_op jit(solution)/shard_map/pallas_call | solution.py:27
  1.1 0.5 collective-permute-done.other_ref
  1.6 0.1 shard_map.74
  1.7 3.7 %collective-permute-start.2 = (bf16[216,384]{1,0:T(8,128)(2,1)S(1)}, bf16[216,384]{1,0:T(8,128)(2,1)S(1)}, u32[]{:S(2)}, u32[]{:S(2)}) collective-permute-start(bf16[216,384]{1,0:T(8,128)(2,1)S(1)} %shard_map.74), channel_id=1, source_target_pairs={{0,4},{1,6},{2,5},{3,7},{4,0},{5,2},{6,1},{7,3},{8,12},{9,14},{10,... | collective-permute-start | bytes 497672 | tf_op jit(solution)/shard_map/ppermute | solution.py:339
  5.4 2.2 %collective-permute-start.1 = (bf16[216,384]{1,0:T(8,128)(2,1)S(1)}, bf16[216,384]{1,0:T(8,128)(2,1)S(1)}, u32[]{:S(2)}, u32[]{:S(2)}) collective-permute-start(bf16[216,384]{1,0:T(8,128)(2,1)S(1)} %shard_map.74), channel_id=1, source_target_pairs={{0,0},{1,2},{2,1},{3,3},{4,4},{5,6},{6,5},{7,7},{8,8},{9,10},{10,9... | collective-permute-start | bytes 497672 | tf_op jit(solution)/shard_map/ppermute | solution.py:339
  7.6 3.4 %collective-permute-start.4 = (bf16[216,384]{1,0:T(8,128)(2,1)S(1)}, bf16[216,384]{1,0:T(8,128)(2,1)S(1)}, u32[]{:S(2)}, u32[]{:S(2)}) collective-permute-start(bf16[216,384]{1,0:T(8,128)(2,1)S(1)} %shard_map.74), channel_id=1, source_target_pairs={{0,12},{1,14},{2,13},{3,15},{4,8},{5,10},{6,9},{7,11},{8,4},{9,6},... | collective-permute-start | bytes 497672 | tf_op jit(solution)/shard_map/ppermute | solution.py:339
  11.0 0.2 collective-permute-start.3
  11.2 1.6 %shard_map.75 = (f32[384]{0:T(512)S(1)}, f32[384]{0:T(512)S(1)}, f32[384]{0:T(512)S(1)}, bf16[3,864,384]{2,1,0:T(8,128)(2,1)S(1)}) custom-call(f32[384]{0:T(512)} %refs_0_.1, f32[384]{0:T(512)} %refs_1_.1, f32[384]{0:T(512)} %refs_2_.1, bf16[3,864,384]{2,1,0:T(8,128)(2,1)} %bitcast.19), custom_call_target="tpu_custom_call" | custom-call | flops 92160 | bytes 368640 | tf_op jit(solution)/shard_map/pallas_call | solution.py:27
  12.8 0.0 collective-permute-done.2.refs_1_
  12.9 0.0 collective-permute-done.1.refs_0_
  12.9 1.1 %shard_map.77.refs_2_ = f32[6,3,48,288]{3,2,1,0:T(8,128)S(1)} custom-call(bf16[216,384]{1,0:T(8,128)(2,1)S(1)} %collective-permute-done.1.refs_0_, bf16[216,384]{1,0:T(8,128)(2,1)S(1)} %collective-permute-done.2.refs_1_, bf16[3,864,384]{2,1,0:T(8,128)(2,1)S(1)} %get-tuple-element.19.refs_5_.refs_2_.refs_3_), custom_call_target="tpu_custom_call" | custom-call | flops 573308928 | bytes 921600 | tf_op jit(solution)/shard_map/pallas_call | solution.py:27
  14.0 3.0 %collective-permute-done.4.refs_3_.refs_1_ = bf16[216,384]{1,0:T(8,128)(2,1)S(1)} collective-permute-done((bf16[216,384]{1,0:T(8,128)(2,1)S(1)}, bf16[216,384]{1,0:T(8,128)(2,1)S(1)}, u32[]{:S(2)}, u32[]{:S(2)}) %collective-permute-start.4) | collective-permute-done | bytes 165920 | tf_op jit(solution)/shard_map/ppermute | solution.py:339
  17.0 6.8 %collective-permute-done.3.refs_2_.refs_0_ = bf16[216,384]{1,0:T(8,128)(2,1)S(1)} collective-permute-done((bf16[216,384]{1,0:T(8,128)(2,1)S(1)}, bf16[216,384]{1,0:T(8,128)(2,1)S(1)}, u32[]{:S(2)}, u32[]{:S(2)}) %collective-permute-start.3) | collective-permute-done | bytes 165920 | tf_op jit(solution)/shard_map/ppermute | solution.py:339
  23.8 1.6 %shard_map.78.refs_0_ = bf16[128,384]{1,0:T(8,128)(2,1)S(1)} custom-call(bf16[216,384]{1,0:T(8,128)(2,1)S(1)} %collective-permute-done.3.refs_2_.refs_0_, bf16[216,384]{1,0:T(8,128)(2,1)S(1)} %collective-permute-done.4.refs_3_.refs_1_, f32[6,3,48,288]{3,2,1,0:T(8,128)S(1)} %shard_map.77.refs_2_, ...), custom_call_target="tpu_custom_call" | custom-call | flops 573308928 | bytes 921600 | tf_op jit(solution)/shard_map/pallas_call | solution.py:27
  25.4 2.0 %collective-permute-start.11 = (bf16[128,384]{1,0:T(8,128)(2,1)S(1)}, bf16[128,384]{1,0:T(8,128)(2,1)S(1)}, u32[]{:S(2)}, u32[]{:S(2)}) collective-permute-start(bf16[128,384]{1,0:T(8,128)(2,1)S(1)} %shard_map.78.refs_0_), channel_id=1, source_target_pairs={{0,12},{4,8},{8,4},{12,0},{1,13},{5,9},{9,5},{13,1},{2,14},{6,10},... | collective-permute-start | bytes 294920 | tf_op jit(solution)/shard_map/ppermute | solution.py:350
  27.4 0.0 collective-permute-start.10
  27.4 1.6 %collective-permute-start.9 = (bf16[128,384]{1,0:T(8,128)(2,1)S(1)}, bf16[128,384]{1,0:T(8,128)(2,1)S(1)}, u32[]{:S(2)}, u32[]{:S(2)}) collective-permute-start(bf16[128,384]{1,0:T(8,128)(2,1)S(1)} %shard_map.78.refs_0_), channel_id=1, source_target_pairs={{0,4},{4,0},{8,12},{12,8},{1,5},{5,1},{9,13},{13,9},{2,6},{6,2},{1... | collective-permute-start | bytes 294920 | tf_op jit(solution)/shard_map/ppermute | solution.py:350
  29.1 0.0 copy-start
  29.1 0.1 pad_maximum_fusion
  29.1 0.1 collective-permute-start.5
  29.2 2.6 %collective-permute-done.11.refs_3_ = bf16[128,384]{1,0:T(8,128)(2,1)S(1)} collective-permute-done((bf16[128,384]{1,0:T(8,128)(2,1)S(1)}, bf16[128,384]{1,0:T(8,128)(2,1)S(1)}, u32[]{:S(2)}, u32[]{:S(2)}) %collective-permute-start.11) | collective-permute-done | bytes 98336 | tf_op jit(solution)/shard_map/ppermute | solution.py:350
  31.9 4.0 %collective-permute-done.10.refs_2_ = bf16[128,384]{1,0:T(8,128)(2,1)S(1)} collective-permute-done((bf16[128,384]{1,0:T(8,128)(2,1)S(1)}, bf16[128,384]{1,0:T(8,128)(2,1)S(1)}, u32[]{:S(2)}, u32[]{:S(2)}) %collective-permute-start.10) | collective-permute-done | bytes 98336 | tf_op jit(solution)/shard_map/ppermute | solution.py:350
  35.9 0.0 collective-permute-done.9.refs_1_
  35.9 0.7 %shard_map.79 = (bf16[4,1,48,384]{3,2,1,0:T(8,128)(2,1)S(1)}, bf16[4,2,48,384]{3,2,1,0:T(8,128)(2,1)S(1)}) custom-call(bf16[128,384]{1,0:T(8,128)(2,1)S(1)} %shard_map.78.refs_0_, bf16[128,384]{1,0:T(8,128)(2,1)S(1)} %collective-permute-done.9.refs_1_, bf16[128,384]{1,0:T(8,128)(2,1)S(1)} %collective-permute-done.10.refs_2_, ...), custom_call_target="tpu_custom_call" | custom-call | flops 3686400 | bytes 1474560 | tf_op jit(solution)/shard_map/pallas_call | solution.py:27
  36.6 0.5 collective-permute-start.12
  37.1 0.0 collective-permute-done.5.refs_4_
  37.1 1.6 %shard_map.76.refs_0_ = bf16[88,384]{1,0:T(8,128)(2,1)S(1)} custom-call(bf16[216,384]{1,0:T(8,128)(2,1)S(1)} %collective-permute-done.1.refs_0_, bf16[216,384]{1,0:T(8,128)(2,1)S(1)} %collective-permute-done.2.refs_1_, bf16[216,384]{1,0:T(8,128)(2,1)S(1)} %collective-permute-done.3.refs_2_.refs_0_, ...), custom_call_target="tpu_custom_call" | custom-call | flops 764411904 | bytes 1843200 | tf_op jit(solution)/shard_map/pallas_call | solution.py:27
  38.8 2.4 %collective-permute-start.8 = (bf16[88,384]{1,0:T(8,128)(2,1)S(1)}, bf16[88,384]{1,0:T(8,128)(2,1)S(1)}, u32[]{:S(2)}, u32[]{:S(2)}) collective-permute-start(bf16[88,384]{1,0:T(8,128)(2,1)S(1)} %shard_map.76.refs_0_), channel_id=1, source_target_pairs={{0,12},{4,8},{8,4},{12,0},{1,13},{5,9},{9,5},{13,1},{2,14},{6,10},... | collective-permute-start | bytes 202760 | tf_op jit(solution)/shard_map/ppermute | solution.py:350
  41.1 0.0 collective-permute-start.7
  41.1 1.2 %collective-permute-start.6 = (bf16[88,384]{1,0:T(8,128)(2,1)S(1)}, bf16[88,384]{1,0:T(8,128)(2,1)S(1)}, u32[]{:S(2)}, u32[]{:S(2)}) collective-permute-start(bf16[88,384]{1,0:T(8,128)(2,1)S(1)} %shard_map.76.refs_0_), channel_id=1, source_target_pairs={{0,4},{4,0},{8,12},{12,8},{1,5},{5,1},{9,13},{13,9},{2,6},{6,2},{1... | collective-permute-start | bytes 202760 | tf_op jit(solution)/shard_map/ppermute | solution.py:350
  42.4 0.0 collective-permute-done.12.past_ref
  42.4 0.0 copy-done
  42.4 2.3 %shard_map.80.refs_4_ = f32[4,5,48,288]{3,2,1,0:T(8,128)S(1)} custom-call(bf16[4,1,48,384]{3,2,1,0:T(8,128)(2,1)S(1)} %get-tuple-element.22.middle_ref, bf16[4,2,48,384]{3,2,1,0:T(8,128)(2,1)S(1)} %get-tuple-element.23.last_ref, bf16[4,2,48,384]{3,2,1,0:T(8,128)(2,1)S(1)} %collective-permute-done.12.past_ref, bf16[3,864,384]{2,1,0:T(8,128)(2,1)S(1)} %bitcast.14), custom_call_target="tpu_custom_call" | custom-call | flops 955514880 | bytes 1843200 | tf_op jit(solution)/shard_map/pallas_call | solution.py:27
  44.7 0.0 collective-permute-done.8.refs_3_
  44.7 2.9 %collective-permute-done.7.refs_2_ = bf16[88,384]{1,0:T(8,128)(2,1)S(1)} collective-permute-done((bf16[88,384]{1,0:T(8,128)(2,1)S(1)}, bf16[88,384]{1,0:T(8,128)(2,1)S(1)}, u32[]{:S(2)}, u32[]{:S(2)}) %collective-permute-start.7) | collective-permute-done | bytes 67616 | tf_op jit(solution)/shard_map/ppermute | solution.py:350
  47.6 0.0 collective-permute-done.6.refs_1_
  47.6 2.2 %shard_map.81 = (bf16[56,384]{1,0:T(8,128)(2,1)S(1)}, bf16[56,384]{1,0:T(8,128)(2,1)S(1)}, bf16[56,384]{1,0:T(8,128)(2,1)S(1)}, bf16[56,384]{1,0:T(8,128)(2,1)S(1)}) custom-call(bf16[88,384]{1,0:T(8,128)(2,1)S(1)} %shard_map.76.refs_0_, bf16[88,384]{1,0:T(8,128)(2,1)S(1)} %collective-permute-done.6.refs_1_, ...), custom_call_target="tpu_custom_call" | custom-call | flops 955514880 | bytes 1843200 | tf_op jit(solution)/shard_map/pallas_call | solution.py:27
  49.8 1.9 %collective-permute-start.13 = (bf16[56,384]{1,0:T(8,128)(2,1)S(1)}, bf16[56,384]{1,0:T(8,128)(2,1)S(1)}, u32[]{:S(2)}, u32[]{:S(2)}) collective-permute-start(bf16[56,384]{1,0:T(8,128)(2,1)S(1)} %get-tuple-element.25), channel_id=1, source_target_pairs={{0,0},{1,2},{2,1},{3,3},{4,4},{5,6},{6,5},{7,7},{8,8},{9,10},{10,9... | collective-permute-start | bytes 129032 | tf_op jit(solution)/shard_map/ppermute | solution.py:339
  51.8 1.6 %collective-permute-start.14 = (bf16[56,384]{1,0:T(8,128)(2,1)S(1)}, bf16[56,384]{1,0:T(8,128)(2,1)S(1)}, u32[]{:S(2)}, u32[]{:S(2)}) collective-permute-start(bf16[56,384]{1,0:T(8,128)(2,1)S(1)} %get-tuple-element.26), channel_id=1, source_target_pairs={{0,4},{1,6},{2,5},{3,7},{4,0},{5,2},{6,1},{7,3},{8,12},{9,14},{10,... | collective-permute-start | bytes 129032 | tf_op jit(solution)/shard_map/ppermute | solution.py:339
  53.4 2.3 %collective-permute-start.15 = (bf16[56,384]{1,0:T(8,128)(2,1)S(1)}, bf16[56,384]{1,0:T(8,128)(2,1)S(1)}, u32[]{:S(2)}, u32[]{:S(2)}) collective-permute-start(bf16[56,384]{1,0:T(8,128)(2,1)S(1)} %get-tuple-element.27), channel_id=1, source_target_pairs={{0,8},{1,10},{2,9},{3,11},{4,12},{5,14},{6,13},{7,15},{8,0},{9,2},... | collective-permute-start | bytes 129032 | tf_op jit(solution)/shard_map/ppermute | solution.py:339
  55.6 2.4 %collective-permute-start.16 = (bf16[56,384]{1,0:T(8,128)(2,1)S(1)}, bf16[56,384]{1,0:T(8,128)(2,1)S(1)}, u32[]{:S(2)}, u32[]{:S(2)}) collective-permute-start(bf16[56,384]{1,0:T(8,128)(2,1)S(1)} %get-tuple-element.28), channel_id=1, source_target_pairs={{0,12},{1,14},{2,13},{3,15},{4,8},{5,10},{6,9},{7,11},{8,4},{9,6},... | collective-permute-start | bytes 129032 | tf_op jit(solution)/shard_map/ppermute | solution.py:339
  58.0 0.0 collective-permute-done.13.refs_0_
  58.0 0.0 collective-permute-done.14.refs_1_
  58.0 0.6 collective-permute-done.15.refs_2_
  58.6 3.2 %collective-permute-done.16.refs_3_ = bf16[56,384]{1,0:T(8,128)(2,1)S(1)} collective-permute-done((bf16[56,384]{1,0:T(8,128)(2,1)S(1)}, bf16[56,384]{1,0:T(8,128)(2,1)S(1)}, u32[]{:S(2)}, u32[]{:S(2)}) %collective-permute-start.16) | collective-permute-done | bytes 43040 | tf_op jit(solution)/shard_map/ppermute | solution.py:339
  61.8 0.0 copy-done.1
  61.8 1.0 %shard_map.82 = bf16[5,40,384]{2,1,0:T(8,128)(2,1)} custom-call(bf16[5,40,384]{2,1,0:T(8,128)(2,1)S(1)} %bitcast.18, bf16[56,384]{1,0:T(8,128)(2,1)S(1)} %collective-permute-done.13.refs_0_, bf16[56,384]{1,0:T(8,128)(2,1)S(1)} %collective-permute-done.14.refs_1_, bf16[56,384]{1,0:T(8,128)(2,1)S(1)} %collective-permute-done.15.refs_2_, ...), custom_call_target="tpu_custom_call" | custom-call | flops 184320 | bytes 552960 | tf_op jit(solution)/shard_map/pallas_call | solution.py:27
  (5 shorter events, 0.0 us)
Async XLA Ops:
  0.0 1.6 %collective-permute-start = (bf16[5,40,384]{2,1,0:T(8,128)(2,1)}, bf16[5,40,384]{2,1,0:T(8,128)(2,1)S(1)}, u32[]{:S(2)}, u32[]{:S(2)}) collective-permute-start(bf16[5,40,384]{2,1,0:T(8,128)(2,1)} %bitcast.16), channel_id=1, source_target_pairs={{0,1},{1,0},{2,3},{3,2},{4,5},{5,4},{6,7},{7,6},{8,9},{9,8},{10,11... | collective-permute-start | bytes 460808 | tf_op jit(solution)/shard_map/ppermute | solution.py:359
  1.7 11.1 %collective-permute-start.2 = (bf16[216,384]{1,0:T(8,128)(2,1)S(1)}, bf16[216,384]{1,0:T(8,128)(2,1)S(1)}, u32[]{:S(2)}, u32[]{:S(2)}) collective-permute-start(bf16[216,384]{1,0:T(8,128)(2,1)S(1)} %shard_map.74), channel_id=1, source_target_pairs={{0,4},{1,6},{2,5},{3,7},{4,0},{5,2},{6,1},{7,3},{8,12},{9,14},{10,... | collective-permute-start | bytes 497672 | tf_op jit(solution)/shard_map/ppermute | solution.py:339
  5.4 7.5 %collective-permute-start.1 = (bf16[216,384]{1,0:T(8,128)(2,1)S(1)}, bf16[216,384]{1,0:T(8,128)(2,1)S(1)}, u32[]{:S(2)}, u32[]{:S(2)}) collective-permute-start(bf16[216,384]{1,0:T(8,128)(2,1)S(1)} %shard_map.74), channel_id=1, source_target_pairs={{0,0},{1,2},{2,1},{3,3},{4,4},{5,6},{6,5},{7,7},{8,8},{9,10},{10,9... | collective-permute-start | bytes 497672 | tf_op jit(solution)/shard_map/ppermute | solution.py:339
  7.6 9.4 %collective-permute-start.4 = (bf16[216,384]{1,0:T(8,128)(2,1)S(1)}, bf16[216,384]{1,0:T(8,128)(2,1)S(1)}, u32[]{:S(2)}, u32[]{:S(2)}) collective-permute-start(bf16[216,384]{1,0:T(8,128)(2,1)S(1)} %shard_map.74), channel_id=1, source_target_pairs={{0,12},{1,14},{2,13},{3,15},{4,8},{5,10},{6,9},{7,11},{8,4},{9,6},... | collective-permute-start | bytes 497672 | tf_op jit(solution)/shard_map/ppermute | solution.py:339
  11.0 12.8 %collective-permute-start.3 = (bf16[216,384]{1,0:T(8,128)(2,1)S(1)}, bf16[216,384]{1,0:T(8,128)(2,1)S(1)}, u32[]{:S(2)}, u32[]{:S(2)}) collective-permute-start(bf16[216,384]{1,0:T(8,128)(2,1)S(1)} %shard_map.74), channel_id=1, source_target_pairs={{0,8},{1,10},{2,9},{3,11},{4,12},{5,14},{6,13},{7,15},{8,0},{9,2},... | collective-permute-start | bytes 497672 | tf_op jit(solution)/shard_map/ppermute | solution.py:339
  25.4 6.5 %collective-permute-start.11 = (bf16[128,384]{1,0:T(8,128)(2,1)S(1)}, bf16[128,384]{1,0:T(8,128)(2,1)S(1)}, u32[]{:S(2)}, u32[]{:S(2)}) collective-permute-start(bf16[128,384]{1,0:T(8,128)(2,1)S(1)} %shard_map.78.refs_0_), channel_id=1, source_target_pairs={{0,12},{4,8},{8,4},{12,0},{1,13},{5,9},{9,5},{13,1},{2,14},{6,10},... | collective-permute-start | bytes 294920 | tf_op jit(solution)/shard_map/ppermute | solution.py:350
  27.4 8.5 %collective-permute-start.10 = (bf16[128,384]{1,0:T(8,128)(2,1)S(1)}, bf16[128,384]{1,0:T(8,128)(2,1)S(1)}, u32[]{:S(2)}, u32[]{:S(2)}) collective-permute-start(bf16[128,384]{1,0:T(8,128)(2,1)S(1)} %shard_map.78.refs_0_), channel_id=1, source_target_pairs={{0,8},{4,12},{8,0},{12,4},{1,9},{5,13},{9,1},{13,5},{2,10},{6,14},... | collective-permute-start | bytes 294920 | tf_op jit(solution)/shard_map/ppermute | solution.py:350
  27.4 8.5 %collective-permute-start.9 = (bf16[128,384]{1,0:T(8,128)(2,1)S(1)}, bf16[128,384]{1,0:T(8,128)(2,1)S(1)}, u32[]{:S(2)}, u32[]{:S(2)}) collective-permute-start(bf16[128,384]{1,0:T(8,128)(2,1)S(1)} %shard_map.78.refs_0_), channel_id=1, source_target_pairs={{0,4},{4,0},{8,12},{12,8},{1,5},{5,1},{9,13},{13,9},{2,6},{6,2},{1... | collective-permute-start | bytes 294920 | tf_op jit(solution)/shard_map/ppermute | solution.py:350
  29.1 13.3 %copy-start = (bf16[27,96,384]{2,1,0:T(8,128)(2,1)S(1)}, bf16[27,96,384]{2,1,0:T(8,128)(2,1)}, u32[]{:S(2)}) copy-start(bf16[27,96,384]{2,1,0:T(8,128)(2,1)} %param.12) | copy-start | bytes 5971972
  29.1 8.0 %collective-permute-start.5 = (bf16[4,96,384]{2,1,0:T(8,128)(2,1)S(1)}, bf16[4,96,384]{2,1,0:T(8,128)(2,1)S(1)}, u32[]{:S(2)}, u32[]{:S(2)}) collective-permute-start(bf16[4,96,384]{2,1,0:T(8,128)(2,1)S(1)} %pad_maximum_fusion), channel_id=1, source_target_pairs={{0,1},{1,0},{2,3},{3,2},{4,5},{5,4},{6,7},{7,6},{8,9},{9,8},{10,11... | collective-permute-start | bytes 884744 | tf_op jit(solution)/shard_map/ppermute | solution.py:339
  36.6 5.7 %collective-permute-start.12 = (bf16[4,2,48,384]{3,2,1,0:T(8,128)(2,1)S(1)}, bf16[4,2,48,384]{3,2,1,0:T(8,128)(2,1)S(1)}, u32[]{:S(2)}, u32[]{:S(2)}) collective-permute-start(bf16[4,2,48,384]{3,2,1,0:T(8,128)(2,1)S(1)} %get-tuple-element.23.last_ref), channel_id=1, source_target_pairs={{0,1},{1,0},{2,3},{3,2},{4,5},{5,4},{6,7},{7,6},{8,9},{9,8},{10,11... | collective-permute-start | bytes 884744 | tf_op jit(solution)/shard_map/ppermute | solution.py:339
  38.8 5.9 %collective-permute-start.8 = (bf16[88,384]{1,0:T(8,128)(2,1)S(1)}, bf16[88,384]{1,0:T(8,128)(2,1)S(1)}, u32[]{:S(2)}, u32[]{:S(2)}) collective-permute-start(bf16[88,384]{1,0:T(8,128)(2,1)S(1)} %shard_map.76.refs_0_), channel_id=1, source_target_pairs={{0,12},{4,8},{8,4},{12,0},{1,13},{5,9},{9,5},{13,1},{2,14},{6,10},... | collective-permute-start | bytes 202760 | tf_op jit(solution)/shard_map/ppermute | solution.py:350
  41.1 6.4 %collective-permute-start.7 = (bf16[88,384]{1,0:T(8,128)(2,1)S(1)}, bf16[88,384]{1,0:T(8,128)(2,1)S(1)}, u32[]{:S(2)}, u32[]{:S(2)}) collective-permute-start(bf16[88,384]{1,0:T(8,128)(2,1)S(1)} %shard_map.76.refs_0_), channel_id=1, source_target_pairs={{0,8},{4,12},{8,0},{12,4},{1,9},{5,13},{9,1},{13,5},{2,10},{6,14},... | collective-permute-start | bytes 202760 | tf_op jit(solution)/shard_map/ppermute | solution.py:350
  41.1 6.4 %collective-permute-start.6 = (bf16[88,384]{1,0:T(8,128)(2,1)S(1)}, bf16[88,384]{1,0:T(8,128)(2,1)S(1)}, u32[]{:S(2)}, u32[]{:S(2)}) collective-permute-start(bf16[88,384]{1,0:T(8,128)(2,1)S(1)} %shard_map.76.refs_0_), channel_id=1, source_target_pairs={{0,4},{4,0},{8,12},{12,8},{1,5},{5,1},{9,13},{13,9},{2,6},{6,2},{1... | collective-permute-start | bytes 202760 | tf_op jit(solution)/shard_map/ppermute | solution.py:350
  44.7 17.1 %copy-start.1 = (bf16[5,1,40,384]{3,2,1,0:T(8,128)(2,1)S(1)}, bf16[5,1,40,384]{3,2,1,0:T(8,128)(2,1)}, u32[]{:S(2)}) copy-start(bf16[5,1,40,384]{3,2,1,0:T(8,128)(2,1)} %param.7) | copy-start | bytes 460804
  49.8 8.2 %collective-permute-start.13 = (bf16[56,384]{1,0:T(8,128)(2,1)S(1)}, bf16[56,384]{1,0:T(8,128)(2,1)S(1)}, u32[]{:S(2)}, u32[]{:S(2)}) collective-permute-start(bf16[56,384]{1,0:T(8,128)(2,1)S(1)} %get-tuple-element.25), channel_id=1, source_target_pairs={{0,0},{1,2},{2,1},{3,3},{4,4},{5,6},{6,5},{7,7},{8,8},{9,10},{10,9... | collective-permute-start | bytes 129032 | tf_op jit(solution)/shard_map/ppermute | solution.py:339
  51.8 6.2 %collective-permute-start.14 = (bf16[56,384]{1,0:T(8,128)(2,1)S(1)}, bf16[56,384]{1,0:T(8,128)(2,1)S(1)}, u32[]{:S(2)}, u32[]{:S(2)}) collective-permute-start(bf16[56,384]{1,0:T(8,128)(2,1)S(1)} %get-tuple-element.26), channel_id=1, source_target_pairs={{0,4},{1,6},{2,5},{3,7},{4,0},{5,2},{6,1},{7,3},{8,12},{9,14},{10,... | collective-permute-start | bytes 129032 | tf_op jit(solution)/shard_map/ppermute | solution.py:339
  53.4 5.2 %collective-permute-start.15 = (bf16[56,384]{1,0:T(8,128)(2,1)S(1)}, bf16[56,384]{1,0:T(8,128)(2,1)S(1)}, u32[]{:S(2)}, u32[]{:S(2)}) collective-permute-start(bf16[56,384]{1,0:T(8,128)(2,1)S(1)} %get-tuple-element.27), channel_id=1, source_target_pairs={{0,8},{1,10},{2,9},{3,11},{4,12},{5,14},{6,13},{7,15},{8,0},{9,2},... | collective-permute-start | bytes 129032 | tf_op jit(solution)/shard_map/ppermute | solution.py:339
  55.6 6.1 %collective-permute-start.16 = (bf16[56,384]{1,0:T(8,128)(2,1)S(1)}, bf16[56,384]{1,0:T(8,128)(2,1)S(1)}, u32[]{:S(2)}, u32[]{:S(2)}) collective-permute-start(bf16[56,384]{1,0:T(8,128)(2,1)S(1)} %get-tuple-element.28), channel_id=1, source_target_pairs={{0,12},{1,14},{2,13},{3,15},{4,8},{5,10},{6,9},{7,11},{8,4},{9,6},... | collective-permute-start | bytes 129032 | tf_op jit(solution)/shard_map/ppermute | solution.py:339

commit v4 on v3

--- a/solution.py
+++ b/solution.py
@@ -21,7 +21,7 @@
     return jax.nn.silu(values * lax.rsqrt(mean_square + 1e-06) * gain_values)
 
 
-def call(body, out_shape, scratch, flops, moved, *operands, far=()):
+def call(body, out_shape, scratch, flops, moved, *operands, far=(), aliases=None):
     operands = [pltpu.with_memory_space_constraint(v, pltpu.HBM) if i in far else v for i, v in enumerate(operands)]
     spaces = [pltpu.HBM if i in far else VMEM for i in range(len(operands))]
     return pl.pallas_call(
@@ -30,6 +30,7 @@
         in_specs=[pl.BlockSpec(memory_space=space) for space in spaces],
         out_specs=jax.tree.map(lambda _: pl.BlockSpec(memory_space=VMEM), out_shape),
         scratch_shapes=scratch,
+        input_output_aliases=aliases or {},
         cost_estimate=pl.CostEstimate(flops=flops, bytes_accessed=moved, transcendentals=0),
         compiler_params=pltpu.CompilerParams(vmem_limit_bytes=48 << 20),
     )(*operands)
@@ -128,28 +129,26 @@
     return [column_sum(row, bias_row) for row in row_sums(product)]
 
 
-def pair_sums(padded, base, weight_ref, total):
-    frames, ring, channels = padded.shape[0] - PAST, padded.shape[2], padded.shape[3]
-    windows = [padded[t : t + frames, pl.ds(base, 2)].reshape(frames * 2 * ring, channels) for t in range(TAPS)]
-    product = multiply(windows, weight_ref, range(TAPS)).reshape(frames, 2, ring, -1)
+def add_rows(padded, rows, weight_ref, total):
+    frames, height, ring, channels = padded.shape[0] - PAST, padded.shape[1], padded.shape[2], padded.shape[3]
+    windows = [padded[t : t + frames].reshape(frames * height * ring, channels) for t in range(TAPS)]
+    product = multiply(windows, weight_ref, range(TAPS)).reshape(frames, height, ring, -1)
     wide = product.shape[3] // TAPS
-    taps = [[product[:, i, :, r * wide : (r + 1) * wide] for r in range(TAPS)] for i in range(2)]
-    total[base] += taps[0][2]
-    total[base + 1] += taps[0][1] + taps[1][2]
-    total[base + 2] += taps[0][0] + taps[1][1]
-    total[base + 3] += taps[1][0]
-
-
-def frame_terms(frames, early):
+    for i, row in enumerate(rows):
+        for r in range(TAPS):
+            total[row + 2 - r] += product[:, i, :, r * wide : (r + 1) * wide]
+
+
+def frame_terms(frames, wanted):
     groups = {}
     for f in range(frames):
-        taps = tuple(t for t in range(TAPS) if (PAST <= f + t < 2 * PAST) == early)
+        taps = tuple(t for t in range(TAPS) if wanted(f + t))
         groups.setdefault(taps, []).append(f)
     return [(taps, outs) for taps, outs in groups.items() if taps]
 
 
-def frame_sums(frame_of, frames, early, weight_ref, height, ring, add):
-    for taps, outs in frame_terms(frames, early):
+def frame_sums(frame_of, frames, wanted, weight_ref, height, ring, add):
+    for taps, outs in frame_terms(frames, wanted):
         windows = [jnp.concatenate([frame_of(f + t) for f in outs], axis=0) for t in taps]
         product = multiply(windows, weight_ref, taps).reshape(len(outs), height, ring, -1)
         for h, row in enumerate(row_sums(product)):
@@ -179,31 +178,28 @@
     return own_part(bias_ref[...].reshape(1, -1), row, weight_ref.shape[1] // TAPS // TAPS)
 
 
-def fill_pair(padded, pieces, base, row, breadth):
+def fill_slots(padded, pieces, breadth):
     frames = padded.shape[0]
+    picks = [(f, f) for f in range(frames)]
     for i, piece in enumerate(pieces):
         values = piece[...].astype(jnp.float32)
-        picks = [(f, f) for f in range(frames)]
-        fill_first(padded, (0, row ^ (base + i)), values, values[frames * breadth :], picks, breadth)
-
-
-def first_near_body(breadth, *refs):
+        fill_first(padded, (0, i), values, values[frames * breadth :], picks, breadth)
+
+
+def first_near_body(breadth, ks, *refs):
     *pieces, weight_ref, total, padded = refs
     row = lax.axis_index("rows")
-    fill_pair(padded, pieces, 0, row, breadth)
+    fill_slots(padded, pieces, breadth)
     total[...] = jnp.zeros_like(total)
-    pair_sums(padded, row // 2 * 2, weight_ref, total)
-
-
-def first_late_body(breadth, *refs):
-    *pieces, near_ref, weight_ref, bias_ref, out_ref, padded, total = refs
-    row = lax.axis_index("rows")
-    fill_pair(padded, pieces, 2, row, breadth)
-    total[...] = near_ref[...]
-    for pair in range(1, len(pieces) // 2 + 1):
-        pair_sums(padded, (row // 2 ^ pair) * 2, weight_ref, total)
+    add_rows(padded, [row ^ k for k in ks], weight_ref, total)
+
+
+def first_late_body(breadth, k, piece_ref, near_ref, weight_ref, bias_ref, out_ref, total, padded):
+    row = lax.axis_index("rows")
+    fill_slots(padded, [piece_ref], breadth)
+    add_rows(padded, [row ^ k], weight_ref, total)
     bias_row = bias_part(bias_ref, row, weight_ref)
-    pack_first([column_sum(total[h + 1], bias_row) for h in range(len(pieces) + 2)], out_ref, breadth)
+    pack_first([column_sum(total[h + 1], bias_row) for h in range(total.shape[0] - 2)], out_ref, breadth)
 
 
 def first_early_body(breadth, height, frames, *refs):
@@ -250,56 +246,63 @@
     regroup(pieces, gain_ref, held, breadth, middle + late, store)
 
 
-def second_part_body(frames, middle_ref, last_ref, past_ref, weight_ref, total):
+def second_late_body(frames, middle_ref, last_ref, weight_ref, total):
     height, middle, ring, channels = middle_ref.shape
-    done = set()
 
     def frame_of(p):
-        if p < PAST:
-            values = past_ref[:, p]
-            values = jnp.where(block_number() > 0, values, jnp.zeros_like(values))
-        elif p < 2 * PAST + middle:
-            values = middle_ref[:, p - 2 * PAST]
-        else:
-            values = last_ref[:, p - 2 * PAST - middle]
+        p -= 2 * PAST
+        values = middle_ref[:, p] if p < middle else last_ref[:, p - middle]
         return values.reshape(height * ring, channels)
 
     def add(f, h, values):
-        done.add(f)
+        total[h, f - PAST] = values
+
+    frame_sums(frame_of, frames, lambda p: p >= 2 * PAST, weight_ref, height, ring, add)
+
+
+def second_past_body(past_ref, weight_ref, total):
+    height, _, ring, channels = past_ref.shape
+
+    def frame_of(p):
+        values = past_ref[:, p]
+        return jnp.where(block_number() > 0, values, jnp.zeros_like(values)).reshape(height * ring, channels)
+
+    def add(f, h, values):
         total[h, f] = values
 
-    frame_sums(frame_of, frames, False, weight_ref, height, ring, add)
-    for f in range(frames):
-        if f not in done:
-            total[:, f] = jnp.zeros((height,) + total.shape[2:], jnp.float32)
+    frame_sums(frame_of, PAST, lambda p: p < PAST, weight_ref, height, ring, add)
 
 
 def second_body(breadth, *refs):
-    height = (len(refs) - 7) // 2
+    height = (len(refs) - 8) // 2
     pieces, refs = refs[:height], refs[height:]
-    part_ref, gain_ref, weight_ref, bias_ref = refs[:4]
-    outs, (early, held, branch) = refs[4 : 4 + height], refs[4 + height :]
+    late_ref, past_ref, gain_ref, weight_ref, bias_ref = refs[:5]
+    outs, (early, held, branch) = refs[5 : 5 + height], refs[5 + height :]
     row = lax.axis_index("rows")
 
     def store(h, f, ring):
         early[f, h] = ring
 
     regroup(pieces, gain_ref, held, breadth, PAST, store)
-    _, frames, ring, _ = part_ref.shape
+    _, frames, ring, _ = late_ref.shape
+    frames += PAST
     channels = early.shape[3]
     sums = {}
 
+    def held_sum(f, h):
+        return past_ref[h, f] if f < PAST else late_ref[h, f - PAST]
+
     def add(f, h, values):
-        sums[f, h] = part_ref[h, f] + values
+        sums[f, h] = held_sum(f, h) + values
 
     def frame_of(p):
         return early[p - PAST].reshape(height * ring, channels)
 
-    frame_sums(frame_of, frames, True, weight_ref, height, ring, add)
+    frame_sums(frame_of, frames, lambda p: PAST <= p < 2 * PAST, weight_ref, height, ring, add)
     bias_row = bias_part(bias_ref, row, weight_ref)
     for h in range(height):
         for f in range(frames):
-            values = sums[f, h] if (f, h) in sums else part_ref[h, f]
+            values = sums[f, h] if (f, h) in sums else held_sum(f, h)
             values = column_sum(values[None], bias_row)[0]
             branch[h, f * breadth : (f + 1) * breadth] = values[0:breadth]
     for k, out_ref in enumerate(outs):
@@ -380,14 +383,17 @@
     )
     past = following(jnp.stack([piece[late * breadth :] for piece in pieces]))
     late_rows, early_rows = padded_rows(late * (breadth + 1)), padded_rows(PAST * (breadth + 1))
+    *ks, last_k = band_order(rows)
+    sums = sds((rows + 2, late, ring, TAPS * width), f32)
     near_sums = call(
-        functools.partial(first_near_body, breadth), sds((rows + 2, late, ring, TAPS * width), f32),
-        [padded(frames)], late * work // 2, 10 * size, *pieces[:2], near,
-    )
-    part = call(
-        functools.partial(first_late_body, breadth), sds((late_rows, channels), bf16),
-        [padded(frames), VMEM((rows + 2, late, ring, TAPS * width), f32)],
-        late * work // 2, 10 * size, *pieces[2:], near_sums, near, bias_one,
+        functools.partial(first_near_body, breadth, ks), sums,
+        [VMEM((frames, rows - 1, ring, channels), bf16)], late * work * (rows - 1) // rows, 10 * size,
+        *[pieces[k] for k in ks], near,
+    )
+    part, _ = call(
+        functools.partial(first_late_body, breadth, last_k), [sds((late_rows, channels), bf16), sums],
+        [VMEM((frames, 1, ring, channels), bf16)], late * work // rows, 10 * size,
+        pieces[last_k], near_sums, near, bias_one, aliases={1: 1},
     )
     late_parts = spread(part)
     part = call(
@@ -402,14 +408,18 @@
     )
     past = following(last)
     back_rows = padded_rows(-(-frames * breadth // rows))
-    part = call(
-        functools.partial(second_part_body, frames), sds((rows, frames, ring, TAPS * width), f32), [],
-        frames * work // 2, 20 * size, second, last, past, weights[1],
+    late_sums = call(
+        functools.partial(second_late_body, frames), sds((rows, late, ring, TAPS * width), f32), [],
+        frames * work // 3, 10 * size, second, last, weights[1],
+    )
+    past_sums = call(
+        second_past_body, sds((rows, PAST, ring, TAPS * width), f32), [],
+        frames * work // 5, 10 * size, past, weights[1],
     )
     branch = call(
         functools.partial(second_body, breadth), [sds((back_rows, channels), bf16)] * rows,
         [padded(PAST), VMEM((rows, early_rows, channels), f32), VMEM((rows, back_rows * rows, width), f32)],
-        frames * work // 2, 20 * size, *early_parts, part, gain_two, weights[1], bias_two,
+        frames * work // 2, 20 * size, *early_parts, late_sums, past_sums, gain_two, weights[1], bias_two,
     )
     branch = turn(branch)
     result = call(
@@ -417,6 +427,11 @@
         2 * size, 6 * size, own, *branch,
     )
     return result.reshape(frames, height, breadth, channels)
+
+
+def band_order(rows):
+    first = [k for k in range(rows - 1, 0, -1) if k != 2]
+    return first + [0] + [k for k in (2,) if k < rows]
 
 
 def solution(mesh):

time: 62.9 us -> 64.5 us (1.025)
  waiting for transfers between devices: 23.5 us -> 24.3 us
    pallas_call x10 -> x11, Pallas kernels: 13.5 us -> 13.9 us  [call(): pl.pallas_call(body, out_shape=out_shape, in_specs=[pl.BlockSpec(memory_s...]
  transfers between devices with their start and end apart: 17 -> 17, of which waited for: 8 -> 7; matrix products, arithmetic and copies ran while one was open for 0% -> 0% of each run, Pallas kernels for 14% -> 17%
where the time goes in v4:
time: 64.5 us; the launch traced here: 64.3 us
  starting transfers between devices  25.8 us (40%)
  waiting for transfers between devices  24.3 us (38%)
  Pallas kernels  13.9 us (22%)
    ppermute x10, starting transfers between devices, moved(): lax.ppermute(values, AXES, [(place[device], place[target(*device)]) for d...  18.6 us
    ppermute x10, waiting for transfers between devices, moved(): lax.ppermute(values, AXES, [(place[device], place[target(*device)]) for d...  14 us
    pallas_call x11, Pallas kernels, call(): pl.pallas_call(body, out_shape=out_shape, in_specs=[pl.BlockSpec(memory_s...  13.9 us
    ppermute x6, waiting for transfers between devices, spread(): lax.ppermute(values, 'rows', [(z, z ^ k) for z in range(rows)])  9.79 us
    ppermute x6, starting transfers between devices, spread(): lax.ppermute(values, 'rows', [(z, z ^ k) for z in range(rows)])  7.23 us
  transfers between devices with their start and end apart: 17, of which 7 were waited for; matrix products, arithmetic and copies ran while one was open for 0% of the time, Pallas kernels for 17%

profile of v4, /device:TPU:1, one launch (start us, length us, event | category | flops | bytes accessed | tf_op | source)
XLA Modules:
  0.0 64.3 jit_solution(9482253458733614958)
XLA Ops:
  0.0 0.0 collective-permute-start
  0.0 1.1 %shard_map.73 = (bf16[200,384]{1,0:T(8,128)(2,1)S(1)}, f32[384]{0:T(512)S(1)}) custom-call(bf16[5,40,384]{2,1,0:T(8,128)(2,1)} %bitcast.18, f32[384]{0:T(512)} %far_gain_ref.1), custom_call_target="tpu_custom_call" | custom-call | flops 921600 | bytes 552960 | tf_op jit(solution)/shard_map/pallas_call | solution.py:27
  1.1 0.5 collective-permute-done.other_ref
  1.6 0.1 shard_map.74
  1.7 5.7 %collective-permute-start.4 = (bf16[216,384]{1,0:T(8,128)(2,1)S(1)}, bf16[216,384]{1,0:T(8,128)(2,1)S(1)}, u32[]{:S(2)}, u32[]{:S(2)}) collective-permute-start(bf16[216,384]{1,0:T(8,128)(2,1)S(1)} %shard_map.74), channel_id=1, source_target_pairs={{0,12},{1,14},{2,13},{3,15},{4,8},{5,10},{6,9},{7,11},{8,4},{9,6},... | collective-permute-start | bytes 497672 | tf_op jit(solution)/shard_map/ppermute | solution.py:342
  7.4 1.6 %shard_map.75 = (f32[384]{0:T(512)S(1)}, f32[384]{0:T(512)S(1)}, f32[384]{0:T(512)S(1)}, bf16[3,864,384]{2,1,0:T(8,128)(2,1)S(1)}) custom-call(f32[384]{0:T(512)} %refs_0_.1, f32[384]{0:T(512)} %refs_1_.1, f32[384]{0:T(512)} %refs_2_.1, bf16[3,864,384]{2,1,0:T(8,128)(2,1)} %bitcast.20), custom_call_target="tpu_custom_call" | custom-call | flops 92160 | bytes 368640 | tf_op jit(solution)/shard_map/pallas_call | solution.py:27
  9.0 0.1 collective-permute-start.3
  9.1 1.4 %collective-permute-start.2 = (bf16[216,384]{1,0:T(8,128)(2,1)S(1)}, bf16[216,384]{1,0:T(8,128)(2,1)S(1)}, u32[]{:S(2)}, u32[]{:S(2)}) collective-permute-start(bf16[216,384]{1,0:T(8,128)(2,1)S(1)} %shard_map.74), channel_id=1, source_target_pairs={{0,4},{1,6},{2,5},{3,7},{4,0},{5,2},{6,1},{7,3},{8,12},{9,14},{10,... | collective-permute-start | bytes 497672 | tf_op jit(solution)/shard_map/ppermute | solution.py:342
  10.5 2.3 %collective-permute-start.1 = (bf16[216,384]{1,0:T(8,128)(2,1)S(1)}, bf16[216,384]{1,0:T(8,128)(2,1)S(1)}, u32[]{:S(2)}, u32[]{:S(2)}) collective-permute-start(bf16[216,384]{1,0:T(8,128)(2,1)S(1)} %shard_map.74), channel_id=1, source_target_pairs={{0,0},{1,2},{2,1},{3,3},{4,4},{5,6},{6,5},{7,7},{8,8},{9,10},{10,9... | collective-permute-start | bytes 497672 | tf_op jit(solution)/shard_map/ppermute | solution.py:342
  12.8 0.0 collective-permute-done.4.refs_3_.refs_0_
  12.8 8.7 %collective-permute-done.3.refs_2_.piece_ref = bf16[216,384]{1,0:T(8,128)(2,1)S(1)} collective-permute-done((bf16[216,384]{1,0:T(8,128)(2,1)S(1)}, bf16[216,384]{1,0:T(8,128)(2,1)S(1)}, u32[]{:S(2)}, u32[]{:S(2)}) %collective-permute-start.3) | collective-permute-done | bytes 165920 | tf_op jit(solution)/shard_map/ppermute | solution.py:342
  21.5 0.0 collective-permute-done.2.refs_1_
  21.5 0.0 collective-permute-done.1.refs_0_.refs_2_
  21.5 0.1 pad_maximum_fusion
  21.6 0.3 collective-permute-start.5
  21.9 1.7 %shard_map.77.near_ref = f32[6,3,48,288]{3,2,1,0:T(8,128)S(1)} custom-call(bf16[216,384]{1,0:T(8,128)(2,1)S(1)} %collective-permute-done.4.refs_3_.refs_0_, bf16[216,384]{1,0:T(8,128)(2,1)S(1)} %collective-permute-done.2.refs_1_, bf16[216,384]{1,0:T(8,128)(2,1)S(1)} %collective-permute-done.1.refs_0_.refs_2_, ...), custom_call_target="tpu_custom_call" | custom-call | flops 859963392 | bytes 921600 | tf_op jit(solution)/shard_map/pallas_call | solution.py:27
  23.6 1.3 %shard_map.78 = (bf16[128,384]{1,0:T(8,128)(2,1)S(1)}, f32[6,3,48,288]{3,2,1,0:T(8,128)S(1)}) custom-call(bf16[216,384]{1,0:T(8,128)(2,1)S(1)} %collective-permute-done.3.refs_2_.piece_ref, f32[6,3,48,288]{3,2,1,0:T(8,128)S(1)} %shard_map.77.near_ref, ...), custom_call_target="tpu_custom_call", output_to_operand_aliasing={{1}: (1, {})} | custom-call | flops 286654464 | bytes 921600 | tf_op jit(solution)/shard_map/pallas_call | solution.py:27
  24.9 0.0 copy-start
  24.9 2.3 %collective-permute-start.11 = (bf16[128,384]{1,0:T(8,128)(2,1)S(1)}, bf16[128,384]{1,0:T(8,128)(2,1)S(1)}, u32[]{:S(2)}, u32[]{:S(2)}) collective-permute-start(bf16[128,384]{1,0:T(8,128)(2,1)S(1)} %get-tuple-element.22.refs_0_), channel_id=1, source_target_pairs={{0,12},{4,8},{8,4},{12,0},{1,13},{5,9},{9,5},{13,1},{2,14},{6,10},... | collective-permute-start | bytes 294920 | tf_op jit(solution)/shard_map/ppermute | solution.py:353
  27.2 0.0 collective-permute-start.10
  27.2 1.3 %collective-permute-start.9 = (bf16[128,384]{1,0:T(8,128)(2,1)S(1)}, bf16[128,384]{1,0:T(8,128)(2,1)S(1)}, u32[]{:S(2)}, u32[]{:S(2)}) collective-permute-start(bf16[128,384]{1,0:T(8,128)(2,1)S(1)} %get-tuple-element.22.refs_0_), channel_id=1, source_target_pairs={{0,4},{4,0},{8,12},{12,8},{1,5},{5,1},{9,13},{13,9},{2,6},{6,2},{1... | collective-permute-start | bytes 294920 | tf_op jit(solution)/shard_map/ppermute | solution.py:353
  28.5 2.3 %collective-permute-done.11.refs_3_ = bf16[128,384]{1,0:T(8,128)(2,1)S(1)} collective-permute-done((bf16[128,384]{1,0:T(8,128)(2,1)S(1)}, bf16[128,384]{1,0:T(8,128)(2,1)S(1)}, u32[]{:S(2)}, u32[]{:S(2)}) %collective-permute-start.11) | collective-permute-done | bytes 98336 | tf_op jit(solution)/shard_map/ppermute | solution.py:353
  30.9 4.9 %collective-permute-done.10.refs_2_ = bf16[128,384]{1,0:T(8,128)(2,1)S(1)} collective-permute-done((bf16[128,384]{1,0:T(8,128)(2,1)S(1)}, bf16[128,384]{1,0:T(8,128)(2,1)S(1)}, u32[]{:S(2)}, u32[]{:S(2)}) %collective-permute-start.10) | collective-permute-done | bytes 98336 | tf_op jit(solution)/shard_map/ppermute | solution.py:353
  35.7 0.0 collective-permute-done.9.refs_1_
  35.7 0.7 %shard_map.79 = (bf16[4,1,48,384]{3,2,1,0:T(8,128)(2,1)S(1)}, bf16[4,2,48,384]{3,2,1,0:T(8,128)(2,1)S(1)}) custom-call(bf16[128,384]{1,0:T(8,128)(2,1)S(1)} %get-tuple-element.22.refs_0_, bf16[128,384]{1,0:T(8,128)(2,1)S(1)} %collective-permute-done.9.refs_1_, bf16[128,384]{1,0:T(8,128)(2,1)S(1)} %collective-permute-done.10.refs_2_, ...), custom_call_target="tpu_custom_call" | custom-call | flops 3686400 | bytes 1474560 | tf_op jit(solution)/shard_map/pallas_call | solution.py:27
  36.5 0.6 collective-permute-start.12
  37.0 0.0 collective-permute-done.5.refs_4_
  37.0 1.6 %shard_map.76.refs_0_ = bf16[88,384]{1,0:T(8,128)(2,1)S(1)} custom-call(bf16[216,384]{1,0:T(8,128)(2,1)S(1)} %collective-permute-done.1.refs_0_.refs_2_, bf16[216,384]{1,0:T(8,128)(2,1)S(1)} %collective-permute-done.2.refs_1_, bf16[216,384]{1,0:T(8,128)(2,1)S(1)} %collective-permute-done.3.refs_2_.piece_ref, ...), custom_call_target="tpu_custom_call" | custom-call | flops 764411904 | bytes 1843200 | tf_op jit(solution)/shard_map/pallas_call | solution.py:27
  38.7 2.3 %collective-permute-start.8 = (bf16[88,384]{1,0:T(8,128)(2,1)S(1)}, bf16[88,384]{1,0:T(8,128)(2,1)S(1)}, u32[]{:S(2)}, u32[]{:S(2)}) collective-permute-start(bf16[88,384]{1,0:T(8,128)(2,1)S(1)} %shard_map.76.refs_0_), channel_id=1, source_target_pairs={{0,12},{4,8},{8,4},{12,0},{1,13},{5,9},{9,5},{13,1},{2,14},{6,10},... | collective-permute-start | bytes 202760 | tf_op jit(solution)/shard_map/ppermute | solution.py:353
  40.9 0.0 collective-permute-start.7
  40.9 1.3 %collective-permute-start.6 = (bf16[88,384]{1,0:T(8,128)(2,1)S(1)}, bf16[88,384]{1,0:T(8,128)(2,1)S(1)}, u32[]{:S(2)}, u32[]{:S(2)}) collective-permute-start(bf16[88,384]{1,0:T(8,128)(2,1)S(1)} %shard_map.76.refs_0_), channel_id=1, source_target_pairs={{0,4},{4,0},{8,12},{12,8},{1,5},{5,1},{9,13},{13,9},{2,6},{6,2},{1... | collective-permute-start | bytes 202760 | tf_op jit(solution)/shard_map/ppermute | solution.py:353
  42.3 1.6 %shard_map.80.refs_4_ = f32[4,3,48,288]{3,2,1,0:T(8,128)S(1)} custom-call(bf16[4,1,48,384]{3,2,1,0:T(8,128)(2,1)S(1)} %get-tuple-element.24.middle_ref, bf16[4,2,48,384]{3,2,1,0:T(8,128)(2,1)S(1)} %get-tuple-element.25.last_ref, bf16[3,864,384]{2,1,0:T(8,128)(2,1)S(1)} %bitcast.14), custom_call_target="tpu_custom_call" | custom-call | flops 637009920 | bytes 921600 | tf_op jit(solution)/shard_map/pallas_call | solution.py:27
  43.9 0.0 collective-permute-done.12.past_ref
  43.9 1.0 %shard_map.81.refs_5_ = f32[4,2,48,288]{3,2,1,0:T(8,128)S(1)} custom-call(bf16[4,2,48,384]{3,2,1,0:T(8,128)(2,1)S(1)} %collective-permute-done.12.past_ref, bf16[3,864,384]{2,1,0:T(8,128)(2,1)S(1)} %bitcast.15), custom_call_target="tpu_custom_call" | custom-call | flops 382205952 | bytes 921600 | tf_op jit(solution)/shard_map/pallas_call | solution.py:27
  44.9 0.0 copy-start.1
  44.9 0.0 collective-permute-done.8.refs_3_
  44.9 2.6 %collective-permute-done.7.refs_2_ = bf16[88,384]{1,0:T(8,128)(2,1)S(1)} collective-permute-done((bf16[88,384]{1,0:T(8,128)(2,1)S(1)}, bf16[88,384]{1,0:T(8,128)(2,1)S(1)}, u32[]{:S(2)}, u32[]{:S(2)}) %collective-permute-start.7) | collective-permute-done | bytes 67616 | tf_op jit(solution)/shard_map/ppermute | solution.py:353
  47.5 0.0 collective-permute-done.6.refs_1_
  47.5 2.2 %shard_map.82 = (bf16[56,384]{1,0:T(8,128)(2,1)S(1)}, bf16[56,384]{1,0:T(8,128)(2,1)S(1)}, bf16[56,384]{1,0:T(8,128)(2,1)S(1)}, bf16[56,384]{1,0:T(8,128)(2,1)S(1)}) custom-call(bf16[88,384]{1,0:T(8,128)(2,1)S(1)} %shard_map.76.refs_0_, bf16[88,384]{1,0:T(8,128)(2,1)S(1)} %collective-permute-done.6.refs_1_, ...), custom_call_target="tpu_custom_call" | custom-call | flops 955514880 | bytes 1843200 | tf_op jit(solution)/shard_map/pallas_call | solution.py:27
  49.7 3.8 %collective-permute-start.13 = (bf16[56,384]{1,0:T(8,128)(2,1)S(1)}, bf16[56,384]{1,0:T(8,128)(2,1)S(1)}, u32[]{:S(2)}, u32[]{:S(2)}) collective-permute-start(bf16[56,384]{1,0:T(8,128)(2,1)S(1)} %get-tuple-element.27), channel_id=1, source_target_pairs={{0,0},{1,2},{2,1},{3,3},{4,4},{5,6},{6,5},{7,7},{8,8},{9,10},{10,9... | collective-permute-start | bytes 129032 | tf_op jit(solution)/shard_map/ppermute | solution.py:342
  53.5 0.2 collective-permute-start.14
  53.7 3.5 %collective-permute-start.15 = (bf16[56,384]{1,0:T(8,128)(2,1)S(1)}, bf16[56,384]{1,0:T(8,128)(2,1)S(1)}, u32[]{:S(2)}, u32[]{:S(2)}) collective-permute-start(bf16[56,384]{1,0:T(8,128)(2,1)S(1)} %get-tuple-element.29), channel_id=1, source_target_pairs={{0,8},{1,10},{2,9},{3,11},{4,12},{5,14},{6,13},{7,15},{8,0},{9,2},... | collective-permute-start | bytes 129032 | tf_op jit(solution)/shard_map/ppermute | solution.py:342
  57.2 0.8 %collective-permute-start.16 = (bf16[56,384]{1,0:T(8,128)(2,1)S(1)}, bf16[56,384]{1,0:T(8,128)(2,1)S(1)}, u32[]{:S(2)}, u32[]{:S(2)}) collective-permute-start(bf16[56,384]{1,0:T(8,128)(2,1)S(1)} %get-tuple-element.30), channel_id=1, source_target_pairs={{0,12},{1,14},{2,13},{3,15},{4,8},{5,10},{6,9},{7,11},{8,4},{9,6},... | collective-permute-start | bytes 129032 | tf_op jit(solution)/shard_map/ppermute | solution.py:342
  58.0 0.0 collective-permute-done.13.refs_0_
  58.0 0.0 collective-permute-done.14.refs_1_
  58.0 1.7 %collective-permute-done.15.refs_2_ = bf16[56,384]{1,0:T(8,128)(2,1)S(1)} collective-permute-done((bf16[56,384]{1,0:T(8,128)(2,1)S(1)}, bf16[56,384]{1,0:T(8,128)(2,1)S(1)}, u32[]{:S(2)}, u32[]{:S(2)}) %collective-permute-start.15) | collective-permute-done | bytes 43040 | tf_op jit(solution)/shard_map/ppermute | solution.py:342
  59.8 3.6 %collective-permute-done.16.refs_3_ = bf16[56,384]{1,0:T(8,128)(2,1)S(1)} collective-permute-done((bf16[56,384]{1,0:T(8,128)(2,1)S(1)}, bf16[56,384]{1,0:T(8,128)(2,1)S(1)}, u32[]{:S(2)}, u32[]{:S(2)}) %collective-permute-start.16) | collective-permute-done | bytes 43040 | tf_op jit(solution)/shard_map/ppermute | solution.py:342
  63.4 1.0 %shard_map.83 = bf16[5,40,384]{2,1,0:T(8,128)(2,1)} custom-call(bf16[5,40,384]{2,1,0:T(8,128)(2,1)S(1)} %bitcast.19, bf16[56,384]{1,0:T(8,128)(2,1)S(1)} %collective-permute-done.13.refs_0_, bf16[56,384]{1,0:T(8,128)(2,1)S(1)} %collective-permute-done.14.refs_1_, bf16[56,384]{1,0:T(8,128)(2,1)S(1)} %collective-permute-done.15.refs_2_, ...), custom_call_target="tpu_custom_call" | custom-call | flops 184320 | bytes 552960 | tf_op jit(solution)/shard_map/pallas_call | solution.py:27
  (6 shorter events, 0.0 us)
Async XLA Ops:
  0.0 1.6 %collective-permute-start = (bf16[5,40,384]{2,1,0:T(8,128)(2,1)}, bf16[5,40,384]{2,1,0:T(8,128)(2,1)S(1)}, u32[]{:S(2)}, u32[]{:S(2)}) collective-permute-start(bf16[5,40,384]{2,1,0:T(8,128)(2,1)} %bitcast.17), channel_id=1, source_target_pairs={{0,1},{1,0},{2,3},{3,2},{4,5},{5,4},{6,7},{7,6},{8,9},{9,8},{10,11... | collective-permute-start | bytes 460808 | tf_op jit(solution)/shard_map/ppermute | solution.py:362
  1.7 11.1 %collective-permute-start.4 = (bf16[216,384]{1,0:T(8,128)(2,1)S(1)}, bf16[216,384]{1,0:T(8,128)(2,1)S(1)}, u32[]{:S(2)}, u32[]{:S(2)}) collective-permute-start(bf16[216,384]{1,0:T(8,128)(2,1)S(1)} %shard_map.74), channel_id=1, source_target_pairs={{0,12},{1,14},{2,13},{3,15},{4,8},{5,10},{6,9},{7,11},{8,4},{9,6},... | collective-permute-start | bytes 497672 | tf_op jit(solution)/shard_map/ppermute | solution.py:342
  9.0 12.4 %collective-permute-start.3 = (bf16[216,384]{1,0:T(8,128)(2,1)S(1)}, bf16[216,384]{1,0:T(8,128)(2,1)S(1)}, u32[]{:S(2)}, u32[]{:S(2)}) collective-permute-start(bf16[216,384]{1,0:T(8,128)(2,1)S(1)} %shard_map.74), channel_id=1, source_target_pairs={{0,8},{1,10},{2,9},{3,11},{4,12},{5,14},{6,13},{7,15},{8,0},{9,2},... | collective-permute-start | bytes 497672 | tf_op jit(solution)/shard_map/ppermute | solution.py:342
  9.1 12.4 %collective-permute-start.2 = (bf16[216,384]{1,0:T(8,128)(2,1)S(1)}, bf16[216,384]{1,0:T(8,128)(2,1)S(1)}, u32[]{:S(2)}, u32[]{:S(2)}) collective-permute-start(bf16[216,384]{1,0:T(8,128)(2,1)S(1)} %shard_map.74), channel_id=1, source_target_pairs={{0,4},{1,6},{2,5},{3,7},{4,0},{5,2},{6,1},{7,3},{8,12},{9,14},{10,... | collective-permute-start | bytes 497672 | tf_op jit(solution)/shard_map/ppermute | solution.py:342
  10.5 11.0 %collective-permute-start.1 = (bf16[216,384]{1,0:T(8,128)(2,1)S(1)}, bf16[216,384]{1,0:T(8,128)(2,1)S(1)}, u32[]{:S(2)}, u32[]{:S(2)}) collective-permute-start(bf16[216,384]{1,0:T(8,128)(2,1)S(1)} %shard_map.74), channel_id=1, source_target_pairs={{0,0},{1,2},{2,1},{3,3},{4,4},{5,6},{6,5},{7,7},{8,8},{9,10},{10,9... | collective-permute-start | bytes 497672 | tf_op jit(solution)/shard_map/ppermute | solution.py:342
  21.6 15.4 %collective-permute-start.5 = (bf16[4,96,384]{2,1,0:T(8,128)(2,1)S(1)}, bf16[4,96,384]{2,1,0:T(8,128)(2,1)S(1)}, u32[]{:S(2)}, u32[]{:S(2)}) collective-permute-start(bf16[4,96,384]{2,1,0:T(8,128)(2,1)S(1)} %pad_maximum_fusion), channel_id=1, source_target_pairs={{0,1},{1,0},{2,3},{3,2},{4,5},{5,4},{6,7},{7,6},{8,9},{9,8},{10,11... | collective-permute-start | bytes 884744 | tf_op jit(solution)/shard_map/ppermute | solution.py:342
  24.9 17.4 %copy-start = (bf16[27,96,384]{2,1,0:T(8,128)(2,1)S(1)}, bf16[27,96,384]{2,1,0:T(8,128)(2,1)}, u32[]{:S(2)}) copy-start(bf16[27,96,384]{2,1,0:T(8,128)(2,1)} %param.12) | copy-start | bytes 5971972
  24.9 5.9 %collective-permute-start.11 = (bf16[128,384]{1,0:T(8,128)(2,1)S(1)}, bf16[128,384]{1,0:T(8,128)(2,1)S(1)}, u32[]{:S(2)}, u32[]{:S(2)}) collective-permute-start(bf16[128,384]{1,0:T(8,128)(2,1)S(1)} %get-tuple-element.22.refs_0_), channel_id=1, source_target_pairs={{0,12},{4,8},{8,4},{12,0},{1,13},{5,9},{9,5},{13,1},{2,14},{6,10},... | collective-permute-start | bytes 294920 | tf_op jit(solution)/shard_map/ppermute | solution.py:353
  27.2 8.5 %collective-permute-start.10 = (bf16[128,384]{1,0:T(8,128)(2,1)S(1)}, bf16[128,384]{1,0:T(8,128)(2,1)S(1)}, u32[]{:S(2)}, u32[]{:S(2)}) collective-permute-start(bf16[128,384]{1,0:T(8,128)(2,1)S(1)} %get-tuple-element.22.refs_0_), channel_id=1, source_target_pairs={{0,8},{4,12},{8,0},{12,4},{1,9},{5,13},{9,1},{13,5},{2,10},{6,14},... | collective-permute-start | bytes 294920 | tf_op jit(solution)/shard_map/ppermute | solution.py:353
  27.2 8.5 %collective-permute-start.9 = (bf16[128,384]{1,0:T(8,128)(2,1)S(1)}, bf16[128,384]{1,0:T(8,128)(2,1)S(1)}, u32[]{:S(2)}, u32[]{:S(2)}) collective-permute-start(bf16[128,384]{1,0:T(8,128)(2,1)S(1)} %get-tuple-element.22.refs_0_), channel_id=1, source_target_pairs={{0,4},{4,0},{8,12},{12,8},{1,5},{5,1},{9,13},{13,9},{2,6},{6,2},{1... | collective-permute-start | bytes 294920 | tf_op jit(solution)/shard_map/ppermute | solution.py:353
  36.5 7.4 %collective-permute-start.12 = (bf16[4,2,48,384]{3,2,1,0:T(8,128)(2,1)S(1)}, bf16[4,2,48,384]{3,2,1,0:T(8,128)(2,1)S(1)}, u32[]{:S(2)}, u32[]{:S(2)}) collective-permute-start(bf16[4,2,48,384]{3,2,1,0:T(8,128)(2,1)S(1)} %get-tuple-element.25.last_ref), channel_id=1, source_target_pairs={{0,1},{1,0},{2,3},{3,2},{4,5},{5,4},{6,7},{7,6},{8,9},{9,8},{10,11... | collective-permute-start | bytes 884744 | tf_op jit(solution)/shard_map/ppermute | solution.py:342
  38.7 6.2 %collective-permute-start.8 = (bf16[88,384]{1,0:T(8,128)(2,1)S(1)}, bf16[88,384]{1,0:T(8,128)(2,1)S(1)}, u32[]{:S(2)}, u32[]{:S(2)}) collective-permute-start(bf16[88,384]{1,0:T(8,128)(2,1)S(1)} %shard_map.76.refs_0_), channel_id=1, source_target_pairs={{0,12},{4,8},{8,4},{12,0},{1,13},{5,9},{9,5},{13,1},{2,14},{6,10},... | collective-permute-start | bytes 202760 | tf_op jit(solution)/shard_map/ppermute | solution.py:353
  40.9 6.6 %collective-permute-start.7 = (bf16[88,384]{1,0:T(8,128)(2,1)S(1)}, bf16[88,384]{1,0:T(8,128)(2,1)S(1)}, u32[]{:S(2)}, u32[]{:S(2)}) collective-permute-start(bf16[88,384]{1,0:T(8,128)(2,1)S(1)} %shard_map.76.refs_0_), channel_id=1, source_target_pairs={{0,8},{4,12},{8,0},{12,4},{1,9},{5,13},{9,1},{13,5},{2,10},{6,14},... | collective-permute-start | bytes 202760 | tf_op jit(solution)/shard_map/ppermute | solution.py:353
  40.9 6.6 %collective-permute-start.6 = (bf16[88,384]{1,0:T(8,128)(2,1)S(1)}, bf16[88,384]{1,0:T(8,128)(2,1)S(1)}, u32[]{:S(2)}, u32[]{:S(2)}) collective-permute-start(bf16[88,384]{1,0:T(8,128)(2,1)S(1)} %shard_map.76.refs_0_), channel_id=1, source_target_pairs={{0,4},{4,0},{8,12},{12,8},{1,5},{5,1},{9,13},{13,9},{2,6},{6,2},{1... | collective-permute-start | bytes 202760 | tf_op jit(solution)/shard_map/ppermute | solution.py:353
  44.9 18.5 %copy-start.1 = (bf16[5,1,40,384]{3,2,1,0:T(8,128)(2,1)S(1)}, bf16[5,1,40,384]{3,2,1,0:T(8,128)(2,1)}, u32[]{:S(2)}) copy-start(bf16[5,1,40,384]{3,2,1,0:T(8,128)(2,1)} %param.7) | copy-start | bytes 460804
  49.7 8.3 %collective-permute-start.13 = (bf16[56,384]{1,0:T(8,128)(2,1)S(1)}, bf16[56,384]{1,0:T(8,128)(2,1)S(1)}, u32[]{:S(2)}, u32[]{:S(2)}) collective-permute-start(bf16[56,384]{1,0:T(8,128)(2,1)S(1)} %get-tuple-element.27), channel_id=1, source_target_pairs={{0,0},{1,2},{2,1},{3,3},{4,4},{5,6},{6,5},{7,7},{8,8},{9,10},{10,9... | collective-permute-start | bytes 129032 | tf_op jit(solution)/shard_map/ppermute | solution.py:342
  53.5 4.5 %collective-permute-start.14 = (bf16[56,384]{1,0:T(8,128)(2,1)S(1)}, bf16[56,384]{1,0:T(8,128)(2,1)S(1)}, u32[]{:S(2)}, u32[]{:S(2)}) collective-permute-start(bf16[56,384]{1,0:T(8,128)(2,1)S(1)} %get-tuple-element.28), channel_id=1, source_target_pairs={{0,4},{1,6},{2,5},{3,7},{4,0},{5,2},{6,1},{7,3},{8,12},{9,14},{10,... | collective-permute-start | bytes 129032 | tf_op jit(solution)/shard_map/ppermute | solution.py:342
  53.7 6.0 %collective-permute-start.15 = (bf16[56,384]{1,0:T(8,128)(2,1)S(1)}, bf16[56,384]{1,0:T(8,128)(2,1)S(1)}, u32[]{:S(2)}, u32[]{:S(2)}) collective-permute-start(bf16[56,384]{1,0:T(8,128)(2,1)S(1)} %get-tuple-element.29), channel_id=1, source_target_pairs={{0,8},{1,10},{2,9},{3,11},{4,12},{5,14},{6,13},{7,15},{8,0},{9,2},... | collective-permute-start | bytes 129032 | tf_op jit(solution)/shard_map/ppermute | solution.py:342
  57.2 6.1 %collective-permute-start.16 = (bf16[56,384]{1,0:T(8,128)(2,1)S(1)}, bf16[56,384]{1,0:T(8,128)(2,1)S(1)}, u32[]{:S(2)}, u32[]{:S(2)}) collective-permute-start(bf16[56,384]{1,0:T(8,128)(2,1)S(1)} %get-tuple-element.30), channel_id=1, source_target_pairs={{0,12},{1,14},{2,13},{3,15},{4,8},{5,10},{6,9},{7,11},{8,4},{9,6},... | collective-permute-start | bytes 129032 | tf_op jit(solution)/shard_map/ppermute | solution.py:342

commit v5 on v4

--- a/solution.py
+++ b/solution.py
@@ -157,7 +157,7 @@
 
 
 def block_number():
-    return lax.axis_index("tm") // 2 * 2 + lax.axis_index("cols")
+    return lax.axis_index("tm") // 2 * 2 + 1 - lax.axis_index("cols")
 
 
 def pack_first(rows, out_ref, breadth):
@@ -342,10 +342,13 @@
         return lax.ppermute(values, AXES, [(place[device], place[target(*device)]) for device in every])
 
     def turned(values, k):
-        return moved(values, lambda z, x, c: (z ^ k, x // 2 * 2 + c, x % 2))
+        return moved(values, lambda z, x, c: (z ^ k, x // 2 * 2 + c, 1 - x % 2))
+
+    def returned(values, k):
+        return moved(values, lambda z, x, c: (z ^ k, x // 2 * 2 + 1 - c, x % 2))
 
     def following(values):
-        return moved(values, lambda z, x, c: (z, x, 1) if c == 0 else (z, (x + 2) % tm, 0))
+        return moved(values, lambda z, x, c: (z, x, 0) if c == 1 else (z, (x + 2) % tm, 1))
 
     def spread(values):
         parts = [values]
@@ -353,10 +356,10 @@
             parts.append(lax.ppermute(values, "rows", [(z, z ^ k) for z in range(rows)]))
         return parts
 
-    def turn(values):
+    def turn(values, way):
         parts = []
         for k in range(rows):
-            parts.append(turned(values[k], k))
+            parts.append(way(values[k], k))
         return parts
 
     other = lax.ppermute(own, "cols", [(0, 1), (1, 0)])
@@ -375,7 +378,7 @@
     )
     total = frames * breadth + padded_rows(EDGE * frames)
     band = call(ends_body, sds((total, channels), bf16), [], size, 4 * size, center, other, gain_one)
-    pieces = turn([band] * rows)
+    pieces = turn([band] * rows, turned)
     small = (bias_one, gain_two, bias_two, weights[0])
     bias_one, gain_two, bias_two, near = call(
         stage_body, [sds(v.shape, v.dtype) for v in small], [pltpu.SemaphoreType.DMA((len(small),))],
@@ -421,7 +424,7 @@
         [padded(PAST), VMEM((rows, early_rows, channels), f32), VMEM((rows, back_rows * rows, width), f32)],
         frames * work // 2, 20 * size, *early_parts, late_sums, past_sums, gain_two, weights[1], bias_two,
     )
-    branch = turn(branch)
+    branch = turn(branch, returned)
     result = call(
         last_body, sds((frames, breadth, channels), bf16), [VMEM((rows, back_rows * rows, width), f32)],
         2 * size, 6 * size, own, *branch,

time: 64.5 us -> 61.1 us (0.947)
  the two profiles are of different devices: /device:TPU:1 before, /device:TPU:0 now
where the time goes in v5:
time: 61.1 us; the launch traced here: 60.9 us
  waiting for transfers between devices  25.6 us (42%)
  starting transfers between devices  21.1 us (35%)
  Pallas kernels  13.9 us (23%)
    ppermute x10, waiting for transfers between devices, moved(): lax.ppermute(values, AXES, [(place[device], place[target(*device)]) for d...  16.5 us
    pallas_call x11, Pallas kernels, call(): pl.pallas_call(body, out_shape=out_shape, in_specs=[pl.BlockSpec(memory_s...  13.9 us
    ppermute x10, starting transfers between devices, moved(): lax.ppermute(values, AXES, [(place[device], place[target(*device)]) for d...  11.7 us
    ppermute x6, waiting for transfers between devices, spread(): lax.ppermute(values, 'rows', [(z, z ^ k) for z in range(rows)])  9.01 us
    ppermute x6, starting transfers between devices, spread(): lax.ppermute(values, 'rows', [(z, z ^ k) for z in range(rows)])  8.91 us
  transfers between devices with their start and end apart: 17, of which 8 were waited for; matrix products, arithmetic and copies ran while one was open for 0% of the time, Pallas kernels for 18%

profile of v5, /device:TPU:0, one launch (start us, length us, event | category | flops | bytes accessed | tf_op | source)
XLA Modules:
  0.0 60.9 jit_solution(14055058750779021714)
XLA Ops:
  0.0 0.5 collective-permute-start
  0.5 1.1 %shard_map.73 = (bf16[200,384]{1,0:T(8,128)(2,1)S(1)}, f32[384]{0:T(512)S(1)}) custom-call(bf16[5,40,384]{2,1,0:T(8,128)(2,1)} %bitcast.18, f32[384]{0:T(512)} %far_gain_ref.1), custom_call_target="tpu_custom_call" | custom-call | flops 921600 | bytes 552960 | tf_op jit(solution)/shard_map/pallas_call | solution.py:27
  1.6 0.1 collective-permute-done.other_ref
  1.7 0.1 shard_map.74
  1.8 4.8 %collective-permute-start.4 = (bf16[216,384]{1,0:T(8,128)(2,1)S(1)}, bf16[216,384]{1,0:T(8,128)(2,1)S(1)}, u32[]{:S(2)}, u32[]{:S(2)}) collective-permute-start(bf16[216,384]{1,0:T(8,128)(2,1)S(1)} %shard_map.74), channel_id=1, source_target_pairs={{0,13},{1,15},{2,12},{3,14},{4,9},{5,11},{6,8},{7,10},{8,5},{9,7},... | collective-permute-start | bytes 497672 | tf_op jit(solution)/shard_map/ppermute | solution.py:342
  6.6 1.6 %shard_map.75 = (f32[384]{0:T(512)S(1)}, f32[384]{0:T(512)S(1)}, f32[384]{0:T(512)S(1)}, bf16[3,864,384]{2,1,0:T(8,128)(2,1)S(1)}) custom-call(f32[384]{0:T(512)} %refs_0_.1, f32[384]{0:T(512)} %refs_1_.1, f32[384]{0:T(512)} %refs_2_.1, bf16[3,864,384]{2,1,0:T(8,128)(2,1)} %bitcast.20), custom_call_target="tpu_custom_call" | custom-call | flops 92160 | bytes 368640 | tf_op jit(solution)/shard_map/pallas_call | solution.py:27
  8.2 0.1 collective-permute-start.3
  8.4 1.3 %collective-permute-start.2 = (bf16[216,384]{1,0:T(8,128)(2,1)S(1)}, bf16[216,384]{1,0:T(8,128)(2,1)S(1)}, u32[]{:S(2)}, u32[]{:S(2)}) collective-permute-start(bf16[216,384]{1,0:T(8,128)(2,1)S(1)} %shard_map.74), channel_id=1, source_target_pairs={{0,5},{1,7},{2,4},{3,6},{4,1},{5,3},{6,0},{7,2},{8,13},{9,15},{10,... | collective-permute-start | bytes 497672 | tf_op jit(solution)/shard_map/ppermute | solution.py:342
  9.7 0.2 collective-permute-start.1
  9.9 3.0 %collective-permute-done.4.refs_3_.refs_0_ = bf16[216,384]{1,0:T(8,128)(2,1)S(1)} collective-permute-done((bf16[216,384]{1,0:T(8,128)(2,1)S(1)}, bf16[216,384]{1,0:T(8,128)(2,1)S(1)}, u32[]{:S(2)}, u32[]{:S(2)}) %collective-permute-start.4) | collective-permute-done | bytes 165920 | tf_op jit(solution)/shard_map/ppermute | solution.py:342
  12.9 9.5 %collective-permute-done.3.refs_2_.piece_ref = bf16[216,384]{1,0:T(8,128)(2,1)S(1)} collective-permute-done((bf16[216,384]{1,0:T(8,128)(2,1)S(1)}, bf16[216,384]{1,0:T(8,128)(2,1)S(1)}, u32[]{:S(2)}, u32[]{:S(2)}) %collective-permute-start.3) | collective-permute-done | bytes 165920 | tf_op jit(solution)/shard_map/ppermute | solution.py:342
  22.4 0.0 collective-permute-done.2.refs_1_
  22.4 0.0 collective-permute-done.1.refs_0_.refs_2_
  22.5 0.1 pad_maximum_fusion
  22.5 0.1 collective-permute-start.5
  22.6 1.7 %shard_map.77.near_ref = f32[6,3,48,288]{3,2,1,0:T(8,128)S(1)} custom-call(bf16[216,384]{1,0:T(8,128)(2,1)S(1)} %collective-permute-done.4.refs_3_.refs_0_, bf16[216,384]{1,0:T(8,128)(2,1)S(1)} %collective-permute-done.2.refs_1_, bf16[216,384]{1,0:T(8,128)(2,1)S(1)} %collective-permute-done.1.refs_0_.refs_2_, ...), custom_call_target="tpu_custom_call" | custom-call | flops 859963392 | bytes 921600 | tf_op jit(solution)/shard_map/pallas_call | solution.py:27
  24.3 1.3 %shard_map.78 = (bf16[128,384]{1,0:T(8,128)(2,1)S(1)}, f32[6,3,48,288]{3,2,1,0:T(8,128)S(1)}) custom-call(bf16[216,384]{1,0:T(8,128)(2,1)S(1)} %collective-permute-done.3.refs_2_.piece_ref, f32[6,3,48,288]{3,2,1,0:T(8,128)S(1)} %shard_map.77.near_ref, ...), custom_call_target="tpu_custom_call", output_to_operand_aliasing={{1}: (1, {})} | custom-call | flops 286654464 | bytes 921600 | tf_op jit(solution)/shard_map/pallas_call | solution.py:27
  25.6 0.0 copy-start
  25.6 2.5 %collective-permute-start.11 = (bf16[128,384]{1,0:T(8,128)(2,1)S(1)}, bf16[128,384]{1,0:T(8,128)(2,1)S(1)}, u32[]{:S(2)}, u32[]{:S(2)}) collective-permute-start(bf16[128,384]{1,0:T(8,128)(2,1)S(1)} %get-tuple-element.22.refs_0_), channel_id=1, source_target_pairs={{0,12},{4,8},{8,4},{12,0},{1,13},{5,9},{9,5},{13,1},{2,14},{6,10},... | collective-permute-start | bytes 294920 | tf_op jit(solution)/shard_map/ppermute | solution.py:356
  28.2 0.0 collective-permute-start.10
  28.2 1.9 %collective-permute-start.9 = (bf16[128,384]{1,0:T(8,128)(2,1)S(1)}, bf16[128,384]{1,0:T(8,128)(2,1)S(1)}, u32[]{:S(2)}, u32[]{:S(2)}) collective-permute-start(bf16[128,384]{1,0:T(8,128)(2,1)S(1)} %get-tuple-element.22.refs_0_), channel_id=1, source_target_pairs={{0,4},{4,0},{8,12},{12,8},{1,5},{5,1},{9,13},{13,9},{2,6},{6,2},{1... | collective-permute-start | bytes 294920 | tf_op jit(solution)/shard_map/ppermute | solution.py:356
  30.1 3.2 %collective-permute-done.11.refs_3_ = bf16[128,384]{1,0:T(8,128)(2,1)S(1)} collective-permute-done((bf16[128,384]{1,0:T(8,128)(2,1)S(1)}, bf16[128,384]{1,0:T(8,128)(2,1)S(1)}, u32[]{:S(2)}, u32[]{:S(2)}) %collective-permute-start.11) | collective-permute-done | bytes 98336 | tf_op jit(solution)/shard_map/ppermute | solution.py:356
  33.2 3.6 %collective-permute-done.10.refs_2_ = bf16[128,384]{1,0:T(8,128)(2,1)S(1)} collective-permute-done((bf16[128,384]{1,0:T(8,128)(2,1)S(1)}, bf16[128,384]{1,0:T(8,128)(2,1)S(1)}, u32[]{:S(2)}, u32[]{:S(2)}) %collective-permute-start.10) | collective-permute-done | bytes 98336 | tf_op jit(solution)/shard_map/ppermute | solution.py:356
  36.9 0.0 collective-permute-done.9.refs_1_
  36.9 0.7 %shard_map.79 = (bf16[4,1,48,384]{3,2,1,0:T(8,128)(2,1)S(1)}, bf16[4,2,48,384]{3,2,1,0:T(8,128)(2,1)S(1)}) custom-call(bf16[128,384]{1,0:T(8,128)(2,1)S(1)} %get-tuple-element.22.refs_0_, bf16[128,384]{1,0:T(8,128)(2,1)S(1)} %collective-permute-done.9.refs_1_, bf16[128,384]{1,0:T(8,128)(2,1)S(1)} %collective-permute-done.10.refs_2_, ...), custom_call_target="tpu_custom_call" | custom-call | flops 3686400 | bytes 1474560 | tf_op jit(solution)/shard_map/pallas_call | solution.py:27
  37.6 0.1 collective-permute-start.12
  37.7 0.0 collective-permute-done.5.refs_4_
  37.8 1.6 %shard_map.76.refs_0_ = bf16[88,384]{1,0:T(8,128)(2,1)S(1)} custom-call(bf16[216,384]{1,0:T(8,128)(2,1)S(1)} %collective-permute-done.1.refs_0_.refs_2_, bf16[216,384]{1,0:T(8,128)(2,1)S(1)} %collective-permute-done.2.refs_1_, bf16[216,384]{1,0:T(8,128)(2,1)S(1)} %collective-permute-done.3.refs_2_.piece_ref, ...), custom_call_target="tpu_custom_call" | custom-call | flops 764411904 | bytes 1843200 | tf_op jit(solution)/shard_map/pallas_call | solution.py:27
  39.4 2.5 %collective-permute-start.8 = (bf16[88,384]{1,0:T(8,128)(2,1)S(1)}, bf16[88,384]{1,0:T(8,128)(2,1)S(1)}, u32[]{:S(2)}, u32[]{:S(2)}) collective-permute-start(bf16[88,384]{1,0:T(8,128)(2,1)S(1)} %shard_map.76.refs_0_), channel_id=1, source_target_pairs={{0,12},{4,8},{8,4},{12,0},{1,13},{5,9},{9,5},{13,1},{2,14},{6,10},... | collective-permute-start | bytes 202760 | tf_op jit(solution)/shard_map/ppermute | solution.py:356
  41.9 0.0 collective-permute-start.7
  41.9 1.9 %collective-permute-start.6 = (bf16[88,384]{1,0:T(8,128)(2,1)S(1)}, bf16[88,384]{1,0:T(8,128)(2,1)S(1)}, u32[]{:S(2)}, u32[]{:S(2)}) collective-permute-start(bf16[88,384]{1,0:T(8,128)(2,1)S(1)} %shard_map.76.refs_0_), channel_id=1, source_target_pairs={{0,4},{4,0},{8,12},{12,8},{1,5},{5,1},{9,13},{13,9},{2,6},{6,2},{1... | collective-permute-start | bytes 202760 | tf_op jit(solution)/shard_map/ppermute | solution.py:356
  43.8 1.6 %shard_map.80.refs_4_ = f32[4,3,48,288]{3,2,1,0:T(8,128)S(1)} custom-call(bf16[4,1,48,384]{3,2,1,0:T(8,128)(2,1)S(1)} %get-tuple-element.24.middle_ref, bf16[4,2,48,384]{3,2,1,0:T(8,128)(2,1)S(1)} %get-tuple-element.25.last_ref, bf16[3,864,384]{2,1,0:T(8,128)(2,1)S(1)} %bitcast.14), custom_call_target="tpu_custom_call" | custom-call | flops 637009920 | bytes 921600 | tf_op jit(solution)/shard_map/pallas_call | solution.py:27
  45.5 0.0 collective-permute-done.12.past_ref
  45.5 1.0 %shard_map.81.refs_5_ = f32[4,2,48,288]{3,2,1,0:T(8,128)S(1)} custom-call(bf16[4,2,48,384]{3,2,1,0:T(8,128)(2,1)S(1)} %collective-permute-done.12.past_ref, bf16[3,864,384]{2,1,0:T(8,128)(2,1)S(1)} %bitcast.15), custom_call_target="tpu_custom_call" | custom-call | flops 382205952 | bytes 921600 | tf_op jit(solution)/shard_map/pallas_call | solution.py:27
  46.4 0.0 copy-start.1
  46.5 0.0 collective-permute-done.8.refs_3_
  46.5 2.2 %collective-permute-done.7.refs_2_ = bf16[88,384]{1,0:T(8,128)(2,1)S(1)} collective-permute-done((bf16[88,384]{1,0:T(8,128)(2,1)S(1)}, bf16[88,384]{1,0:T(8,128)(2,1)S(1)}, u32[]{:S(2)}, u32[]{:S(2)}) %collective-permute-start.7) | collective-permute-done | bytes 67616 | tf_op jit(solution)/shard_map/ppermute | solution.py:356
  48.6 0.0 collective-permute-done.6.refs_1_
  48.7 2.2 %shard_map.82 = (bf16[56,384]{1,0:T(8,128)(2,1)S(1)}, bf16[56,384]{1,0:T(8,128)(2,1)S(1)}, bf16[56,384]{1,0:T(8,128)(2,1)S(1)}, bf16[56,384]{1,0:T(8,128)(2,1)S(1)}) custom-call(bf16[88,384]{1,0:T(8,128)(2,1)S(1)} %shard_map.76.refs_0_, bf16[88,384]{1,0:T(8,128)(2,1)S(1)} %collective-permute-done.6.refs_1_, ...), custom_call_target="tpu_custom_call" | custom-call | flops 955514880 | bytes 1843200 | tf_op jit(solution)/shard_map/pallas_call | solution.py:27
  50.8 0.2 collective-permute-start.13
  51.0 0.2 collective-permute-start.14
  51.3 3.4 %collective-permute-start.15 = (bf16[56,384]{1,0:T(8,128)(2,1)S(1)}, bf16[56,384]{1,0:T(8,128)(2,1)S(1)}, u32[]{:S(2)}, u32[]{:S(2)}) collective-permute-start(bf16[56,384]{1,0:T(8,128)(2,1)S(1)} %get-tuple-element.29), channel_id=1, source_target_pairs={{0,10},{1,8},{2,11},{3,9},{4,14},{5,12},{6,15},{7,13},{8,2},{9,0},... | collective-permute-start | bytes 129032 | tf_op jit(solution)/shard_map/ppermute | solution.py:342
  54.7 1.3 %collective-permute-start.16 = (bf16[56,384]{1,0:T(8,128)(2,1)S(1)}, bf16[56,384]{1,0:T(8,128)(2,1)S(1)}, u32[]{:S(2)}, u32[]{:S(2)}) collective-permute-start(bf16[56,384]{1,0:T(8,128)(2,1)S(1)} %get-tuple-element.30), channel_id=1, source_target_pairs={{0,14},{1,12},{2,15},{3,13},{4,10},{5,8},{6,11},{7,9},{8,6},{9,4},... | collective-permute-start | bytes 129032 | tf_op jit(solution)/shard_map/ppermute | solution.py:342
  56.0 0.0 collective-permute-done.13.refs_0_
  56.0 0.0 collective-permute-done.14.refs_1_
  56.0 0.4 collective-permute-done.15.refs_2_
  56.4 3.6 %collective-permute-done.16.refs_3_ = bf16[56,384]{1,0:T(8,128)(2,1)S(1)} collective-permute-done((bf16[56,384]{1,0:T(8,128)(2,1)S(1)}, bf16[56,384]{1,0:T(8,128)(2,1)S(1)}, u32[]{:S(2)}, u32[]{:S(2)}) %collective-permute-start.16) | collective-permute-done | bytes 43040 | tf_op jit(solution)/shard_map/ppermute | solution.py:342
  60.0 1.0 %shard_map.83 = bf16[5,40,384]{2,1,0:T(8,128)(2,1)} custom-call(bf16[5,40,384]{2,1,0:T(8,128)(2,1)S(1)} %bitcast.19, bf16[56,384]{1,0:T(8,128)(2,1)S(1)} %collective-permute-done.13.refs_0_, bf16[56,384]{1,0:T(8,128)(2,1)S(1)} %collective-permute-done.14.refs_1_, bf16[56,384]{1,0:T(8,128)(2,1)S(1)} %collective-permute-done.15.refs_2_, ...), custom_call_target="tpu_custom_call" | custom-call | flops 184320 | bytes 552960 | tf_op jit(solution)/shard_map/pallas_call | solution.py:27
  (6 shorter events, 0.0 us)
Async XLA Ops:
  0.0 1.7 %collective-permute-start = (bf16[5,40,384]{2,1,0:T(8,128)(2,1)}, bf16[5,40,384]{2,1,0:T(8,128)(2,1)S(1)}, u32[]{:S(2)}, u32[]{:S(2)}) collective-permute-start(bf16[5,40,384]{2,1,0:T(8,128)(2,1)} %bitcast.17), channel_id=1, source_target_pairs={{0,1},{1,0},{2,3},{3,2},{4,5},{5,4},{6,7},{7,6},{8,9},{9,8},{10,11... | collective-permute-start | bytes 460808 | tf_op jit(solution)/shard_map/ppermute | solution.py:365
  1.8 11.0 %collective-permute-start.4 = (bf16[216,384]{1,0:T(8,128)(2,1)S(1)}, bf16[216,384]{1,0:T(8,128)(2,1)S(1)}, u32[]{:S(2)}, u32[]{:S(2)}) collective-permute-start(bf16[216,384]{1,0:T(8,128)(2,1)S(1)} %shard_map.74), channel_id=1, source_target_pairs={{0,13},{1,15},{2,12},{3,14},{4,9},{5,11},{6,8},{7,10},{8,5},{9,7},... | collective-permute-start | bytes 497672 | tf_op jit(solution)/shard_map/ppermute | solution.py:342
  8.2 14.2 %collective-permute-start.3 = (bf16[216,384]{1,0:T(8,128)(2,1)S(1)}, bf16[216,384]{1,0:T(8,128)(2,1)S(1)}, u32[]{:S(2)}, u32[]{:S(2)}) collective-permute-start(bf16[216,384]{1,0:T(8,128)(2,1)S(1)} %shard_map.74), channel_id=1, source_target_pairs={{0,9},{1,11},{2,8},{3,10},{4,13},{5,15},{6,12},{7,14},{8,1},{9,3},... | collective-permute-start | bytes 497672 | tf_op jit(solution)/shard_map/ppermute | solution.py:342
  8.4 14.0 %collective-permute-start.2 = (bf16[216,384]{1,0:T(8,128)(2,1)S(1)}, bf16[216,384]{1,0:T(8,128)(2,1)S(1)}, u32[]{:S(2)}, u32[]{:S(2)}) collective-permute-start(bf16[216,384]{1,0:T(8,128)(2,1)S(1)} %shard_map.74), channel_id=1, source_target_pairs={{0,5},{1,7},{2,4},{3,6},{4,1},{5,3},{6,0},{7,2},{8,13},{9,15},{10,... | collective-permute-start | bytes 497672 | tf_op jit(solution)/shard_map/ppermute | solution.py:342
  9.7 12.7 %collective-permute-start.1 = (bf16[216,384]{1,0:T(8,128)(2,1)S(1)}, bf16[216,384]{1,0:T(8,128)(2,1)S(1)}, u32[]{:S(2)}, u32[]{:S(2)}) collective-permute-start(bf16[216,384]{1,0:T(8,128)(2,1)S(1)} %shard_map.74), channel_id=1, source_target_pairs={{0,1},{1,3},{2,0},{3,2},{4,5},{5,7},{6,4},{7,6},{8,9},{9,11},{10,8... | collective-permute-start | bytes 497672 | tf_op jit(solution)/shard_map/ppermute | solution.py:342
  22.5 15.2 %collective-permute-start.5 = (bf16[4,96,384]{2,1,0:T(8,128)(2,1)S(1)}, bf16[4,96,384]{2,1,0:T(8,128)(2,1)S(1)}, u32[]{:S(2)}, u32[]{:S(2)}) collective-permute-start(bf16[4,96,384]{2,1,0:T(8,128)(2,1)S(1)} %pad_maximum_fusion), channel_id=1, source_target_pairs={{0,1},{1,0},{2,3},{3,2},{4,5},{5,4},{6,7},{7,6},{8,9},{9,8},{10,11... | collective-permute-start | bytes 884744 | tf_op jit(solution)/shard_map/ppermute | solution.py:342
  25.6 18.2 %copy-start = (bf16[27,96,384]{2,1,0:T(8,128)(2,1)S(1)}, bf16[27,96,384]{2,1,0:T(8,128)(2,1)}, u32[]{:S(2)}) copy-start(bf16[27,96,384]{2,1,0:T(8,128)(2,1)} %param.12) | copy-start | bytes 5971972
  25.6 7.6 %collective-permute-start.11 = (bf16[128,384]{1,0:T(8,128)(2,1)S(1)}, bf16[128,384]{1,0:T(8,128)(2,1)S(1)}, u32[]{:S(2)}, u32[]{:S(2)}) collective-permute-start(bf16[128,384]{1,0:T(8,128)(2,1)S(1)} %get-tuple-element.22.refs_0_), channel_id=1, source_target_pairs={{0,12},{4,8},{8,4},{12,0},{1,13},{5,9},{9,5},{13,1},{2,14},{6,10},... | collective-permute-start | bytes 294920 | tf_op jit(solution)/shard_map/ppermute | solution.py:356
  28.2 8.7 %collective-permute-start.10 = (bf16[128,384]{1,0:T(8,128)(2,1)S(1)}, bf16[128,384]{1,0:T(8,128)(2,1)S(1)}, u32[]{:S(2)}, u32[]{:S(2)}) collective-permute-start(bf16[128,384]{1,0:T(8,128)(2,1)S(1)} %get-tuple-element.22.refs_0_), channel_id=1, source_target_pairs={{0,8},{4,12},{8,0},{12,4},{1,9},{5,13},{9,1},{13,5},{2,10},{6,14},... | collective-permute-start | bytes 294920 | tf_op jit(solution)/shard_map/ppermute | solution.py:356
  28.2 8.7 %collective-permute-start.9 = (bf16[128,384]{1,0:T(8,128)(2,1)S(1)}, bf16[128,384]{1,0:T(8,128)(2,1)S(1)}, u32[]{:S(2)}, u32[]{:S(2)}) collective-permute-start(bf16[128,384]{1,0:T(8,128)(2,1)S(1)} %get-tuple-element.22.refs_0_), channel_id=1, source_target_pairs={{0,4},{4,0},{8,12},{12,8},{1,5},{5,1},{9,13},{13,9},{2,6},{6,2},{1... | collective-permute-start | bytes 294920 | tf_op jit(solution)/shard_map/ppermute | solution.py:356
  37.6 7.8 %collective-permute-start.12 = (bf16[4,2,48,384]{3,2,1,0:T(8,128)(2,1)S(1)}, bf16[4,2,48,384]{3,2,1,0:T(8,128)(2,1)S(1)}, u32[]{:S(2)}, u32[]{:S(2)}) collective-permute-start(bf16[4,2,48,384]{3,2,1,0:T(8,128)(2,1)S(1)} %get-tuple-element.25.last_ref), channel_id=1, source_target_pairs={{0,1},{1,0},{2,3},{3,2},{4,5},{5,4},{6,7},{7,6},{8,9},{9,8},{10,11... | collective-permute-start | bytes 884744 | tf_op jit(solution)/shard_map/ppermute | solution.py:342
  39.4 7.1 %collective-permute-start.8 = (bf16[88,384]{1,0:T(8,128)(2,1)S(1)}, bf16[88,384]{1,0:T(8,128)(2,1)S(1)}, u32[]{:S(2)}, u32[]{:S(2)}) collective-permute-start(bf16[88,384]{1,0:T(8,128)(2,1)S(1)} %shard_map.76.refs_0_), channel_id=1, source_target_pairs={{0,12},{4,8},{8,4},{12,0},{1,13},{5,9},{9,5},{13,1},{2,14},{6,10},... | collective-permute-start | bytes 202760 | tf_op jit(solution)/shard_map/ppermute | solution.py:356
  41.9 6.7 %collective-permute-start.7 = (bf16[88,384]{1,0:T(8,128)(2,1)S(1)}, bf16[88,384]{1,0:T(8,128)(2,1)S(1)}, u32[]{:S(2)}, u32[]{:S(2)}) collective-permute-start(bf16[88,384]{1,0:T(8,128)(2,1)S(1)} %shard_map.76.refs_0_), channel_id=1, source_target_pairs={{0,8},{4,12},{8,0},{12,4},{1,9},{5,13},{9,1},{13,5},{2,10},{6,14},... | collective-permute-start | bytes 202760 | tf_op jit(solution)/shard_map/ppermute | solution.py:356
  41.9 6.7 %collective-permute-start.6 = (bf16[88,384]{1,0:T(8,128)(2,1)S(1)}, bf16[88,384]{1,0:T(8,128)(2,1)S(1)}, u32[]{:S(2)}, u32[]{:S(2)}) collective-permute-start(bf16[88,384]{1,0:T(8,128)(2,1)S(1)} %shard_map.76.refs_0_), channel_id=1, source_target_pairs={{0,4},{4,0},{8,12},{12,8},{1,5},{5,1},{9,13},{13,9},{2,6},{6,2},{1... | collective-permute-start | bytes 202760 | tf_op jit(solution)/shard_map/ppermute | solution.py:356
  46.4 13.5 %copy-start.1 = (bf16[5,1,40,384]{3,2,1,0:T(8,128)(2,1)S(1)}, bf16[5,1,40,384]{3,2,1,0:T(8,128)(2,1)}, u32[]{:S(2)}) copy-start(bf16[5,1,40,384]{3,2,1,0:T(8,128)(2,1)} %param.7) | copy-start | bytes 460804
  50.8 5.1 %collective-permute-start.13 = (bf16[56,384]{1,0:T(8,128)(2,1)S(1)}, bf16[56,384]{1,0:T(8,128)(2,1)S(1)}, u32[]{:S(2)}, u32[]{:S(2)}) collective-permute-start(bf16[56,384]{1,0:T(8,128)(2,1)S(1)} %get-tuple-element.27), channel_id=1, source_target_pairs={{0,2},{1,0},{2,3},{3,1},{4,6},{5,4},{6,7},{7,5},{8,10},{9,8},{10,1... | collective-permute-start | bytes 129032 | tf_op jit(solution)/shard_map/ppermute | solution.py:342
  51.0 4.9 %collective-permute-start.14 = (bf16[56,384]{1,0:T(8,128)(2,1)S(1)}, bf16[56,384]{1,0:T(8,128)(2,1)S(1)}, u32[]{:S(2)}, u32[]{:S(2)}) collective-permute-start(bf16[56,384]{1,0:T(8,128)(2,1)S(1)} %get-tuple-element.28), channel_id=1, source_target_pairs={{0,6},{1,4},{2,7},{3,5},{4,2},{5,0},{6,3},{7,1},{8,14},{9,12},{10,... | collective-permute-start | bytes 129032 | tf_op jit(solution)/shard_map/ppermute | solution.py:342
  51.3 5.1 %collective-permute-start.15 = (bf16[56,384]{1,0:T(8,128)(2,1)S(1)}, bf16[56,384]{1,0:T(8,128)(2,1)S(1)}, u32[]{:S(2)}, u32[]{:S(2)}) collective-permute-start(bf16[56,384]{1,0:T(8,128)(2,1)S(1)} %get-tuple-element.29), channel_id=1, source_target_pairs={{0,10},{1,8},{2,11},{3,9},{4,14},{5,12},{6,15},{7,13},{8,2},{9,0},... | collective-permute-start | bytes 129032 | tf_op jit(solution)/shard_map/ppermute | solution.py:342
  54.7 5.2 %collective-permute-start.16 = (bf16[56,384]{1,0:T(8,128)(2,1)S(1)}, bf16[56,384]{1,0:T(8,128)(2,1)S(1)}, u32[]{:S(2)}, u32[]{:S(2)}) collective-permute-start(bf16[56,384]{1,0:T(8,128)(2,1)S(1)} %get-tuple-element.30), channel_id=1, source_target_pairs={{0,14},{1,12},{2,15},{3,13},{4,10},{5,8},{6,11},{7,9},{8,6},{9,4},... | collective-permute-start | bytes 129032 | tf_op jit(solution)/shard_map/ppermute | solution.py:342

commit v6 on v5

--- a/solution.py
+++ b/solution.py
@@ -10,6 +10,7 @@
 
 AXES = ("rows", "tm", "cols")
 EDGE = 2
+LANES = 128
 PAST = 2
 TAPS = 3
 VMEM = pltpu.VMEM
@@ -47,6 +48,30 @@
     return -(-count // 8) * 8
 
 
+def packed_rows(count, ends, channels):
+    blocks = channels // LANES
+    return count * blocks + padded_rows(ends * blocks)
+
+
+def lane_blocks(values):
+    return [values[:, i : i + LANES] for i in range(0, values.shape[1], LANES)]
+
+
+def pack(center, ends, out_ref):
+    parts = lane_blocks(center) + lane_blocks(ends)
+    rest = out_ref.shape[0] - sum(part.shape[0] for part in parts)
+    if rest:
+        parts.append(jnp.zeros((rest, LANES), jnp.float32))
+    out_ref[...] = jnp.concatenate(parts, axis=0).astype(jnp.bfloat16)
+
+
+def unpack(values, count, ends, channels):
+    blocks = channels // LANES
+    center = jnp.concatenate([values[i * count : (i + 1) * count] for i in range(blocks)], axis=1)
+    start = blocks * count
+    return center, jnp.concatenate([values[start + i * ends : start + (i + 1) * ends] for i in range(blocks)], axis=1)
+
+
 def own_part(vector, row, width):
     parts = vector.shape[1] // width
     return sum(jnp.where(row == s, vector[:, s * width : (s + 1) * width], 0.0) for s in range(parts))
@@ -63,7 +88,8 @@
         copy.wait()
     frames, breadth, channels = held.shape
     values = activate(held[...], gain_ref[...].reshape(1, channels))
-    out_ref[...] = values.reshape(frames * breadth, channels).astype(jnp.bfloat16)
+    blocks = lane_blocks(values.reshape(frames * breadth, channels))
+    out_ref[...] = jnp.concatenate(blocks, axis=0).astype(jnp.bfloat16)
 
 
 def ends_body(center_ref, other_ref, gain_ref, out_ref):
@@ -72,12 +98,13 @@
     chosen = jnp.where(half == 0, other_ref[:, 0:8].astype(jnp.float32), other_ref[:, breadth - 8 :].astype(jnp.float32))
     values = activate(chosen, gain_ref[...].reshape(1, channels))
     ends = [jnp.where(half == 0, values[f, 0:EDGE], values[f, 8 - EDGE : 8]) for f in range(frames)]
-    count = frames * breadth
-    rest = out_ref.shape[0] - count - EDGE * frames
+    blocks = lane_blocks(jnp.concatenate(ends, axis=0))
+    count = center_ref.shape[0]
+    rest = out_ref.shape[0] - count - len(blocks) * EDGE * frames
     if rest:
-        ends.append(jnp.zeros((rest, channels), jnp.float32))
+        blocks.append(jnp.zeros((rest, LANES), jnp.float32))
     out_ref[0:count] = center_ref[...]
-    out_ref[count:] = jnp.concatenate(ends, axis=0).astype(jnp.bfloat16)
+    out_ref[count:] = jnp.concatenate(blocks, axis=0).astype(jnp.bfloat16)
 
 
 def stage_body(*refs):
@@ -115,18 +142,18 @@
     return rows
 
 
-def column_sum(row, bias_row):
+def column_sum(row):
     ring, width = row.shape[1], row.shape[2] // TAPS
     before = pltpu.roll(row[:, :, 0:width], 1, 1)
     after = pltpu.roll(row[:, :, 2 * width : 3 * width], ring - 1, 1)
-    return before + row[:, :, width : 2 * width] + after + bias_row
+    return before + row[:, :, width : 2 * width] + after
 
 
 def conv_sum(padded, weight_ref, bias_row):
     frames, height, ring, channels = padded.shape[0] - PAST, padded.shape[1], padded.shape[2], padded.shape[3]
     windows = [padded[t : t + frames].reshape(frames * height * ring, channels) for t in range(TAPS)]
     product = multiply(windows, weight_ref, range(TAPS)).reshape(frames, height, ring, -1)
-    return [column_sum(row, bias_row) for row in row_sums(product)]
+    return [column_sum(row) + bias_row for row in row_sums(product)]
 
 
 def add_rows(padded, rows, weight_ref, total):
@@ -136,7 +163,7 @@
     wide = product.shape[3] // TAPS
     for i, row in enumerate(rows):
         for r in range(TAPS):
-            total[row + 2 - r] += product[:, i, :, r * wide : (r + 1) * wide]
+            total[row + 2 - r] += column_sum(product[:, i, :, r * wide : (r + 1) * wide])
 
 
 def frame_terms(frames, wanted):
@@ -152,8 +179,9 @@
         windows = [jnp.concatenate([frame_of(f + t) for f in outs], axis=0) for t in taps]
         product = multiply(windows, weight_ref, taps).reshape(len(outs), height, ring, -1)
         for h, row in enumerate(row_sums(product)):
+            shifted = column_sum(row)
             for i, f in enumerate(outs):
-                add(f, h, row[i])
+                add(f, h, shifted[i])
 
 
 def block_number():
@@ -163,15 +191,14 @@
 def pack_first(rows, out_ref, breadth):
     half = lax.axis_index("tm") % 2
     frames, ring, width = rows[0].shape
-    rest = out_ref.shape[0] - frames * (breadth + 1)
-    packed = []
-    for row in rows:
-        centers = [row[f, 0:breadth] for f in range(frames)]
-        ends = [jnp.where(half == 0, row[f, breadth : breadth + 1], row[f, ring - 1 : ring]) for f in range(frames)]
-        if rest:
-            ends.append(jnp.zeros((rest, width), jnp.float32))
-        packed.append(jnp.concatenate(centers + ends, axis=0))
-    out_ref[...] = jnp.concatenate(packed, axis=1).astype(jnp.bfloat16)
+    centers = [row[:, 0:breadth].reshape(frames * breadth, width) for row in rows]
+    ends = [
+        jnp.concatenate(
+            [jnp.where(half == 0, row[f, breadth : breadth + 1], row[f, ring - 1 : ring]) for f in range(frames)], axis=0
+        )
+        for row in rows
+    ]
+    pack(jnp.concatenate(centers, axis=1), jnp.concatenate(ends, axis=1), out_ref)
 
 
 def bias_part(bias_ref, row, weight_ref):
@@ -183,7 +210,8 @@
     picks = [(f, f) for f in range(frames)]
     for i, piece in enumerate(pieces):
         values = piece[...].astype(jnp.float32)
-        fill_first(padded, (0, i), values, values[frames * breadth :], picks, breadth)
+        center, ends = unpack(values, frames * breadth, frames * EDGE, padded.shape[3])
+        fill_first(padded, (0, i), center, ends, picks, breadth)
 
 
 def first_near_body(breadth, ks, *refs):
@@ -199,7 +227,16 @@
     fill_slots(padded, [piece_ref], breadth)
     add_rows(padded, [row ^ k], weight_ref, total)
     bias_row = bias_part(bias_ref, row, weight_ref)
-    pack_first([column_sum(total[h + 1], bias_row) for h in range(total.shape[0] - 2)], out_ref, breadth)
+    pack_first([total[h + 1] + bias_row for h in range(total.shape[0] - 2)], out_ref, breadth)
+
+
+def cut_body(count, kept, *refs):
+    *pieces, out_ref = refs
+    for k, piece in enumerate(pieces):
+        blocks = piece.shape[0] // count
+        for i in range(blocks):
+            out_ref[k, i * kept : (i + 1) * kept] = piece[(i + 1) * count - kept : (i + 1) * count]
+        out_ref[k, blocks * kept :] = piece[blocks * count :]
 
 
 def first_early_body(breadth, height, frames, *refs):
@@ -209,20 +246,23 @@
         past = past_ref[k].astype(jnp.float32)
         past = jnp.where(block_number() > 0, past, jnp.zeros_like(past))
         picks = [(j, frames - PAST + j) for j in range(PAST)]
-        fill_first(padded, (0, row ^ k), past[0 : PAST * breadth], past[PAST * breadth :], picks, breadth)
-        center = pieces[k][0 : PAST * breadth].astype(jnp.float32)
-        end = pieces[k][frames * breadth :].astype(jnp.float32)
-        fill_first(padded, (PAST, row ^ k), center, end, [(j, j) for j in range(PAST)], breadth)
+        center, ends = unpack(past, PAST * breadth, frames * EDGE, padded.shape[3])
+        fill_first(padded, (0, row ^ k), center, ends, picks, breadth)
+        center, ends = unpack(pieces[k][...].astype(jnp.float32), frames * breadth, frames * EDGE, padded.shape[3])
+        fill_first(padded, (PAST, row ^ k), center, ends, [(j, j) for j in range(PAST)], breadth)
     pack_first(conv_sum(padded, weight_ref, bias_part(bias_ref, row, weight_ref)), out_ref, breadth)
 
 
 def regroup(pieces, gain_ref, held, breadth, frames, store):
     row = lax.axis_index("rows")
     half = lax.axis_index("tm") % 2
-    height, channels = len(pieces), pieces[0].shape[1]
+    height, channels = len(pieces), held.shape[2]
     width = channels // height
+    count = frames * breadth
     for k, piece in enumerate(pieces):
-        held[row ^ k] = piece[...].astype(jnp.float32)
+        center, ends = unpack(piece[...].astype(jnp.float32), count, frames, channels)
+        held[row ^ k, 0:count] = center
+        held[row ^ k, count : count + frames] = ends
     gain_values = gain_ref[...].reshape(1, channels)
     for h in range(height):
         joined = [held[s, :, h * width : (h + 1) * width] for s in range(height)]
@@ -303,8 +343,7 @@
     for h in range(height):
         for f in range(frames):
             values = sums[f, h] if (f, h) in sums else held_sum(f, h)
-            values = column_sum(values[None], bias_row)[0]
-            branch[h, f * breadth : (f + 1) * breadth] = values[0:breadth]
+            branch[h, f * breadth : (f + 1) * breadth] = values[0:breadth] + bias_row
     for k, out_ref in enumerate(outs):
         chosen = branch[row ^ k]
         rows = out_ref.shape[0]
@@ -372,35 +411,41 @@
         return VMEM((count, rows, ring, channels), bf16)
 
     center, gain_one = call(
-        own_body, [sds((frames * breadth, channels), bf16), sds(gain_one.shape, f32)],
+        own_body, [sds((frames * breadth * channels // LANES, LANES), bf16), sds(gain_one.shape, f32)],
         [VMEM((frames, breadth, channels), bf16), pltpu.SemaphoreType.DMA((2,))],
         10 * size, 6 * size, own, gain_one, far=(0, 1),
     )
-    total = frames * breadth + padded_rows(EDGE * frames)
-    band = call(ends_body, sds((total, channels), bf16), [], size, 4 * size, center, other, gain_one)
+    total = packed_rows(frames * breadth, EDGE * frames, channels)
+    band = call(ends_body, sds((total, LANES), bf16), [], size, 4 * size, center, other, gain_one)
     pieces = turn([band] * rows, turned)
     small = (bias_one, gain_two, bias_two, weights[0])
     bias_one, gain_two, bias_two, near = call(
         stage_body, [sds(v.shape, v.dtype) for v in small], [pltpu.SemaphoreType.DMA((len(small),))],
         size, 4 * size, *small, far=range(len(small)),
     )
-    past = following(jnp.stack([piece[late * breadth :] for piece in pieces]))
-    late_rows, early_rows = padded_rows(late * (breadth + 1)), padded_rows(PAST * (breadth + 1))
+    past_rows = packed_rows(PAST * breadth, EDGE * frames, channels)
+    past = call(
+        functools.partial(cut_body, frames * breadth, PAST * breadth), sds((rows, past_rows, LANES), bf16), [],
+        size, 4 * size, *pieces,
+    )
+    past = following(past)
+    late_sent, early_sent = (packed_rows(count * breadth, count, channels) for count in (late, PAST))
+    late_rows, early_rows = (padded_rows(count * (breadth + 1)) for count in (late, PAST))
     *ks, last_k = band_order(rows)
-    sums = sds((rows + 2, late, ring, TAPS * width), f32)
+    sums = sds((rows + 2, late, ring, width), f32)
     near_sums = call(
         functools.partial(first_near_body, breadth, ks), sums,
         [VMEM((frames, rows - 1, ring, channels), bf16)], late * work * (rows - 1) // rows, 10 * size,
         *[pieces[k] for k in ks], near,
     )
     part, _ = call(
-        functools.partial(first_late_body, breadth, last_k), [sds((late_rows, channels), bf16), sums],
+        functools.partial(first_late_body, breadth, last_k), [sds((late_sent, LANES), bf16), sums],
         [VMEM((frames, 1, ring, channels), bf16)], late * work // rows, 10 * size,
         pieces[last_k], near_sums, near, bias_one, aliases={1: 1},
     )
     late_parts = spread(part)
     part = call(
-        functools.partial(first_early_body, breadth, rows, frames), sds((early_rows, channels), bf16),
+        functools.partial(first_early_body, breadth, rows, frames), sds((early_sent, LANES), bf16),
         [padded(2 * PAST)], PAST * work, 20 * size, *pieces, past, near, bias_one,
     )
     early_parts = spread(part)
@@ -412,11 +457,11 @@
     past = following(last)
     back_rows = padded_rows(-(-frames * breadth // rows))
     late_sums = call(
-        functools.partial(second_late_body, frames), sds((rows, late, ring, TAPS * width), f32), [],
+        functools.partial(second_late_body, frames), sds((rows, late, ring, width), f32), [],
         frames * work // 3, 10 * size, second, last, weights[1],
     )
     past_sums = call(
-        second_past_body, sds((rows, PAST, ring, TAPS * width), f32), [],
+        second_past_body, sds((rows, PAST, ring, width), f32), [],
         frames * work // 5, 10 * size, past, weights[1],
     )
     branch = call(

time: 61.1 us -> 59.9 us (0.980)
  waiting for transfers between devices: 25.6 us -> 24.7 us
    pallas_call x11 -> x12, Pallas kernels: 13.9 us -> 13.8 us  [call(): pl.pallas_call(body, out_shape=out_shape, in_specs=[pl.BlockSpec(memory_s...]
where the time goes in v6:
time: 59.9 us; the launch traced here: 59.8 us
  waiting for transfers between devices  24.7 us (41%)
  starting transfers between devices  21.1 us (35%)
  Pallas kernels  13.8 us (23%)
    ppermute x10, waiting for transfers between devices, moved(): lax.ppermute(values, AXES, [(place[device], place[target(*device)]) for d...  16.1 us
    pallas_call x12, Pallas kernels, call(): pl.pallas_call(body, out_shape=out_shape, in_specs=[pl.BlockSpec(memory_s...  13.8 us
    ppermute x10, starting transfers between devices, moved(): lax.ppermute(values, AXES, [(place[device], place[target(*device)]) for d...  11.7 us
    ppermute x6, starting transfers between devices, spread(): lax.ppermute(values, 'rows', [(z, z ^ k) for z in range(rows)])  8.91 us
    ppermute x6, waiting for transfers between devices, spread(): lax.ppermute(values, 'rows', [(z, z ^ k) for z in range(rows)])  8.45 us
  transfers between devices with their start and end apart: 17, of which 8 were waited for; matrix products, arithmetic and copies ran while one was open for 0% of the time, Pallas kernels for 18%

profile of v6, /device:TPU:0, one launch (start us, length us, event | category | flops | bytes accessed | tf_op | source)
XLA Modules:
  0.0 59.8 jit_solution(16771362064547610953)
XLA Ops:
  0.0 0.5 collective-permute-start
  0.5 1.1 %shard_map.73 = (bf16[600,128]{1,0:T(8,128)(2,1)S(1)}, f32[384]{0:T(512)S(1)}) custom-call(bf16[5,40,384]{2,1,0:T(8,128)(2,1)} %bitcast.10, f32[384]{0:T(512)} %far_gain_ref.1), custom_call_target="tpu_custom_call" | custom-call | flops 921600 | bytes 552960 | tf_op jit(solution)/shard_map/pallas_call | solution.py:28
  1.6 0.1 collective-permute-done.other_ref
  1.7 0.1 shard_map.74
  1.8 4.8 %collective-permute-start.4 = (bf16[632,128]{1,0:T(8,128)(2,1)S(1)}, bf16[632,128]{1,0:T(8,128)(2,1)S(1)}, u32[]{:S(2)}, u32[]{:S(2)}) collective-permute-start(bf16[632,128]{1,0:T(8,128)(2,1)S(1)} %shard_map.74), channel_id=1, source_target_pairs={{0,13},{1,15},{2,12},{3,14},{4,9},{5,11},{6,8},{7,10},{8,5},{9,7},... | collective-permute-start | bytes 485384 | tf_op jit(solution)/shard_map/ppermute | solution.py:381
  6.6 0.1 collective-permute-start.3
  6.7 1.3 %collective-permute-start.2 = (bf16[632,128]{1,0:T(8,128)(2,1)S(1)}, bf16[632,128]{1,0:T(8,128)(2,1)S(1)}, u32[]{:S(2)}, u32[]{:S(2)}) collective-permute-start(bf16[632,128]{1,0:T(8,128)(2,1)S(1)} %shard_map.74), channel_id=1, source_target_pairs={{0,5},{1,7},{2,4},{3,6},{4,1},{5,3},{6,0},{7,2},{8,13},{9,15},{10,... | collective-permute-start | bytes 485384 | tf_op jit(solution)/shard_map/ppermute | solution.py:381
  8.0 0.2 collective-permute-start.1
  8.3 1.6 %shard_map.76 = (f32[384]{0:T(512)S(1)}, f32[384]{0:T(512)S(1)}, f32[384]{0:T(512)S(1)}, bf16[3,864,384]{2,1,0:T(8,128)(2,1)S(1)}) custom-call(f32[384]{0:T(512)} %refs_0_.1, f32[384]{0:T(512)} %refs_1_.1, f32[384]{0:T(512)} %refs_2_.1, bf16[3,864,384]{2,1,0:T(8,128)(2,1)} %bitcast.12), custom_call_target="tpu_custom_call" | custom-call | flops 92160 | bytes 368640 | tf_op jit(solution)/shard_map/pallas_call | solution.py:28
  9.9 3.0 %collective-permute-done.4.refs_3_.refs_0_ = bf16[632,128]{1,0:T(8,128)(2,1)S(1)} collective-permute-done((bf16[632,128]{1,0:T(8,128)(2,1)S(1)}, bf16[632,128]{1,0:T(8,128)(2,1)S(1)}, u32[]{:S(2)}, u32[]{:S(2)}) %collective-permute-start.4) | collective-permute-done | bytes 161824 | tf_op jit(solution)/shard_map/ppermute | solution.py:381
  12.9 9.2 %collective-permute-done.3.refs_2_.piece_ref = bf16[632,128]{1,0:T(8,128)(2,1)S(1)} collective-permute-done((bf16[632,128]{1,0:T(8,128)(2,1)S(1)}, bf16[632,128]{1,0:T(8,128)(2,1)S(1)}, u32[]{:S(2)}, u32[]{:S(2)}) %collective-permute-start.3) | collective-permute-done | bytes 161824 | tf_op jit(solution)/shard_map/ppermute | solution.py:381
  22.1 0.0 collective-permute-done.2.refs_1_
  22.1 0.0 collective-permute-done.1.refs_0_.refs_2_
  22.1 0.1 collective-permute-start.5
  22.2 1.7 %shard_map.78.near_ref = f32[6,3,48,96]{3,2,1,0:T(8,128)S(1)} custom-call(bf16[632,128]{1,0:T(8,128)(2,1)S(1)} %collective-permute-done.4.refs_3_.refs_0_, bf16[632,128]{1,0:T(8,128)(2,1)S(1)} %collective-permute-done.2.refs_1_, bf16[632,128]{1,0:T(8,128)(2,1)S(1)} %collective-permute-done.1.refs_0_.refs_2_, ...), custom_call_target="tpu_custom_call" | custom-call | flops 859963392 | bytes 921600 | tf_op jit(solution)/shard_map/pallas_call | solution.py:28
  23.8 1.0 %shard_map.79 = (bf16[376,128]{1,0:T(8,128)(2,1)S(1)}, f32[6,3,48,96]{3,2,1,0:T(8,128)S(1)}) custom-call(bf16[632,128]{1,0:T(8,128)(2,1)S(1)} %collective-permute-done.3.refs_2_.piece_ref, f32[6,3,48,96]{3,2,1,0:T(8,128)S(1)} %shard_map.78.near_ref, ...), custom_call_target="tpu_custom_call", output_to_operand_aliasing={{1}: (1, {})} | custom-call | flops 286654464 | bytes 921600 | tf_op jit(solution)/shard_map/pallas_call | solution.py:28
  24.8 0.0 copy-start
  24.8 2.5 %collective-permute-start.11 = (bf16[376,128]{1,0:T(8,128)(2,1)S(1)}, bf16[376,128]{1,0:T(8,128)(2,1)S(1)}, u32[]{:S(2)}, u32[]{:S(2)}) collective-permute-start(bf16[376,128]{1,0:T(8,128)(2,1)S(1)} %get-tuple-element.22.refs_0_), channel_id=1, source_target_pairs={{0,12},{4,8},{8,4},{12,0},{1,13},{5,9},{9,5},{13,1},{2,14},{6,10},... | collective-permute-start | bytes 288776 | tf_op jit(solution)/shard_map/ppermute | solution.py:395
  27.4 0.0 collective-permute-start.10
  27.4 1.9 %collective-permute-start.9 = (bf16[376,128]{1,0:T(8,128)(2,1)S(1)}, bf16[376,128]{1,0:T(8,128)(2,1)S(1)}, u32[]{:S(2)}, u32[]{:S(2)}) collective-permute-start(bf16[376,128]{1,0:T(8,128)(2,1)S(1)} %get-tuple-element.22.refs_0_), channel_id=1, source_target_pairs={{0,4},{4,0},{8,12},{12,8},{1,5},{5,1},{9,13},{13,9},{2,6},{6,2},{1... | collective-permute-start | bytes 288776 | tf_op jit(solution)/shard_map/ppermute | solution.py:395
  29.3 3.1 %collective-permute-done.11.refs_3_ = bf16[376,128]{1,0:T(8,128)(2,1)S(1)} collective-permute-done((bf16[376,128]{1,0:T(8,128)(2,1)S(1)}, bf16[376,128]{1,0:T(8,128)(2,1)S(1)}, u32[]{:S(2)}, u32[]{:S(2)}) %collective-permute-start.11) | collective-permute-done | bytes 96288 | tf_op jit(solution)/shard_map/ppermute | solution.py:395
  32.4 3.6 %collective-permute-done.10.refs_2_ = bf16[376,128]{1,0:T(8,128)(2,1)S(1)} collective-permute-done((bf16[376,128]{1,0:T(8,128)(2,1)S(1)}, bf16[376,128]{1,0:T(8,128)(2,1)S(1)}, u32[]{:S(2)}, u32[]{:S(2)}) %collective-permute-start.10) | collective-permute-done | bytes 96288 | tf_op jit(solution)/shard_map/ppermute | solution.py:395
  36.0 0.0 collective-permute-done.9.refs_1_
  36.0 0.7 %shard_map.80 = (bf16[4,1,48,384]{3,2,1,0:T(8,128)(2,1)S(1)}, bf16[4,2,48,384]{3,2,1,0:T(8,128)(2,1)S(1)}) custom-call(bf16[376,128]{1,0:T(8,128)(2,1)S(1)} %get-tuple-element.22.refs_0_, bf16[376,128]{1,0:T(8,128)(2,1)S(1)} %collective-permute-done.9.refs_1_, bf16[376,128]{1,0:T(8,128)(2,1)S(1)} %collective-permute-done.10.refs_2_, ...), custom_call_target="tpu_custom_call" | custom-call | flops 3686400 | bytes 1474560 | tf_op jit(solution)/shard_map/pallas_call | solution.py:28
  36.7 0.1 collective-permute-start.12
  36.8 0.0 collective-permute-done.5.refs_4_
  36.8 1.6 %shard_map.77.refs_0_ = bf16[248,128]{1,0:T(8,128)(2,1)S(1)} custom-call(bf16[632,128]{1,0:T(8,128)(2,1)S(1)} %collective-permute-done.1.refs_0_.refs_2_, bf16[632,128]{1,0:T(8,128)(2,1)S(1)} %collective-permute-done.2.refs_1_, bf16[632,128]{1,0:T(8,128)(2,1)S(1)} %collective-permute-done.3.refs_2_.piece_ref, ...), custom_call_target="tpu_custom_call" | custom-call | flops 764411904 | bytes 1843200 | tf_op jit(solution)/shard_map/pallas_call | solution.py:28
  38.5 2.5 %collective-permute-start.8 = (bf16[248,128]{1,0:T(8,128)(2,1)S(1)}, bf16[248,128]{1,0:T(8,128)(2,1)S(1)}, u32[]{:S(2)}, u32[]{:S(2)}) collective-permute-start(bf16[248,128]{1,0:T(8,128)(2,1)S(1)} %shard_map.77.refs_0_), channel_id=1, source_target_pairs={{0,12},{4,8},{8,4},{12,0},{1,13},{5,9},{9,5},{13,1},{2,14},{6,10},... | collective-permute-start | bytes 190472 | tf_op jit(solution)/shard_map/ppermute | solution.py:395
  41.0 0.0 collective-permute-start.7
  41.0 1.9 %collective-permute-start.6 = (bf16[248,128]{1,0:T(8,128)(2,1)S(1)}, bf16[248,128]{1,0:T(8,128)(2,1)S(1)}, u32[]{:S(2)}, u32[]{:S(2)}) collective-permute-start(bf16[248,128]{1,0:T(8,128)(2,1)S(1)} %shard_map.77.refs_0_), channel_id=1, source_target_pairs={{0,4},{4,0},{8,12},{12,8},{1,5},{5,1},{9,13},{13,9},{2,6},{6,2},{1... | collective-permute-start | bytes 190472 | tf_op jit(solution)/shard_map/ppermute | solution.py:395
  42.9 0.0 copy-done
  42.9 1.7 %shard_map.81.refs_4_ = f32[4,3,48,96]{3,2,1,0:T(8,128)S(1)} custom-call(bf16[4,1,48,384]{3,2,1,0:T(8,128)(2,1)S(1)} %get-tuple-element.24.middle_ref, bf16[4,2,48,384]{3,2,1,0:T(8,128)(2,1)S(1)} %get-tuple-element.25.last_ref, bf16[3,864,384]{2,1,0:T(8,128)(2,1)S(1)} %bitcast.6), custom_call_target="tpu_custom_call" | custom-call | flops 637009920 | bytes 921600 | tf_op jit(solution)/shard_map/pallas_call | solution.py:28
  44.6 0.0 collective-permute-done.12.past_ref
  44.7 1.1 %shard_map.82.refs_5_ = f32[4,2,48,96]{3,2,1,0:T(8,128)S(1)} custom-call(bf16[4,2,48,384]{3,2,1,0:T(8,128)(2,1)S(1)} %collective-permute-done.12.past_ref, bf16[3,864,384]{2,1,0:T(8,128)(2,1)S(1)} %bitcast.7), custom_call_target="tpu_custom_call" | custom-call | flops 382205952 | bytes 921600 | tf_op jit(solution)/shard_map/pallas_call | solution.py:28
  45.7 0.0 copy-start.1
  45.7 0.0 collective-permute-done.8.refs_3_
  45.7 1.8 %collective-permute-done.7.refs_2_ = bf16[248,128]{1,0:T(8,128)(2,1)S(1)} collective-permute-done((bf16[248,128]{1,0:T(8,128)(2,1)S(1)}, bf16[248,128]{1,0:T(8,128)(2,1)S(1)}, u32[]{:S(2)}, u32[]{:S(2)}) %collective-permute-start.7) | collective-permute-done | bytes 63520 | tf_op jit(solution)/shard_map/ppermute | solution.py:395
  47.5 0.0 collective-permute-done.6.refs_1_
  47.5 2.2 %shard_map.83 = (bf16[56,384]{1,0:T(8,128)(2,1)S(1)}, bf16[56,384]{1,0:T(8,128)(2,1)S(1)}, bf16[56,384]{1,0:T(8,128)(2,1)S(1)}, bf16[56,384]{1,0:T(8,128)(2,1)S(1)}) custom-call(bf16[248,128]{1,0:T(8,128)(2,1)S(1)} %shard_map.77.refs_0_, bf16[248,128]{1,0:T(8,128)(2,1)S(1)} %collective-permute-done.6.refs_1_, ...), custom_call_target="tpu_custom_call" | custom-call | flops 955514880 | bytes 1843200 | tf_op jit(solution)/shard_map/pallas_call | solution.py:28
  49.7 0.2 collective-permute-start.13
  49.9 0.2 collective-permute-start.14
  50.1 3.5 %collective-permute-start.15 = (bf16[56,384]{1,0:T(8,128)(2,1)S(1)}, bf16[56,384]{1,0:T(8,128)(2,1)S(1)}, u32[]{:S(2)}, u32[]{:S(2)}) collective-permute-start(bf16[56,384]{1,0:T(8,128)(2,1)S(1)} %get-tuple-element.29), channel_id=1, source_target_pairs={{0,10},{1,8},{2,11},{3,9},{4,14},{5,12},{6,15},{7,13},{8,2},{9,0},... | collective-permute-start | bytes 129032 | tf_op jit(solution)/shard_map/ppermute | solution.py:381
  53.5 1.3 %collective-permute-start.16 = (bf16[56,384]{1,0:T(8,128)(2,1)S(1)}, bf16[56,384]{1,0:T(8,128)(2,1)S(1)}, u32[]{:S(2)}, u32[]{:S(2)}) collective-permute-start(bf16[56,384]{1,0:T(8,128)(2,1)S(1)} %get-tuple-element.30), channel_id=1, source_target_pairs={{0,14},{1,12},{2,15},{3,13},{4,10},{5,8},{6,11},{7,9},{8,6},{9,4},... | collective-permute-start | bytes 129032 | tf_op jit(solution)/shard_map/ppermute | solution.py:381
  54.8 0.0 collective-permute-done.13.refs_0_
  54.8 0.0 collective-permute-done.14.refs_1_
  54.8 0.4 collective-permute-done.15.refs_2_
  55.2 3.6 %collective-permute-done.16.refs_3_ = bf16[56,384]{1,0:T(8,128)(2,1)S(1)} collective-permute-done((bf16[56,384]{1,0:T(8,128)(2,1)S(1)}, bf16[56,384]{1,0:T(8,128)(2,1)S(1)}, u32[]{:S(2)}, u32[]{:S(2)}) %collective-permute-start.16) | collective-permute-done | bytes 43040 | tf_op jit(solution)/shard_map/ppermute | solution.py:381
  58.8 1.0 %shard_map.84 = bf16[5,40,384]{2,1,0:T(8,128)(2,1)} custom-call(bf16[5,40,384]{2,1,0:T(8,128)(2,1)S(1)} %bitcast.11, bf16[56,384]{1,0:T(8,128)(2,1)S(1)} %collective-permute-done.13.refs_0_, bf16[56,384]{1,0:T(8,128)(2,1)S(1)} %collective-permute-done.14.refs_1_, bf16[56,384]{1,0:T(8,128)(2,1)S(1)} %collective-permute-done.15.refs_2_, ...), custom_call_target="tpu_custom_call" | custom-call | flops 184320 | bytes 552960 | tf_op jit(solution)/shard_map/pallas_call | solution.py:28
  (2 shorter events, 0.0 us)
Async XLA Ops:
  0.0 1.7 %collective-permute-start = (bf16[5,40,384]{2,1,0:T(8,128)(2,1)}, bf16[5,40,384]{2,1,0:T(8,128)(2,1)S(1)}, u32[]{:S(2)}, u32[]{:S(2)}) collective-permute-start(bf16[5,40,384]{2,1,0:T(8,128)(2,1)} %bitcast.9), channel_id=1, source_target_pairs={{0,1},{1,0},{2,3},{3,2},{4,5},{5,4},{6,7},{7,6},{8,9},{9,8},{10,11... | collective-permute-start | bytes 460808 | tf_op jit(solution)/shard_map/ppermute | solution.py:404
  1.8 11.1 %collective-permute-start.4 = (bf16[632,128]{1,0:T(8,128)(2,1)S(1)}, bf16[632,128]{1,0:T(8,128)(2,1)S(1)}, u32[]{:S(2)}, u32[]{:S(2)}) collective-permute-start(bf16[632,128]{1,0:T(8,128)(2,1)S(1)} %shard_map.74), channel_id=1, source_target_pairs={{0,13},{1,15},{2,12},{3,14},{4,9},{5,11},{6,8},{7,10},{8,5},{9,7},... | collective-permute-start | bytes 485384 | tf_op jit(solution)/shard_map/ppermute | solution.py:381
  6.6 15.4 %collective-permute-start.3 = (bf16[632,128]{1,0:T(8,128)(2,1)S(1)}, bf16[632,128]{1,0:T(8,128)(2,1)S(1)}, u32[]{:S(2)}, u32[]{:S(2)}) collective-permute-start(bf16[632,128]{1,0:T(8,128)(2,1)S(1)} %shard_map.74), channel_id=1, source_target_pairs={{0,9},{1,11},{2,8},{3,10},{4,13},{5,15},{6,12},{7,14},{8,1},{9,3},... | collective-permute-start | bytes 485384 | tf_op jit(solution)/shard_map/ppermute | solution.py:381
  6.7 15.4 %collective-permute-start.2 = (bf16[632,128]{1,0:T(8,128)(2,1)S(1)}, bf16[632,128]{1,0:T(8,128)(2,1)S(1)}, u32[]{:S(2)}, u32[]{:S(2)}) collective-permute-start(bf16[632,128]{1,0:T(8,128)(2,1)S(1)} %shard_map.74), channel_id=1, source_target_pairs={{0,5},{1,7},{2,4},{3,6},{4,1},{5,3},{6,0},{7,2},{8,13},{9,15},{10,... | collective-permute-start | bytes 485384 | tf_op jit(solution)/shard_map/ppermute | solution.py:381
  8.0 14.0 %collective-permute-start.1 = (bf16[632,128]{1,0:T(8,128)(2,1)S(1)}, bf16[632,128]{1,0:T(8,128)(2,1)S(1)}, u32[]{:S(2)}, u32[]{:S(2)}) collective-permute-start(bf16[632,128]{1,0:T(8,128)(2,1)S(1)} %shard_map.74), channel_id=1, source_target_pairs={{0,1},{1,3},{2,0},{3,2},{4,5},{5,7},{6,4},{7,6},{8,9},{9,11},{10,8... | collective-permute-start | bytes 485384 | tf_op jit(solution)/shard_map/ppermute | solution.py:381
  22.1 14.8 %collective-permute-start.5 = (bf16[4,272,128]{2,1,0:T(8,128)(2,1)S(1)}, bf16[4,272,128]{2,1,0:T(8,128)(2,1)S(1)}, u32[]{:S(2)}, u32[]{:S(2)}) collective-permute-start(bf16[4,272,128]{2,1,0:T(8,128)(2,1)S(1)} %shard_map.75), channel_id=1, source_target_pairs={{0,1},{1,0},{2,3},{3,2},{4,5},{5,4},{6,7},{7,6},{8,9},{9,8},{10,11... | collective-permute-start | bytes 835592 | tf_op jit(solution)/shard_map/ppermute | solution.py:381
  24.8 18.1 %copy-start = (bf16[27,96,384]{2,1,0:T(8,128)(2,1)S(1)}, bf16[27,96,384]{2,1,0:T(8,128)(2,1)}, u32[]{:S(2)}) copy-start(bf16[27,96,384]{2,1,0:T(8,128)(2,1)} %param.12) | copy-start | bytes 5971972
  24.8 7.6 %collective-permute-start.11 = (bf16[376,128]{1,0:T(8,128)(2,1)S(1)}, bf16[376,128]{1,0:T(8,128)(2,1)S(1)}, u32[]{:S(2)}, u32[]{:S(2)}) collective-permute-start(bf16[376,128]{1,0:T(8,128)(2,1)S(1)} %get-tuple-element.22.refs_0_), channel_id=1, source_target_pairs={{0,12},{4,8},{8,4},{12,0},{1,13},{5,9},{9,5},{13,1},{2,14},{6,10},... | collective-permute-start | bytes 288776 | tf_op jit(solution)/shard_map/ppermute | solution.py:395
  27.4 8.6 %collective-permute-start.10 = (bf16[376,128]{1,0:T(8,128)(2,1)S(1)}, bf16[376,128]{1,0:T(8,128)(2,1)S(1)}, u32[]{:S(2)}, u32[]{:S(2)}) collective-permute-start(bf16[376,128]{1,0:T(8,128)(2,1)S(1)} %get-tuple-element.22.refs_0_), channel_id=1, source_target_pairs={{0,8},{4,12},{8,0},{12,4},{1,9},{5,13},{9,1},{13,5},{2,10},{6,14},... | collective-permute-start | bytes 288776 | tf_op jit(solution)/shard_map/ppermute | solution.py:395
  27.4 8.6 %collective-permute-start.9 = (bf16[376,128]{1,0:T(8,128)(2,1)S(1)}, bf16[376,128]{1,0:T(8,128)(2,1)S(1)}, u32[]{:S(2)}, u32[]{:S(2)}) collective-permute-start(bf16[376,128]{1,0:T(8,128)(2,1)S(1)} %get-tuple-element.22.refs_0_), channel_id=1, source_target_pairs={{0,4},{4,0},{8,12},{12,8},{1,5},{5,1},{9,13},{13,9},{2,6},{6,2},{1... | collective-permute-start | bytes 288776 | tf_op jit(solution)/shard_map/ppermute | solution.py:395
  36.7 7.9 %collective-permute-start.12 = (bf16[4,2,48,384]{3,2,1,0:T(8,128)(2,1)S(1)}, bf16[4,2,48,384]{3,2,1,0:T(8,128)(2,1)S(1)}, u32[]{:S(2)}, u32[]{:S(2)}) collective-permute-start(bf16[4,2,48,384]{3,2,1,0:T(8,128)(2,1)S(1)} %get-tuple-element.25.last_ref), channel_id=1, source_target_pairs={{0,1},{1,0},{2,3},{3,2},{4,5},{5,4},{6,7},{7,6},{8,9},{9,8},{10,11... | collective-permute-start | bytes 884744 | tf_op jit(solution)/shard_map/ppermute | solution.py:381
  38.5 7.2 %collective-permute-start.8 = (bf16[248,128]{1,0:T(8,128)(2,1)S(1)}, bf16[248,128]{1,0:T(8,128)(2,1)S(1)}, u32[]{:S(2)}, u32[]{:S(2)}) collective-permute-start(bf16[248,128]{1,0:T(8,128)(2,1)S(1)} %shard_map.77.refs_0_), channel_id=1, source_target_pairs={{0,12},{4,8},{8,4},{12,0},{1,13},{5,9},{9,5},{13,1},{2,14},{6,10},... | collective-permute-start | bytes 190472 | tf_op jit(solution)/shard_map/ppermute | solution.py:395
  41.0 6.5 %collective-permute-start.7 = (bf16[248,128]{1,0:T(8,128)(2,1)S(1)}, bf16[248,128]{1,0:T(8,128)(2,1)S(1)}, u32[]{:S(2)}, u32[]{:S(2)}) collective-permute-start(bf16[248,128]{1,0:T(8,128)(2,1)S(1)} %shard_map.77.refs_0_), channel_id=1, source_target_pairs={{0,8},{4,12},{8,0},{12,4},{1,9},{5,13},{9,1},{13,5},{2,10},{6,14},... | collective-permute-start | bytes 190472 | tf_op jit(solution)/shard_map/ppermute | solution.py:395
  41.0 6.5 %collective-permute-start.6 = (bf16[248,128]{1,0:T(8,128)(2,1)S(1)}, bf16[248,128]{1,0:T(8,128)(2,1)S(1)}, u32[]{:S(2)}, u32[]{:S(2)}) collective-permute-start(bf16[248,128]{1,0:T(8,128)(2,1)S(1)} %shard_map.77.refs_0_), channel_id=1, source_target_pairs={{0,4},{4,0},{8,12},{12,8},{1,5},{5,1},{9,13},{13,9},{2,6},{6,2},{1... | collective-permute-start | bytes 190472 | tf_op jit(solution)/shard_map/ppermute | solution.py:395
  45.7 13.1 %copy-start.1 = (bf16[5,1,40,384]{3,2,1,0:T(8,128)(2,1)S(1)}, bf16[5,1,40,384]{3,2,1,0:T(8,128)(2,1)}, u32[]{:S(2)}) copy-start(bf16[5,1,40,384]{3,2,1,0:T(8,128)(2,1)} %param.7) | copy-start | bytes 460804
  49.7 5.1 %collective-permute-start.13 = (bf16[56,384]{1,0:T(8,128)(2,1)S(1)}, bf16[56,384]{1,0:T(8,128)(2,1)S(1)}, u32[]{:S(2)}, u32[]{:S(2)}) collective-permute-start(bf16[56,384]{1,0:T(8,128)(2,1)S(1)} %get-tuple-element.27), channel_id=1, source_target_pairs={{0,2},{1,0},{2,3},{3,1},{4,6},{5,4},{6,7},{7,5},{8,10},{9,8},{10,1... | collective-permute-start | bytes 129032 | tf_op jit(solution)/shard_map/ppermute | solution.py:381
  49.9 4.9 %collective-permute-start.14 = (bf16[56,384]{1,0:T(8,128)(2,1)S(1)}, bf16[56,384]{1,0:T(8,128)(2,1)S(1)}, u32[]{:S(2)}, u32[]{:S(2)}) collective-permute-start(bf16[56,384]{1,0:T(8,128)(2,1)S(1)} %get-tuple-element.28), channel_id=1, source_target_pairs={{0,6},{1,4},{2,7},{3,5},{4,2},{5,0},{6,3},{7,1},{8,14},{9,12},{10,... | collective-permute-start | bytes 129032 | tf_op jit(solution)/shard_map/ppermute | solution.py:381
  50.1 5.1 %collective-permute-start.15 = (bf16[56,384]{1,0:T(8,128)(2,1)S(1)}, bf16[56,384]{1,0:T(8,128)(2,1)S(1)}, u32[]{:S(2)}, u32[]{:S(2)}) collective-permute-start(bf16[56,384]{1,0:T(8,128)(2,1)S(1)} %get-tuple-element.29), channel_id=1, source_target_pairs={{0,10},{1,8},{2,11},{3,9},{4,14},{5,12},{6,15},{7,13},{8,2},{9,0},... | collective-permute-start | bytes 129032 | tf_op jit(solution)/shard_map/ppermute | solution.py:381
  53.5 5.2 %collective-permute-start.16 = (bf16[56,384]{1,0:T(8,128)(2,1)S(1)}, bf16[56,384]{1,0:T(8,128)(2,1)S(1)}, u32[]{:S(2)}, u32[]{:S(2)}) collective-permute-start(bf16[56,384]{1,0:T(8,128)(2,1)S(1)} %get-tuple-element.30), channel_id=1, source_target_pairs={{0,14},{1,12},{2,15},{3,13},{4,10},{5,8},{6,11},{7,9},{8,6},{9,4},... | collective-permute-start | bytes 129032 | tf_op jit(solution)/shard_map/ppermute | solution.py:381

commit v7 on v6

--- a/solution.py
+++ b/solution.py
@@ -184,6 +184,12 @@
                 add(f, h, shifted[i])
 
 
+def piece_rows(height, sibling=False):
+    crossed = (lax.axis_index("tm") % 2 == lax.axis_index("cols")) != sibling
+    row = lax.axis_index("rows")
+    return [row ^ jnp.where(crossed, a, b) for a, b in zip(band_order(height, True), band_order(height, False))]
+
+
 def block_number():
     return lax.axis_index("tm") // 2 * 2 + 1 - lax.axis_index("cols")
 
@@ -214,20 +220,19 @@
         fill_first(padded, (0, i), center, ends, picks, breadth)
 
 
-def first_near_body(breadth, ks, *refs):
+def first_near_body(breadth, height, *refs):
     *pieces, weight_ref, total, padded = refs
-    row = lax.axis_index("rows")
     fill_slots(padded, pieces, breadth)
     total[...] = jnp.zeros_like(total)
-    add_rows(padded, [row ^ k for k in ks], weight_ref, total)
-
-
-def first_late_body(breadth, k, piece_ref, near_ref, weight_ref, bias_ref, out_ref, total, padded):
+    add_rows(padded, piece_rows(height)[:-1], weight_ref, total)
+
+
+def first_late_body(breadth, height, piece_ref, near_ref, weight_ref, bias_ref, out_ref, total, padded):
     row = lax.axis_index("rows")
     fill_slots(padded, [piece_ref], breadth)
-    add_rows(padded, [row ^ k], weight_ref, total)
+    add_rows(padded, piece_rows(height)[-1:], weight_ref, total)
     bias_row = bias_part(bias_ref, row, weight_ref)
-    pack_first([total[h + 1] + bias_row for h in range(total.shape[0] - 2)], out_ref, breadth)
+    pack_first([total[h + 1] + bias_row for h in range(height)], out_ref, breadth)
 
 
 def cut_body(count, kept, *refs):
@@ -242,14 +247,14 @@
 def first_early_body(breadth, height, frames, *refs):
     *pieces, past_ref, weight_ref, bias_ref, out_ref, padded = refs
     row = lax.axis_index("rows")
-    for k in range(height):
+    for k, (own, other) in enumerate(zip(piece_rows(height), piece_rows(height, True))):
         past = past_ref[k].astype(jnp.float32)
         past = jnp.where(block_number() > 0, past, jnp.zeros_like(past))
         picks = [(j, frames - PAST + j) for j in range(PAST)]
         center, ends = unpack(past, PAST * breadth, frames * EDGE, padded.shape[3])
-        fill_first(padded, (0, row ^ k), center, ends, picks, breadth)
+        fill_first(padded, (0, other), center, ends, picks, breadth)
         center, ends = unpack(pieces[k][...].astype(jnp.float32), frames * breadth, frames * EDGE, padded.shape[3])
-        fill_first(padded, (PAST, row ^ k), center, ends, [(j, j) for j in range(PAST)], breadth)
+        fill_first(padded, (PAST, own), center, ends, [(j, j) for j in range(PAST)], breadth)
     pack_first(conv_sum(padded, weight_ref, bias_part(bias_ref, row, weight_ref)), out_ref, breadth)
 
 
@@ -381,7 +386,8 @@
         return lax.ppermute(values, AXES, [(place[device], place[target(*device)]) for device in every])
 
     def turned(values, k):
-        return moved(values, lambda z, x, c: (z ^ k, x // 2 * 2 + c, 1 - x % 2))
+        steps = {crosses: band_order(rows, crosses)[k] for crosses in (True, False)}
+        return moved(values, lambda z, x, c: (z ^ steps[x % 2 != c], x // 2 * 2 + c, 1 - x % 2))
 
     def returned(values, k):
         return moved(values, lambda z, x, c: (z ^ k, x // 2 * 2 + 1 - c, x % 2))
@@ -431,17 +437,16 @@
     past = following(past)
     late_sent, early_sent = (packed_rows(count * breadth, count, channels) for count in (late, PAST))
     late_rows, early_rows = (padded_rows(count * (breadth + 1)) for count in (late, PAST))
-    *ks, last_k = band_order(rows)
     sums = sds((rows + 2, late, ring, width), f32)
     near_sums = call(
-        functools.partial(first_near_body, breadth, ks), sums,
+        functools.partial(first_near_body, breadth, rows), sums,
         [VMEM((frames, rows - 1, ring, channels), bf16)], late * work * (rows - 1) // rows, 10 * size,
-        *[pieces[k] for k in ks], near,
+        *pieces[:-1], near,
     )
     part, _ = call(
-        functools.partial(first_late_body, breadth, last_k), [sds((late_sent, LANES), bf16), sums],
+        functools.partial(first_late_body, breadth, rows), [sds((late_sent, LANES), bf16), sums],
         [VMEM((frames, 1, ring, channels), bf16)], late * work // rows, 10 * size,
-        pieces[last_k], near_sums, near, bias_one, aliases={1: 1},
+        pieces[-1], near_sums, near, bias_one, aliases={1: 1},
     )
     late_parts = spread(part)
     part = call(
@@ -477,9 +482,10 @@
     return result.reshape(frames, height, breadth, channels)
 
 
-def band_order(rows):
+def band_order(rows, crosses):
     first = [k for k in range(rows - 1, 0, -1) if k != 2]
-    return first + [0] + [k for k in (2,) if k < rows]
+    order = first + [0] + [k for k in (2,) if k < rows]
+    return [{1: 2, 2: 1}.get(k, k) if crosses and rows > 2 else k for k in order]
 
 
 def solution(mesh):

time: 59.9 us -> 59.5 us (level)
  waiting for transfers between devices: 24.7 us -> 21.4 us
  starting transfers between devices: 21.1 us -> 24 us
    ppermute x10, waiting for transfers between devices: 16.1 us -> 11.6 us  [moved(): lax.ppermute(values, AXES, [(place[device], place[target(*device)]) for d...]
    ppermute x10, starting transfers between devices: 11.7 us -> 13.7 us  [moved(): lax.ppermute(values, AXES, [(place[device], place[target(*device)]) for d...]
    ppermute x6, waiting for transfers between devices: 8.45 us -> 9.63 us  [spread(): lax.ppermute(values, 'rows', [(z, z ^ k) for z in range(rows)])]
    ppermute x6, starting transfers between devices: 8.91 us -> 9.83 us  [spread(): lax.ppermute(values, 'rows', [(z, z ^ k) for z in range(rows)])]
  transfers between devices with their start and end apart: 17 -> 17, of which waited for: 8 -> 7; matrix products, arithmetic and copies ran while one was open for 0% -> 0% of each run, Pallas kernels for 18% -> 18%
where the time goes in v7:
time: 59.5 us; the launch traced here: 59.3 us
  starting transfers between devices  24 us (40%)
  waiting for transfers between devices  21.4 us (36%)
  Pallas kernels  13.8 us (23%)
    pallas_call x12, Pallas kernels, call(): pl.pallas_call(body, out_shape=out_shape, in_specs=[pl.BlockSpec(memory_s...  13.8 us
    ppermute x10, starting transfers between devices, moved(): lax.ppermute(values, AXES, [(place[device], place[target(*device)]) for d...  13.7 us
    ppermute x10, waiting for transfers between devices, moved(): lax.ppermute(values, AXES, [(place[device], place[target(*device)]) for d...  11.6 us
    ppermute x6, starting transfers between devices, spread(): lax.ppermute(values, 'rows', [(z, z ^ k) for z in range(rows)])  9.83 us
    ppermute x6, waiting for transfers between devices, spread(): lax.ppermute(values, 'rows', [(z, z ^ k) for z in range(rows)])  9.63 us
  transfers between devices with their start and end apart: 17, of which 7 were waited for; matrix products, arithmetic and copies ran while one was open for 0% of the time, Pallas kernels for 18%

profile of v7, /device:TPU:0, one launch (start us, length us, event | category | flops | bytes accessed | tf_op | source)
XLA Modules:
  0.0 59.3 jit_solution(389215836750010198)
XLA Ops:
  0.0 0.5 collective-permute-start
  0.5 1.1 %shard_map.73 = (bf16[600,128]{1,0:T(8,128)(2,1)S(1)}, f32[384]{0:T(512)S(1)}) custom-call(bf16[5,40,384]{2,1,0:T(8,128)(2,1)} %bitcast.10, f32[384]{0:T(512)} %far_gain_ref.1), custom_call_target="tpu_custom_call" | custom-call | flops 921600 | bytes 552960 | tf_op jit(solution)/shard_map/pallas_call | solution.py:28
  1.6 0.1 collective-permute-done.other_ref
  1.7 0.1 shard_map.74
  1.8 3.7 %collective-permute-start.4 = (bf16[632,128]{1,0:T(8,128)(2,1)S(1)}, bf16[632,128]{1,0:T(8,128)(2,1)S(1)}, u32[]{:S(2)}, u32[]{:S(2)}) collective-permute-start(bf16[632,128]{1,0:T(8,128)(2,1)S(1)} %shard_map.74), channel_id=1, source_target_pairs={{0,9},{1,7},{2,4},{3,10},{4,13},{5,3},{6,0},{7,14},{8,1},{9,15},{1... | collective-permute-start | bytes 485384 | tf_op jit(solution)/shard_map/ppermute | solution.py:386
  5.6 0.0 collective-permute-start.3
  5.6 2.7 %collective-permute-start.2 = (bf16[632,128]{1,0:T(8,128)(2,1)S(1)}, bf16[632,128]{1,0:T(8,128)(2,1)S(1)}, u32[]{:S(2)}, u32[]{:S(2)}) collective-permute-start(bf16[632,128]{1,0:T(8,128)(2,1)S(1)} %shard_map.74), channel_id=1, source_target_pairs={{0,5},{1,11},{2,8},{3,6},{4,1},{5,15},{6,12},{7,2},{8,13},{9,3},{1... | collective-permute-start | bytes 485384 | tf_op jit(solution)/shard_map/ppermute | solution.py:386
  8.3 1.8 %collective-permute-start.1 = (bf16[632,128]{1,0:T(8,128)(2,1)S(1)}, bf16[632,128]{1,0:T(8,128)(2,1)S(1)}, u32[]{:S(2)}, u32[]{:S(2)}) collective-permute-start(bf16[632,128]{1,0:T(8,128)(2,1)S(1)} %shard_map.74), channel_id=1, source_target_pairs={{0,13},{1,15},{2,12},{3,14},{4,9},{5,11},{6,8},{7,10},{8,5},{9,7},... | collective-permute-start | bytes 485384 | tf_op jit(solution)/shard_map/ppermute | solution.py:386
  10.2 1.6 %shard_map.76 = (f32[384]{0:T(512)S(1)}, f32[384]{0:T(512)S(1)}, f32[384]{0:T(512)S(1)}, bf16[3,864,384]{2,1,0:T(8,128)(2,1)S(1)}) custom-call(f32[384]{0:T(512)} %refs_0_.1, f32[384]{0:T(512)} %refs_1_.1, f32[384]{0:T(512)} %refs_2_.1, bf16[3,864,384]{2,1,0:T(8,128)(2,1)} %bitcast.12), custom_call_target="tpu_custom_call" | custom-call | flops 92160 | bytes 368640 | tf_op jit(solution)/shard_map/pallas_call | solution.py:28
  11.8 0.0 collective-permute-done.4.refs_3_.piece_ref
  11.8 0.5 collective-permute-done.3.refs_2_
  12.3 7.5 %collective-permute-done.2.refs_1_ = bf16[632,128]{1,0:T(8,128)(2,1)S(1)} collective-permute-done((bf16[632,128]{1,0:T(8,128)(2,1)S(1)}, bf16[632,128]{1,0:T(8,128)(2,1)S(1)}, u32[]{:S(2)}, u32[]{:S(2)}) %collective-permute-start.2) | collective-permute-done | bytes 161824 | tf_op jit(solution)/shard_map/ppermute | solution.py:386
  19.8 0.0 collective-permute-done.1.refs_0_
  19.9 0.1 collective-permute-start.5
  19.9 1.7 %shard_map.78.near_ref = f32[6,3,48,96]{3,2,1,0:T(8,128)S(1)} custom-call(bf16[632,128]{1,0:T(8,128)(2,1)S(1)} %collective-permute-done.1.refs_0_, bf16[632,128]{1,0:T(8,128)(2,1)S(1)} %collective-permute-done.2.refs_1_, bf16[632,128]{1,0:T(8,128)(2,1)S(1)} %collective-permute-done.3.refs_2_, ...), custom_call_target="tpu_custom_call" | custom-call | flops 859963392 | bytes 921600 | tf_op jit(solution)/shard_map/pallas_call | solution.py:28
  21.6 1.0 %shard_map.79 = (bf16[376,128]{1,0:T(8,128)(2,1)S(1)}, f32[6,3,48,96]{3,2,1,0:T(8,128)S(1)}) custom-call(bf16[632,128]{1,0:T(8,128)(2,1)S(1)} %collective-permute-done.4.refs_3_.piece_ref, f32[6,3,48,96]{3,2,1,0:T(8,128)S(1)} %shard_map.78.near_ref, ...), custom_call_target="tpu_custom_call", output_to_operand_aliasing={{1}: (1, {})} | custom-call | flops 286654464 | bytes 921600 | tf_op jit(solution)/shard_map/pallas_call | solution.py:28
  22.6 0.0 copy-start
  22.6 3.1 %collective-permute-start.11 = (bf16[376,128]{1,0:T(8,128)(2,1)S(1)}, bf16[376,128]{1,0:T(8,128)(2,1)S(1)}, u32[]{:S(2)}, u32[]{:S(2)}) collective-permute-start(bf16[376,128]{1,0:T(8,128)(2,1)S(1)} %get-tuple-element.22.refs_0_), channel_id=1, source_target_pairs={{0,12},{4,8},{8,4},{12,0},{1,13},{5,9},{9,5},{13,1},{2,14},{6,10},... | collective-permute-start | bytes 288776 | tf_op jit(solution)/shard_map/ppermute | solution.py:401
  25.8 1.8 %collective-permute-start.10 = (bf16[376,128]{1,0:T(8,128)(2,1)S(1)}, bf16[376,128]{1,0:T(8,128)(2,1)S(1)}, u32[]{:S(2)}, u32[]{:S(2)}) collective-permute-start(bf16[376,128]{1,0:T(8,128)(2,1)S(1)} %get-tuple-element.22.refs_0_), channel_id=1, source_target_pairs={{0,8},{4,12},{8,0},{12,4},{1,9},{5,13},{9,1},{13,5},{2,10},{6,14},... | collective-permute-start | bytes 288776 | tf_op jit(solution)/shard_map/ppermute | solution.py:401
  27.5 0.5 collective-permute-start.9
  28.0 1.7 %collective-permute-done.11.refs_3_ = bf16[376,128]{1,0:T(8,128)(2,1)S(1)} collective-permute-done((bf16[376,128]{1,0:T(8,128)(2,1)S(1)}, bf16[376,128]{1,0:T(8,128)(2,1)S(1)}, u32[]{:S(2)}, u32[]{:S(2)}) %collective-permute-start.11) | collective-permute-done | bytes 96288 | tf_op jit(solution)/shard_map/ppermute | solution.py:401
  29.7 6.1 %collective-permute-done.10.refs_2_ = bf16[376,128]{1,0:T(8,128)(2,1)S(1)} collective-permute-done((bf16[376,128]{1,0:T(8,128)(2,1)S(1)}, bf16[376,128]{1,0:T(8,128)(2,1)S(1)}, u32[]{:S(2)}, u32[]{:S(2)}) %collective-permute-start.10) | collective-permute-done | bytes 96288 | tf_op jit(solution)/shard_map/ppermute | solution.py:401
  35.8 0.0 collective-permute-done.9.refs_1_
  35.8 0.7 %shard_map.80 = (bf16[4,1,48,384]{3,2,1,0:T(8,128)(2,1)S(1)}, bf16[4,2,48,384]{3,2,1,0:T(8,128)(2,1)S(1)}) custom-call(bf16[376,128]{1,0:T(8,128)(2,1)S(1)} %get-tuple-element.22.refs_0_, bf16[376,128]{1,0:T(8,128)(2,1)S(1)} %collective-permute-done.9.refs_1_, bf16[376,128]{1,0:T(8,128)(2,1)S(1)} %collective-permute-done.10.refs_2_, ...), custom_call_target="tpu_custom_call" | custom-call | flops 3686400 | bytes 1474560 | tf_op jit(solution)/shard_map/pallas_call | solution.py:28
  36.6 0.2 collective-permute-start.12
  36.7 0.0 collective-permute-done.5.refs_4_
  36.7 1.6 %shard_map.77.refs_0_ = bf16[248,128]{1,0:T(8,128)(2,1)S(1)} custom-call(bf16[632,128]{1,0:T(8,128)(2,1)S(1)} %collective-permute-done.1.refs_0_, bf16[632,128]{1,0:T(8,128)(2,1)S(1)} %collective-permute-done.2.refs_1_, bf16[632,128]{1,0:T(8,128)(2,1)S(1)} %collective-permute-done.3.refs_2_, bf16[632,128]{1,0:T(8,128)(2,1)S(1)} %collective-permute-done.4.refs_3_.piece_ref, ...), custom_call_target="tpu_custom_call" | custom-call | flops 764411904 | bytes 1843200 | tf_op jit(solution)/shard_map/pallas_call | solution.py:28
  38.4 3.1 %collective-permute-start.8 = (bf16[248,128]{1,0:T(8,128)(2,1)S(1)}, bf16[248,128]{1,0:T(8,128)(2,1)S(1)}, u32[]{:S(2)}, u32[]{:S(2)}) collective-permute-start(bf16[248,128]{1,0:T(8,128)(2,1)S(1)} %shard_map.77.refs_0_), channel_id=1, source_target_pairs={{0,12},{4,8},{8,4},{12,0},{1,13},{5,9},{9,5},{13,1},{2,14},{6,10},... | collective-permute-start | bytes 190472 | tf_op jit(solution)/shard_map/ppermute | solution.py:401
  41.5 0.0 collective-permute-start.7
  41.5 1.3 %collective-permute-start.6 = (bf16[248,128]{1,0:T(8,128)(2,1)S(1)}, bf16[248,128]{1,0:T(8,128)(2,1)S(1)}, u32[]{:S(2)}, u32[]{:S(2)}) collective-permute-start(bf16[248,128]{1,0:T(8,128)(2,1)S(1)} %shard_map.77.refs_0_), channel_id=1, source_target_pairs={{0,4},{4,0},{8,12},{12,8},{1,5},{5,1},{9,13},{13,9},{2,6},{6,2},{1... | collective-permute-start | bytes 190472 | tf_op jit(solution)/shard_map/ppermute | solution.py:401
  42.8 1.7 %shard_map.81.refs_4_ = f32[4,3,48,96]{3,2,1,0:T(8,128)S(1)} custom-call(bf16[4,1,48,384]{3,2,1,0:T(8,128)(2,1)S(1)} %get-tuple-element.24.middle_ref, bf16[4,2,48,384]{3,2,1,0:T(8,128)(2,1)S(1)} %get-tuple-element.25.last_ref, bf16[3,864,384]{2,1,0:T(8,128)(2,1)S(1)} %bitcast.6), custom_call_target="tpu_custom_call" | custom-call | flops 637009920 | bytes 921600 | tf_op jit(solution)/shard_map/pallas_call | solution.py:28
  44.5 0.0 collective-permute-done.12.past_ref
  44.6 1.1 %shard_map.82.refs_5_ = f32[4,2,48,96]{3,2,1,0:T(8,128)S(1)} custom-call(bf16[4,2,48,384]{3,2,1,0:T(8,128)(2,1)S(1)} %collective-permute-done.12.past_ref, bf16[3,864,384]{2,1,0:T(8,128)(2,1)S(1)} %bitcast.7), custom_call_target="tpu_custom_call" | custom-call | flops 382205952 | bytes 921600 | tf_op jit(solution)/shard_map/pallas_call | solution.py:28
  45.6 0.0 copy-start.1
  45.6 0.0 collective-permute-done.8.refs_3_
  45.6 1.8 %collective-permute-done.7.refs_2_ = bf16[248,128]{1,0:T(8,128)(2,1)S(1)} collective-permute-done((bf16[248,128]{1,0:T(8,128)(2,1)S(1)}, bf16[248,128]{1,0:T(8,128)(2,1)S(1)}, u32[]{:S(2)}, u32[]{:S(2)}) %collective-permute-start.7) | collective-permute-done | bytes 63520 | tf_op jit(solution)/shard_map/ppermute | solution.py:401
  47.4 0.0 collective-permute-done.6.refs_1_
  47.4 2.2 %shard_map.83 = (bf16[56,384]{1,0:T(8,128)(2,1)S(1)}, bf16[56,384]{1,0:T(8,128)(2,1)S(1)}, bf16[56,384]{1,0:T(8,128)(2,1)S(1)}, bf16[56,384]{1,0:T(8,128)(2,1)S(1)}) custom-call(bf16[248,128]{1,0:T(8,128)(2,1)S(1)} %shard_map.77.refs_0_, bf16[248,128]{1,0:T(8,128)(2,1)S(1)} %collective-permute-done.6.refs_1_, ...), custom_call_target="tpu_custom_call" | custom-call | flops 955514880 | bytes 1843200 | tf_op jit(solution)/shard_map/pallas_call | solution.py:28
  49.6 0.0 collective-permute-start.13
  49.6 0.6 collective-permute-start.14
  50.2 2.9 %collective-permute-start.15 = (bf16[56,384]{1,0:T(8,128)(2,1)S(1)}, bf16[56,384]{1,0:T(8,128)(2,1)S(1)}, u32[]{:S(2)}, u32[]{:S(2)}) collective-permute-start(bf16[56,384]{1,0:T(8,128)(2,1)S(1)} %get-tuple-element.29), channel_id=1, source_target_pairs={{0,10},{1,8},{2,11},{3,9},{4,14},{5,12},{6,15},{7,13},{8,2},{9,0},... | collective-permute-start | bytes 129032 | tf_op jit(solution)/shard_map/ppermute | solution.py:386
  53.1 1.7 %collective-permute-start.16 = (bf16[56,384]{1,0:T(8,128)(2,1)S(1)}, bf16[56,384]{1,0:T(8,128)(2,1)S(1)}, u32[]{:S(2)}, u32[]{:S(2)}) collective-permute-start(bf16[56,384]{1,0:T(8,128)(2,1)S(1)} %get-tuple-element.30), channel_id=1, source_target_pairs={{0,14},{1,12},{2,15},{3,13},{4,10},{5,8},{6,11},{7,9},{8,6},{9,4},... | collective-permute-start | bytes 129032 | tf_op jit(solution)/shard_map/ppermute | solution.py:386
  54.8 0.0 collective-permute-done.13.refs_0_
  54.8 0.0 collective-permute-done.14.refs_1_
  54.8 0.0 collective-permute-done.15.refs_2_
  54.8 3.6 %collective-permute-done.16.refs_3_ = bf16[56,384]{1,0:T(8,128)(2,1)S(1)} collective-permute-done((bf16[56,384]{1,0:T(8,128)(2,1)S(1)}, bf16[56,384]{1,0:T(8,128)(2,1)S(1)}, u32[]{:S(2)}, u32[]{:S(2)}) %collective-permute-start.16) | collective-permute-done | bytes 43040 | tf_op jit(solution)/shard_map/ppermute | solution.py:386
  58.3 0.0 copy-done.1
  58.3 1.0 %shard_map.84 = bf16[5,40,384]{2,1,0:T(8,128)(2,1)} custom-call(bf16[5,40,384]{2,1,0:T(8,128)(2,1)S(1)} %bitcast.11, bf16[56,384]{1,0:T(8,128)(2,1)S(1)} %collective-permute-done.13.refs_0_, bf16[56,384]{1,0:T(8,128)(2,1)S(1)} %collective-permute-done.14.refs_1_, bf16[56,384]{1,0:T(8,128)(2,1)S(1)} %collective-permute-done.15.refs_2_, ...), custom_call_target="tpu_custom_call" | custom-call | flops 184320 | bytes 552960 | tf_op jit(solution)/shard_map/pallas_call | solution.py:28
  (2 shorter events, 0.0 us)
Async XLA Ops:
  0.0 1.7 %collective-permute-start = (bf16[5,40,384]{2,1,0:T(8,128)(2,1)}, bf16[5,40,384]{2,1,0:T(8,128)(2,1)S(1)}, u32[]{:S(2)}, u32[]{:S(2)}) collective-permute-start(bf16[5,40,384]{2,1,0:T(8,128)(2,1)} %bitcast.9), channel_id=1, source_target_pairs={{0,1},{1,0},{2,3},{3,2},{4,5},{5,4},{6,7},{7,6},{8,9},{9,8},{10,11... | collective-permute-start | bytes 460808 | tf_op jit(solution)/shard_map/ppermute | solution.py:410
  1.8 10.0 %collective-permute-start.4 = (bf16[632,128]{1,0:T(8,128)(2,1)S(1)}, bf16[632,128]{1,0:T(8,128)(2,1)S(1)}, u32[]{:S(2)}, u32[]{:S(2)}) collective-permute-start(bf16[632,128]{1,0:T(8,128)(2,1)S(1)} %shard_map.74), channel_id=1, source_target_pairs={{0,9},{1,7},{2,4},{3,10},{4,13},{5,3},{6,0},{7,14},{8,1},{9,15},{1... | collective-permute-start | bytes 485384 | tf_op jit(solution)/shard_map/ppermute | solution.py:386
  5.6 6.7 %collective-permute-start.3 = (bf16[632,128]{1,0:T(8,128)(2,1)S(1)}, bf16[632,128]{1,0:T(8,128)(2,1)S(1)}, u32[]{:S(2)}, u32[]{:S(2)}) collective-permute-start(bf16[632,128]{1,0:T(8,128)(2,1)S(1)} %shard_map.74), channel_id=1, source_target_pairs={{0,1},{1,3},{2,0},{3,2},{4,5},{5,7},{6,4},{7,6},{8,9},{9,11},{10,8... | collective-permute-start | bytes 485384 | tf_op jit(solution)/shard_map/ppermute | solution.py:386
  5.6 14.2 %collective-permute-start.2 = (bf16[632,128]{1,0:T(8,128)(2,1)S(1)}, bf16[632,128]{1,0:T(8,128)(2,1)S(1)}, u32[]{:S(2)}, u32[]{:S(2)}) collective-permute-start(bf16[632,128]{1,0:T(8,128)(2,1)S(1)} %shard_map.74), channel_id=1, source_target_pairs={{0,5},{1,11},{2,8},{3,6},{4,1},{5,15},{6,12},{7,2},{8,13},{9,3},{1... | collective-permute-start | bytes 485384 | tf_op jit(solution)/shard_map/ppermute | solution.py:386
  8.3 11.5 %collective-permute-start.1 = (bf16[632,128]{1,0:T(8,128)(2,1)S(1)}, bf16[632,128]{1,0:T(8,128)(2,1)S(1)}, u32[]{:S(2)}, u32[]{:S(2)}) collective-permute-start(bf16[632,128]{1,0:T(8,128)(2,1)S(1)} %shard_map.74), channel_id=1, source_target_pairs={{0,13},{1,15},{2,12},{3,14},{4,9},{5,11},{6,8},{7,10},{8,5},{9,7},... | collective-permute-start | bytes 485384 | tf_op jit(solution)/shard_map/ppermute | solution.py:386
  19.9 16.9 %collective-permute-start.5 = (bf16[4,272,128]{2,1,0:T(8,128)(2,1)S(1)}, bf16[4,272,128]{2,1,0:T(8,128)(2,1)S(1)}, u32[]{:S(2)}, u32[]{:S(2)}) collective-permute-start(bf16[4,272,128]{2,1,0:T(8,128)(2,1)S(1)} %shard_map.75), channel_id=1, source_target_pairs={{0,1},{1,0},{2,3},{3,2},{4,5},{5,4},{6,7},{7,6},{8,9},{9,8},{10,11... | collective-permute-start | bytes 835592 | tf_op jit(solution)/shard_map/ppermute | solution.py:386
  22.6 20.2 %copy-start = (bf16[27,96,384]{2,1,0:T(8,128)(2,1)S(1)}, bf16[27,96,384]{2,1,0:T(8,128)(2,1)}, u32[]{:S(2)}) copy-start(bf16[27,96,384]{2,1,0:T(8,128)(2,1)} %param.12) | copy-start | bytes 5971972
  22.6 7.1 %collective-permute-start.11 = (bf16[376,128]{1,0:T(8,128)(2,1)S(1)}, bf16[376,128]{1,0:T(8,128)(2,1)S(1)}, u32[]{:S(2)}, u32[]{:S(2)}) collective-permute-start(bf16[376,128]{1,0:T(8,128)(2,1)S(1)} %get-tuple-element.22.refs_0_), channel_id=1, source_target_pairs={{0,12},{4,8},{8,4},{12,0},{1,13},{5,9},{9,5},{13,1},{2,14},{6,10},... | collective-permute-start | bytes 288776 | tf_op jit(solution)/shard_map/ppermute | solution.py:401
  25.8 10.1 %collective-permute-start.10 = (bf16[376,128]{1,0:T(8,128)(2,1)S(1)}, bf16[376,128]{1,0:T(8,128)(2,1)S(1)}, u32[]{:S(2)}, u32[]{:S(2)}) collective-permute-start(bf16[376,128]{1,0:T(8,128)(2,1)S(1)} %get-tuple-element.22.refs_0_), channel_id=1, source_target_pairs={{0,8},{4,12},{8,0},{12,4},{1,9},{5,13},{9,1},{13,5},{2,10},{6,14},... | collective-permute-start | bytes 288776 | tf_op jit(solution)/shard_map/ppermute | solution.py:401
  27.5 8.3 %collective-permute-start.9 = (bf16[376,128]{1,0:T(8,128)(2,1)S(1)}, bf16[376,128]{1,0:T(8,128)(2,1)S(1)}, u32[]{:S(2)}, u32[]{:S(2)}) collective-permute-start(bf16[376,128]{1,0:T(8,128)(2,1)S(1)} %get-tuple-element.22.refs_0_), channel_id=1, source_target_pairs={{0,4},{4,0},{8,12},{12,8},{1,5},{5,1},{9,13},{13,9},{2,6},{6,2},{1... | collective-permute-start | bytes 288776 | tf_op jit(solution)/shard_map/ppermute | solution.py:401
  36.6 8.0 %collective-permute-start.12 = (bf16[4,2,48,384]{3,2,1,0:T(8,128)(2,1)S(1)}, bf16[4,2,48,384]{3,2,1,0:T(8,128)(2,1)S(1)}, u32[]{:S(2)}, u32[]{:S(2)}) collective-permute-start(bf16[4,2,48,384]{3,2,1,0:T(8,128)(2,1)S(1)} %get-tuple-element.25.last_ref), channel_id=1, source_target_pairs={{0,1},{1,0},{2,3},{3,2},{4,5},{5,4},{6,7},{7,6},{8,9},{9,8},{10,11... | collective-permute-start | bytes 884744 | tf_op jit(solution)/shard_map/ppermute | solution.py:386
  38.4 7.2 %collective-permute-start.8 = (bf16[248,128]{1,0:T(8,128)(2,1)S(1)}, bf16[248,128]{1,0:T(8,128)(2,1)S(1)}, u32[]{:S(2)}, u32[]{:S(2)}) collective-permute-start(bf16[248,128]{1,0:T(8,128)(2,1)S(1)} %shard_map.77.refs_0_), channel_id=1, source_target_pairs={{0,12},{4,8},{8,4},{12,0},{1,13},{5,9},{9,5},{13,1},{2,14},{6,10},... | collective-permute-start | bytes 190472 | tf_op jit(solution)/shard_map/ppermute | solution.py:401
  41.5 5.9 %collective-permute-start.7 = (bf16[248,128]{1,0:T(8,128)(2,1)S(1)}, bf16[248,128]{1,0:T(8,128)(2,1)S(1)}, u32[]{:S(2)}, u32[]{:S(2)}) collective-permute-start(bf16[248,128]{1,0:T(8,128)(2,1)S(1)} %shard_map.77.refs_0_), channel_id=1, source_target_pairs={{0,8},{4,12},{8,0},{12,4},{1,9},{5,13},{9,1},{13,5},{2,10},{6,14},... | collective-permute-start | bytes 190472 | tf_op jit(solution)/shard_map/ppermute | solution.py:401
  41.5 5.9 %collective-permute-start.6 = (bf16[248,128]{1,0:T(8,128)(2,1)S(1)}, bf16[248,128]{1,0:T(8,128)(2,1)S(1)}, u32[]{:S(2)}, u32[]{:S(2)}) collective-permute-start(bf16[248,128]{1,0:T(8,128)(2,1)S(1)} %shard_map.77.refs_0_), channel_id=1, source_target_pairs={{0,4},{4,0},{8,12},{12,8},{1,5},{5,1},{9,13},{13,9},{2,6},{6,2},{1... | collective-permute-start | bytes 190472 | tf_op jit(solution)/shard_map/ppermute | solution.py:401
  45.6 12.7 %copy-start.1 = (bf16[5,1,40,384]{3,2,1,0:T(8,128)(2,1)S(1)}, bf16[5,1,40,384]{3,2,1,0:T(8,128)(2,1)}, u32[]{:S(2)}) copy-start(bf16[5,1,40,384]{3,2,1,0:T(8,128)(2,1)} %param.7) | copy-start | bytes 460804
  49.6 5.1 %collective-permute-start.13 = (bf16[56,384]{1,0:T(8,128)(2,1)S(1)}, bf16[56,384]{1,0:T(8,128)(2,1)S(1)}, u32[]{:S(2)}, u32[]{:S(2)}) collective-permute-start(bf16[56,384]{1,0:T(8,128)(2,1)S(1)} %get-tuple-element.27), channel_id=1, source_target_pairs={{0,2},{1,0},{2,3},{3,1},{4,6},{5,4},{6,7},{7,5},{8,10},{9,8},{10,1... | collective-permute-start | bytes 129032 | tf_op jit(solution)/shard_map/ppermute | solution.py:386
  49.6 5.1 %collective-permute-start.14 = (bf16[56,384]{1,0:T(8,128)(2,1)S(1)}, bf16[56,384]{1,0:T(8,128)(2,1)S(1)}, u32[]{:S(2)}, u32[]{:S(2)}) collective-permute-start(bf16[56,384]{1,0:T(8,128)(2,1)S(1)} %get-tuple-element.28), channel_id=1, source_target_pairs={{0,6},{1,4},{2,7},{3,5},{4,2},{5,0},{6,3},{7,1},{8,14},{9,12},{10,... | collective-permute-start | bytes 129032 | tf_op jit(solution)/shard_map/ppermute | solution.py:386
  50.2 4.6 %collective-permute-start.15 = (bf16[56,384]{1,0:T(8,128)(2,1)S(1)}, bf16[56,384]{1,0:T(8,128)(2,1)S(1)}, u32[]{:S(2)}, u32[]{:S(2)}) collective-permute-start(bf16[56,384]{1,0:T(8,128)(2,1)S(1)} %get-tuple-element.29), channel_id=1, source_target_pairs={{0,10},{1,8},{2,11},{3,9},{4,14},{5,12},{6,15},{7,13},{8,2},{9,0},... | collective-permute-start | bytes 129032 | tf_op jit(solution)/shard_map/ppermute | solution.py:386
  53.1 5.2 %collective-permute-start.16 = (bf16[56,384]{1,0:T(8,128)(2,1)S(1)}, bf16[56,384]{1,0:T(8,128)(2,1)S(1)}, u32[]{:S(2)}, u32[]{:S(2)}) collective-permute-start(bf16[56,384]{1,0:T(8,128)(2,1)S(1)} %get-tuple-element.30), channel_id=1, source_target_pairs={{0,14},{1,12},{2,15},{3,13},{4,10},{5,8},{6,11},{7,9},{8,6},{9,4},... | collective-permute-start | bytes 129032 | tf_op jit(solution)/shard_map/ppermute | solution.py:386

commit v8 on v7

--- a/solution.py
+++ b/solution.py
@@ -11,6 +11,7 @@
 AXES = ("rows", "tm", "cols")
 EDGE = 2
 LANES = 128
+LAST = 2
 PAST = 2
 TAPS = 3
 VMEM = pltpu.VMEM
@@ -224,13 +225,14 @@
     *pieces, weight_ref, total, padded = refs
     fill_slots(padded, pieces, breadth)
     total[...] = jnp.zeros_like(total)
-    add_rows(padded, piece_rows(height)[:-1], weight_ref, total)
-
-
-def first_late_body(breadth, height, piece_ref, near_ref, weight_ref, bias_ref, out_ref, total, padded):
+    add_rows(padded, piece_rows(height)[:-LAST], weight_ref, total)
+
+
+def first_late_body(breadth, height, *refs):
+    *pieces, near_ref, weight_ref, bias_ref, out_ref, total, padded = refs
     row = lax.axis_index("rows")
-    fill_slots(padded, [piece_ref], breadth)
-    add_rows(padded, piece_rows(height)[-1:], weight_ref, total)
+    fill_slots(padded, pieces, breadth)
+    add_rows(padded, piece_rows(height)[-LAST:], weight_ref, total)
     bias_row = bias_part(bias_ref, row, weight_ref)
     pack_first([total[h + 1] + bias_row for h in range(height)], out_ref, breadth)
 
@@ -440,13 +442,13 @@
     sums = sds((rows + 2, late, ring, width), f32)
     near_sums = call(
         functools.partial(first_near_body, breadth, rows), sums,
-        [VMEM((frames, rows - 1, ring, channels), bf16)], late * work * (rows - 1) // rows, 10 * size,
-        *pieces[:-1], near,
+        [VMEM((frames, rows - LAST, ring, channels), bf16)], late * work * (rows - LAST) // rows, 10 * size,
+        *pieces[:-LAST], near,
     )
     part, _ = call(
         functools.partial(first_late_body, breadth, rows), [sds((late_sent, LANES), bf16), sums],
-        [VMEM((frames, 1, ring, channels), bf16)], late * work // rows, 10 * size,
-        pieces[-1], near_sums, near, bias_one, aliases={1: 1},
+        [VMEM((frames, LAST, ring, channels), bf16)], late * work * LAST // rows, 10 * size,
+        *pieces[-LAST:], near_sums, near, bias_one, aliases={LAST: 1},
     )
     late_parts = spread(part)
     part = call(
@@ -483,9 +485,7 @@
 
 
 def band_order(rows, crosses):
-    first = [k for k in range(rows - 1, 0, -1) if k != 2]
-    order = first + [0] + [k for k in (2,) if k < rows]
-    return [{1: 2, 2: 1}.get(k, k) if crosses and rows > 2 else k for k in order]
+    return [*range(rows - 1, 2, -1), 0] + ([2, 1] if crosses else [1, 2])
 
 
 def solution(mesh):

time: 59.5 us -> 59.6 us (level)
  waiting for transfers between devices: 21.4 us -> 22 us
  transfers between devices with their start and end apart: 17 -> 17, of which waited for: 7 -> 7; matrix products, arithmetic and copies ran while one was open for 0% -> 0% of each run, Pallas kernels for 18% -> 17%
where the time goes in v8:
time: 59.6 us; the launch traced here: 59.4 us
  starting transfers between devices  23.7 us (40%)
  waiting for transfers between devices  22 us (37%)
  Pallas kernels  13.6 us (23%)
    ppermute x10, starting transfers between devices, moved(): lax.ppermute(values, AXES, [(place[device], place[target(*device)]) for d...  13.7 us
    pallas_call x12, Pallas kernels, call(): pl.pallas_call(body, out_shape=out_shape, in_specs=[pl.BlockSpec(memory_s...  13.6 us
    ppermute x10, waiting for transfers between devices, moved(): lax.ppermute(values, AXES, [(place[device], place[target(*device)]) for d...  12.1 us
    ppermute x6, waiting for transfers between devices, spread(): lax.ppermute(values, 'rows', [(z, z ^ k) for z in range(rows)])  9.78 us
    ppermute x6, starting transfers between devices, spread(): lax.ppermute(values, 'rows', [(z, z ^ k) for z in range(rows)])  9.58 us
  transfers between devices with their start and end apart: 17, of which 7 were waited for; matrix products, arithmetic and copies ran while one was open for 0% of the time, Pallas kernels for 17%

profile of v8, /device:TPU:0, one launch (start us, length us, event | category | flops | bytes accessed | tf_op | source)
XLA Modules:
  0.0 59.4 jit_solution(12803044769119568502)
XLA Ops:
  0.0 0.5 collective-permute-start
  0.5 1.1 %shard_map.73 = (bf16[600,128]{1,0:T(8,128)(2,1)S(1)}, f32[384]{0:T(512)S(1)}) custom-call(bf16[5,40,384]{2,1,0:T(8,128)(2,1)} %bitcast.10, f32[384]{0:T(512)} %far_gain_ref.1), custom_call_target="tpu_custom_call" | custom-call | flops 921600 | bytes 552960 | tf_op jit(solution)/shard_map/pallas_call | solution.py:29
  1.6 0.1 collective-permute-done.other_ref
  1.7 0.1 shard_map.74
  1.8 3.7 %collective-permute-start.4 = (bf16[632,128]{1,0:T(8,128)(2,1)S(1)}, bf16[632,128]{1,0:T(8,128)(2,1)S(1)}, u32[]{:S(2)}, u32[]{:S(2)}) collective-permute-start(bf16[632,128]{1,0:T(8,128)(2,1)S(1)} %shard_map.74), channel_id=1, source_target_pairs={{0,9},{1,7},{2,4},{3,10},{4,13},{5,3},{6,0},{7,14},{8,1},{9,15},{1... | collective-permute-start | bytes 485384 | tf_op jit(solution)/shard_map/ppermute | solution.py:388
  5.6 0.1 collective-permute-start.3
  5.7 1.3 %collective-permute-start.2 = (bf16[632,128]{1,0:T(8,128)(2,1)S(1)}, bf16[632,128]{1,0:T(8,128)(2,1)S(1)}, u32[]{:S(2)}, u32[]{:S(2)}) collective-permute-start(bf16[632,128]{1,0:T(8,128)(2,1)S(1)} %shard_map.74), channel_id=1, source_target_pairs={{0,1},{1,3},{2,0},{3,2},{4,5},{5,7},{6,4},{7,6},{8,9},{9,11},{10,8... | collective-permute-start | bytes 485384 | tf_op jit(solution)/shard_map/ppermute | solution.py:388
  6.9 3.2 %collective-permute-start.1 = (bf16[632,128]{1,0:T(8,128)(2,1)S(1)}, bf16[632,128]{1,0:T(8,128)(2,1)S(1)}, u32[]{:S(2)}, u32[]{:S(2)}) collective-permute-start(bf16[632,128]{1,0:T(8,128)(2,1)S(1)} %shard_map.74), channel_id=1, source_target_pairs={{0,13},{1,15},{2,12},{3,14},{4,9},{5,11},{6,8},{7,10},{8,5},{9,7},... | collective-permute-start | bytes 485384 | tf_op jit(solution)/shard_map/ppermute | solution.py:388
  10.2 1.6 %shard_map.76 = (f32[384]{0:T(512)S(1)}, f32[384]{0:T(512)S(1)}, f32[384]{0:T(512)S(1)}, bf16[3,864,384]{2,1,0:T(8,128)(2,1)S(1)}) custom-call(f32[384]{0:T(512)} %refs_0_.1, f32[384]{0:T(512)} %refs_1_.1, f32[384]{0:T(512)} %refs_2_.1, bf16[3,864,384]{2,1,0:T(8,128)(2,1)} %bitcast.12), custom_call_target="tpu_custom_call" | custom-call | flops 92160 | bytes 368640 | tf_op jit(solution)/shard_map/pallas_call | solution.py:29
  11.8 0.0 collective-permute-done.4.refs_3_.refs_1_
  11.8 8.3 %collective-permute-done.3.refs_2_.refs_0_ = bf16[632,128]{1,0:T(8,128)(2,1)S(1)} collective-permute-done((bf16[632,128]{1,0:T(8,128)(2,1)S(1)}, bf16[632,128]{1,0:T(8,128)(2,1)S(1)}, u32[]{:S(2)}, u32[]{:S(2)}) %collective-permute-start.3) | collective-permute-done | bytes 161824 | tf_op jit(solution)/shard_map/ppermute | solution.py:388
  20.1 0.0 collective-permute-done.2.refs_1_
  20.1 0.0 collective-permute-done.1.refs_0_
  20.1 0.1 collective-permute-start.5
  20.2 1.2 %shard_map.78.refs_2_ = f32[6,3,48,96]{3,2,1,0:T(8,128)S(1)} custom-call(bf16[632,128]{1,0:T(8,128)(2,1)S(1)} %collective-permute-done.1.refs_0_, bf16[632,128]{1,0:T(8,128)(2,1)S(1)} %collective-permute-done.2.refs_1_, bf16[3,864,384]{2,1,0:T(8,128)(2,1)S(1)} %get-tuple-element.20.refs_5_.refs_2_.refs_3_), custom_call_target="tpu_custom_call" | custom-call | flops 573308928 | bytes 921600 | tf_op jit(solution)/shard_map/pallas_call | solution.py:29
  21.4 1.3 %shard_map.79 = (bf16[376,128]{1,0:T(8,128)(2,1)S(1)}, f32[6,3,48,96]{3,2,1,0:T(8,128)S(1)}) custom-call(bf16[632,128]{1,0:T(8,128)(2,1)S(1)} %collective-permute-done.3.refs_2_.refs_0_, bf16[632,128]{1,0:T(8,128)(2,1)S(1)} %collective-permute-done.4.refs_3_.refs_1_, f32[6,3,48,96]{3,2,1,0:T(8,128)S(1)} %shard_map.78.refs_2_, ...), custom_call_target="tpu_custom_call", output_to_operand_aliasing={{1}: (2, {})} | custom-call | flops 573308928 | bytes 921600 | tf_op jit(solution)/shard_map/pallas_call | solution.py:29
  22.7 0.0 copy-start
  22.7 2.3 %collective-permute-start.11 = (bf16[376,128]{1,0:T(8,128)(2,1)S(1)}, bf16[376,128]{1,0:T(8,128)(2,1)S(1)}, u32[]{:S(2)}, u32[]{:S(2)}) collective-permute-start(bf16[376,128]{1,0:T(8,128)(2,1)S(1)} %get-tuple-element.22.refs_0_), channel_id=1, source_target_pairs={{0,12},{4,8},{8,4},{12,0},{1,13},{5,9},{9,5},{13,1},{2,14},{6,10},... | collective-permute-start | bytes 288776 | tf_op jit(solution)/shard_map/ppermute | solution.py:403
  25.0 2.3 %collective-permute-start.10 = (bf16[376,128]{1,0:T(8,128)(2,1)S(1)}, bf16[376,128]{1,0:T(8,128)(2,1)S(1)}, u32[]{:S(2)}, u32[]{:S(2)}) collective-permute-start(bf16[376,128]{1,0:T(8,128)(2,1)S(1)} %get-tuple-element.22.refs_0_), channel_id=1, source_target_pairs={{0,8},{4,12},{8,0},{12,4},{1,9},{5,13},{9,1},{13,5},{2,10},{6,14},... | collective-permute-start | bytes 288776 | tf_op jit(solution)/shard_map/ppermute | solution.py:403
  27.3 0.5 collective-permute-start.9
  27.8 2.0 %collective-permute-done.11.refs_3_ = bf16[376,128]{1,0:T(8,128)(2,1)S(1)} collective-permute-done((bf16[376,128]{1,0:T(8,128)(2,1)S(1)}, bf16[376,128]{1,0:T(8,128)(2,1)S(1)}, u32[]{:S(2)}, u32[]{:S(2)}) %collective-permute-start.11) | collective-permute-done | bytes 96288 | tf_op jit(solution)/shard_map/ppermute | solution.py:403
  29.8 6.1 %collective-permute-done.10.refs_2_ = bf16[376,128]{1,0:T(8,128)(2,1)S(1)} collective-permute-done((bf16[376,128]{1,0:T(8,128)(2,1)S(1)}, bf16[376,128]{1,0:T(8,128)(2,1)S(1)}, u32[]{:S(2)}, u32[]{:S(2)}) %collective-permute-start.10) | collective-permute-done | bytes 96288 | tf_op jit(solution)/shard_map/ppermute | solution.py:403
  35.9 0.0 collective-permute-done.9.refs_1_
  35.9 0.7 %shard_map.80 = (bf16[4,1,48,384]{3,2,1,0:T(8,128)(2,1)S(1)}, bf16[4,2,48,384]{3,2,1,0:T(8,128)(2,1)S(1)}) custom-call(bf16[376,128]{1,0:T(8,128)(2,1)S(1)} %get-tuple-element.22.refs_0_, bf16[376,128]{1,0:T(8,128)(2,1)S(1)} %collective-permute-done.9.refs_1_, bf16[376,128]{1,0:T(8,128)(2,1)S(1)} %collective-permute-done.10.refs_2_, ...), custom_call_target="tpu_custom_call" | custom-call | flops 3686400 | bytes 1474560 | tf_op jit(solution)/shard_map/pallas_call | solution.py:29
  36.6 0.2 collective-permute-start.12
  36.8 0.0 collective-permute-done.5.refs_4_
  36.8 1.6 %shard_map.77.refs_0_ = bf16[248,128]{1,0:T(8,128)(2,1)S(1)} custom-call(bf16[632,128]{1,0:T(8,128)(2,1)S(1)} %collective-permute-done.1.refs_0_, bf16[632,128]{1,0:T(8,128)(2,1)S(1)} %collective-permute-done.2.refs_1_, bf16[632,128]{1,0:T(8,128)(2,1)S(1)} %collective-permute-done.3.refs_2_.refs_0_, ...), custom_call_target="tpu_custom_call" | custom-call | flops 764411904 | bytes 1843200 | tf_op jit(solution)/shard_map/pallas_call | solution.py:29
  38.4 2.3 %collective-permute-start.8 = (bf16[248,128]{1,0:T(8,128)(2,1)S(1)}, bf16[248,128]{1,0:T(8,128)(2,1)S(1)}, u32[]{:S(2)}, u32[]{:S(2)}) collective-permute-start(bf16[248,128]{1,0:T(8,128)(2,1)S(1)} %shard_map.77.refs_0_), channel_id=1, source_target_pairs={{0,12},{4,8},{8,4},{12,0},{1,13},{5,9},{9,5},{13,1},{2,14},{6,10},... | collective-permute-start | bytes 190472 | tf_op jit(solution)/shard_map/ppermute | solution.py:403
  40.7 0.0 collective-permute-start.7
  40.7 2.2 %collective-permute-start.6 = (bf16[248,128]{1,0:T(8,128)(2,1)S(1)}, bf16[248,128]{1,0:T(8,128)(2,1)S(1)}, u32[]{:S(2)}, u32[]{:S(2)}) collective-permute-start(bf16[248,128]{1,0:T(8,128)(2,1)S(1)} %shard_map.77.refs_0_), channel_id=1, source_target_pairs={{0,4},{4,0},{8,12},{12,8},{1,5},{5,1},{9,13},{13,9},{2,6},{6,2},{1... | collective-permute-start | bytes 190472 | tf_op jit(solution)/shard_map/ppermute | solution.py:403
  42.9 0.0 copy-done
  42.9 1.7 %shard_map.81.refs_4_ = f32[4,3,48,96]{3,2,1,0:T(8,128)S(1)} custom-call(bf16[4,1,48,384]{3,2,1,0:T(8,128)(2,1)S(1)} %get-tuple-element.24.middle_ref, bf16[4,2,48,384]{3,2,1,0:T(8,128)(2,1)S(1)} %get-tuple-element.25.last_ref, bf16[3,864,384]{2,1,0:T(8,128)(2,1)S(1)} %bitcast.6), custom_call_target="tpu_custom_call" | custom-call | flops 637009920 | bytes 921600 | tf_op jit(solution)/shard_map/pallas_call | solution.py:29
  44.6 0.0 collective-permute-done.12.past_ref
  44.6 1.1 %shard_map.82.refs_5_ = f32[4,2,48,96]{3,2,1,0:T(8,128)S(1)} custom-call(bf16[4,2,48,384]{3,2,1,0:T(8,128)(2,1)S(1)} %collective-permute-done.12.past_ref, bf16[3,864,384]{2,1,0:T(8,128)(2,1)S(1)} %bitcast.7), custom_call_target="tpu_custom_call" | custom-call | flops 382205952 | bytes 921600 | tf_op jit(solution)/shard_map/pallas_call | solution.py:29
  45.7 0.0 copy-start.1
  45.7 0.0 collective-permute-done.8.refs_3_
  45.7 1.7 %collective-permute-done.7.refs_2_ = bf16[248,128]{1,0:T(8,128)(2,1)S(1)} collective-permute-done((bf16[248,128]{1,0:T(8,128)(2,1)S(1)}, bf16[248,128]{1,0:T(8,128)(2,1)S(1)}, u32[]{:S(2)}, u32[]{:S(2)}) %collective-permute-start.7) | collective-permute-done | bytes 63520 | tf_op jit(solution)/shard_map/ppermute | solution.py:403
  47.4 0.0 collective-permute-done.6.refs_1_
  47.4 2.2 %shard_map.83 = (bf16[56,384]{1,0:T(8,128)(2,1)S(1)}, bf16[56,384]{1,0:T(8,128)(2,1)S(1)}, bf16[56,384]{1,0:T(8,128)(2,1)S(1)}, bf16[56,384]{1,0:T(8,128)(2,1)S(1)}) custom-call(bf16[248,128]{1,0:T(8,128)(2,1)S(1)} %shard_map.77.refs_0_, bf16[248,128]{1,0:T(8,128)(2,1)S(1)} %collective-permute-done.6.refs_1_, ...), custom_call_target="tpu_custom_call" | custom-call | flops 955514880 | bytes 1843200 | tf_op jit(solution)/shard_map/pallas_call | solution.py:29
  49.6 0.0 collective-permute-start.13
  49.6 0.2 collective-permute-start.14
  49.8 3.4 %collective-permute-start.15 = (bf16[56,384]{1,0:T(8,128)(2,1)S(1)}, bf16[56,384]{1,0:T(8,128)(2,1)S(1)}, u32[]{:S(2)}, u32[]{:S(2)}) collective-permute-start(bf16[56,384]{1,0:T(8,128)(2,1)S(1)} %get-tuple-element.29), channel_id=1, source_target_pairs={{0,10},{1,8},{2,11},{3,9},{4,14},{5,12},{6,15},{7,13},{8,2},{9,0},... | collective-permute-start | bytes 129032 | tf_op jit(solution)/shard_map/ppermute | solution.py:388
  53.2 1.5 %collective-permute-start.16 = (bf16[56,384]{1,0:T(8,128)(2,1)S(1)}, bf16[56,384]{1,0:T(8,128)(2,1)S(1)}, u32[]{:S(2)}, u32[]{:S(2)}) collective-permute-start(bf16[56,384]{1,0:T(8,128)(2,1)S(1)} %get-tuple-element.30), channel_id=1, source_target_pairs={{0,14},{1,12},{2,15},{3,13},{4,10},{5,8},{6,11},{7,9},{8,6},{9,4},... | collective-permute-start | bytes 129032 | tf_op jit(solution)/shard_map/ppermute | solution.py:388
  54.7 0.0 collective-permute-done.13.refs_0_
  54.7 0.0 collective-permute-done.14.refs_1_
  54.7 0.2 collective-permute-done.15.refs_2_
  54.9 3.6 %collective-permute-done.16.refs_3_ = bf16[56,384]{1,0:T(8,128)(2,1)S(1)} collective-permute-done((bf16[56,384]{1,0:T(8,128)(2,1)S(1)}, bf16[56,384]{1,0:T(8,128)(2,1)S(1)}, u32[]{:S(2)}, u32[]{:S(2)}) %collective-permute-start.16) | collective-permute-done | bytes 43040 | tf_op jit(solution)/shard_map/ppermute | solution.py:388
  58.5 1.0 %shard_map.84 = bf16[5,40,384]{2,1,0:T(8,128)(2,1)} custom-call(bf16[5,40,384]{2,1,0:T(8,128)(2,1)S(1)} %bitcast.11, bf16[56,384]{1,0:T(8,128)(2,1)S(1)} %collective-permute-done.13.refs_0_, bf16[56,384]{1,0:T(8,128)(2,1)S(1)} %collective-permute-done.14.refs_1_, bf16[56,384]{1,0:T(8,128)(2,1)S(1)} %collective-permute-done.15.refs_2_, ...), custom_call_target="tpu_custom_call" | custom-call | flops 184320 | bytes 552960 | tf_op jit(solution)/shard_map/pallas_call | solution.py:29
  (2 shorter events, 0.0 us)
Async XLA Ops:
  0.0 1.7 %collective-permute-start = (bf16[5,40,384]{2,1,0:T(8,128)(2,1)}, bf16[5,40,384]{2,1,0:T(8,128)(2,1)S(1)}, u32[]{:S(2)}, u32[]{:S(2)}) collective-permute-start(bf16[5,40,384]{2,1,0:T(8,128)(2,1)} %bitcast.9), channel_id=1, source_target_pairs={{0,1},{1,0},{2,3},{3,2},{4,5},{5,4},{6,7},{7,6},{8,9},{9,8},{10,11... | collective-permute-start | bytes 460808 | tf_op jit(solution)/shard_map/ppermute | solution.py:412
  1.8 10.0 %collective-permute-start.4 = (bf16[632,128]{1,0:T(8,128)(2,1)S(1)}, bf16[632,128]{1,0:T(8,128)(2,1)S(1)}, u32[]{:S(2)}, u32[]{:S(2)}) collective-permute-start(bf16[632,128]{1,0:T(8,128)(2,1)S(1)} %shard_map.74), channel_id=1, source_target_pairs={{0,9},{1,7},{2,4},{3,10},{4,13},{5,3},{6,0},{7,14},{8,1},{9,15},{1... | collective-permute-start | bytes 485384 | tf_op jit(solution)/shard_map/ppermute | solution.py:388
  5.6 14.5 %collective-permute-start.3 = (bf16[632,128]{1,0:T(8,128)(2,1)S(1)}, bf16[632,128]{1,0:T(8,128)(2,1)S(1)}, u32[]{:S(2)}, u32[]{:S(2)}) collective-permute-start(bf16[632,128]{1,0:T(8,128)(2,1)S(1)} %shard_map.74), channel_id=1, source_target_pairs={{0,5},{1,11},{2,8},{3,6},{4,1},{5,15},{6,12},{7,2},{8,13},{9,3},{1... | collective-permute-start | bytes 485384 | tf_op jit(solution)/shard_map/ppermute | solution.py:388
  5.7 14.4 %collective-permute-start.2 = (bf16[632,128]{1,0:T(8,128)(2,1)S(1)}, bf16[632,128]{1,0:T(8,128)(2,1)S(1)}, u32[]{:S(2)}, u32[]{:S(2)}) collective-permute-start(bf16[632,128]{1,0:T(8,128)(2,1)S(1)} %shard_map.74), channel_id=1, source_target_pairs={{0,1},{1,3},{2,0},{3,2},{4,5},{5,7},{6,4},{7,6},{8,9},{9,11},{10,8... | collective-permute-start | bytes 485384 | tf_op jit(solution)/shard_map/ppermute | solution.py:388
  6.9 13.2 %collective-permute-start.1 = (bf16[632,128]{1,0:T(8,128)(2,1)S(1)}, bf16[632,128]{1,0:T(8,128)(2,1)S(1)}, u32[]{:S(2)}, u32[]{:S(2)}) collective-permute-start(bf16[632,128]{1,0:T(8,128)(2,1)S(1)} %shard_map.74), channel_id=1, source_target_pairs={{0,13},{1,15},{2,12},{3,14},{4,9},{5,11},{6,8},{7,10},{8,5},{9,7},... | collective-permute-start | bytes 485384 | tf_op jit(solution)/shard_map/ppermute | solution.py:388
  20.1 16.7 %collective-permute-start.5 = (bf16[4,272,128]{2,1,0:T(8,128)(2,1)S(1)}, bf16[4,272,128]{2,1,0:T(8,128)(2,1)S(1)}, u32[]{:S(2)}, u32[]{:S(2)}) collective-permute-start(bf16[4,272,128]{2,1,0:T(8,128)(2,1)S(1)} %shard_map.75), channel_id=1, source_target_pairs={{0,1},{1,0},{2,3},{3,2},{4,5},{5,4},{6,7},{7,6},{8,9},{9,8},{10,11... | collective-permute-start | bytes 835592 | tf_op jit(solution)/shard_map/ppermute | solution.py:388
  22.7 20.2 %copy-start = (bf16[27,96,384]{2,1,0:T(8,128)(2,1)S(1)}, bf16[27,96,384]{2,1,0:T(8,128)(2,1)}, u32[]{:S(2)}) copy-start(bf16[27,96,384]{2,1,0:T(8,128)(2,1)} %param.12) | copy-start | bytes 5971972
  22.7 7.1 %collective-permute-start.11 = (bf16[376,128]{1,0:T(8,128)(2,1)S(1)}, bf16[376,128]{1,0:T(8,128)(2,1)S(1)}, u32[]{:S(2)}, u32[]{:S(2)}) collective-permute-start(bf16[376,128]{1,0:T(8,128)(2,1)S(1)} %get-tuple-element.22.refs_0_), channel_id=1, source_target_pairs={{0,12},{4,8},{8,4},{12,0},{1,13},{5,9},{9,5},{13,1},{2,14},{6,10},... | collective-permute-start | bytes 288776 | tf_op jit(solution)/shard_map/ppermute | solution.py:403
  25.0 10.9 %collective-permute-start.10 = (bf16[376,128]{1,0:T(8,128)(2,1)S(1)}, bf16[376,128]{1,0:T(8,128)(2,1)S(1)}, u32[]{:S(2)}, u32[]{:S(2)}) collective-permute-start(bf16[376,128]{1,0:T(8,128)(2,1)S(1)} %get-tuple-element.22.refs_0_), channel_id=1, source_target_pairs={{0,8},{4,12},{8,0},{12,4},{1,9},{5,13},{9,1},{13,5},{2,10},{6,14},... | collective-permute-start | bytes 288776 | tf_op jit(solution)/shard_map/ppermute | solution.py:403
  27.3 8.6 %collective-permute-start.9 = (bf16[376,128]{1,0:T(8,128)(2,1)S(1)}, bf16[376,128]{1,0:T(8,128)(2,1)S(1)}, u32[]{:S(2)}, u32[]{:S(2)}) collective-permute-start(bf16[376,128]{1,0:T(8,128)(2,1)S(1)} %get-tuple-element.22.refs_0_), channel_id=1, source_target_pairs={{0,4},{4,0},{8,12},{12,8},{1,5},{5,1},{9,13},{13,9},{2,6},{6,2},{1... | collective-permute-start | bytes 288776 | tf_op jit(solution)/shard_map/ppermute | solution.py:403
  36.6 8.0 %collective-permute-start.12 = (bf16[4,2,48,384]{3,2,1,0:T(8,128)(2,1)S(1)}, bf16[4,2,48,384]{3,2,1,0:T(8,128)(2,1)S(1)}, u32[]{:S(2)}, u32[]{:S(2)}) collective-permute-start(bf16[4,2,48,384]{3,2,1,0:T(8,128)(2,1)S(1)} %get-tuple-element.25.last_ref), channel_id=1, source_target_pairs={{0,1},{1,0},{2,3},{3,2},{4,5},{5,4},{6,7},{7,6},{8,9},{9,8},{10,11... | collective-permute-start | bytes 884744 | tf_op jit(solution)/shard_map/ppermute | solution.py:388
  38.4 7.2 %collective-permute-start.8 = (bf16[248,128]{1,0:T(8,128)(2,1)S(1)}, bf16[248,128]{1,0:T(8,128)(2,1)S(1)}, u32[]{:S(2)}, u32[]{:S(2)}) collective-permute-start(bf16[248,128]{1,0:T(8,128)(2,1)S(1)} %shard_map.77.refs_0_), channel_id=1, source_target_pairs={{0,12},{4,8},{8,4},{12,0},{1,13},{5,9},{9,5},{13,1},{2,14},{6,10},... | collective-permute-start | bytes 190472 | tf_op jit(solution)/shard_map/ppermute | solution.py:403
  40.7 6.7 %collective-permute-start.7 = (bf16[248,128]{1,0:T(8,128)(2,1)S(1)}, bf16[248,128]{1,0:T(8,128)(2,1)S(1)}, u32[]{:S(2)}, u32[]{:S(2)}) collective-permute-start(bf16[248,128]{1,0:T(8,128)(2,1)S(1)} %shard_map.77.refs_0_), channel_id=1, source_target_pairs={{0,8},{4,12},{8,0},{12,4},{1,9},{5,13},{9,1},{13,5},{2,10},{6,14},... | collective-permute-start | bytes 190472 | tf_op jit(solution)/shard_map/ppermute | solution.py:403
  40.7 6.7 %collective-permute-start.6 = (bf16[248,128]{1,0:T(8,128)(2,1)S(1)}, bf16[248,128]{1,0:T(8,128)(2,1)S(1)}, u32[]{:S(2)}, u32[]{:S(2)}) collective-permute-start(bf16[248,128]{1,0:T(8,128)(2,1)S(1)} %shard_map.77.refs_0_), channel_id=1, source_target_pairs={{0,4},{4,0},{8,12},{12,8},{1,5},{5,1},{9,13},{13,9},{2,6},{6,2},{1... | collective-permute-start | bytes 190472 | tf_op jit(solution)/shard_map/ppermute | solution.py:403
  45.7 12.8 %copy-start.1 = (bf16[5,1,40,384]{3,2,1,0:T(8,128)(2,1)S(1)}, bf16[5,1,40,384]{3,2,1,0:T(8,128)(2,1)}, u32[]{:S(2)}) copy-start(bf16[5,1,40,384]{3,2,1,0:T(8,128)(2,1)} %param.7) | copy-start | bytes 460804
  49.6 5.1 %collective-permute-start.13 = (bf16[56,384]{1,0:T(8,128)(2,1)S(1)}, bf16[56,384]{1,0:T(8,128)(2,1)S(1)}, u32[]{:S(2)}, u32[]{:S(2)}) collective-permute-start(bf16[56,384]{1,0:T(8,128)(2,1)S(1)} %get-tuple-element.27), channel_id=1, source_target_pairs={{0,2},{1,0},{2,3},{3,1},{4,6},{5,4},{6,7},{7,5},{8,10},{9,8},{10,1... | collective-permute-start | bytes 129032 | tf_op jit(solution)/shard_map/ppermute | solution.py:388
  49.6 5.1 %collective-permute-start.14 = (bf16[56,384]{1,0:T(8,128)(2,1)S(1)}, bf16[56,384]{1,0:T(8,128)(2,1)S(1)}, u32[]{:S(2)}, u32[]{:S(2)}) collective-permute-start(bf16[56,384]{1,0:T(8,128)(2,1)S(1)} %get-tuple-element.28), channel_id=1, source_target_pairs={{0,6},{1,4},{2,7},{3,5},{4,2},{5,0},{6,3},{7,1},{8,14},{9,12},{10,... | collective-permute-start | bytes 129032 | tf_op jit(solution)/shard_map/ppermute | solution.py:388
  49.8 5.1 %collective-permute-start.15 = (bf16[56,384]{1,0:T(8,128)(2,1)S(1)}, bf16[56,384]{1,0:T(8,128)(2,1)S(1)}, u32[]{:S(2)}, u32[]{:S(2)}) collective-permute-start(bf16[56,384]{1,0:T(8,128)(2,1)S(1)} %get-tuple-element.29), channel_id=1, source_target_pairs={{0,10},{1,8},{2,11},{3,9},{4,14},{5,12},{6,15},{7,13},{8,2},{9,0},... | collective-permute-start | bytes 129032 | tf_op jit(solution)/shard_map/ppermute | solution.py:388
  53.2 5.2 %collective-permute-start.16 = (bf16[56,384]{1,0:T(8,128)(2,1)S(1)}, bf16[56,384]{1,0:T(8,128)(2,1)S(1)}, u32[]{:S(2)}, u32[]{:S(2)}) collective-permute-start(bf16[56,384]{1,0:T(8,128)(2,1)S(1)} %get-tuple-element.30), channel_id=1, source_target_pairs={{0,14},{1,12},{2,15},{3,13},{4,10},{5,8},{6,11},{7,9},{8,6},{9,4},... | collective-permute-start | bytes 129032 | tf_op jit(solution)/shard_map/ppermute | solution.py:388

commit v9 on v8

--- a/solution.py
+++ b/solution.py
@@ -266,10 +266,12 @@
     height, channels = len(pieces), held.shape[2]
     width = channels // height
     count = frames * breadth
-    for k, piece in enumerate(pieces):
+    first = lax.axis_index("cols") == 0
+    sources = [row] + [row ^ jnp.where(first, a, b) for a, b in zip(*send_orders(height))]
+    for source, piece in zip(sources, pieces):
         center, ends = unpack(piece[...].astype(jnp.float32), count, frames, channels)
-        held[row ^ k, 0:count] = center
-        held[row ^ k, count : count + frames] = ends
+        held[source, 0:count] = center
+        held[source, count : count + frames] = ends
     gain_values = gain_ref[...].reshape(1, channels)
     for h in range(height):
         joined = [held[s, :, h * width : (h + 1) * width] for s in range(height)]
@@ -399,8 +401,9 @@
 
     def spread(values):
         parts = [values]
-        for k in range(1, rows):
-            parts.append(lax.ppermute(values, "rows", [(z, z ^ k) for z in range(rows)]))
+        for steps in zip(*send_orders(rows)):
+            pairs = [(z * cols + c, (z ^ steps[c]) * cols + c) for z in range(rows) for c in range(cols)]
+            parts.append(lax.ppermute(values, ("rows", "cols"), pairs))
         return parts
 
     def turn(values, way):
@@ -486,6 +489,10 @@
 
 def band_order(rows, crosses):
     return [*range(rows - 1, 2, -1), 0] + ([2, 1] if crosses else [1, 2])
+
+
+def send_orders(rows):
+    return [*range(rows - 1, 0, -1)], [1, *range(rows - 1, 1, -1)]
 
 
 def solution(mesh):

time: 59.6 us -> 58.9 us (0.988)
  waiting for transfers between devices: 22 us -> 20 us
  starting transfers between devices: 23.7 us -> 25.1 us
    ppermute x6, starting transfers between devices: 9.58 us -> 11 us  [spread(): parts.append(lax.ppermute(values, ('rows', 'cols'), pairs))]
    ppermute x6, waiting for transfers between devices: 9.78 us -> 8.42 us  [spread(): parts.append(lax.ppermute(values, ('rows', 'cols'), pairs))]
    ppermute x10, waiting for transfers between devices: 12.1 us -> 11.4 us  [moved(): lax.ppermute(values, AXES, [(place[device], place[target(*device)]) for d...]
  transfers between devices with their start and end apart: 17 -> 17, of which waited for: 7 -> 7; matrix products, arithmetic and copies ran while one was open for 0% -> 0% of each run, Pallas kernels for 17% -> 18%
where the time goes in v9:
time: 58.9 us; the launch traced here: 58.8 us
  starting transfers between devices  25.1 us (43%)
  waiting for transfers between devices  20 us (34%)
  Pallas kernels  13.6 us (23%)
    ppermute x10, starting transfers between devices, moved(): lax.ppermute(values, AXES, [(place[device], place[target(*device)]) for d...  13.6 us
    pallas_call x12, Pallas kernels, call(): pl.pallas_call(body, out_shape=out_shape, in_specs=[pl.BlockSpec(memory_s...  13.6 us
    ppermute x10, waiting for transfers between devices, moved(): lax.ppermute(values, AXES, [(place[device], place[target(*device)]) for d...  11.4 us
    ppermute x6, starting transfers between devices, spread(): parts.append(lax.ppermute(values, ('rows', 'cols'), pairs))  11 us
    ppermute x6, waiting for transfers between devices, spread(): parts.append(lax.ppermute(values, ('rows', 'cols'), pairs))  8.42 us
  transfers between devices with their start and end apart: 17, of which 7 were waited for; matrix products, arithmetic and copies ran while one was open for 0% of the time, Pallas kernels for 18%

profile of v9, /device:TPU:0, one launch (start us, length us, event | category | flops | bytes accessed | tf_op | source)
XLA Modules:
  0.0 58.8 jit_solution(5045678948955078752)
XLA Ops:
  0.0 0.5 collective-permute-start
  0.5 1.1 %shard_map.73 = (bf16[600,128]{1,0:T(8,128)(2,1)S(1)}, f32[384]{0:T(512)S(1)}) custom-call(bf16[5,40,384]{2,1,0:T(8,128)(2,1)} %bitcast.10, f32[384]{0:T(512)} %far_gain_ref.1), custom_call_target="tpu_custom_call" | custom-call | flops 921600 | bytes 552960 | tf_op jit(solution)/shard_map/pallas_call | solution.py:29
  1.6 0.1 collective-permute-done.other_ref
  1.7 0.1 shard_map.74
  1.8 3.7 %collective-permute-start.4 = (bf16[632,128]{1,0:T(8,128)(2,1)S(1)}, bf16[632,128]{1,0:T(8,128)(2,1)S(1)}, u32[]{:S(2)}, u32[]{:S(2)}) collective-permute-start(bf16[632,128]{1,0:T(8,128)(2,1)S(1)} %shard_map.74), channel_id=1, source_target_pairs={{0,9},{1,7},{2,4},{3,10},{4,13},{5,3},{6,0},{7,14},{8,1},{9,15},{1... | collective-permute-start | bytes 485384 | tf_op jit(solution)/shard_map/ppermute | solution.py:390
  5.6 0.1 collective-permute-start.3
  5.7 1.3 %collective-permute-start.2 = (bf16[632,128]{1,0:T(8,128)(2,1)S(1)}, bf16[632,128]{1,0:T(8,128)(2,1)S(1)}, u32[]{:S(2)}, u32[]{:S(2)}) collective-permute-start(bf16[632,128]{1,0:T(8,128)(2,1)S(1)} %shard_map.74), channel_id=1, source_target_pairs={{0,1},{1,3},{2,0},{3,2},{4,5},{5,7},{6,4},{7,6},{8,9},{9,11},{10,8... | collective-permute-start | bytes 485384 | tf_op jit(solution)/shard_map/ppermute | solution.py:390
  6.9 3.2 %collective-permute-start.1 = (bf16[632,128]{1,0:T(8,128)(2,1)S(1)}, bf16[632,128]{1,0:T(8,128)(2,1)S(1)}, u32[]{:S(2)}, u32[]{:S(2)}) collective-permute-start(bf16[632,128]{1,0:T(8,128)(2,1)S(1)} %shard_map.74), channel_id=1, source_target_pairs={{0,13},{1,15},{2,12},{3,14},{4,9},{5,11},{6,8},{7,10},{8,5},{9,7},... | collective-permute-start | bytes 485384 | tf_op jit(solution)/shard_map/ppermute | solution.py:390
  10.2 1.6 %shard_map.76 = (f32[384]{0:T(512)S(1)}, f32[384]{0:T(512)S(1)}, f32[384]{0:T(512)S(1)}, bf16[3,864,384]{2,1,0:T(8,128)(2,1)S(1)}) custom-call(f32[384]{0:T(512)} %refs_0_.1, f32[384]{0:T(512)} %refs_1_.1, f32[384]{0:T(512)} %refs_2_.1, bf16[3,864,384]{2,1,0:T(8,128)(2,1)} %bitcast.12), custom_call_target="tpu_custom_call" | custom-call | flops 92160 | bytes 368640 | tf_op jit(solution)/shard_map/pallas_call | solution.py:29
  11.8 0.0 collective-permute-done.4.refs_3_.refs_1_
  11.8 8.3 %collective-permute-done.3.refs_2_.refs_0_ = bf16[632,128]{1,0:T(8,128)(2,1)S(1)} collective-permute-done((bf16[632,128]{1,0:T(8,128)(2,1)S(1)}, bf16[632,128]{1,0:T(8,128)(2,1)S(1)}, u32[]{:S(2)}, u32[]{:S(2)}) %collective-permute-start.3) | collective-permute-done | bytes 161824 | tf_op jit(solution)/shard_map/ppermute | solution.py:390
  20.1 0.0 collective-permute-done.2.refs_1_
  20.1 0.0 collective-permute-done.1.refs_0_
  20.1 0.1 collective-permute-start.5
  20.2 1.2 %shard_map.78.refs_2_ = f32[6,3,48,96]{3,2,1,0:T(8,128)S(1)} custom-call(bf16[632,128]{1,0:T(8,128)(2,1)S(1)} %collective-permute-done.1.refs_0_, bf16[632,128]{1,0:T(8,128)(2,1)S(1)} %collective-permute-done.2.refs_1_, bf16[3,864,384]{2,1,0:T(8,128)(2,1)S(1)} %get-tuple-element.20.refs_5_.refs_2_.refs_3_), custom_call_target="tpu_custom_call" | custom-call | flops 573308928 | bytes 921600 | tf_op jit(solution)/shard_map/pallas_call | solution.py:29
  21.4 1.3 %shard_map.79 = (bf16[376,128]{1,0:T(8,128)(2,1)S(1)}, f32[6,3,48,96]{3,2,1,0:T(8,128)S(1)}) custom-call(bf16[632,128]{1,0:T(8,128)(2,1)S(1)} %collective-permute-done.3.refs_2_.refs_0_, bf16[632,128]{1,0:T(8,128)(2,1)S(1)} %collective-permute-done.4.refs_3_.refs_1_, f32[6,3,48,96]{3,2,1,0:T(8,128)S(1)} %shard_map.78.refs_2_, ...), custom_call_target="tpu_custom_call", output_to_operand_aliasing={{1}: (2, {})} | custom-call | flops 573308928 | bytes 921600 | tf_op jit(solution)/shard_map/pallas_call | solution.py:29
  22.7 0.0 copy-start
  22.7 2.5 %collective-permute-start.11 = (bf16[376,128]{1,0:T(8,128)(2,1)S(1)}, bf16[376,128]{1,0:T(8,128)(2,1)S(1)}, u32[]{:S(2)}, u32[]{:S(2)}) collective-permute-start(bf16[376,128]{1,0:T(8,128)(2,1)S(1)} %get-tuple-element.22.refs_0_), channel_id=1, source_target_pairs={{0,4},{1,9},{4,0},{5,13},{8,12},{9,1},{12,8},{13,5},{2,6},{3,11},{... | collective-permute-start | bytes 288776 | tf_op jit(solution)/shard_map/ppermute | solution.py:406
  25.2 2.1 %collective-permute-start.10 = (bf16[376,128]{1,0:T(8,128)(2,1)S(1)}, bf16[376,128]{1,0:T(8,128)(2,1)S(1)}, u32[]{:S(2)}, u32[]{:S(2)}) collective-permute-start(bf16[376,128]{1,0:T(8,128)(2,1)S(1)} %get-tuple-element.22.refs_0_), channel_id=1, source_target_pairs={{0,8},{1,13},{4,12},{5,9},{8,0},{9,5},{12,4},{13,1},{2,10},{3,15},... | collective-permute-start | bytes 288776 | tf_op jit(solution)/shard_map/ppermute | solution.py:406
  27.3 1.4 %collective-permute-start.9 = (bf16[376,128]{1,0:T(8,128)(2,1)S(1)}, bf16[376,128]{1,0:T(8,128)(2,1)S(1)}, u32[]{:S(2)}, u32[]{:S(2)}) collective-permute-start(bf16[376,128]{1,0:T(8,128)(2,1)S(1)} %get-tuple-element.22.refs_0_), channel_id=1, source_target_pairs={{0,12},{1,5},{4,8},{5,1},{8,4},{9,13},{12,0},{13,9},{2,14},{3,7},{... | collective-permute-start | bytes 288776 | tf_op jit(solution)/shard_map/ppermute | solution.py:406
  28.7 0.0 collective-permute-done.11.refs_3_
  28.7 6.2 %collective-permute-done.10.refs_2_ = bf16[376,128]{1,0:T(8,128)(2,1)S(1)} collective-permute-done((bf16[376,128]{1,0:T(8,128)(2,1)S(1)}, bf16[376,128]{1,0:T(8,128)(2,1)S(1)}, u32[]{:S(2)}, u32[]{:S(2)}) %collective-permute-start.10) | collective-permute-done | bytes 96288 | tf_op jit(solution)/shard_map/ppermute | solution.py:406
  34.9 0.0 collective-permute-done.9.refs_1_
  34.9 0.7 %shard_map.80 = (bf16[4,1,48,384]{3,2,1,0:T(8,128)(2,1)S(1)}, bf16[4,2,48,384]{3,2,1,0:T(8,128)(2,1)S(1)}) custom-call(bf16[376,128]{1,0:T(8,128)(2,1)S(1)} %get-tuple-element.22.refs_0_, bf16[376,128]{1,0:T(8,128)(2,1)S(1)} %collective-permute-done.9.refs_1_, bf16[376,128]{1,0:T(8,128)(2,1)S(1)} %collective-permute-done.10.refs_2_, ...), custom_call_target="tpu_custom_call" | custom-call | flops 3686400 | bytes 1474560 | tf_op jit(solution)/shard_map/pallas_call | solution.py:29
  35.7 0.1 collective-permute-start.12
  35.7 0.0 collective-permute-done.5.refs_4_
  35.8 1.6 %shard_map.77.refs_0_ = bf16[248,128]{1,0:T(8,128)(2,1)S(1)} custom-call(bf16[632,128]{1,0:T(8,128)(2,1)S(1)} %collective-permute-done.1.refs_0_, bf16[632,128]{1,0:T(8,128)(2,1)S(1)} %collective-permute-done.2.refs_1_, bf16[632,128]{1,0:T(8,128)(2,1)S(1)} %collective-permute-done.3.refs_2_.refs_0_, ...), custom_call_target="tpu_custom_call" | custom-call | flops 764411904 | bytes 1843200 | tf_op jit(solution)/shard_map/pallas_call | solution.py:29
  37.4 2.5 %collective-permute-start.8 = (bf16[248,128]{1,0:T(8,128)(2,1)S(1)}, bf16[248,128]{1,0:T(8,128)(2,1)S(1)}, u32[]{:S(2)}, u32[]{:S(2)}) collective-permute-start(bf16[248,128]{1,0:T(8,128)(2,1)S(1)} %shard_map.77.refs_0_), channel_id=1, source_target_pairs={{0,4},{1,9},{4,0},{5,13},{8,12},{9,1},{12,8},{13,5},{2,6},{3,11},{... | collective-permute-start | bytes 190472 | tf_op jit(solution)/shard_map/ppermute | solution.py:406
  39.9 0.8 %collective-permute-start.7 = (bf16[248,128]{1,0:T(8,128)(2,1)S(1)}, bf16[248,128]{1,0:T(8,128)(2,1)S(1)}, u32[]{:S(2)}, u32[]{:S(2)}) collective-permute-start(bf16[248,128]{1,0:T(8,128)(2,1)S(1)} %shard_map.77.refs_0_), channel_id=1, source_target_pairs={{0,8},{1,13},{4,12},{5,9},{8,0},{9,5},{12,4},{13,1},{2,10},{3,15},... | collective-permute-start | bytes 190472 | tf_op jit(solution)/shard_map/ppermute | solution.py:406
  40.7 1.6 %collective-permute-start.6 = (bf16[248,128]{1,0:T(8,128)(2,1)S(1)}, bf16[248,128]{1,0:T(8,128)(2,1)S(1)}, u32[]{:S(2)}, u32[]{:S(2)}) collective-permute-start(bf16[248,128]{1,0:T(8,128)(2,1)S(1)} %shard_map.77.refs_0_), channel_id=1, source_target_pairs={{0,12},{1,5},{4,8},{5,1},{8,4},{9,13},{12,0},{13,9},{2,14},{3,7},{... | collective-permute-start | bytes 190472 | tf_op jit(solution)/shard_map/ppermute | solution.py:406
  42.4 0.0 copy-done
  42.4 1.7 %shard_map.81.refs_4_ = f32[4,3,48,96]{3,2,1,0:T(8,128)S(1)} custom-call(bf16[4,1,48,384]{3,2,1,0:T(8,128)(2,1)S(1)} %get-tuple-element.24.middle_ref, bf16[4,2,48,384]{3,2,1,0:T(8,128)(2,1)S(1)} %get-tuple-element.25.last_ref, bf16[3,864,384]{2,1,0:T(8,128)(2,1)S(1)} %bitcast.6), custom_call_target="tpu_custom_call" | custom-call | flops 637009920 | bytes 921600 | tf_op jit(solution)/shard_map/pallas_call | solution.py:29
  44.1 0.0 collective-permute-done.12.past_ref
  44.1 1.1 %shard_map.82.refs_5_ = f32[4,2,48,96]{3,2,1,0:T(8,128)S(1)} custom-call(bf16[4,2,48,384]{3,2,1,0:T(8,128)(2,1)S(1)} %collective-permute-done.12.past_ref, bf16[3,864,384]{2,1,0:T(8,128)(2,1)S(1)} %bitcast.7), custom_call_target="tpu_custom_call" | custom-call | flops 382205952 | bytes 921600 | tf_op jit(solution)/shard_map/pallas_call | solution.py:29
  45.2 0.0 copy-start.1
  45.2 0.0 collective-permute-done.8.refs_3_
  45.2 2.1 %collective-permute-done.7.refs_2_ = bf16[248,128]{1,0:T(8,128)(2,1)S(1)} collective-permute-done((bf16[248,128]{1,0:T(8,128)(2,1)S(1)}, bf16[248,128]{1,0:T(8,128)(2,1)S(1)}, u32[]{:S(2)}, u32[]{:S(2)}) %collective-permute-start.7) | collective-permute-done | bytes 63520 | tf_op jit(solution)/shard_map/ppermute | solution.py:406
  47.2 0.1 collective-permute-done.6.refs_1_
  47.4 2.2 %shard_map.83 = (bf16[56,384]{1,0:T(8,128)(2,1)S(1)}, bf16[56,384]{1,0:T(8,128)(2,1)S(1)}, bf16[56,384]{1,0:T(8,128)(2,1)S(1)}, bf16[56,384]{1,0:T(8,128)(2,1)S(1)}) custom-call(bf16[248,128]{1,0:T(8,128)(2,1)S(1)} %shard_map.77.refs_0_, bf16[248,128]{1,0:T(8,128)(2,1)S(1)} %collective-permute-done.6.refs_1_, ...), custom_call_target="tpu_custom_call" | custom-call | flops 955514880 | bytes 1843200 | tf_op jit(solution)/shard_map/pallas_call | solution.py:29
  49.5 0.1 collective-permute-start.13
  49.7 0.8 %collective-permute-start.14 = (bf16[56,384]{1,0:T(8,128)(2,1)S(1)}, bf16[56,384]{1,0:T(8,128)(2,1)S(1)}, u32[]{:S(2)}, u32[]{:S(2)}) collective-permute-start(bf16[56,384]{1,0:T(8,128)(2,1)S(1)} %get-tuple-element.28), channel_id=1, source_target_pairs={{0,6},{1,4},{2,7},{3,5},{4,2},{5,0},{6,3},{7,1},{8,14},{9,12},{10,... | collective-permute-start | bytes 129032 | tf_op jit(solution)/shard_map/ppermute | solution.py:390
  50.4 2.2 %collective-permute-start.15 = (bf16[56,384]{1,0:T(8,128)(2,1)S(1)}, bf16[56,384]{1,0:T(8,128)(2,1)S(1)}, u32[]{:S(2)}, u32[]{:S(2)}) collective-permute-start(bf16[56,384]{1,0:T(8,128)(2,1)S(1)} %get-tuple-element.29), channel_id=1, source_target_pairs={{0,10},{1,8},{2,11},{3,9},{4,14},{5,12},{6,15},{7,13},{8,2},{9,0},... | collective-permute-start | bytes 129032 | tf_op jit(solution)/shard_map/ppermute | solution.py:390
  52.6 2.1 %collective-permute-start.16 = (bf16[56,384]{1,0:T(8,128)(2,1)S(1)}, bf16[56,384]{1,0:T(8,128)(2,1)S(1)}, u32[]{:S(2)}, u32[]{:S(2)}) collective-permute-start(bf16[56,384]{1,0:T(8,128)(2,1)S(1)} %get-tuple-element.30), channel_id=1, source_target_pairs={{0,14},{1,12},{2,15},{3,13},{4,10},{5,8},{6,11},{7,9},{8,6},{9,4},... | collective-permute-start | bytes 129032 | tf_op jit(solution)/shard_map/ppermute | solution.py:390
  54.7 0.0 collective-permute-done.13.refs_0_
  54.7 0.0 collective-permute-done.14.refs_1_
  54.7 0.7 %collective-permute-done.15.refs_2_ = bf16[56,384]{1,0:T(8,128)(2,1)S(1)} collective-permute-done((bf16[56,384]{1,0:T(8,128)(2,1)S(1)}, bf16[56,384]{1,0:T(8,128)(2,1)S(1)}, u32[]{:S(2)}, u32[]{:S(2)}) %collective-permute-start.15) | collective-permute-done | bytes 43040 | tf_op jit(solution)/shard_map/ppermute | solution.py:390
  55.4 2.4 %collective-permute-done.16.refs_3_ = bf16[56,384]{1,0:T(8,128)(2,1)S(1)} collective-permute-done((bf16[56,384]{1,0:T(8,128)(2,1)S(1)}, bf16[56,384]{1,0:T(8,128)(2,1)S(1)}, u32[]{:S(2)}, u32[]{:S(2)}) %collective-permute-start.16) | collective-permute-done | bytes 43040 | tf_op jit(solution)/shard_map/ppermute | solution.py:390
  57.8 1.0 %shard_map.84 = bf16[5,40,384]{2,1,0:T(8,128)(2,1)} custom-call(bf16[5,40,384]{2,1,0:T(8,128)(2,1)S(1)} %bitcast.11, bf16[56,384]{1,0:T(8,128)(2,1)S(1)} %collective-permute-done.13.refs_0_, bf16[56,384]{1,0:T(8,128)(2,1)S(1)} %collective-permute-done.14.refs_1_, bf16[56,384]{1,0:T(8,128)(2,1)S(1)} %collective-permute-done.15.refs_2_, ...), custom_call_target="tpu_custom_call" | custom-call | flops 184320 | bytes 552960 | tf_op jit(solution)/shard_map/pallas_call | solution.py:29
  (2 shorter events, 0.0 us)
Async XLA Ops:
  0.0 1.7 %collective-permute-start = (bf16[5,40,384]{2,1,0:T(8,128)(2,1)}, bf16[5,40,384]{2,1,0:T(8,128)(2,1)S(1)}, u32[]{:S(2)}, u32[]{:S(2)}) collective-permute-start(bf16[5,40,384]{2,1,0:T(8,128)(2,1)} %bitcast.9), channel_id=1, source_target_pairs={{0,1},{1,0},{2,3},{3,2},{4,5},{5,4},{6,7},{7,6},{8,9},{9,8},{10,11... | collective-permute-start | bytes 460808 | tf_op jit(solution)/shard_map/ppermute | solution.py:415
  1.8 10.0 %collective-permute-start.4 = (bf16[632,128]{1,0:T(8,128)(2,1)S(1)}, bf16[632,128]{1,0:T(8,128)(2,1)S(1)}, u32[]{:S(2)}, u32[]{:S(2)}) collective-permute-start(bf16[632,128]{1,0:T(8,128)(2,1)S(1)} %shard_map.74), channel_id=1, source_target_pairs={{0,9},{1,7},{2,4},{3,10},{4,13},{5,3},{6,0},{7,14},{8,1},{9,15},{1... | collective-permute-start | bytes 485384 | tf_op jit(solution)/shard_map/ppermute | solution.py:390
  5.6 14.5 %collective-permute-start.3 = (bf16[632,128]{1,0:T(8,128)(2,1)S(1)}, bf16[632,128]{1,0:T(8,128)(2,1)S(1)}, u32[]{:S(2)}, u32[]{:S(2)}) collective-permute-start(bf16[632,128]{1,0:T(8,128)(2,1)S(1)} %shard_map.74), channel_id=1, source_target_pairs={{0,5},{1,11},{2,8},{3,6},{4,1},{5,15},{6,12},{7,2},{8,13},{9,3},{1... | collective-permute-start | bytes 485384 | tf_op jit(solution)/shard_map/ppermute | solution.py:390
  5.7 14.4 %collective-permute-start.2 = (bf16[632,128]{1,0:T(8,128)(2,1)S(1)}, bf16[632,128]{1,0:T(8,128)(2,1)S(1)}, u32[]{:S(2)}, u32[]{:S(2)}) collective-permute-start(bf16[632,128]{1,0:T(8,128)(2,1)S(1)} %shard_map.74), channel_id=1, source_target_pairs={{0,1},{1,3},{2,0},{3,2},{4,5},{5,7},{6,4},{7,6},{8,9},{9,11},{10,8... | collective-permute-start | bytes 485384 | tf_op jit(solution)/shard_map/ppermute | solution.py:390
  6.9 13.2 %collective-permute-start.1 = (bf16[632,128]{1,0:T(8,128)(2,1)S(1)}, bf16[632,128]{1,0:T(8,128)(2,1)S(1)}, u32[]{:S(2)}, u32[]{:S(2)}) collective-permute-start(bf16[632,128]{1,0:T(8,128)(2,1)S(1)} %shard_map.74), channel_id=1, source_target_pairs={{0,13},{1,15},{2,12},{3,14},{4,9},{5,11},{6,8},{7,10},{8,5},{9,7},... | collective-permute-start | bytes 485384 | tf_op jit(solution)/shard_map/ppermute | solution.py:390
  20.1 15.6 %collective-permute-start.5 = (bf16[4,272,128]{2,1,0:T(8,128)(2,1)S(1)}, bf16[4,272,128]{2,1,0:T(8,128)(2,1)S(1)}, u32[]{:S(2)}, u32[]{:S(2)}) collective-permute-start(bf16[4,272,128]{2,1,0:T(8,128)(2,1)S(1)} %shard_map.75), channel_id=1, source_target_pairs={{0,1},{1,0},{2,3},{3,2},{4,5},{5,4},{6,7},{7,6},{8,9},{9,8},{10,11... | collective-permute-start | bytes 835592 | tf_op jit(solution)/shard_map/ppermute | solution.py:390
  22.7 19.7 %copy-start = (bf16[27,96,384]{2,1,0:T(8,128)(2,1)S(1)}, bf16[27,96,384]{2,1,0:T(8,128)(2,1)}, u32[]{:S(2)}) copy-start(bf16[27,96,384]{2,1,0:T(8,128)(2,1)} %param.12) | copy-start | bytes 5971972
  22.7 6.0 %collective-permute-start.11 = (bf16[376,128]{1,0:T(8,128)(2,1)S(1)}, bf16[376,128]{1,0:T(8,128)(2,1)S(1)}, u32[]{:S(2)}, u32[]{:S(2)}) collective-permute-start(bf16[376,128]{1,0:T(8,128)(2,1)S(1)} %get-tuple-element.22.refs_0_), channel_id=1, source_target_pairs={{0,4},{1,9},{4,0},{5,13},{8,12},{9,1},{12,8},{13,5},{2,6},{3,11},{... | collective-permute-start | bytes 288776 | tf_op jit(solution)/shard_map/ppermute | solution.py:406
  25.2 9.7 %collective-permute-start.10 = (bf16[376,128]{1,0:T(8,128)(2,1)S(1)}, bf16[376,128]{1,0:T(8,128)(2,1)S(1)}, u32[]{:S(2)}, u32[]{:S(2)}) collective-permute-start(bf16[376,128]{1,0:T(8,128)(2,1)S(1)} %get-tuple-element.22.refs_0_), channel_id=1, source_target_pairs={{0,8},{1,13},{4,12},{5,9},{8,0},{9,5},{12,4},{13,1},{2,10},{3,15},... | collective-permute-start | bytes 288776 | tf_op jit(solution)/shard_map/ppermute | solution.py:406
  27.3 7.6 %collective-permute-start.9 = (bf16[376,128]{1,0:T(8,128)(2,1)S(1)}, bf16[376,128]{1,0:T(8,128)(2,1)S(1)}, u32[]{:S(2)}, u32[]{:S(2)}) collective-permute-start(bf16[376,128]{1,0:T(8,128)(2,1)S(1)} %get-tuple-element.22.refs_0_), channel_id=1, source_target_pairs={{0,12},{1,5},{4,8},{5,1},{8,4},{9,13},{12,0},{13,9},{2,14},{3,7},{... | collective-permute-start | bytes 288776 | tf_op jit(solution)/shard_map/ppermute | solution.py:406
  35.7 8.4 %collective-permute-start.12 = (bf16[4,2,48,384]{3,2,1,0:T(8,128)(2,1)S(1)}, bf16[4,2,48,384]{3,2,1,0:T(8,128)(2,1)S(1)}, u32[]{:S(2)}, u32[]{:S(2)}) collective-permute-start(bf16[4,2,48,384]{3,2,1,0:T(8,128)(2,1)S(1)} %get-tuple-element.25.last_ref), channel_id=1, source_target_pairs={{0,1},{1,0},{2,3},{3,2},{4,5},{5,4},{6,7},{7,6},{8,9},{9,8},{10,11... | collective-permute-start | bytes 884744 | tf_op jit(solution)/shard_map/ppermute | solution.py:390
  37.4 7.8 %collective-permute-start.8 = (bf16[248,128]{1,0:T(8,128)(2,1)S(1)}, bf16[248,128]{1,0:T(8,128)(2,1)S(1)}, u32[]{:S(2)}, u32[]{:S(2)}) collective-permute-start(bf16[248,128]{1,0:T(8,128)(2,1)S(1)} %shard_map.77.refs_0_), channel_id=1, source_target_pairs={{0,4},{1,9},{4,0},{5,13},{8,12},{9,1},{12,8},{13,5},{2,6},{3,11},{... | collective-permute-start | bytes 190472 | tf_op jit(solution)/shard_map/ppermute | solution.py:406
  39.9 7.3 %collective-permute-start.7 = (bf16[248,128]{1,0:T(8,128)(2,1)S(1)}, bf16[248,128]{1,0:T(8,128)(2,1)S(1)}, u32[]{:S(2)}, u32[]{:S(2)}) collective-permute-start(bf16[248,128]{1,0:T(8,128)(2,1)S(1)} %shard_map.77.refs_0_), channel_id=1, source_target_pairs={{0,8},{1,13},{4,12},{5,9},{8,0},{9,5},{12,4},{13,1},{2,10},{3,15},... | collective-permute-start | bytes 190472 | tf_op jit(solution)/shard_map/ppermute | solution.py:406
  40.7 6.6 %collective-permute-start.6 = (bf16[248,128]{1,0:T(8,128)(2,1)S(1)}, bf16[248,128]{1,0:T(8,128)(2,1)S(1)}, u32[]{:S(2)}, u32[]{:S(2)}) collective-permute-start(bf16[248,128]{1,0:T(8,128)(2,1)S(1)} %shard_map.77.refs_0_), channel_id=1, source_target_pairs={{0,12},{1,5},{4,8},{5,1},{8,4},{9,13},{12,0},{13,9},{2,14},{3,7},{... | collective-permute-start | bytes 190472 | tf_op jit(solution)/shard_map/ppermute | solution.py:406
  45.2 12.7 %copy-start.1 = (bf16[5,1,40,384]{3,2,1,0:T(8,128)(2,1)S(1)}, bf16[5,1,40,384]{3,2,1,0:T(8,128)(2,1)}, u32[]{:S(2)}) copy-start(bf16[5,1,40,384]{3,2,1,0:T(8,128)(2,1)} %param.7) | copy-start | bytes 460804
  49.5 5.1 %collective-permute-start.13 = (bf16[56,384]{1,0:T(8,128)(2,1)S(1)}, bf16[56,384]{1,0:T(8,128)(2,1)S(1)}, u32[]{:S(2)}, u32[]{:S(2)}) collective-permute-start(bf16[56,384]{1,0:T(8,128)(2,1)S(1)} %get-tuple-element.27), channel_id=1, source_target_pairs={{0,2},{1,0},{2,3},{3,1},{4,6},{5,4},{6,7},{7,5},{8,10},{9,8},{10,1... | collective-permute-start | bytes 129032 | tf_op jit(solution)/shard_map/ppermute | solution.py:390
  49.7 5.0 %collective-permute-start.14 = (bf16[56,384]{1,0:T(8,128)(2,1)S(1)}, bf16[56,384]{1,0:T(8,128)(2,1)S(1)}, u32[]{:S(2)}, u32[]{:S(2)}) collective-permute-start(bf16[56,384]{1,0:T(8,128)(2,1)S(1)} %get-tuple-element.28), channel_id=1, source_target_pairs={{0,6},{1,4},{2,7},{3,5},{4,2},{5,0},{6,3},{7,1},{8,14},{9,12},{10,... | collective-permute-start | bytes 129032 | tf_op jit(solution)/shard_map/ppermute | solution.py:390
  50.4 5.0 %collective-permute-start.15 = (bf16[56,384]{1,0:T(8,128)(2,1)S(1)}, bf16[56,384]{1,0:T(8,128)(2,1)S(1)}, u32[]{:S(2)}, u32[]{:S(2)}) collective-permute-start(bf16[56,384]{1,0:T(8,128)(2,1)S(1)} %get-tuple-element.29), channel_id=1, source_target_pairs={{0,10},{1,8},{2,11},{3,9},{4,14},{5,12},{6,15},{7,13},{8,2},{9,0},... | collective-permute-start | bytes 129032 | tf_op jit(solution)/shard_map/ppermute | solution.py:390
  52.6 5.2 %collective-permute-start.16 = (bf16[56,384]{1,0:T(8,128)(2,1)S(1)}, bf16[56,384]{1,0:T(8,128)(2,1)S(1)}, u32[]{:S(2)}, u32[]{:S(2)}) collective-permute-start(bf16[56,384]{1,0:T(8,128)(2,1)S(1)} %get-tuple-element.30), channel_id=1, source_target_pairs={{0,14},{1,12},{2,15},{3,13},{4,10},{5,8},{6,11},{7,9},{8,6},{9,4},... | collective-permute-start | bytes 129032 | tf_op jit(solution)/shard_map/ppermute | solution.py:390

commit v10 on v9

--- a/solution.py
+++ b/solution.py
@@ -260,14 +260,14 @@
     pack_first(conv_sum(padded, weight_ref, bias_part(bias_ref, row, weight_ref)), out_ref, breadth)
 
 
-def regroup(pieces, gain_ref, held, breadth, frames, store):
+def regroup(pieces, gain_ref, held, breadth, frames, store, name):
     row = lax.axis_index("rows")
     half = lax.axis_index("tm") % 2
     height, channels = len(pieces), held.shape[2]
     width = channels // height
     count = frames * breadth
     first = lax.axis_index("cols") == 0
-    sources = [row] + [row ^ jnp.where(first, a, b) for a, b in zip(*send_orders(height))]
+    sources = [row] + [row ^ jnp.where(first, a, b) for a, b in zip(*send_orders(height, name))]
     for source, piece in zip(sources, pieces):
         center, ends = unpack(piece[...].astype(jnp.float32), count, frames, channels)
         held[source, 0:count] = center
@@ -292,7 +292,7 @@
         else:
             last_ref[h, f - middle] = ring
 
-    regroup(pieces, gain_ref, held, breadth, middle + late, store)
+    regroup(pieces, gain_ref, held, breadth, middle + late, store, "late")
 
 
 def second_late_body(frames, middle_ref, last_ref, weight_ref, total):
@@ -332,7 +332,7 @@
     def store(h, f, ring):
         early[f, h] = ring
 
-    regroup(pieces, gain_ref, held, breadth, PAST, store)
+    regroup(pieces, gain_ref, held, breadth, PAST, store, "early")
     _, frames, ring, _ = late_ref.shape
     frames += PAST
     channels = early.shape[3]
@@ -399,9 +399,9 @@
     def following(values):
         return moved(values, lambda z, x, c: (z, x, 0) if c == 1 else (z, (x + 2) % tm, 1))
 
-    def spread(values):
+    def spread(values, name):
         parts = [values]
-        for steps in zip(*send_orders(rows)):
+        for steps in zip(*send_orders(rows, name)):
             pairs = [(z * cols + c, (z ^ steps[c]) * cols + c) for z in range(rows) for c in range(cols)]
             parts.append(lax.ppermute(values, ("rows", "cols"), pairs))
         return parts
@@ -453,12 +453,12 @@
         [VMEM((frames, LAST, ring, channels), bf16)], late * work * LAST // rows, 10 * size,
         *pieces[-LAST:], near_sums, near, bias_one, aliases={LAST: 1},
     )
-    late_parts = spread(part)
+    late_parts = spread(part, "late")
     part = call(
         functools.partial(first_early_body, breadth, rows, frames), sds((early_sent, LANES), bf16),
         [padded(2 * PAST)], PAST * work, 20 * size, *pieces, past, near, bias_one,
     )
-    early_parts = spread(part)
+    early_parts = spread(part, "early")
     second, last = call(
         functools.partial(regroup_body, breadth),
         [sds((rows, middle, ring, channels), bf16), sds((rows, PAST, ring, channels), bf16)],
@@ -491,8 +491,9 @@
     return [*range(rows - 1, 2, -1), 0] + ([2, 1] if crosses else [1, 2])
 
 
-def send_orders(rows):
-    return [*range(rows - 1, 0, -1)], [1, *range(rows - 1, 1, -1)]
+def send_orders(rows, name):
+    far = list(range(rows - 1, 0, -1))
+    return far, far if name == "late" else far[-1:] + far[:-1]
 
 
 def solution(mesh):

time: 58.9 us -> 60.7 us (1.031)
  waiting for transfers between devices: 20 us -> 21.7 us
    ppermute x6, waiting for transfers between devices: 8.42 us -> 9.7 us  [spread(): parts.append(lax.ppermute(values, ('rows', 'cols'), pairs))]
  transfers between devices with their start and end apart: 17 -> 17, of which waited for: 7 -> 7; matrix products, arithmetic and copies ran while one was open for 0% -> 0% of each run, Pallas kernels for 18% -> 17%
where the time goes in v10:
time: 60.7 us; the launch traced here: 60.5 us
  starting transfers between devices  25.2 us (42%)
  waiting for transfers between devices  21.7 us (36%)
  Pallas kernels  13.6 us (22%)
    ppermute x10, starting transfers between devices, moved(): lax.ppermute(values, AXES, [(place[device], place[target(*device)]) for d...  13.6 us
    pallas_call x12, Pallas kernels, call(): pl.pallas_call(body, out_shape=out_shape, in_specs=[pl.BlockSpec(memory_s...  13.6 us
    ppermute x10, waiting for transfers between devices, moved(): lax.ppermute(values, AXES, [(place[device], place[target(*device)]) for d...  11.8 us
    ppermute x6, starting transfers between devices, spread(): parts.append(lax.ppermute(values, ('rows', 'cols'), pairs))  11.1 us
    ppermute x6, waiting for transfers between devices, spread(): parts.append(lax.ppermute(values, ('rows', 'cols'), pairs))  9.7 us
  transfers between devices with their start and end apart: 17, of which 7 were waited for; matrix products, arithmetic and copies ran while one was open for 0% of the time, Pallas kernels for 17%

profile of v10, /device:TPU:0, one launch (start us, length us, event | category | flops | bytes accessed | tf_op | source)
XLA Modules:
  0.0 60.5 jit_solution(220746564015160715)
XLA Ops:
  0.0 0.5 collective-permute-start
  0.5 1.1 %shard_map.73 = (bf16[600,128]{1,0:T(8,128)(2,1)S(1)}, f32[384]{0:T(512)S(1)}) custom-call(bf16[5,40,384]{2,1,0:T(8,128)(2,1)} %bitcast.10, f32[384]{0:T(512)} %far_gain_ref.1), custom_call_target="tpu_custom_call" | custom-call | flops 921600 | bytes 552960 | tf_op jit(solution)/shard_map/pallas_call | solution.py:29
  1.6 0.1 collective-permute-done.other_ref
  1.7 0.1 shard_map.74
  1.8 3.7 %collective-permute-start.4 = (bf16[632,128]{1,0:T(8,128)(2,1)S(1)}, bf16[632,128]{1,0:T(8,128)(2,1)S(1)}, u32[]{:S(2)}, u32[]{:S(2)}) collective-permute-start(bf16[632,128]{1,0:T(8,128)(2,1)S(1)} %shard_map.74), channel_id=1, source_target_pairs={{0,9},{1,7},{2,4},{3,10},{4,13},{5,3},{6,0},{7,14},{8,1},{9,15},{1... | collective-permute-start | bytes 485384 | tf_op jit(solution)/shard_map/ppermute | solution.py:390
  5.6 0.1 collective-permute-start.3
  5.7 1.3 %collective-permute-start.2 = (bf16[632,128]{1,0:T(8,128)(2,1)S(1)}, bf16[632,128]{1,0:T(8,128)(2,1)S(1)}, u32[]{:S(2)}, u32[]{:S(2)}) collective-permute-start(bf16[632,128]{1,0:T(8,128)(2,1)S(1)} %shard_map.74), channel_id=1, source_target_pairs={{0,1},{1,3},{2,0},{3,2},{4,5},{5,7},{6,4},{7,6},{8,9},{9,11},{10,8... | collective-permute-start | bytes 485384 | tf_op jit(solution)/shard_map/ppermute | solution.py:390
  6.9 3.2 %collective-permute-start.1 = (bf16[632,128]{1,0:T(8,128)(2,1)S(1)}, bf16[632,128]{1,0:T(8,128)(2,1)S(1)}, u32[]{:S(2)}, u32[]{:S(2)}) collective-permute-start(bf16[632,128]{1,0:T(8,128)(2,1)S(1)} %shard_map.74), channel_id=1, source_target_pairs={{0,13},{1,15},{2,12},{3,14},{4,9},{5,11},{6,8},{7,10},{8,5},{9,7},... | collective-permute-start | bytes 485384 | tf_op jit(solution)/shard_map/ppermute | solution.py:390
  10.2 1.6 %shard_map.76 = (f32[384]{0:T(512)S(1)}, f32[384]{0:T(512)S(1)}, f32[384]{0:T(512)S(1)}, bf16[3,864,384]{2,1,0:T(8,128)(2,1)S(1)}) custom-call(f32[384]{0:T(512)} %refs_0_.1, f32[384]{0:T(512)} %refs_1_.1, f32[384]{0:T(512)} %refs_2_.1, bf16[3,864,384]{2,1,0:T(8,128)(2,1)} %bitcast.12), custom_call_target="tpu_custom_call" | custom-call | flops 92160 | bytes 368640 | tf_op jit(solution)/shard_map/pallas_call | solution.py:29
  11.8 0.0 collective-permute-done.4.refs_3_.refs_1_
  11.8 8.3 %collective-permute-done.3.refs_2_.refs_0_ = bf16[632,128]{1,0:T(8,128)(2,1)S(1)} collective-permute-done((bf16[632,128]{1,0:T(8,128)(2,1)S(1)}, bf16[632,128]{1,0:T(8,128)(2,1)S(1)}, u32[]{:S(2)}, u32[]{:S(2)}) %collective-permute-start.3) | collective-permute-done | bytes 161824 | tf_op jit(solution)/shard_map/ppermute | solution.py:390
  20.1 0.0 collective-permute-done.2.refs_1_
  20.1 0.0 collective-permute-done.1.refs_0_
  20.1 0.1 collective-permute-start.5
  20.2 1.2 %shard_map.78.refs_2_ = f32[6,3,48,96]{3,2,1,0:T(8,128)S(1)} custom-call(bf16[632,128]{1,0:T(8,128)(2,1)S(1)} %collective-permute-done.1.refs_0_, bf16[632,128]{1,0:T(8,128)(2,1)S(1)} %collective-permute-done.2.refs_1_, bf16[3,864,384]{2,1,0:T(8,128)(2,1)S(1)} %get-tuple-element.20.refs_5_.refs_2_.refs_3_), custom_call_target="tpu_custom_call" | custom-call | flops 573308928 | bytes 921600 | tf_op jit(solution)/shard_map/pallas_call | solution.py:29
  21.4 1.3 %shard_map.79 = (bf16[376,128]{1,0:T(8,128)(2,1)S(1)}, f32[6,3,48,96]{3,2,1,0:T(8,128)S(1)}) custom-call(bf16[632,128]{1,0:T(8,128)(2,1)S(1)} %collective-permute-done.3.refs_2_.refs_0_, bf16[632,128]{1,0:T(8,128)(2,1)S(1)} %collective-permute-done.4.refs_3_.refs_1_, f32[6,3,48,96]{3,2,1,0:T(8,128)S(1)} %shard_map.78.refs_2_, ...), custom_call_target="tpu_custom_call", output_to_operand_aliasing={{1}: (2, {})} | custom-call | flops 573308928 | bytes 921600 | tf_op jit(solution)/shard_map/pallas_call | solution.py:29
  22.7 0.0 copy-start
  22.7 2.5 %collective-permute-start.11 = (bf16[376,128]{1,0:T(8,128)(2,1)S(1)}, bf16[376,128]{1,0:T(8,128)(2,1)S(1)}, u32[]{:S(2)}, u32[]{:S(2)}) collective-permute-start(bf16[376,128]{1,0:T(8,128)(2,1)S(1)} %get-tuple-element.22.refs_0_), channel_id=1, source_target_pairs={{0,4},{1,5},{4,0},{5,1},{8,12},{9,13},{12,8},{13,9},{2,6},{3,7},{6... | collective-permute-start | bytes 288776 | tf_op jit(solution)/shard_map/ppermute | solution.py:406
  25.2 2.1 %collective-permute-start.10 = (bf16[376,128]{1,0:T(8,128)(2,1)S(1)}, bf16[376,128]{1,0:T(8,128)(2,1)S(1)}, u32[]{:S(2)}, u32[]{:S(2)}) collective-permute-start(bf16[376,128]{1,0:T(8,128)(2,1)S(1)} %get-tuple-element.22.refs_0_), channel_id=1, source_target_pairs={{0,8},{1,9},{4,12},{5,13},{8,0},{9,1},{12,4},{13,5},{2,10},{3,11},... | collective-permute-start | bytes 288776 | tf_op jit(solution)/shard_map/ppermute | solution.py:406
  27.3 1.4 %collective-permute-start.9 = (bf16[376,128]{1,0:T(8,128)(2,1)S(1)}, bf16[376,128]{1,0:T(8,128)(2,1)S(1)}, u32[]{:S(2)}, u32[]{:S(2)}) collective-permute-start(bf16[376,128]{1,0:T(8,128)(2,1)S(1)} %get-tuple-element.22.refs_0_), channel_id=1, source_target_pairs={{0,12},{1,13},{4,8},{5,9},{8,4},{9,5},{12,0},{13,1},{2,14},{3,15},... | collective-permute-start | bytes 288776 | tf_op jit(solution)/shard_map/ppermute | solution.py:406
  28.7 0.0 collective-permute-done.11.refs_3_
  28.7 2.3 %collective-permute-done.10.refs_2_ = bf16[376,128]{1,0:T(8,128)(2,1)S(1)} collective-permute-done((bf16[376,128]{1,0:T(8,128)(2,1)S(1)}, bf16[376,128]{1,0:T(8,128)(2,1)S(1)}, u32[]{:S(2)}, u32[]{:S(2)}) %collective-permute-start.10) | collective-permute-done | bytes 96288 | tf_op jit(solution)/shard_map/ppermute | solution.py:406
  31.0 5.1 %collective-permute-done.9.refs_1_ = bf16[376,128]{1,0:T(8,128)(2,1)S(1)} collective-permute-done((bf16[376,128]{1,0:T(8,128)(2,1)S(1)}, bf16[376,128]{1,0:T(8,128)(2,1)S(1)}, u32[]{:S(2)}, u32[]{:S(2)}) %collective-permute-start.9) | collective-permute-done | bytes 96288 | tf_op jit(solution)/shard_map/ppermute | solution.py:406
  36.0 0.7 %shard_map.80 = (bf16[4,1,48,384]{3,2,1,0:T(8,128)(2,1)S(1)}, bf16[4,2,48,384]{3,2,1,0:T(8,128)(2,1)S(1)}) custom-call(bf16[376,128]{1,0:T(8,128)(2,1)S(1)} %get-tuple-element.22.refs_0_, bf16[376,128]{1,0:T(8,128)(2,1)S(1)} %collective-permute-done.9.refs_1_, bf16[376,128]{1,0:T(8,128)(2,1)S(1)} %collective-permute-done.10.refs_2_, ...), custom_call_target="tpu_custom_call" | custom-call | flops 3686400 | bytes 1474560 | tf_op jit(solution)/shard_map/pallas_call | solution.py:29
  36.8 0.1 collective-permute-start.12
  36.9 0.0 collective-permute-done.5.refs_4_
  36.9 1.6 %shard_map.77.refs_0_ = bf16[248,128]{1,0:T(8,128)(2,1)S(1)} custom-call(bf16[632,128]{1,0:T(8,128)(2,1)S(1)} %collective-permute-done.1.refs_0_, bf16[632,128]{1,0:T(8,128)(2,1)S(1)} %collective-permute-done.2.refs_1_, bf16[632,128]{1,0:T(8,128)(2,1)S(1)} %collective-permute-done.3.refs_2_.refs_0_, ...), custom_call_target="tpu_custom_call" | custom-call | flops 764411904 | bytes 1843200 | tf_op jit(solution)/shard_map/pallas_call | solution.py:29
  38.5 2.0 %collective-permute-start.8 = (bf16[248,128]{1,0:T(8,128)(2,1)S(1)}, bf16[248,128]{1,0:T(8,128)(2,1)S(1)}, u32[]{:S(2)}, u32[]{:S(2)}) collective-permute-start(bf16[248,128]{1,0:T(8,128)(2,1)S(1)} %shard_map.77.refs_0_), channel_id=1, source_target_pairs={{0,4},{1,9},{4,0},{5,13},{8,12},{9,1},{12,8},{13,5},{2,6},{3,11},{... | collective-permute-start | bytes 190472 | tf_op jit(solution)/shard_map/ppermute | solution.py:406
  40.5 1.7 %collective-permute-start.7 = (bf16[248,128]{1,0:T(8,128)(2,1)S(1)}, bf16[248,128]{1,0:T(8,128)(2,1)S(1)}, u32[]{:S(2)}, u32[]{:S(2)}) collective-permute-start(bf16[248,128]{1,0:T(8,128)(2,1)S(1)} %shard_map.77.refs_0_), channel_id=1, source_target_pairs={{0,8},{1,13},{4,12},{5,9},{8,0},{9,5},{12,4},{13,1},{2,10},{3,15},... | collective-permute-start | bytes 190472 | tf_op jit(solution)/shard_map/ppermute | solution.py:406
  42.2 1.4 %collective-permute-start.6 = (bf16[248,128]{1,0:T(8,128)(2,1)S(1)}, bf16[248,128]{1,0:T(8,128)(2,1)S(1)}, u32[]{:S(2)}, u32[]{:S(2)}) collective-permute-start(bf16[248,128]{1,0:T(8,128)(2,1)S(1)} %shard_map.77.refs_0_), channel_id=1, source_target_pairs={{0,12},{1,5},{4,8},{5,1},{8,4},{9,13},{12,0},{13,9},{2,14},{3,7},{... | collective-permute-start | bytes 190472 | tf_op jit(solution)/shard_map/ppermute | solution.py:406
  43.6 0.0 copy-done
  43.6 1.7 %shard_map.81.refs_4_ = f32[4,3,48,96]{3,2,1,0:T(8,128)S(1)} custom-call(bf16[4,1,48,384]{3,2,1,0:T(8,128)(2,1)S(1)} %get-tuple-element.24.middle_ref, bf16[4,2,48,384]{3,2,1,0:T(8,128)(2,1)S(1)} %get-tuple-element.25.last_ref, bf16[3,864,384]{2,1,0:T(8,128)(2,1)S(1)} %bitcast.6), custom_call_target="tpu_custom_call" | custom-call | flops 637009920 | bytes 921600 | tf_op jit(solution)/shard_map/pallas_call | solution.py:29
  45.3 0.0 collective-permute-done.12.past_ref
  45.3 1.1 %shard_map.82.refs_5_ = f32[4,2,48,96]{3,2,1,0:T(8,128)S(1)} custom-call(bf16[4,2,48,384]{3,2,1,0:T(8,128)(2,1)S(1)} %collective-permute-done.12.past_ref, bf16[3,864,384]{2,1,0:T(8,128)(2,1)S(1)} %bitcast.7), custom_call_target="tpu_custom_call" | custom-call | flops 382205952 | bytes 921600 | tf_op jit(solution)/shard_map/pallas_call | solution.py:29
  46.4 0.0 copy-start.1
  46.4 0.0 collective-permute-done.8.refs_3_
  46.4 1.1 %collective-permute-done.7.refs_2_ = bf16[248,128]{1,0:T(8,128)(2,1)S(1)} collective-permute-done((bf16[248,128]{1,0:T(8,128)(2,1)S(1)}, bf16[248,128]{1,0:T(8,128)(2,1)S(1)}, u32[]{:S(2)}, u32[]{:S(2)}) %collective-permute-start.7) | collective-permute-done | bytes 63520 | tf_op jit(solution)/shard_map/ppermute | solution.py:406
  47.5 1.2 %collective-permute-done.6.refs_1_ = bf16[248,128]{1,0:T(8,128)(2,1)S(1)} collective-permute-done((bf16[248,128]{1,0:T(8,128)(2,1)S(1)}, bf16[248,128]{1,0:T(8,128)(2,1)S(1)}, u32[]{:S(2)}, u32[]{:S(2)}) %collective-permute-start.6) | collective-permute-done | bytes 63520 | tf_op jit(solution)/shard_map/ppermute | solution.py:406
  48.7 2.2 %shard_map.83 = (bf16[56,384]{1,0:T(8,128)(2,1)S(1)}, bf16[56,384]{1,0:T(8,128)(2,1)S(1)}, bf16[56,384]{1,0:T(8,128)(2,1)S(1)}, bf16[56,384]{1,0:T(8,128)(2,1)S(1)}) custom-call(bf16[248,128]{1,0:T(8,128)(2,1)S(1)} %shard_map.77.refs_0_, bf16[248,128]{1,0:T(8,128)(2,1)S(1)} %collective-permute-done.6.refs_1_, ...), custom_call_target="tpu_custom_call" | custom-call | flops 955514880 | bytes 1843200 | tf_op jit(solution)/shard_map/pallas_call | solution.py:29
  50.9 0.4 collective-permute-start.13
  51.3 0.2 collective-permute-start.14
  51.5 2.7 %collective-permute-start.15 = (bf16[56,384]{1,0:T(8,128)(2,1)S(1)}, bf16[56,384]{1,0:T(8,128)(2,1)S(1)}, u32[]{:S(2)}, u32[]{:S(2)}) collective-permute-start(bf16[56,384]{1,0:T(8,128)(2,1)S(1)} %get-tuple-element.29), channel_id=1, source_target_pairs={{0,10},{1,8},{2,11},{3,9},{4,14},{5,12},{6,15},{7,13},{8,2},{9,0},... | collective-permute-start | bytes 129032 | tf_op jit(solution)/shard_map/ppermute | solution.py:390
  54.2 1.9 %collective-permute-start.16 = (bf16[56,384]{1,0:T(8,128)(2,1)S(1)}, bf16[56,384]{1,0:T(8,128)(2,1)S(1)}, u32[]{:S(2)}, u32[]{:S(2)}) collective-permute-start(bf16[56,384]{1,0:T(8,128)(2,1)S(1)} %get-tuple-element.30), channel_id=1, source_target_pairs={{0,14},{1,12},{2,15},{3,13},{4,10},{5,8},{6,11},{7,9},{8,6},{9,4},... | collective-permute-start | bytes 129032 | tf_op jit(solution)/shard_map/ppermute | solution.py:390
  56.0 0.0 collective-permute-done.13.refs_0_
  56.0 0.0 collective-permute-done.14.refs_1_
  56.0 0.0 collective-permute-done.15.refs_2_
  56.1 3.5 %collective-permute-done.16.refs_3_ = bf16[56,384]{1,0:T(8,128)(2,1)S(1)} collective-permute-done((bf16[56,384]{1,0:T(8,128)(2,1)S(1)}, bf16[56,384]{1,0:T(8,128)(2,1)S(1)}, u32[]{:S(2)}, u32[]{:S(2)}) %collective-permute-start.16) | collective-permute-done | bytes 43040 | tf_op jit(solution)/shard_map/ppermute | solution.py:390
  59.6 1.0 %shard_map.84 = bf16[5,40,384]{2,1,0:T(8,128)(2,1)} custom-call(bf16[5,40,384]{2,1,0:T(8,128)(2,1)S(1)} %bitcast.11, bf16[56,384]{1,0:T(8,128)(2,1)S(1)} %collective-permute-done.13.refs_0_, bf16[56,384]{1,0:T(8,128)(2,1)S(1)} %collective-permute-done.14.refs_1_, bf16[56,384]{1,0:T(8,128)(2,1)S(1)} %collective-permute-done.15.refs_2_, ...), custom_call_target="tpu_custom_call" | custom-call | flops 184320 | bytes 552960 | tf_op jit(solution)/shard_map/pallas_call | solution.py:29
  (2 shorter events, 0.0 us)
Async XLA Ops:
  0.0 1.7 %collective-permute-start = (bf16[5,40,384]{2,1,0:T(8,128)(2,1)}, bf16[5,40,384]{2,1,0:T(8,128)(2,1)S(1)}, u32[]{:S(2)}, u32[]{:S(2)}) collective-permute-start(bf16[5,40,384]{2,1,0:T(8,128)(2,1)} %bitcast.9), channel_id=1, source_target_pairs={{0,1},{1,0},{2,3},{3,2},{4,5},{5,4},{6,7},{7,6},{8,9},{9,8},{10,11... | collective-permute-start | bytes 460808 | tf_op jit(solution)/shard_map/ppermute | solution.py:415
  1.8 10.0 %collective-permute-start.4 = (bf16[632,128]{1,0:T(8,128)(2,1)S(1)}, bf16[632,128]{1,0:T(8,128)(2,1)S(1)}, u32[]{:S(2)}, u32[]{:S(2)}) collective-permute-start(bf16[632,128]{1,0:T(8,128)(2,1)S(1)} %shard_map.74), channel_id=1, source_target_pairs={{0,9},{1,7},{2,4},{3,10},{4,13},{5,3},{6,0},{7,14},{8,1},{9,15},{1... | collective-permute-start | bytes 485384 | tf_op jit(solution)/shard_map/ppermute | solution.py:390
  5.6 14.5 %collective-permute-start.3 = (bf16[632,128]{1,0:T(8,128)(2,1)S(1)}, bf16[632,128]{1,0:T(8,128)(2,1)S(1)}, u32[]{:S(2)}, u32[]{:S(2)}) collective-permute-start(bf16[632,128]{1,0:T(8,128)(2,1)S(1)} %shard_map.74), channel_id=1, source_target_pairs={{0,5},{1,11},{2,8},{3,6},{4,1},{5,15},{6,12},{7,2},{8,13},{9,3},{1... | collective-permute-start | bytes 485384 | tf_op jit(solution)/shard_map/ppermute | solution.py:390
  5.7 14.4 %collective-permute-start.2 = (bf16[632,128]{1,0:T(8,128)(2,1)S(1)}, bf16[632,128]{1,0:T(8,128)(2,1)S(1)}, u32[]{:S(2)}, u32[]{:S(2)}) collective-permute-start(bf16[632,128]{1,0:T(8,128)(2,1)S(1)} %shard_map.74), channel_id=1, source_target_pairs={{0,1},{1,3},{2,0},{3,2},{4,5},{5,7},{6,4},{7,6},{8,9},{9,11},{10,8... | collective-permute-start | bytes 485384 | tf_op jit(solution)/shard_map/ppermute | solution.py:390
  6.9 13.2 %collective-permute-start.1 = (bf16[632,128]{1,0:T(8,128)(2,1)S(1)}, bf16[632,128]{1,0:T(8,128)(2,1)S(1)}, u32[]{:S(2)}, u32[]{:S(2)}) collective-permute-start(bf16[632,128]{1,0:T(8,128)(2,1)S(1)} %shard_map.74), channel_id=1, source_target_pairs={{0,13},{1,15},{2,12},{3,14},{4,9},{5,11},{6,8},{7,10},{8,5},{9,7},... | collective-permute-start | bytes 485384 | tf_op jit(solution)/shard_map/ppermute | solution.py:390
  20.1 16.8 %collective-permute-start.5 = (bf16[4,272,128]{2,1,0:T(8,128)(2,1)S(1)}, bf16[4,272,128]{2,1,0:T(8,128)(2,1)S(1)}, u32[]{:S(2)}, u32[]{:S(2)}) collective-permute-start(bf16[4,272,128]{2,1,0:T(8,128)(2,1)S(1)} %shard_map.75), channel_id=1, source_target_pairs={{0,1},{1,0},{2,3},{3,2},{4,5},{5,4},{6,7},{7,6},{8,9},{9,8},{10,11... | collective-permute-start | bytes 835592 | tf_op jit(solution)/shard_map/ppermute | solution.py:390
  22.7 20.9 %copy-start = (bf16[27,96,384]{2,1,0:T(8,128)(2,1)S(1)}, bf16[27,96,384]{2,1,0:T(8,128)(2,1)}, u32[]{:S(2)}) copy-start(bf16[27,96,384]{2,1,0:T(8,128)(2,1)} %param.12) | copy-start | bytes 5971972
  22.7 6.0 %collective-permute-start.11 = (bf16[376,128]{1,0:T(8,128)(2,1)S(1)}, bf16[376,128]{1,0:T(8,128)(2,1)S(1)}, u32[]{:S(2)}, u32[]{:S(2)}) collective-permute-start(bf16[376,128]{1,0:T(8,128)(2,1)S(1)} %get-tuple-element.22.refs_0_), channel_id=1, source_target_pairs={{0,4},{1,5},{4,0},{5,1},{8,12},{9,13},{12,8},{13,9},{2,6},{3,7},{6... | collective-permute-start | bytes 288776 | tf_op jit(solution)/shard_map/ppermute | solution.py:406
  25.2 5.8 %collective-permute-start.10 = (bf16[376,128]{1,0:T(8,128)(2,1)S(1)}, bf16[376,128]{1,0:T(8,128)(2,1)S(1)}, u32[]{:S(2)}, u32[]{:S(2)}) collective-permute-start(bf16[376,128]{1,0:T(8,128)(2,1)S(1)} %get-tuple-element.22.refs_0_), channel_id=1, source_target_pairs={{0,8},{1,9},{4,12},{5,13},{8,0},{9,1},{12,4},{13,5},{2,10},{3,11},... | collective-permute-start | bytes 288776 | tf_op jit(solution)/shard_map/ppermute | solution.py:406
  27.3 8.7 %collective-permute-start.9 = (bf16[376,128]{1,0:T(8,128)(2,1)S(1)}, bf16[376,128]{1,0:T(8,128)(2,1)S(1)}, u32[]{:S(2)}, u32[]{:S(2)}) collective-permute-start(bf16[376,128]{1,0:T(8,128)(2,1)S(1)} %get-tuple-element.22.refs_0_), channel_id=1, source_target_pairs={{0,12},{1,13},{4,8},{5,9},{8,4},{9,5},{12,0},{13,1},{2,14},{3,15},... | collective-permute-start | bytes 288776 | tf_op jit(solution)/shard_map/ppermute | solution.py:406
  36.8 8.5 %collective-permute-start.12 = (bf16[4,2,48,384]{3,2,1,0:T(8,128)(2,1)S(1)}, bf16[4,2,48,384]{3,2,1,0:T(8,128)(2,1)S(1)}, u32[]{:S(2)}, u32[]{:S(2)}) collective-permute-start(bf16[4,2,48,384]{3,2,1,0:T(8,128)(2,1)S(1)} %get-tuple-element.25.last_ref), channel_id=1, source_target_pairs={{0,1},{1,0},{2,3},{3,2},{4,5},{5,4},{6,7},{7,6},{8,9},{9,8},{10,11... | collective-permute-start | bytes 884744 | tf_op jit(solution)/shard_map/ppermute | solution.py:390
  38.5 7.8 %collective-permute-start.8 = (bf16[248,128]{1,0:T(8,128)(2,1)S(1)}, bf16[248,128]{1,0:T(8,128)(2,1)S(1)}, u32[]{:S(2)}, u32[]{:S(2)}) collective-permute-start(bf16[248,128]{1,0:T(8,128)(2,1)S(1)} %shard_map.77.refs_0_), channel_id=1, source_target_pairs={{0,4},{1,9},{4,0},{5,13},{8,12},{9,1},{12,8},{13,5},{2,6},{3,11},{... | collective-permute-start | bytes 190472 | tf_op jit(solution)/shard_map/ppermute | solution.py:406
  40.5 7.0 %collective-permute-start.7 = (bf16[248,128]{1,0:T(8,128)(2,1)S(1)}, bf16[248,128]{1,0:T(8,128)(2,1)S(1)}, u32[]{:S(2)}, u32[]{:S(2)}) collective-permute-start(bf16[248,128]{1,0:T(8,128)(2,1)S(1)} %shard_map.77.refs_0_), channel_id=1, source_target_pairs={{0,8},{1,13},{4,12},{5,9},{8,0},{9,5},{12,4},{13,1},{2,10},{3,15},... | collective-permute-start | bytes 190472 | tf_op jit(solution)/shard_map/ppermute | solution.py:406
  42.2 6.5 %collective-permute-start.6 = (bf16[248,128]{1,0:T(8,128)(2,1)S(1)}, bf16[248,128]{1,0:T(8,128)(2,1)S(1)}, u32[]{:S(2)}, u32[]{:S(2)}) collective-permute-start(bf16[248,128]{1,0:T(8,128)(2,1)S(1)} %shard_map.77.refs_0_), channel_id=1, source_target_pairs={{0,12},{1,5},{4,8},{5,1},{8,4},{9,13},{12,0},{13,9},{2,14},{3,7},{... | collective-permute-start | bytes 190472 | tf_op jit(solution)/shard_map/ppermute | solution.py:406
  46.4 13.2 %copy-start.1 = (bf16[5,1,40,384]{3,2,1,0:T(8,128)(2,1)S(1)}, bf16[5,1,40,384]{3,2,1,0:T(8,128)(2,1)}, u32[]{:S(2)}) copy-start(bf16[5,1,40,384]{3,2,1,0:T(8,128)(2,1)} %param.7) | copy-start | bytes 460804
  50.9 5.1 %collective-permute-start.13 = (bf16[56,384]{1,0:T(8,128)(2,1)S(1)}, bf16[56,384]{1,0:T(8,128)(2,1)S(1)}, u32[]{:S(2)}, u32[]{:S(2)}) collective-permute-start(bf16[56,384]{1,0:T(8,128)(2,1)S(1)} %get-tuple-element.27), channel_id=1, source_target_pairs={{0,2},{1,0},{2,3},{3,1},{4,6},{5,4},{6,7},{7,5},{8,10},{9,8},{10,1... | collective-permute-start | bytes 129032 | tf_op jit(solution)/shard_map/ppermute | solution.py:390
  51.3 4.8 %collective-permute-start.14 = (bf16[56,384]{1,0:T(8,128)(2,1)S(1)}, bf16[56,384]{1,0:T(8,128)(2,1)S(1)}, u32[]{:S(2)}, u32[]{:S(2)}) collective-permute-start(bf16[56,384]{1,0:T(8,128)(2,1)S(1)} %get-tuple-element.28), channel_id=1, source_target_pairs={{0,6},{1,4},{2,7},{3,5},{4,2},{5,0},{6,3},{7,1},{8,14},{9,12},{10,... | collective-permute-start | bytes 129032 | tf_op jit(solution)/shard_map/ppermute | solution.py:390
  51.5 4.6 %collective-permute-start.15 = (bf16[56,384]{1,0:T(8,128)(2,1)S(1)}, bf16[56,384]{1,0:T(8,128)(2,1)S(1)}, u32[]{:S(2)}, u32[]{:S(2)}) collective-permute-start(bf16[56,384]{1,0:T(8,128)(2,1)S(1)} %get-tuple-element.29), channel_id=1, source_target_pairs={{0,10},{1,8},{2,11},{3,9},{4,14},{5,12},{6,15},{7,13},{8,2},{9,0},... | collective-permute-start | bytes 129032 | tf_op jit(solution)/shard_map/ppermute | solution.py:390
  54.2 5.4 %collective-permute-start.16 = (bf16[56,384]{1,0:T(8,128)(2,1)S(1)}, bf16[56,384]{1,0:T(8,128)(2,1)S(1)}, u32[]{:S(2)}, u32[]{:S(2)}) collective-permute-start(bf16[56,384]{1,0:T(8,128)(2,1)S(1)} %get-tuple-element.30), channel_id=1, source_target_pairs={{0,14},{1,12},{2,15},{3,13},{4,10},{5,8},{6,11},{7,9},{8,6},{9,4},... | collective-permute-start | bytes 129032 | tf_op jit(solution)/shard_map/ppermute | solution.py:390

commit v11 on v6

--- a/solution.py
+++ b/solution.py
@@ -389,10 +389,13 @@
     def following(values):
         return moved(values, lambda z, x, c: (z, x, 0) if c == 1 else (z, (x + 2) % tm, 1))
 
+    def handed(values, k):
+        return lax.ppermute(values, "rows", [(z, z ^ k) for z in range(rows)])
+
     def spread(values):
         parts = [values]
         for k in range(1, rows):
-            parts.append(lax.ppermute(values, "rows", [(z, z ^ k) for z in range(rows)]))
+            parts.append(handed(values, k))
         return parts
 
     def turn(values, way):
@@ -401,6 +404,12 @@
             parts.append(way(values[k], k))
         return parts
 
+    def gather(values):
+        parts = []
+        for k in range(rows):
+            parts.append(handed(parts[k - 1], 1) if k % 2 and k > 1 else turned(values, k))
+        return parts
+
     other = lax.ppermute(own, "cols", [(0, 1), (1, 0)])
     weights = [w.reshape(TAPS, TAPS * TAPS * width, channels) for w in (conv_one, conv_two)]
     sds = jax.ShapeDtypeStruct
@@ -417,7 +426,7 @@
     )
     total = packed_rows(frames * breadth, EDGE * frames, channels)
     band = call(ends_body, sds((total, LANES), bf16), [], size, 4 * size, center, other, gain_one)
-    pieces = turn([band] * rows, turned)
+    pieces = gather(band)
     small = (bias_one, gain_two, bias_two, weights[0])
     bias_one, gain_two, bias_two, near = call(
         stage_body, [sds(v.shape, v.dtype) for v in small], [pltpu.SemaphoreType.DMA((len(small),))],
@@ -478,8 +487,7 @@
 
 
 def band_order(rows):
-    first = [k for k in range(rows - 1, 0, -1) if k != 2]
-    return first + [0] + [k for k in (2,) if k < rows]
+    return [1, *range(rows - 2, 0, -2), 0, *range(3, rows, 2)]
 
 
 def solution(mesh):

time: 59.9 us -> 57.7 us (0.963)
  waiting for transfers between devices: 24.7 us -> 22.6 us
    ppermute x10 -> x9, waiting for transfers between devices: 16.1 us -> 11.1 us  [moved(): lax.ppermute(values, AXES, [(place[device], place[target(*device)]) for d...]
    ppermute x6 -> x7, waiting for transfers between devices: 8.45 us -> 11.4 us  [handed(): return lax.ppermute(values, 'rows', [(z, z ^ k) for z in range(rows)])]
    ppermute x10 -> x9, starting transfers between devices: 11.7 us -> 11.6 us  [moved(): lax.ppermute(values, AXES, [(place[device], place[target(*device)]) for d...]
    ppermute x6 -> x7, starting transfers between devices: 8.91 us -> 8.91 us  [handed(): return lax.ppermute(values, 'rows', [(z, z ^ k) for z in range(rows)])]
where the time goes in v11:
time: 57.7 us; the launch traced here: 57.6 us
  waiting for transfers between devices  22.6 us (39%)
  starting transfers between devices  21 us (36%)
  Pallas kernels  13.8 us (24%)
    pallas_call x12, Pallas kernels, call(): pl.pallas_call(body, out_shape=out_shape, in_specs=[pl.BlockSpec(memory_s...  13.8 us
    ppermute x9, starting transfers between devices, moved(): lax.ppermute(values, AXES, [(place[device], place[target(*device)]) for d...  11.6 us
    ppermute x7, waiting for transfers between devices, handed(): return lax.ppermute(values, 'rows', [(z, z ^ k) for z in range(rows)])  11.4 us
    ppermute x9, waiting for transfers between devices, moved(): lax.ppermute(values, AXES, [(place[device], place[target(*device)]) for d...  11.1 us
    ppermute x7, starting transfers between devices, handed(): return lax.ppermute(values, 'rows', [(z, z ^ k) for z in range(rows)])  8.91 us
  transfers between devices with their start and end apart: 17, of which 8 were waited for; matrix products, arithmetic and copies ran while one was open for 0% of the time, Pallas kernels for 18%

profile of v11, /device:TPU:0, one launch (start us, length us, event | category | flops | bytes accessed | tf_op | source)
XLA Modules:
  0.0 57.6 jit_solution(2530202535936390205)
XLA Ops:
  0.0 0.5 collective-permute-start
  0.5 1.1 %shard_map.73 = (bf16[600,128]{1,0:T(8,128)(2,1)S(1)}, f32[384]{0:T(512)S(1)}) custom-call(bf16[5,40,384]{2,1,0:T(8,128)(2,1)} %bitcast.10, f32[384]{0:T(512)} %far_gain_ref.1), custom_call_target="tpu_custom_call" | custom-call | flops 921600 | bytes 552960 | tf_op jit(solution)/shard_map/pallas_call | solution.py:28
  1.6 0.1 collective-permute-done.other_ref
  1.7 0.1 shard_map.74
  1.8 3.7 %collective-permute-start.3 = (bf16[632,128]{1,0:T(8,128)(2,1)S(1)}, bf16[632,128]{1,0:T(8,128)(2,1)S(1)}, u32[]{:S(2)}, u32[]{:S(2)}) collective-permute-start(bf16[632,128]{1,0:T(8,128)(2,1)S(1)} %shard_map.74), channel_id=1, source_target_pairs={{0,9},{1,11},{2,8},{3,10},{4,13},{5,15},{6,12},{7,14},{8,1},{9,3},... | collective-permute-start | bytes 485384 | tf_op jit(solution)/shard_map/ppermute | solution.py:381
  5.6 2.2 %collective-permute-start.2 = (bf16[632,128]{1,0:T(8,128)(2,1)S(1)}, bf16[632,128]{1,0:T(8,128)(2,1)S(1)}, u32[]{:S(2)}, u32[]{:S(2)}) collective-permute-start(bf16[632,128]{1,0:T(8,128)(2,1)S(1)} %shard_map.74), channel_id=1, source_target_pairs={{0,5},{1,7},{2,4},{3,6},{4,1},{5,3},{6,0},{7,2},{8,13},{9,15},{10,... | collective-permute-start | bytes 485384 | tf_op jit(solution)/shard_map/ppermute | solution.py:381
  7.8 0.4 collective-permute-start.1
  8.2 6.9 %collective-permute-done.3.refs_2_.refs_1_ = bf16[632,128]{1,0:T(8,128)(2,1)S(1)} collective-permute-done((bf16[632,128]{1,0:T(8,128)(2,1)S(1)}, bf16[632,128]{1,0:T(8,128)(2,1)S(1)}, u32[]{:S(2)}, u32[]{:S(2)}) %collective-permute-start.3) | collective-permute-done | bytes 161824 | tf_op jit(solution)/shard_map/ppermute | solution.py:381
  15.1 0.0 collective-permute-start.4
  15.1 1.6 %shard_map.76 = (f32[384]{0:T(512)S(1)}, f32[384]{0:T(512)S(1)}, f32[384]{0:T(512)S(1)}, bf16[3,864,384]{2,1,0:T(8,128)(2,1)S(1)}) custom-call(f32[384]{0:T(512)} %refs_0_.1, f32[384]{0:T(512)} %refs_1_.1, f32[384]{0:T(512)} %refs_2_.1, bf16[3,864,384]{2,1,0:T(8,128)(2,1)} %bitcast.12), custom_call_target="tpu_custom_call" | custom-call | flops 92160 | bytes 368640 | tf_op jit(solution)/shard_map/pallas_call | solution.py:28
  16.8 0.0 collective-permute-done.2.refs_1_.refs_0_
  16.8 0.0 collective-permute-done.1.refs_0_.refs_2_
  16.8 1.7 %shard_map.78.near_ref = f32[6,3,48,96]{3,2,1,0:T(8,128)S(1)} custom-call(bf16[632,128]{1,0:T(8,128)(2,1)S(1)} %collective-permute-done.2.refs_1_.refs_0_, bf16[632,128]{1,0:T(8,128)(2,1)S(1)} %collective-permute-done.3.refs_2_.refs_1_, bf16[632,128]{1,0:T(8,128)(2,1)S(1)} %collective-permute-done.1.refs_0_.refs_2_, ...), custom_call_target="tpu_custom_call" | custom-call | flops 859963392 | bytes 921600 | tf_op jit(solution)/shard_map/pallas_call | solution.py:28
  18.4 2.0 %collective-permute-done.4.refs_3_.piece_ref = bf16[632,128]{1,0:T(8,128)(2,1)S(1)} collective-permute-done((bf16[632,128]{1,0:T(8,128)(2,1)S(1)}, bf16[632,128]{1,0:T(8,128)(2,1)S(1)}, u32[]{:S(2)}, u32[]{:S(2)}) %collective-permute-start.4) | collective-permute-done | bytes 161824 | tf_op jit(solution)/shard_map/ppermute | solution.py:393
  20.4 0.1 collective-permute-start.5
  20.5 1.0 %shard_map.79 = (bf16[376,128]{1,0:T(8,128)(2,1)S(1)}, f32[6,3,48,96]{3,2,1,0:T(8,128)S(1)}) custom-call(bf16[632,128]{1,0:T(8,128)(2,1)S(1)} %collective-permute-done.4.refs_3_.piece_ref, f32[6,3,48,96]{3,2,1,0:T(8,128)S(1)} %shard_map.78.near_ref, ...), custom_call_target="tpu_custom_call", output_to_operand_aliasing={{1}: (1, {})} | custom-call | flops 286654464 | bytes 921600 | tf_op jit(solution)/shard_map/pallas_call | solution.py:28
  21.5 0.0 copy-start
  21.5 3.7 %collective-permute-start.11 = (bf16[376,128]{1,0:T(8,128)(2,1)S(1)}, bf16[376,128]{1,0:T(8,128)(2,1)S(1)}, u32[]{:S(2)}, u32[]{:S(2)}) collective-permute-start(bf16[376,128]{1,0:T(8,128)(2,1)S(1)} %get-tuple-element.22.refs_0_), channel_id=1, source_target_pairs={{0,12},{4,8},{8,4},{12,0},{1,13},{5,9},{9,5},{13,1},{2,14},{6,10},... | collective-permute-start | bytes 288776 | tf_op jit(solution)/shard_map/ppermute | solution.py:393
  25.2 0.0 collective-permute-start.10
  25.2 0.8 %collective-permute-start.9 = (bf16[376,128]{1,0:T(8,128)(2,1)S(1)}, bf16[376,128]{1,0:T(8,128)(2,1)S(1)}, u32[]{:S(2)}, u32[]{:S(2)}) collective-permute-start(bf16[376,128]{1,0:T(8,128)(2,1)S(1)} %get-tuple-element.22.refs_0_), channel_id=1, source_target_pairs={{0,4},{4,0},{8,12},{12,8},{1,5},{5,1},{9,13},{13,9},{2,6},{6,2},{1... | collective-permute-start | bytes 288776 | tf_op jit(solution)/shard_map/ppermute | solution.py:393
  26.0 3.1 %collective-permute-done.11.refs_3_ = bf16[376,128]{1,0:T(8,128)(2,1)S(1)} collective-permute-done((bf16[376,128]{1,0:T(8,128)(2,1)S(1)}, bf16[376,128]{1,0:T(8,128)(2,1)S(1)}, u32[]{:S(2)}, u32[]{:S(2)}) %collective-permute-start.11) | collective-permute-done | bytes 96288 | tf_op jit(solution)/shard_map/ppermute | solution.py:393
  29.1 4.5 %collective-permute-done.10.refs_2_ = bf16[376,128]{1,0:T(8,128)(2,1)S(1)} collective-permute-done((bf16[376,128]{1,0:T(8,128)(2,1)S(1)}, bf16[376,128]{1,0:T(8,128)(2,1)S(1)}, u32[]{:S(2)}, u32[]{:S(2)}) %collective-permute-start.10) | collective-permute-done | bytes 96288 | tf_op jit(solution)/shard_map/ppermute | solution.py:393
  33.6 0.0 collective-permute-done.9.refs_1_
  33.6 0.7 %shard_map.80 = (bf16[4,1,48,384]{3,2,1,0:T(8,128)(2,1)S(1)}, bf16[4,2,48,384]{3,2,1,0:T(8,128)(2,1)S(1)}) custom-call(bf16[376,128]{1,0:T(8,128)(2,1)S(1)} %get-tuple-element.22.refs_0_, bf16[376,128]{1,0:T(8,128)(2,1)S(1)} %collective-permute-done.9.refs_1_, bf16[376,128]{1,0:T(8,128)(2,1)S(1)} %collective-permute-done.10.refs_2_, ...), custom_call_target="tpu_custom_call" | custom-call | flops 3686400 | bytes 1474560 | tf_op jit(solution)/shard_map/pallas_call | solution.py:28
  34.4 0.1 collective-permute-start.12
  34.5 0.0 collective-permute-done.5.refs_4_
  34.5 1.6 %shard_map.77.refs_0_ = bf16[248,128]{1,0:T(8,128)(2,1)S(1)} custom-call(bf16[632,128]{1,0:T(8,128)(2,1)S(1)} %collective-permute-done.1.refs_0_.refs_2_, bf16[632,128]{1,0:T(8,128)(2,1)S(1)} %collective-permute-done.2.refs_1_.refs_0_, bf16[632,128]{1,0:T(8,128)(2,1)S(1)} %collective-permute-done.3.refs_2_.refs_1_, ...), custom_call_target="tpu_custom_call" | custom-call | flops 764411904 | bytes 1843200 | tf_op jit(solution)/shard_map/pallas_call | solution.py:28
  36.1 2.7 %collective-permute-start.8 = (bf16[248,128]{1,0:T(8,128)(2,1)S(1)}, bf16[248,128]{1,0:T(8,128)(2,1)S(1)}, u32[]{:S(2)}, u32[]{:S(2)}) collective-permute-start(bf16[248,128]{1,0:T(8,128)(2,1)S(1)} %shard_map.77.refs_0_), channel_id=1, source_target_pairs={{0,12},{4,8},{8,4},{12,0},{1,13},{5,9},{9,5},{13,1},{2,14},{6,10},... | collective-permute-start | bytes 190472 | tf_op jit(solution)/shard_map/ppermute | solution.py:393
  38.8 0.0 collective-permute-start.7
  38.8 1.7 %collective-permute-start.6 = (bf16[248,128]{1,0:T(8,128)(2,1)S(1)}, bf16[248,128]{1,0:T(8,128)(2,1)S(1)}, u32[]{:S(2)}, u32[]{:S(2)}) collective-permute-start(bf16[248,128]{1,0:T(8,128)(2,1)S(1)} %shard_map.77.refs_0_), channel_id=1, source_target_pairs={{0,4},{4,0},{8,12},{12,8},{1,5},{5,1},{9,13},{13,9},{2,6},{6,2},{1... | collective-permute-start | bytes 190472 | tf_op jit(solution)/shard_map/ppermute | solution.py:393
  40.6 0.0 copy-done
  40.6 1.7 %shard_map.81.refs_4_ = f32[4,3,48,96]{3,2,1,0:T(8,128)S(1)} custom-call(bf16[4,1,48,384]{3,2,1,0:T(8,128)(2,1)S(1)} %get-tuple-element.24.middle_ref, bf16[4,2,48,384]{3,2,1,0:T(8,128)(2,1)S(1)} %get-tuple-element.25.last_ref, bf16[3,864,384]{2,1,0:T(8,128)(2,1)S(1)} %bitcast.6), custom_call_target="tpu_custom_call" | custom-call | flops 637009920 | bytes 921600 | tf_op jit(solution)/shard_map/pallas_call | solution.py:28
  42.3 0.0 collective-permute-done.12.past_ref
  42.3 1.1 %shard_map.82.refs_5_ = f32[4,2,48,96]{3,2,1,0:T(8,128)S(1)} custom-call(bf16[4,2,48,384]{3,2,1,0:T(8,128)(2,1)S(1)} %collective-permute-done.12.past_ref, bf16[3,864,384]{2,1,0:T(8,128)(2,1)S(1)} %bitcast.7), custom_call_target="tpu_custom_call" | custom-call | flops 382205952 | bytes 921600 | tf_op jit(solution)/shard_map/pallas_call | solution.py:28
  43.3 0.0 copy-start.1
  43.3 0.0 collective-permute-done.8.refs_3_
  43.4 1.8 %collective-permute-done.7.refs_2_ = bf16[248,128]{1,0:T(8,128)(2,1)S(1)} collective-permute-done((bf16[248,128]{1,0:T(8,128)(2,1)S(1)}, bf16[248,128]{1,0:T(8,128)(2,1)S(1)}, u32[]{:S(2)}, u32[]{:S(2)}) %collective-permute-start.7) | collective-permute-done | bytes 63520 | tf_op jit(solution)/shard_map/ppermute | solution.py:393
  45.1 0.0 collective-permute-done.6.refs_1_
  45.1 2.2 %shard_map.83 = (bf16[56,384]{1,0:T(8,128)(2,1)S(1)}, bf16[56,384]{1,0:T(8,128)(2,1)S(1)}, bf16[56,384]{1,0:T(8,128)(2,1)S(1)}, bf16[56,384]{1,0:T(8,128)(2,1)S(1)}) custom-call(bf16[248,128]{1,0:T(8,128)(2,1)S(1)} %shard_map.77.refs_0_, bf16[248,128]{1,0:T(8,128)(2,1)S(1)} %collective-permute-done.6.refs_1_, ...), custom_call_target="tpu_custom_call" | custom-call | flops 955514880 | bytes 1843200 | tf_op jit(solution)/shard_map/pallas_call | solution.py:28
  47.3 1.2 %collective-permute-start.13 = (bf16[56,384]{1,0:T(8,128)(2,1)S(1)}, bf16[56,384]{1,0:T(8,128)(2,1)S(1)}, u32[]{:S(2)}, u32[]{:S(2)}) collective-permute-start(bf16[56,384]{1,0:T(8,128)(2,1)S(1)} %get-tuple-element.27), channel_id=1, source_target_pairs={{0,2},{1,0},{2,3},{3,1},{4,6},{5,4},{6,7},{7,5},{8,10},{9,8},{10,1... | collective-permute-start | bytes 129032 | tf_op jit(solution)/shard_map/ppermute | solution.py:381
  48.5 0.4 collective-permute-start.14
  48.9 2.4 %collective-permute-start.15 = (bf16[56,384]{1,0:T(8,128)(2,1)S(1)}, bf16[56,384]{1,0:T(8,128)(2,1)S(1)}, u32[]{:S(2)}, u32[]{:S(2)}) collective-permute-start(bf16[56,384]{1,0:T(8,128)(2,1)S(1)} %get-tuple-element.29), channel_id=1, source_target_pairs={{0,10},{1,8},{2,11},{3,9},{4,14},{5,12},{6,15},{7,13},{8,2},{9,0},... | collective-permute-start | bytes 129032 | tf_op jit(solution)/shard_map/ppermute | solution.py:381
  51.4 1.1 %collective-permute-start.16 = (bf16[56,384]{1,0:T(8,128)(2,1)S(1)}, bf16[56,384]{1,0:T(8,128)(2,1)S(1)}, u32[]{:S(2)}, u32[]{:S(2)}) collective-permute-start(bf16[56,384]{1,0:T(8,128)(2,1)S(1)} %get-tuple-element.30), channel_id=1, source_target_pairs={{0,14},{1,12},{2,15},{3,13},{4,10},{5,8},{6,11},{7,9},{8,6},{9,4},... | collective-permute-start | bytes 129032 | tf_op jit(solution)/shard_map/ppermute | solution.py:381
  52.4 0.0 collective-permute-done.13.refs_0_
  52.5 0.0 collective-permute-done.14.refs_1_
  52.5 1.0 %collective-permute-done.15.refs_2_ = bf16[56,384]{1,0:T(8,128)(2,1)S(1)} collective-permute-done((bf16[56,384]{1,0:T(8,128)(2,1)S(1)}, bf16[56,384]{1,0:T(8,128)(2,1)S(1)}, u32[]{:S(2)}, u32[]{:S(2)}) %collective-permute-start.15) | collective-permute-done | bytes 43040 | tf_op jit(solution)/shard_map/ppermute | solution.py:381
  53.5 3.1 %collective-permute-done.16.refs_3_ = bf16[56,384]{1,0:T(8,128)(2,1)S(1)} collective-permute-done((bf16[56,384]{1,0:T(8,128)(2,1)S(1)}, bf16[56,384]{1,0:T(8,128)(2,1)S(1)}, u32[]{:S(2)}, u32[]{:S(2)}) %collective-permute-start.16) | collective-permute-done | bytes 43040 | tf_op jit(solution)/shard_map/ppermute | solution.py:381
  56.6 1.0 %shard_map.84 = bf16[5,40,384]{2,1,0:T(8,128)(2,1)} custom-call(bf16[5,40,384]{2,1,0:T(8,128)(2,1)S(1)} %bitcast.11, bf16[56,384]{1,0:T(8,128)(2,1)S(1)} %collective-permute-done.13.refs_0_, bf16[56,384]{1,0:T(8,128)(2,1)S(1)} %collective-permute-done.14.refs_1_, bf16[56,384]{1,0:T(8,128)(2,1)S(1)} %collective-permute-done.15.refs_2_, ...), custom_call_target="tpu_custom_call" | custom-call | flops 184320 | bytes 552960 | tf_op jit(solution)/shard_map/pallas_call | solution.py:28
  (2 shorter events, 0.0 us)
Async XLA Ops:
  0.0 1.7 %collective-permute-start = (bf16[5,40,384]{2,1,0:T(8,128)(2,1)}, bf16[5,40,384]{2,1,0:T(8,128)(2,1)S(1)}, u32[]{:S(2)}, u32[]{:S(2)}) collective-permute-start(bf16[5,40,384]{2,1,0:T(8,128)(2,1)} %bitcast.9), channel_id=1, source_target_pairs={{0,1},{1,0},{2,3},{3,2},{4,5},{5,4},{6,7},{7,6},{8,9},{9,8},{10,11... | collective-permute-start | bytes 460808 | tf_op jit(solution)/shard_map/ppermute | solution.py:413
  1.8 13.3 %collective-permute-start.3 = (bf16[632,128]{1,0:T(8,128)(2,1)S(1)}, bf16[632,128]{1,0:T(8,128)(2,1)S(1)}, u32[]{:S(2)}, u32[]{:S(2)}) collective-permute-start(bf16[632,128]{1,0:T(8,128)(2,1)S(1)} %shard_map.74), channel_id=1, source_target_pairs={{0,9},{1,11},{2,8},{3,10},{4,13},{5,15},{6,12},{7,14},{8,1},{9,3},... | collective-permute-start | bytes 485384 | tf_op jit(solution)/shard_map/ppermute | solution.py:381
  5.6 11.2 %collective-permute-start.2 = (bf16[632,128]{1,0:T(8,128)(2,1)S(1)}, bf16[632,128]{1,0:T(8,128)(2,1)S(1)}, u32[]{:S(2)}, u32[]{:S(2)}) collective-permute-start(bf16[632,128]{1,0:T(8,128)(2,1)S(1)} %shard_map.74), channel_id=1, source_target_pairs={{0,5},{1,7},{2,4},{3,6},{4,1},{5,3},{6,0},{7,2},{8,13},{9,15},{10,... | collective-permute-start | bytes 485384 | tf_op jit(solution)/shard_map/ppermute | solution.py:381
  7.8 9.0 %collective-permute-start.1 = (bf16[632,128]{1,0:T(8,128)(2,1)S(1)}, bf16[632,128]{1,0:T(8,128)(2,1)S(1)}, u32[]{:S(2)}, u32[]{:S(2)}) collective-permute-start(bf16[632,128]{1,0:T(8,128)(2,1)S(1)} %shard_map.74), channel_id=1, source_target_pairs={{0,1},{1,3},{2,0},{3,2},{4,5},{5,7},{6,4},{7,6},{8,9},{9,11},{10,8... | collective-permute-start | bytes 485384 | tf_op jit(solution)/shard_map/ppermute | solution.py:381
  15.1 5.3 %collective-permute-start.4 = (bf16[632,128]{1,0:T(8,128)(2,1)S(1)}, bf16[632,128]{1,0:T(8,128)(2,1)S(1)}, u32[]{:S(2)}, u32[]{:S(2)}) collective-permute-start(bf16[632,128]{1,0:T(8,128)(2,1)S(1)} %collective-permute-done.3.refs_2_.refs_1_), channel_id=1, source_target_pairs={{0,4},{4,0},{8,12},{12,8},{1,5},{5,1},{9,13},{13,9},{2,6},{6,2},{1... | collective-permute-start | bytes 485384 | tf_op jit(solution)/shard_map/ppermute | solution.py:393
  20.4 14.0 %collective-permute-start.5 = (bf16[4,272,128]{2,1,0:T(8,128)(2,1)S(1)}, bf16[4,272,128]{2,1,0:T(8,128)(2,1)S(1)}, u32[]{:S(2)}, u32[]{:S(2)}) collective-permute-start(bf16[4,272,128]{2,1,0:T(8,128)(2,1)S(1)} %shard_map.75), channel_id=1, source_target_pairs={{0,1},{1,0},{2,3},{3,2},{4,5},{5,4},{6,7},{7,6},{8,9},{9,8},{10,11... | collective-permute-start | bytes 835592 | tf_op jit(solution)/shard_map/ppermute | solution.py:381
  21.5 19.1 %copy-start = (bf16[27,96,384]{2,1,0:T(8,128)(2,1)S(1)}, bf16[27,96,384]{2,1,0:T(8,128)(2,1)}, u32[]{:S(2)}) copy-start(bf16[27,96,384]{2,1,0:T(8,128)(2,1)} %param.12) | copy-start | bytes 5971972
  21.5 7.6 %collective-permute-start.11 = (bf16[376,128]{1,0:T(8,128)(2,1)S(1)}, bf16[376,128]{1,0:T(8,128)(2,1)S(1)}, u32[]{:S(2)}, u32[]{:S(2)}) collective-permute-start(bf16[376,128]{1,0:T(8,128)(2,1)S(1)} %get-tuple-element.22.refs_0_), channel_id=1, source_target_pairs={{0,12},{4,8},{8,4},{12,0},{1,13},{5,9},{9,5},{13,1},{2,14},{6,10},... | collective-permute-start | bytes 288776 | tf_op jit(solution)/shard_map/ppermute | solution.py:393
  25.2 8.4 %collective-permute-start.10 = (bf16[376,128]{1,0:T(8,128)(2,1)S(1)}, bf16[376,128]{1,0:T(8,128)(2,1)S(1)}, u32[]{:S(2)}, u32[]{:S(2)}) collective-permute-start(bf16[376,128]{1,0:T(8,128)(2,1)S(1)} %get-tuple-element.22.refs_0_), channel_id=1, source_target_pairs={{0,8},{4,12},{8,0},{12,4},{1,9},{5,13},{9,1},{13,5},{2,10},{6,14},... | collective-permute-start | bytes 288776 | tf_op jit(solution)/shard_map/ppermute | solution.py:393
  25.2 8.4 %collective-permute-start.9 = (bf16[376,128]{1,0:T(8,128)(2,1)S(1)}, bf16[376,128]{1,0:T(8,128)(2,1)S(1)}, u32[]{:S(2)}, u32[]{:S(2)}) collective-permute-start(bf16[376,128]{1,0:T(8,128)(2,1)S(1)} %get-tuple-element.22.refs_0_), channel_id=1, source_target_pairs={{0,4},{4,0},{8,12},{12,8},{1,5},{5,1},{9,13},{13,9},{2,6},{6,2},{1... | collective-permute-start | bytes 288776 | tf_op jit(solution)/shard_map/ppermute | solution.py:393
  34.4 7.9 %collective-permute-start.12 = (bf16[4,2,48,384]{3,2,1,0:T(8,128)(2,1)S(1)}, bf16[4,2,48,384]{3,2,1,0:T(8,128)(2,1)S(1)}, u32[]{:S(2)}, u32[]{:S(2)}) collective-permute-start(bf16[4,2,48,384]{3,2,1,0:T(8,128)(2,1)S(1)} %get-tuple-element.25.last_ref), channel_id=1, source_target_pairs={{0,1},{1,0},{2,3},{3,2},{4,5},{5,4},{6,7},{7,6},{8,9},{9,8},{10,11... | collective-permute-start | bytes 884744 | tf_op jit(solution)/shard_map/ppermute | solution.py:381
  36.1 7.2 %collective-permute-start.8 = (bf16[248,128]{1,0:T(8,128)(2,1)S(1)}, bf16[248,128]{1,0:T(8,128)(2,1)S(1)}, u32[]{:S(2)}, u32[]{:S(2)}) collective-permute-start(bf16[248,128]{1,0:T(8,128)(2,1)S(1)} %shard_map.77.refs_0_), channel_id=1, source_target_pairs={{0,12},{4,8},{8,4},{12,0},{1,13},{5,9},{9,5},{13,1},{2,14},{6,10},... | collective-permute-start | bytes 190472 | tf_op jit(solution)/shard_map/ppermute | solution.py:393
  38.8 6.3 %collective-permute-start.7 = (bf16[248,128]{1,0:T(8,128)(2,1)S(1)}, bf16[248,128]{1,0:T(8,128)(2,1)S(1)}, u32[]{:S(2)}, u32[]{:S(2)}) collective-permute-start(bf16[248,128]{1,0:T(8,128)(2,1)S(1)} %shard_map.77.refs_0_), channel_id=1, source_target_pairs={{0,8},{4,12},{8,0},{12,4},{1,9},{5,13},{9,1},{13,5},{2,10},{6,14},... | collective-permute-start | bytes 190472 | tf_op jit(solution)/shard_map/ppermute | solution.py:393
  38.8 6.3 %collective-permute-start.6 = (bf16[248,128]{1,0:T(8,128)(2,1)S(1)}, bf16[248,128]{1,0:T(8,128)(2,1)S(1)}, u32[]{:S(2)}, u32[]{:S(2)}) collective-permute-start(bf16[248,128]{1,0:T(8,128)(2,1)S(1)} %shard_map.77.refs_0_), channel_id=1, source_target_pairs={{0,4},{4,0},{8,12},{12,8},{1,5},{5,1},{9,13},{13,9},{2,6},{6,2},{1... | collective-permute-start | bytes 190472 | tf_op jit(solution)/shard_map/ppermute | solution.py:393
  43.3 13.3 %copy-start.1 = (bf16[5,1,40,384]{3,2,1,0:T(8,128)(2,1)S(1)}, bf16[5,1,40,384]{3,2,1,0:T(8,128)(2,1)}, u32[]{:S(2)}) copy-start(bf16[5,1,40,384]{3,2,1,0:T(8,128)(2,1)} %param.7) | copy-start | bytes 460804
  47.3 5.1 %collective-permute-start.13 = (bf16[56,384]{1,0:T(8,128)(2,1)S(1)}, bf16[56,384]{1,0:T(8,128)(2,1)S(1)}, u32[]{:S(2)}, u32[]{:S(2)}) collective-permute-start(bf16[56,384]{1,0:T(8,128)(2,1)S(1)} %get-tuple-element.27), channel_id=1, source_target_pairs={{0,2},{1,0},{2,3},{3,1},{4,6},{5,4},{6,7},{7,5},{8,10},{9,8},{10,1... | collective-permute-start | bytes 129032 | tf_op jit(solution)/shard_map/ppermute | solution.py:381
  48.5 3.9 %collective-permute-start.14 = (bf16[56,384]{1,0:T(8,128)(2,1)S(1)}, bf16[56,384]{1,0:T(8,128)(2,1)S(1)}, u32[]{:S(2)}, u32[]{:S(2)}) collective-permute-start(bf16[56,384]{1,0:T(8,128)(2,1)S(1)} %get-tuple-element.28), channel_id=1, source_target_pairs={{0,6},{1,4},{2,7},{3,5},{4,2},{5,0},{6,3},{7,1},{8,14},{9,12},{10,... | collective-permute-start | bytes 129032 | tf_op jit(solution)/shard_map/ppermute | solution.py:381
  48.9 4.6 %collective-permute-start.15 = (bf16[56,384]{1,0:T(8,128)(2,1)S(1)}, bf16[56,384]{1,0:T(8,128)(2,1)S(1)}, u32[]{:S(2)}, u32[]{:S(2)}) collective-permute-start(bf16[56,384]{1,0:T(8,128)(2,1)S(1)} %get-tuple-element.29), channel_id=1, source_target_pairs={{0,10},{1,8},{2,11},{3,9},{4,14},{5,12},{6,15},{7,13},{8,2},{9,0},... | collective-permute-start | bytes 129032 | tf_op jit(solution)/shard_map/ppermute | solution.py:381
  51.4 5.2 %collective-permute-start.16 = (bf16[56,384]{1,0:T(8,128)(2,1)S(1)}, bf16[56,384]{1,0:T(8,128)(2,1)S(1)}, u32[]{:S(2)}, u32[]{:S(2)}) collective-permute-start(bf16[56,384]{1,0:T(8,128)(2,1)S(1)} %get-tuple-element.30), channel_id=1, source_target_pairs={{0,14},{1,12},{2,15},{3,13},{4,10},{5,8},{6,11},{7,9},{8,6},{9,4},... | collective-permute-start | bytes 129032 | tf_op jit(solution)/shard_map/ppermute | solution.py:381
